TPU v7x, 128 devices: a whole 4x4x4 slice. The times are simulated.
128 devices in a mesh: lift: 8 (over z, x_lo), tile: 16 (over x_hi, y, core).
Axes of the slice: x: 4 (x_hi: 2, x_lo: 2; x = x_hi * 2 + x_lo), y: 4, z: 4, core: 2. Of those that a mesh axis runs over, the one named last changes fastest.
Arguments:
- oxygen: float32 [8, 16, 16, 256, 256], P('lift', None, 'tile'), may hold values from 0 to 1
- velocity: float32 [8, 16, 16, 256, 256], P('lift', None, 'tile'), may hold values from 0.2 to 1
- spacing: float32 [8], P('lift'), may hold values from 1 to 2
- inlets: int32 [8, 16, 256, 256], P('lift', 'tile'), may hold values 0 or 1
- proj_x: float32 [8, 16, 4, 256, 256], P('lift', 'tile'), may hold values from -1 to 1
- proj_y: float32 [8, 16, 4, 256, 256], P('lift', 'tile'), may hold values from -1 to 1
- sources: int32 [8, 16, 4], P('lift', 'tile'), may hold values from 0 to 15, as said below
Outputs:
- oxygen_next: float32 [8, 16, 16, 256, 256], P('lift', None, 'tile')
Inputs may be any that keep to these rules, and one draw needn't show every extreme that they name: sources[l, t, 0] is the tile (t + 8) % 16; the other entries may be any tile of the lift below; entries of lift 0 are not used.
All inputs are finite; a program needn't handle non-finite values. No bound on the sum of `inlets` on one device may be relied on, other than what follows from the above.
Results may differ from a plain program's by a relative error of at most 0.0001.
Values sent between devices are 32-bit elements; how exact they have to be, the bound alone decides.
No kernel may reach another device: no remote copies, remote signals or barrier semaphores. Data moves between devices by JAX's collectives and lax.ppermute only.
A program may use at most 128 MiB of HBM per device.

v0:
```python
import jax
import jax.numpy as jnp
from jax import lax
from jax.sharding import PartitionSpec as P

TCOL = 4
STEPS = 2


TIME_STEP = 0.1
INJECT_RATE = 2.0
AMBIENT = 1.0
HIGHEST = lax.Precision.HIGHEST


def shifted(value, axis, steps):
    count = lax.axis_size(axis)
    initial, last = (max(0, -steps), min(count, count - steps))
    return lax.ppermute(value, axis, [(source, source + steps) for source in range(initial, last)])


def on_device(oxygen, velocity, spacing, inlets, proj_x, proj_y, sources):
    field = oxygen[0, :, 0]
    speed = velocity[0, :, 0]
    inverse = 1.0 / (spacing[0] * spacing[0])
    inject = INJECT_RATE * inlets[0, 0].astype(jnp.float32)
    blocks_x = proj_x[0, 0]
    blocks_y = proj_y[0, 0]
    listed = sources[0, 0]
    tile_count = lax.axis_size("tile")
    tile_index = lax.axis_index("tile")
    lift_index = lax.axis_index("lift")
    is_top = lift_index == lax.axis_size("lift") - 1
    column = tile_index % TCOL
    onehot = (listed[:, None] == jnp.arange(tile_count, dtype=jnp.int32)[None, :]).astype(
        jnp.float32
    )
    depth = field.shape[0]
    for step_index in range(STEPS):
        rims = [
            (TCOL, field[:, -1, :]),
            (-TCOL, field[:, 0, :]),
            (1, field[:, :, -1]),
            (-1, field[:, :, 0]),
        ]
        arrived = []
        for offset, rim in rims:
            arrived.append(shifted(rim, "tile", offset))
        low_y = jnp.where(column == 0, 0.0, arrived[2])
        high_y = jnp.where(column == TCOL - 1, 0.0, arrived[3])
        beside_x = jnp.concatenate([arrived[0][:, None, :], field, arrived[1][:, None, :]], axis=1)
        beside_y = jnp.concatenate([low_y[:, :, None], field, high_y[:, :, None]], axis=2)
        beside_all = (
            beside_x[:, 2:, :] + beside_x[:, :-2, :] + beside_y[:, :, 2:] + beside_y[:, :, :-2]
        )
        lapl = (beside_all - 4.0 * field) * inverse
        top_plane = field[depth - 1]
        bottom_plane = field[0]
        pieces = jnp.einsum("kba,bc,kcd->kad", blocks_x, bottom_plane, blocks_y, precision=HIGHEST)
        outgoing = jnp.einsum("ks,kad->sad", onehot, pieces, precision=HIGHEST)
        whole_tops = lax.all_gather(top_plane[None], "tile", axis=0, tiled=True)
        tops_below = shifted(whole_tops, "lift", 1)
        terms_above = shifted(outgoing, "lift", -1)
        summed = lax.psum_scatter(terms_above, "tile", scatter_dimension=0, tiled=True)[0]
        picked = jnp.take(tops_below, listed, axis=0)
        ghost_below = jnp.einsum("kab,kbc,kdc->ad", blocks_x, picked, blocks_y, precision=HIGHEST)
        ghost_above = jnp.where(is_top, AMBIENT, summed)
        stacked = jnp.concatenate([ghost_below[None], field, ghost_above[None]], axis=0)
        under = stacked[:-2]
        over = stacked[2:]
        change = lapl + over + under - 2.0 * field - speed * (field - under)
        change = change.at[0].add(inject * (1.0 - field[0]))
        field = field + TIME_STEP * change
    return field[None, :, None]


def solution(mesh):
    return jax.shard_map(
        on_device,
        mesh=mesh,
        in_specs=(
            P("lift", None, "tile", None, None),
            P("lift", None, "tile", None, None),
            P("lift"),
            P("lift", "tile", None, None),
            P("lift", "tile", None, None, None),
            P("lift", "tile", None, None, None),
            P("lift", "tile", None),
        ),
        out_specs=P("lift", None, "tile", None, None),
        check_vma=False,
    )
```

profile of v0, /device:TPU:6, one launch (start us, length us, event | category | flops | bytes accessed | tf_op | source)
XLA Modules:
  0.0 525.5 jit_solution(16741836837715238766)
XLA Ops:
  8.6 2.8 fusion.34
  12.5 3.9 fusion.38
  16.4 5.3 %copy.131 = f32[16,256,256]{1,2,0:T(8,128)} copy(f32[16,256,256]{2,0,1:T(8,128)} %fusion.38) | data formatting | bytes 8388608 | tf_op jit(solution)/shard_map/ks,kad->sad/dot_general | solution.py:60
  21.6 2.7 collective-permute-start.4
  24.4 104.8 %collective-permute-done.4 = f32[16,256,256]{1,2,0:T(8,128)} collective-permute-done((f32[16,256,256]{1,2,0:T(8,128)}, f32[16,256,256]{1,2,0:T(8,128)}, u32[]{:S(2)}, u32[]{:S(2)}) %collective-permute-start.4) | collective-permute-done | bytes 4194336 | tf_op jit(solution)/shard_map/ppermute | solution.py:19
  129.3 3.1 collective-permute-start.5
  132.4 4.9 fusion.61
  137.3 2.3 copy.162
  139.6 4.4 collective-permute-start.2
  148.3 5.5 %copy.121 = f32[1,16,1,256,256]{3,4,1,2,0:T(8,128)} copy(f32[1,16,1,256,256]{4,3,2,1,0:T(8,128)} %param.13) | data formatting | bytes 8388608 | tf_op args[0]
  153.8 4.0 slice_reduce_fusion.3
  157.8 3.9 collective-permute-start
  161.7 3.6 collective-permute-start.1
  165.4 5.4 %copy.135 = f32[1,16,1,256,256]{3,4,1,2,0:T(8,128)} copy(f32[1,16,1,256,256]{4,3,2,1,0:T(8,128)} %param.14) | data formatting | bytes 8388608 | tf_op args[1]
  172.5 64.1 %collective-permute-done.2 = f32[16,256]{1,0:T(8,128)S(1)} collective-permute-done((f32[16,256]{1,0:T(8,128)S(1)}, f32[16,256]{1,0:T(8,128)S(1)}, u32[]{:S(2)}, u32[]{:S(2)}) %collective-permute-start.2) | collective-permute-done | bytes 16416 | tf_op jit(solution)/shard_map/ppermute | solution.py:19
  236.6 2.8 collective-permute-done.3
  244.4 3.8 gather_fusion
  248.2 2.7 fusion.32
  251.9 7.6 %fusion.14 = f32[16,256,256]{1,2,0:T(8,128)S(1)} fusion(f32[16,256,256]{1,2,0:T(8,128)S(1)} %bitcast.85, f32[1,256,256]{1,2,0:T(8,128)S(1)} %convolution_bitcast_fusion.1, f32[1,256,256]{1,2,0:T(8,128)S(1)} %broadcast_select_fusion.1, f32[16,256,1]{1,2,0:T(1,128)S(1)} %copy.127, f32[16,256,1]{1,2,0:T(1,128)S(1)} %copy.125, f32[16,1,256]{1,2,0:T(8,128)} %copy.123, ...), kind=kLoop, calls=%fused_computation.23 | loop fusion | flops 19922944 | bytes 13172740 | tf_op jit(solution)/shard_map/sub | solution.py:71
  264.1 2.8 fusion.30
  268.1 3.9 fusion.36
  272.0 5.3 %copy.144 = f32[16,256,256]{1,2,0:T(8,128)} copy(f32[16,256,256]{2,0,1:T(8,128)} %fusion.36) | data formatting | bytes 8388608 | tf_op jit(solution)/shard_map/ks,kad->sad/dot_general | solution.py:60
  279.2 103.0 %collective-permute-done.10 = f32[16,256,256]{1,2,0:T(8,128)} collective-permute-done((f32[16,256,256]{1,2,0:T(8,128)}, f32[16,256,256]{1,2,0:T(8,128)}, u32[]{:S(2)}, u32[]{:S(2)}) %collective-permute-start.10) | collective-permute-done | bytes 4194336 | tf_op jit(solution)/shard_map/ppermute | solution.py:19
  387.3 3.9 slice_reduce_fusion.1
  391.2 7.0 %collective-permute-start.6 = (f32[16,256]{1,0:T(8,128)S(1)}, f32[16,256]{1,0:T(8,128)S(1)}, u32[]{:S(2)}, u32[]{:S(2)}) collective-permute-start(f32[16,256]{1,0:T(8,128)S(1)} %get-tuple-element.30), channel_id=1, source_target_pairs={{4,0},{5,1},{6,2},{7,3},{8,4},{9,5},{10,6},{11,7},{12,8},{13,9},{1... | collective-permute-start | bytes 49160 | tf_op jit(solution)/shard_map/ppermute | solution.py:19
  400.2 7.7 %collective-permute-start.8 = (f32[16,256]{1,0:T(8,128)S(1)}, f32[16,256]{1,0:T(8,128)S(1)}, u32[]{:S(2)}, u32[]{:S(2)}) collective-permute-start(f32[16,256]{1,0:T(8,128)S(1)} %bitcast.93), channel_id=1, source_target_pairs={{1,0},{2,1},{3,2},{4,3},{5,4},{6,5},{7,6},{8,7},{9,8},{10,9},{11,1... | collective-permute-start | bytes 49160 | tf_op jit(solution)/shard_map/ppermute | solution.py:19
  407.9 82.9 %collective-permute-done.9 = f32[16,256]{1,0:T(8,128)S(1)} collective-permute-done((f32[16,256]{1,0:T(8,128)S(1)}, f32[16,256]{1,0:T(8,128)S(1)}, u32[]{:S(2)}, u32[]{:S(2)}) %collective-permute-start.9) | collective-permute-done | bytes 16416 | tf_op jit(solution)/shard_map/ppermute | solution.py:19
  495.9 3.8 gather_fusion.1
  499.7 2.7 fusion.28
  503.4 7.6 %fusion.3 = f32[16,256,256]{1,2,0:T(8,128)S(1)} fusion(f32[16,256,256]{1,2,0:T(8,128)S(1)} %copy-done.2, f32[1,256,256]{1,2,0:T(8,128)S(1)} %convolution_bitcast_fusion, f32[1,256,256]{1,2,0:T(8,128)S(1)} %broadcast_select_fusion, f32[16,256,1]{1,2,0:T(1,128)S(1)} %broadcast_in_dim.70, f32[16,256,1]{1,2,0:T(1,128)S(1)} %copy.140, f32[16,1,256]{1,2,0:T(8,128)} %copy.138, ...), kind=kLoop, calls=%fused_computation.6 | loop fusion | flops 19922944 | bytes 13172740 | tf_op jit(solution)/shard_map/sub | solution.py:71
  511.1 2.5 add_bitcast_fusion
  513.6 5.3 %copy.149 = f32[1,16,1,256,256]{4,3,2,1,0:T(8,128)} copy(f32[1,16,1,256,256]{3,4,1,2,0:T(8,128)} %add_bitcast_fusion) | data formatting | bytes 8388608 | tf_op jit(solution)/shard_map/broadcast_in_dim | solution.py:74
  (71 shorter events, 35.2 us)
Async XLA Ops:
  6.5 2.0 copy-start
  6.5 4.8 copy-start.4
  6.5 6.0 %copy-start.6 = (s32[1,1,4]{2,1,0:T(1,128)S(1)}, s32[1,1,4]{2,1,0:T(1,128)}, u32[]{:S(2)}) copy-start(s32[1,1,4]{2,1,0:T(1,128)} %param.19) | copy-start | bytes 52
  6.5 122.7 %all-gather.6.cloned.1.call-start = ((), (), s32[]{:S(2)}) async-start(), calls=%async_computation.5 | async-start | bytes 4456448 | tf_op jit(solution)/shard_map/all_gather | solution.py:61
  8.5 235.0 %reduce-scatter.3.cloned.1.call-start = ((), (), s32[]{:S(2)}) async-start(), calls=%async_computation.2 | async-start | bytes 4456448 | tf_op jit(solution)/shard_map/reduce_scatter | solution.py:64
  21.6 107.5 %collective-permute-start.4 = (f32[16,256,256]{1,2,0:T(8,128)}, f32[16,256,256]{1,2,0:T(8,128)}, u32[]{:S(2)}, u32[]{:S(2)}) collective-permute-start(f32[16,256,256]{1,2,0:T(8,128)} %copy.131), channel_id=1, source_target_pairs={{16,0},{32,16},{48,32},{64,48},{80,64},{96,80},{112,96},{17,1},{33... | collective-permute-start | bytes 12582920 | tf_op jit(solution)/shard_map/ppermute | solution.py:19
  129.2 253.0 %all-gather.4.cloned.1.call-start = ((), (), s32[]{:S(2)}) async-start(), calls=%async_computation.4 | async-start | bytes 4456448 | tf_op jit(solution)/shard_map/all_gather | solution.py:61
  129.3 115.2 %collective-permute-start.5 = (f32[16,256,256]{2,1,0:T(8,128)}, f32[16,256,256]{2,1,0:T(8,128)}, u32[]{:S(2)}, u32[]{:S(2)}) collective-permute-start(f32[16,256,256]{2,1,0:T(8,128)} %bitcast.97), channel_id=1, source_target_pairs={{0,16},{16,32},{32,48},{48,64},{64,80},{80,96},{96,112},{1,17},{17... | collective-permute-start | bytes 12582920 | tf_op jit(solution)/shard_map/ppermute | solution.py:19
  139.6 97.0 %collective-permute-start.2 = (f32[16,256]{1,0:T(8,128)S(1)}, f32[16,256]{1,0:T(8,128)S(1)}, u32[]{:S(2)}, u32[]{:S(2)}) collective-permute-start(f32[16,256]{1,0:T(8,128)S(1)} %bitcast.89), channel_id=1, source_target_pairs={{1,0},{2,1},{3,2},{4,3},{5,4},{6,5},{7,6},{8,7},{9,8},{10,9},{11,1... | collective-permute-start | bytes 49160 | tf_op jit(solution)/shard_map/ppermute | solution.py:19
  146.4 93.1 %collective-permute-start.3 = (f32[16,256]{1,0:T(8,128)S(1)}, f32[16,256]{1,0:T(8,128)S(1)}, u32[]{:S(2)}, u32[]{:S(2)}) collective-permute-start(f32[16,256]{1,0:T(8,128)S(1)} %bitcast.90), channel_id=1, source_target_pairs={{0,1},{1,2},{2,3},{3,4},{4,5},{5,6},{6,7},{7,8},{8,9},{9,10},{10,1... | collective-permute-start | bytes 49160 | tf_op jit(solution)/shard_map/ppermute | solution.py:19
  157.8 81.7 %collective-permute-start = (f32[16,256]{1,0:T(8,128)S(1)}, f32[16,256]{1,0:T(8,128)S(1)}, u32[]{:S(2)}, u32[]{:S(2)}) collective-permute-start(f32[16,256]{1,0:T(8,128)S(1)} %get-tuple-element.32), channel_id=1, source_target_pairs={{4,0},{5,1},{6,2},{7,3},{8,4},{9,5},{10,6},{11,7},{12,8},{13,9},{1... | collective-permute-start | bytes 49160 | tf_op jit(solution)/shard_map/ppermute | solution.py:19
  161.7 79.8 %collective-permute-start.1 = (f32[16,256]{1,0:T(8,128)S(1)}, f32[16,256]{1,0:T(8,128)S(1)}, u32[]{:S(2)}, u32[]{:S(2)}) collective-permute-start(f32[16,256]{1,0:T(8,128)S(1)} %get-tuple-element.33), channel_id=1, source_target_pairs={{0,4},{1,5},{2,6},{3,7},{4,8},{5,9},{6,10},{7,11},{8,12},{9,13},{1... | collective-permute-start | bytes 49160 | tf_op jit(solution)/shard_map/ppermute | solution.py:19
  165.4 6.9 %copy-start.5 = (s32[1,1,256,256]{3,2,1,0:T(8,128)S(1)}, s32[1,1,256,256]{3,2,1,0:T(8,128)}, u32[]{:S(2)}) copy-start(s32[1,1,256,256]{3,2,1,0:T(8,128)} %param.16) | copy-start | bytes 786436
  248.2 3.7 copy-start.3
  261.2 2.0 copy-start.1
  264.1 230.8 %reduce-scatter.5.cloned.1.call-start = ((), (), s32[]{:S(2)}) async-start(), calls=%async_computation.3 | async-start | bytes 4456448 | tf_op jit(solution)/shard_map/reduce_scatter | solution.py:64
  277.3 104.9 %collective-permute-start.10 = (f32[16,256,256]{1,2,0:T(8,128)}, f32[16,256,256]{1,2,0:T(8,128)}, u32[]{:S(2)}, u32[]{:S(2)}) collective-permute-start(f32[16,256,256]{1,2,0:T(8,128)} %copy.144), channel_id=1, source_target_pairs={{16,0},{32,16},{48,32},{64,48},{80,64},{96,80},{112,96},{17,1},{33... | collective-permute-start | bytes 12582920 | tf_op jit(solution)/shard_map/ppermute | solution.py:19
  382.2 113.7 %collective-permute-start.11 = (f32[16,256,256]{2,1,0:T(8,128)}, f32[16,256,256]{2,1,0:T(8,128)}, u32[]{:S(2)}, u32[]{:S(2)}) collective-permute-start(f32[16,256,256]{2,1,0:T(8,128)} %all-gather.4.cloned.1.call-done), channel_id=1, source_target_pairs={{0,16},{16,32},{32,48},{48,64},{64,80},{80,96},{96,112},{1,17},{17... | collective-permute-start | bytes 12582920 | tf_op jit(solution)/shard_map/ppermute | solution.py:19
  385.1 105.7 %collective-permute-start.9 = (f32[16,256]{1,0:T(8,128)S(1)}, f32[16,256]{1,0:T(8,128)S(1)}, u32[]{:S(2)}, u32[]{:S(2)}) collective-permute-start(f32[16,256]{1,0:T(8,128)S(1)} %bitcast.94), channel_id=1, source_target_pairs={{0,1},{1,2},{2,3},{3,4},{4,5},{5,6},{6,7},{7,8},{8,9},{9,10},{10,1... | collective-permute-start | bytes 49160 | tf_op jit(solution)/shard_map/ppermute | solution.py:19
  391.2 99.6 %collective-permute-start.6 = (f32[16,256]{1,0:T(8,128)S(1)}, f32[16,256]{1,0:T(8,128)S(1)}, u32[]{:S(2)}, u32[]{:S(2)}) collective-permute-start(f32[16,256]{1,0:T(8,128)S(1)} %get-tuple-element.30), channel_id=1, source_target_pairs={{4,0},{5,1},{6,2},{7,3},{8,4},{9,5},{10,6},{11,7},{12,8},{13,9},{1... | collective-permute-start | bytes 49160 | tf_op jit(solution)/shard_map/ppermute | solution.py:19
  398.3 94.5 %collective-permute-start.7 = (f32[16,256]{1,0:T(8,128)S(1)}, f32[16,256]{1,0:T(8,128)S(1)}, u32[]{:S(2)}, u32[]{:S(2)}) collective-permute-start(f32[16,256]{1,0:T(8,128)S(1)} %get-tuple-element.31), channel_id=1, source_target_pairs={{0,4},{1,5},{2,6},{3,7},{4,8},{5,9},{6,10},{7,11},{8,12},{9,13},{1... | collective-permute-start | bytes 49160 | tf_op jit(solution)/shard_map/ppermute | solution.py:19
  400.2 94.6 %collective-permute-start.8 = (f32[16,256]{1,0:T(8,128)S(1)}, f32[16,256]{1,0:T(8,128)S(1)}, u32[]{:S(2)}, u32[]{:S(2)}) collective-permute-start(f32[16,256]{1,0:T(8,128)S(1)} %bitcast.93), channel_id=1, source_target_pairs={{1,0},{2,1},{3,2},{4,3},{5,4},{6,5},{7,6},{8,7},{9,8},{10,9},{11,1... | collective-permute-start | bytes 49160 | tf_op jit(solution)/shard_map/ppermute | solution.py:19
  499.7 3.7 copy-start.2
Sparse Core Ops, SparseCore 0:
  9.8 67.6 all-gather.5
  129.3 93.8 reduce-scatter.2
  264.2 66.6 all-gather.3
  382.3 92.8 reduce-scatter.4
where the time goes:
time: 527 us; the launch traced here: 526 us
  waiting for transfers between devices  358 us (68%)
  local copies, waits for them, and re-layouts  66.6 us (13%)
  starting transfers between devices  42.4 us (8%)
  matrix products  23 us (4%)
  other arithmetic  21.5 us (4%)
  between operations  14.3 us (3%)
    ppermute x12, waiting for transfers between devices, shifted(): lax.ppermute(value, axis, [(source, source + steps) for source in range(i...  358 us
    ppermute x12, starting transfers between devices, shifted(): lax.ppermute(value, axis, [(source, source + steps) for source in range(i...  42.3 us
    unnamed x22, local copies, waits for them, and re-layouts  18.6 us
    sub x2, other arithmetic, on_device(): change = lapl + over + under - 2.0 * field - speed * (field - under)  15.3 us
    dot_general x2, local copies, waits for them, and re-layouts, on_device(): outgoing = jnp.einsum('ks,kad->sad', onehot, pieces, precision=HIGHEST)  10.6 us
  transfers between devices with their start and end apart: 16, of which 5 were waited for; matrix products, arithmetic and copies ran while one was open for 13% of the time, Pallas kernels for 0%

commit v1 on v0

v1 whole, which is shorter than its diff:
```python
import functools

import jax
import jax.numpy as jnp
from jax import lax
from jax.experimental import pallas as pl
from jax.experimental.pallas import tpu as pltpu
from jax.sharding import PartitionSpec as P

TCOL = 4
STEPS = 2
LIFTS = 8
TILES = 16
NZ = 16
W = 256
TIME_STEP = 0.1
INJECT_RATE = 2.0
AMBIENT = 1.0
F32 = jnp.float32
BF16 = jnp.bfloat16
MIB = 1 << 20


def tile_of(x_half, y, core):
    return x_half * 8 + (y % 4) * 2 + core


def coords(tile):
    return tile // 8, (tile // 2) % 4, tile % 2


def along_y(steps):
    return [(t, tile_of(coords(t)[0], coords(t)[1] + steps, coords(t)[2])) for t in range(TILES)]


OTHER_CORE = [(t, t ^ 1) for t in range(TILES)]


def to_lift(steps, flip):
    pairs = []
    for lift in range(LIFTS):
        if 0 <= lift + steps < LIFTS:
            for t in range(TILES):
                pairs.append((lift * TILES + t, (lift + steps) * TILES + (t ^ (8 if flip else 0))))
    return pairs


def split(value):
    high = value.astype(BF16)
    return high, (value - high.astype(F32)).astype(BF16)


def product(a, b, dims):
    def one(u, v):
        return lax.dot_general(u, v, (dims, ((), ())), preferred_element_type=F32)

    return one(a[0], b[0]) + (one(a[0], b[1]) + one(a[1], b[0]))


def relative(table, k):
    source, tile = table[k], table[4]
    x_step = ((source >> 3) ^ (tile >> 3)) & 1
    y_step = ((source >> 1) - (tile >> 1)) & 3
    core_step = (source ^ tile) & 1
    return core_step, y_step, x_step


def pieces_kernel(table, px, py, bottom, first, rest, keep):
    first[...] = jnp.zeros_like(first)
    rest[...] = jnp.zeros_like(rest)
    keep[...] = jnp.zeros_like(keep)
    plane = split(bottom[...])
    for k in range(4):
        left = product(split(px[k]), plane, ((0,), (0,)))
        piece = product(split(left), split(py[k]), ((1,), (0,)))
        core_step, y_step, x_step = relative(table, k)

        @pl.when(core_step == 0)
        def _():
            slot = y_step * 2 + x_step
            keep[slot] = keep[slot] + piece

        @pl.when((core_step == 1) & (y_step == 2))
        def _():
            first[x_step] = first[x_step] + piece

        @pl.when((core_step == 1) & (y_step != 2))
        def _():
            slot = jnp.minimum(y_step, 2) * 2 + x_step
            rest[slot] = rest[slot] + piece


def full(shape):
    return pl.BlockSpec(shape, lambda *_: (0,) * len(shape))


SMEM_SPEC = pl.BlockSpec(memory_space=pltpu.SMEM)


def plane_shape(count=None):
    return jax.ShapeDtypeStruct((W, W) if count is None else (count, W, W), F32)


def pieces_of(table, px, py, bottom):
    return pl.pallas_call(
        pieces_kernel,
        out_shape=(plane_shape(2), plane_shape(6), plane_shape(8)),
        in_specs=[SMEM_SPEC] + [pl.BlockSpec(memory_space=pltpu.VMEM)] * 3,
        out_specs=[pl.BlockSpec(memory_space=pltpu.VMEM)] * 3,
        compiler_params=pltpu.CompilerParams(vmem_limit_bytes=24 * MIB),
        cost_estimate=pl.CostEstimate(flops=8 * 6 * W**3, bytes_accessed=7 * MIB, transcendentals=0),
        name="pieces",
    )(table, px, py, bottom)


def below_kernel(table, px, py, speed, field, *refs):
    tops, (out, bottom, picked, sems) = refs[:16], refs[16:]
    for k in range(4):
        core_step, y_step, x_step = relative(table, k)
        slot = core_step * 8 + y_step * 2 + x_step
        for j in range(16):

            @pl.when(slot == j)
            def _():
                pltpu.make_async_copy(tops[j], picked.at[k], sems.at[k]).start()

    total = jnp.zeros((W, W), F32)
    for k in range(4):
        pltpu.make_async_copy(tops[0], picked.at[k], sems.at[k]).wait()
        left = product(split(px[k]), split(picked[k]), ((1,), (0,)))
        total = total + product(split(left), split(py[k]), ((1,), (1,)))
    new = field[0] + TIME_STEP * (total + speed[0] * total)
    out[0] = new
    bottom[...] = new


def below_update(table, px, py, speed, field, tops):
    plane0 = pl.BlockSpec((1, W, W), lambda i: (0, 0, 0))
    return pl.pallas_call(
        below_kernel,
        grid=(1,),
        out_shape=(plane_shape(NZ), plane_shape()),
        in_specs=[SMEM_SPEC, full((4, W, W)), full((4, W, W)), plane0, plane0]
        + [pl.BlockSpec(memory_space=pl.ANY)] * 16,
        out_specs=[plane0, full((W, W))],
        scratch_shapes=[pltpu.VMEM((4, W, W), F32), pltpu.SemaphoreType.DMA((4,))],
        input_output_aliases={4: 0},
        compiler_params=pltpu.CompilerParams(vmem_limit_bytes=24 * MIB),
        cost_estimate=pl.CostEstimate(flops=8 * 6 * W**3, bytes_accessed=5 * MIB, transcendentals=0),
        name="below",
    )(table, px, py, speed, field, *tops)


def above_kernel(table, straight, flipped, field, out, top):
    ghost = straight[...] + flipped[...]
    ghost = jnp.where(table[5] == 1, AMBIENT, ghost)
    new = field[0] + TIME_STEP * ghost
    out[0] = new
    top[...] = new


def above_update(table, straight, flipped, field):
    last = pl.BlockSpec((1, W, W), lambda i: (NZ - 1, 0, 0))
    return pl.pallas_call(
        above_kernel,
        grid=(1,),
        out_shape=(plane_shape(NZ), plane_shape()),
        in_specs=[SMEM_SPEC, full((W, W)), full((W, W)), last],
        out_specs=[last, full((W, W))],
        input_output_aliases={3: 0},
        compiler_params=pltpu.CompilerParams(vmem_limit_bytes=8 * MIB),
        cost_estimate=pl.CostEstimate(flops=3 * W * W, bytes_accessed=MIB, transcendentals=0),
        name="above",
    )(table, straight, flipped, field)


def rims_kernel(field, row_low, row_high, col_low, col_high, low, high):
    z = pl.program_id(0)
    plane = field[0]
    row_low[pl.ds(z, 1), :] = plane[0:1, :]
    row_high[pl.ds(z, 1), :] = plane[W - 1 : W, :]
    lane = lax.broadcasted_iota(jnp.int32, (W, 128), 1)

    @pl.when(z == 0)
    def _():
        low[...] = jnp.zeros_like(low)
        high[...] = jnp.zeros_like(high)

    low[...] = jnp.where(lane == z, plane[:, 0:1], low[...])
    high[...] = jnp.where(lane == z, plane[:, W - 1 : W], high[...])

    @pl.when(z == NZ - 1)
    def _():
        col_low[...] = low[...].T[:NZ]
        col_high[...] = high[...].T[:NZ]


def rims_of(field):
    rim = jax.ShapeDtypeStruct((NZ, W), F32)
    return pl.pallas_call(
        rims_kernel,
        grid=(NZ,),
        out_shape=(rim,) * 4,
        in_specs=[pl.BlockSpec((1, W, W), lambda z: (z, 0, 0))],
        out_specs=[full((NZ, W))] * 4,
        scratch_shapes=[pltpu.VMEM((W, 128), F32)] * 2,
        compiler_params=pltpu.CompilerParams(vmem_limit_bytes=8 * MIB),
        cost_estimate=pl.CostEstimate(flops=NZ * W * W, bytes_accessed=4 * MIB, transcendentals=0),
        name="rims",
    )(field)


def stencil_kernel(inverse, here, below, above, speed, inlets, x_low, x_high, y_low, y_high, out, low, high):
    z = pl.program_id(0)

    @pl.when(z == 0)
    def _():
        pad = jnp.zeros((128 - NZ, W), F32)
        low[...] = jnp.concatenate([y_low[...], pad], axis=0).T
        high[...] = jnp.concatenate([y_high[...], pad], axis=0).T

    field = here[0]
    pick = lax.broadcasted_iota(jnp.int32, (W, 128), 1) == z
    col_low = jnp.sum(jnp.where(pick, low[...], 0.0), axis=1, keepdims=True)
    col_high = jnp.sum(jnp.where(pick, high[...], 0.0), axis=1, keepdims=True)
    row = lax.broadcasted_iota(jnp.int32, (W, W), 0)
    lane = lax.broadcasted_iota(jnp.int32, (W, W), 1)
    beside = jnp.where(row == 0, x_low[pl.ds(z, 1), :], pltpu.roll(field, 1, 0))
    beside = beside + jnp.where(row == W - 1, x_high[pl.ds(z, 1), :], pltpu.roll(field, W - 1, 0))
    beside = beside + jnp.where(lane == 0, col_low, pltpu.roll(field, 1, 1))
    beside = beside + jnp.where(lane == W - 1, col_high, pltpu.roll(field, W - 1, 1))
    lapl = (beside - 4.0 * field) * inverse[0]
    under = jnp.where(z == 0, 0.0, below[0])
    over = jnp.where(z == NZ - 1, 0.0, above[0])
    change = lapl + over + under - 2.0 * field - speed[0] * (field - under)
    out[0] = field + TIME_STEP * change

    @pl.when(z == 0)
    def _():
        inject = INJECT_RATE * inlets[...].astype(F32)
        out[0] = out[0] + TIME_STEP * (inject * (1.0 - here[0]))


def stencil(inverse, field, speed, inlets, halos):
    rim = full((NZ, W))
    return pl.pallas_call(
        stencil_kernel,
        grid=(NZ,),
        out_shape=plane_shape(NZ),
        in_specs=[
            SMEM_SPEC,
            pl.BlockSpec((1, W, W), lambda z: (z, 0, 0)),
            pl.BlockSpec((1, W, W), lambda z: (jnp.maximum(z - 1, 0), 0, 0)),
            pl.BlockSpec((1, W, W), lambda z: (jnp.minimum(z + 1, NZ - 1), 0, 0)),
            pl.BlockSpec((1, W, W), lambda z: (z, 0, 0)),
            full((W, W)),
            rim,
            rim,
            rim,
            rim,
        ],
        out_specs=pl.BlockSpec((1, W, W), lambda z: (z, 0, 0)),
        scratch_shapes=[pltpu.VMEM((W, 128), F32)] * 2,
        compiler_params=pltpu.CompilerParams(vmem_limit_bytes=16 * MIB),
        cost_estimate=pl.CostEstimate(flops=16 * NZ * W * W, bytes_accessed=12 * MIB, transcendentals=0),
        name="stencil",
    )(inverse, field, field, field, speed, inlets, *halos)


def exchange_rims(field):
    row_low, row_high, col_low, col_high = rims_of(field)
    x_low = lax.ppermute(row_high, "tile", [(t, t + TCOL) for t in range(TILES - TCOL)])
    x_high = lax.ppermute(row_low, "tile", [(t + TCOL, t) for t in range(TILES - TCOL)])
    inside = [t for t in range(TILES) if t % TCOL < TCOL - 1]
    y_low = lax.ppermute(col_high, "tile", [(t, t + 1) for t in inside])
    y_high = lax.ppermute(col_low, "tile", [(t + 1, t) for t in inside])
    return x_low, x_high, y_low, y_high


def send_y(value, steps):
    return lax.ppermute(value, "tile", along_y(steps))


def send_lift(value, steps, flip):
    return lax.ppermute(value, ("lift", "tile"), to_lift(steps, flip))


def other_core(value):
    return lax.ppermute(value, "tile", OTHER_CORE)


def gather_tops(top):
    mine = send_lift(top, 1, False)
    flip = send_lift(top, 1, True)
    left_mine = send_y(mine, 1)
    right_flip = send_y(flip, -1)
    left_flip = send_y(flip, 1)
    right_mine = send_y(mine, -1)
    far_mine = send_y(left_mine, 1)
    far_flip = send_y(right_flip, -1)
    near = [mine, flip, right_mine, right_flip, far_mine, far_flip, left_mine, left_flip]
    return near + [other_core(value) for value in near]


def reduce_pieces(first, rest, keep):
    first = other_core(first)
    rest = other_core(rest)
    far_mine = send_y(keep[4] + first[0], 1)
    far_flip = send_y(keep[5] + first[1], -1)
    right_flip = send_y(keep[3] + rest[3], 1)
    left_mine = send_y(keep[6] + rest[4], -1)
    right_mine = send_y(keep[2] + rest[2] + far_mine, 1)
    left_flip = send_y(keep[7] + rest[5] + far_flip, -1)
    mine = keep[0] + rest[0] + left_mine + right_mine
    flip = keep[1] + rest[1] + left_flip + right_flip
    return send_lift(mine, -1, False), send_lift(flip, -1, True)


def on_device(oxygen, velocity, spacing, inlets, proj_x, proj_y, sources):
    field = oxygen.reshape(NZ, W, W)
    speed = velocity.reshape(NZ, W, W)
    inlets = inlets.reshape(W, W)
    px = proj_x.reshape(4, W, W)
    py = proj_y.reshape(4, W, W)
    inverse = 1.0 / (spacing * spacing)
    tile = lax.axis_index("tile").astype(jnp.int32)
    is_top = (lax.axis_index("lift") == LIFTS - 1).astype(jnp.int32)
    table = jnp.concatenate([sources.reshape(4) & (TILES - 1), tile[None], is_top[None]])
    top, bottom = field[NZ - 1], field[0]
    for _ in range(STEPS):
        tops = gather_tops(top)
        parts = reduce_pieces(*pieces_of(table, px, py, bottom))
        halos = exchange_rims(field)
        field = stencil(inverse, field, speed, inlets, halos)
        field, bottom = below_update(table, px, py, speed, field, tops)
        field, top = above_update(table, *parts, field)
    return field.reshape(1, NZ, 1, W, W)


def solution(mesh):
    return jax.shard_map(
        on_device,
        mesh=mesh,
        in_specs=(
            P("lift", None, "tile", None, None),
            P("lift", None, "tile", None, None),
            P("lift"),
            P("lift", "tile", None, None),
            P("lift", "tile", None, None, None),
            P("lift", "tile", None, None, None),
            P("lift", "tile", None),
        ),
        out_specs=P("lift", None, "tile", None, None),
        check_vma=False,
    )
```

time: 527 us -> 217 us (0.41)
  waiting for transfers between devices: 358 us -> 73.1 us
  local copies, waits for them, and re-layouts: 66.6 us -> 7.9 us
  starting transfers between devices: 42.4 us -> 92 us
  Pallas kernels: 0 us -> 38.6 us
  matrix products: 23 us -> 0 us
  other arithmetic: 21.5 us -> 1.49 us
  between operations: 14.3 us -> 1.12 us
    ppermute x12 -> x60, waiting for transfers between devices: 358 us -> 73.1 us  [the longest x24 49.1 us: send_y(): return lax.ppermute(value, 'tile', along_y(steps))]
    ppermute x12 -> x60, starting transfers between devices: 42.3 us -> 92 us  [the longest x24 37.8 us: send_y(): return lax.ppermute(value, 'tile', along_y(steps))]
    pallas_call x0 -> x10, Pallas kernels: none -> 38.6 us  [the longest x2 16.3 us: stencil(): pl.pallas_call(stencil_kernel, grid=(NZ,), out_shape=plane_shape(NZ), in_...]
    dot_general x10 -> x0, matrix products: 23 us -> none  [the longest x4 7.82 us: on_device(): jnp.einsum('kba,bc,kcd->kad', blocks_x, bottom_plane, blocks_y, precision...]
    slice x7 -> x0, local copies, waits for them, and re-layouts: 16.6 us -> none  [the longest x2 7.89 us: on_device(): field[:, 0, :]]
    sub x2 -> x0, other arithmetic: 15.3 us -> none  [on_device(): change = lapl + over + under - 2.0 * field - speed * (field - under)]
    broadcast_in_dim x9 -> x0, local copies, waits for them, and re-layouts: 13.3 us -> none  [the longest x1 5.34 us: on_device(): return field[None, :, None]]
    unnamed x22 -> x16, local copies, waits for them, and re-layouts: 18.6 us -> 6.84 us
  transfers between devices with their start and end apart: 16 -> 60, of which waited for: 5 -> 25; matrix products, arithmetic and copies ran while one was open for 13% -> 0% of each run, Pallas kernels for 0% -> 16%
where the time goes in v1:
time: 217 us; the launch traced here: 214 us
  starting transfers between devices  92 us (42%)
  waiting for transfers between devices  73.1 us (34%)
  Pallas kernels  38.6 us (18%)
  local copies, waits for them, and re-layouts  7.9 us (4%)
    ppermute x24, waiting for transfers between devices, send_y(): return lax.ppermute(value, 'tile', along_y(steps))  49.1 us
    ppermute x24, starting transfers between devices, send_y(): return lax.ppermute(value, 'tile', along_y(steps))  37.8 us
    ppermute x8, starting transfers between devices, send_lift(): return lax.ppermute(value, ('lift', 'tile'), to_lift(steps, flip))  23 us
    pallas_call x2, Pallas kernels, stencil(): pl.pallas_call(stencil_kernel, grid=(NZ,), out_shape=plane_shape(NZ), in_...  16.3 us
    ppermute x8, waiting for transfers between devices, send_lift(): return lax.ppermute(value, ('lift', 'tile'), to_lift(steps, flip))  11.3 us
    ppermute x2, starting transfers between devices, exchange_rims(): lax.ppermute(row_high, 'tile', [(t, t + TCOL) for t in range(TILES - TCOL)])  9.97 us
    ppermute x20, starting transfers between devices, other_core(): return lax.ppermute(value, 'tile', OTHER_CORE)  8.8 us
    pallas_call x2, Pallas kernels, below_update(): pl.pallas_call(below_kernel, grid=(1,), out_shape=(plane_shape(NZ), plane...  7.52 us
  transfers between devices with their start and end apart: 60, of which 25 were waited for; matrix products, arithmetic and copies ran while one was open for 0% of the time, Pallas kernels for 16%

profile of v1, /device:TPU:6, one launch (start us, length us, event | category | flops | bytes accessed | tf_op | source)
XLA Modules:
  0.0 214.3 jit_solution(10560390826166944540)
XLA Ops:
  4.3 3.5 %pieces.3 = (f32[2,256,256]{2,1,0:T(8,128)S(1)}, f32[6,256,256]{2,1,0:T(8,128)S(1)}, f32[8,256,256]{2,1,0:T(8,128)S(1)}) custom-call(s32[6]{0:T(128)S(1)} %pad_add_fusion.table, f32[4,256,256]{2,1,0:T(8,128)S(1)} %bitcast.80, f32[4,256,256]{2,1,0:T(8,128)S(1)} %bitcast.84, f32[256,256]{1,0:T(8,128)S(1)} %get-tuple-element.45.bottom), custom_call_target="tpu_custom_call" | custom-call | flops 805306368 | bytes 7340032 | tf_op jit(solution)/shard_map/pieces/pallas_call | solution.py:105
  7.8 4.1 %collective-permute-start.4 = (f32[256,256]{1,0:T(8,128)S(1)}, f32[256,256]{1,0:T(8,128)S(1)}, u32[]{:S(2)}, u32[]{:S(2)}) collective-permute-start(f32[256,256]{1,0:T(8,128)S(1)} %get-tuple-element.46), channel_id=1, source_target_pairs={{0,16},{1,17},{2,18},{3,19},{4,20},{5,21},{6,22},{7,23},{8,24},{9,... | collective-permute-start | bytes 786440 | tf_op jit(solution)/shard_map/ppermute | solution.py:285
  11.9 3.1 %collective-permute-start.5 = (f32[256,256]{1,0:T(8,128)S(1)}, f32[256,256]{1,0:T(8,128)S(1)}, u32[]{:S(2)}, u32[]{:S(2)}) collective-permute-start(f32[256,256]{1,0:T(8,128)S(1)} %get-tuple-element.46), channel_id=1, source_target_pairs={{0,24},{1,25},{2,26},{3,27},{4,28},{5,29},{6,30},{7,31},{8,16},{9,... | collective-permute-start | bytes 786440 | tf_op jit(solution)/shard_map/ppermute | solution.py:285
  15.0 4.9 %collective-permute-done.4.refs_0_ = f32[256,256]{1,0:T(8,128)S(1)} collective-permute-done((f32[256,256]{1,0:T(8,128)S(1)}, f32[256,256]{1,0:T(8,128)S(1)}, u32[]{:S(2)}, u32[]{:S(2)}) %collective-permute-start.4) | collective-permute-done | bytes 262176 | tf_op jit(solution)/shard_map/ppermute | solution.py:285
  19.9 3.0 %collective-permute-start.6 = (f32[256,256]{1,0:T(8,128)S(1)}, f32[256,256]{1,0:T(8,128)S(1)}, u32[]{:S(2)}, u32[]{:S(2)}) collective-permute-start(f32[256,256]{1,0:T(8,128)S(1)} %collective-permute-done.4.refs_0_), channel_id=1, source_target_pairs={{0,6},{1,7},{2,0},{3,1},{4,2},{5,3},{6,4},{7,5},{8,14},{9,15},{10,... | collective-permute-start | bytes 786440 | tf_op jit(solution)/shard_map/ppermute | solution.py:281
  23.4 3.0 %collective-permute-start.7 = (f32[256,256]{1,0:T(8,128)S(1)}, f32[256,256]{1,0:T(8,128)S(1)}, u32[]{:S(2)}, u32[]{:S(2)}) collective-permute-start(f32[256,256]{1,0:T(8,128)S(1)} %collective-permute-done.5.refs_1_), channel_id=1, source_target_pairs={{0,6},{1,7},{2,0},{3,1},{4,2},{5,3},{6,4},{7,5},{8,14},{9,15},{10,... | collective-permute-start | bytes 786440 | tf_op jit(solution)/shard_map/ppermute | solution.py:281
  31.3 4.1 %collective-permute-start = (f32[16,256]{1,0:T(8,128)S(1)}, f32[16,256]{1,0:T(8,128)S(1)}, u32[]{:S(2)}, u32[]{:S(2)}) collective-permute-start(f32[16,256]{1,0:T(8,128)S(1)} %get-tuple-element.25), channel_id=1, source_target_pairs={{0,4},{1,5},{2,6},{3,7},{4,8},{5,9},{6,10},{7,11},{8,12},{9,13},{1... | collective-permute-start | bytes 49160 | tf_op jit(solution)/shard_map/ppermute | solution.py:272
  35.4 5.4 %collective-permute-done.x_low = f32[16,256]{1,0:T(8,128)S(1)} collective-permute-done((f32[16,256]{1,0:T(8,128)S(1)}, f32[16,256]{1,0:T(8,128)S(1)}, u32[]{:S(2)}, u32[]{:S(2)}) %collective-permute-start) | collective-permute-done | bytes 16416 | tf_op jit(solution)/shard_map/ppermute | solution.py:272
  40.8 3.4 %collective-permute-start.1 = (f32[16,256]{1,0:T(8,128)S(1)}, f32[16,256]{1,0:T(8,128)S(1)}, u32[]{:S(2)}, u32[]{:S(2)}) collective-permute-start(f32[16,256]{1,0:T(8,128)S(1)} %get-tuple-element.26), channel_id=1, source_target_pairs={{4,0},{5,1},{6,2},{7,3},{8,4},{9,5},{10,6},{11,7},{12,8},{13,9},{1... | collective-permute-start | bytes 49160 | tf_op jit(solution)/shard_map/ppermute | solution.py:273
  44.2 3.7 %collective-permute-done.1.x_high = f32[16,256]{1,0:T(8,128)S(1)} collective-permute-done((f32[16,256]{1,0:T(8,128)S(1)}, f32[16,256]{1,0:T(8,128)S(1)}, u32[]{:S(2)}, u32[]{:S(2)}) %collective-permute-start.1) | collective-permute-done | bytes 16416 | tf_op jit(solution)/shard_map/ppermute | solution.py:273
  53.9 2.9 %collective-permute-start.11 = (f32[256,256]{1,0:T(8,128)S(1)}, f32[256,256]{1,0:T(8,128)S(1)}, u32[]{:S(2)}, u32[]{:S(2)}) collective-permute-start(f32[256,256]{1,0:T(8,128)S(1)} %collective-permute-done.5.refs_1_), channel_id=1, source_target_pairs={{0,2},{1,3},{2,4},{3,5},{4,6},{5,7},{6,0},{7,1},{8,10},{9,11},{10,... | collective-permute-start | bytes 786440 | tf_op jit(solution)/shard_map/ppermute | solution.py:281
  57.4 6.1 %collective-permute-done.11.refs_7_ = f32[256,256]{1,0:T(8,128)S(1)} collective-permute-done((f32[256,256]{1,0:T(8,128)S(1)}, f32[256,256]{1,0:T(8,128)S(1)}, u32[]{:S(2)}, u32[]{:S(2)}) %collective-permute-start.11) | collective-permute-done | bytes 262176 | tf_op jit(solution)/shard_map/ppermute | solution.py:281
  76.5 6.7 %stencil.2.field = f32[16,256,256]{2,1,0:T(8,128)S(1)} custom-call(f32[1]{0:T(128)S(6)} %div.3.inverse, f32[16,256,256]{2,1,0:T(8,128)S(1)} %bitcast.73, f32[16,256,256]{2,1,0:T(8,128)S(1)} %bitcast.74, f32[16,256,256]{2,1,0:T(8,128)S(1)} %bitcast.75, f32[16,256,256]{2,1,0:T(8,128)S(1)} %bitcast.76, s32[256,256]{1,0:T(8,128)S(1)} %bitcast.88, ...), custom_call_target="tpu_custom_call" | custom-call | flops 16777216 | bytes 12582912 | tf_op jit(solution)/shard_map/stencil/pallas_call | solution.py:246
  83.2 3.1 %below.2 = (f32[16,256,256]{2,1,0:T(8,128)S(1)}, f32[256,256]{1,0:T(8,128)S(1)}) custom-call(s32[6]{0:T(128)S(1)} %pad_add_fusion.table, f32[4,256,256]{2,1,0:T(8,128)S(1)} %bitcast.81, f32[4,256,256]{2,1,0:T(8,128)S(1)} %bitcast.85, f32[16,256,256]{2,1,0:T(8,128)S(1)} %bitcast.77, ...), custom_call_target="tpu_custom_call", output_to_operand_aliasing={{0}: (4, {})} | custom-call | flops 805306368 | bytes 5242880 | tf_op jit(solution)/shard_map/below/pallas_call | solution.py:139
  86.4 3.6 %pieces.2 = (f32[2,256,256]{2,1,0:T(8,128)S(1)}, f32[6,256,256]{2,1,0:T(8,128)S(1)}, f32[8,256,256]{2,1,0:T(8,128)S(1)}) custom-call(s32[6]{0:T(128)S(1)} %pad_add_fusion.table, f32[4,256,256]{2,1,0:T(8,128)S(1)} %bitcast.82, f32[4,256,256]{2,1,0:T(8,128)S(1)} %bitcast.86, f32[256,256]{1,0:T(8,128)S(1)} %get-tuple-element.29.bottom), custom_call_target="tpu_custom_call" | custom-call | flops 805306368 | bytes 7340032 | tf_op jit(solution)/shard_map/pieces/pallas_call | solution.py:105
  93.2 5.9 %collective-permute-done.36 = f32[256,256]{1,0:T(8,128)S(1)} collective-permute-done((f32[256,256]{1,0:T(8,128)S(1)}, f32[256,256]{1,0:T(8,128)S(1)}, u32[]{:S(2)}, u32[]{:S(2)}) %collective-permute-start.36) | collective-permute-done | bytes 262176 | tf_op jit(solution)/shard_map/ppermute | solution.py:281
  99.1 3.4 %collective-permute-start.37 = (f32[256,256]{1,0:T(8,128)S(1)}, f32[256,256]{1,0:T(8,128)S(1)}, u32[]{:S(2)}, u32[]{:S(2)}) collective-permute-start(f32[256,256]{1,0:T(8,128)S(1)} %fusion.3), channel_id=1, source_target_pairs={{0,6},{1,7},{2,0},{3,1},{4,2},{5,3},{6,4},{7,5},{8,14},{9,15},{10,... | collective-permute-start | bytes 786440 | tf_op jit(solution)/shard_map/ppermute | solution.py:281
  103.3 4.4 %collective-permute-done.33 = f32[256,256]{1,0:T(8,128)S(1)} collective-permute-done((f32[256,256]{1,0:T(8,128)S(1)}, f32[256,256]{1,0:T(8,128)S(1)}, u32[]{:S(2)}, u32[]{:S(2)}) %collective-permute-start.33) | collective-permute-done | bytes 262176 | tf_op jit(solution)/shard_map/ppermute | solution.py:281
  109.5 3.9 %collective-permute-start.39 = (f32[256,256]{1,0:T(8,128)S(1)}, f32[256,256]{1,0:T(8,128)S(1)}, u32[]{:S(2)}, u32[]{:S(2)}) collective-permute-start(f32[256,256]{1,0:T(8,128)S(1)} %get-tuple-element.47), channel_id=1, source_target_pairs={{16,8},{17,9},{18,10},{19,11},{20,12},{21,13},{22,14},{23,15},{24,... | collective-permute-start | bytes 786440 | tf_op jit(solution)/shard_map/ppermute | solution.py:285
  113.4 4.1 %collective-permute-done.34 = f32[256,256]{1,0:T(8,128)S(1)} collective-permute-done((f32[256,256]{1,0:T(8,128)S(1)}, f32[256,256]{1,0:T(8,128)S(1)}, u32[]{:S(2)}, u32[]{:S(2)}) %collective-permute-start.34) | collective-permute-done | bytes 262176 | tf_op jit(solution)/shard_map/ppermute | solution.py:281
  122.9 4.6 %collective-permute-done.35.straight = f32[256,256]{1,0:T(8,128)S(1)} collective-permute-done((f32[256,256]{1,0:T(8,128)S(1)}, f32[256,256]{1,0:T(8,128)S(1)}, u32[]{:S(2)}, u32[]{:S(2)}) %collective-permute-start.35) | collective-permute-done | bytes 262176 | tf_op jit(solution)/shard_map/ppermute | solution.py:285
  130.8 5.9 %collective-permute-start.40 = (f32[16,256]{1,0:T(8,128)S(1)}, f32[16,256]{1,0:T(8,128)S(1)}, u32[]{:S(2)}, u32[]{:S(2)}) collective-permute-start(f32[16,256]{1,0:T(8,128)S(1)} %get-tuple-element.38), channel_id=1, source_target_pairs={{0,4},{1,5},{2,6},{3,7},{4,8},{5,9},{6,10},{7,11},{8,12},{9,13},{1... | collective-permute-start | bytes 49160 | tf_op jit(solution)/shard_map/ppermute | solution.py:272
  136.7 3.9 %collective-permute-start.41 = (f32[16,256]{1,0:T(8,128)S(1)}, f32[16,256]{1,0:T(8,128)S(1)}, u32[]{:S(2)}, u32[]{:S(2)}) collective-permute-start(f32[16,256]{1,0:T(8,128)S(1)} %get-tuple-element.39), channel_id=1, source_target_pairs={{4,0},{5,1},{6,2},{7,3},{8,4},{9,5},{10,6},{11,7},{12,8},{13,9},{1... | collective-permute-start | bytes 49160 | tf_op jit(solution)/shard_map/ppermute | solution.py:273
  140.6 3.9 %collective-permute-start.44 = (f32[256,256]{1,0:T(8,128)S(1)}, f32[256,256]{1,0:T(8,128)S(1)}, u32[]{:S(2)}, u32[]{:S(2)}) collective-permute-start(f32[256,256]{1,0:T(8,128)S(1)} %get-tuple-element.42), channel_id=1, source_target_pairs={{0,16},{1,17},{2,18},{3,19},{4,20},{5,21},{6,22},{7,23},{8,24},{9,... | collective-permute-start | bytes 786440 | tf_op jit(solution)/shard_map/ppermute | solution.py:285
  149.4 6.5 %collective-permute-start.23 = (f32[256,256]{1,0:T(8,128)S(1)}, f32[256,256]{1,0:T(8,128)S(1)}, u32[]{:S(2)}, u32[]{:S(2)}) collective-permute-start(f32[256,256]{1,0:T(8,128)S(1)} %get-tuple-element.58), channel_id=1, source_target_pairs={{0,2},{1,3},{2,4},{3,5},{4,6},{5,7},{6,0},{7,1},{8,10},{9,11},{10,... | collective-permute-start | bytes 786440 | tf_op jit(solution)/shard_map/ppermute | solution.py:281
  166.3 3.6 %collective-permute-done.46.refs_2_ = f32[256,256]{1,0:T(8,128)S(1)} collective-permute-done((f32[256,256]{1,0:T(8,128)S(1)}, f32[256,256]{1,0:T(8,128)S(1)}, u32[]{:S(2)}, u32[]{:S(2)}) %collective-permute-start.46) | collective-permute-done | bytes 262176 | tf_op jit(solution)/shard_map/ppermute | solution.py:281
  171.4 4.2 %collective-permute-done.27 = f32[256,256]{1,0:T(8,128)S(1)} collective-permute-done((f32[256,256]{1,0:T(8,128)S(1)}, f32[256,256]{1,0:T(8,128)S(1)}, u32[]{:S(2)}, u32[]{:S(2)}) %collective-permute-start.27) | collective-permute-done | bytes 262176 | tf_op jit(solution)/shard_map/ppermute | solution.py:281
  177.7 3.5 %collective-permute-done.47.refs_3_ = f32[256,256]{1,0:T(8,128)S(1)} collective-permute-done((f32[256,256]{1,0:T(8,128)S(1)}, f32[256,256]{1,0:T(8,128)S(1)}, u32[]{:S(2)}, u32[]{:S(2)}) %collective-permute-start.47) | collective-permute-done | bytes 262176 | tf_op jit(solution)/shard_map/ppermute | solution.py:281
  185.8 4.4 %collective-permute-done.50.refs_5_ = f32[256,256]{1,0:T(8,128)S(1)} collective-permute-done((f32[256,256]{1,0:T(8,128)S(1)}, f32[256,256]{1,0:T(8,128)S(1)}, u32[]{:S(2)}, u32[]{:S(2)}) %collective-permute-start.50) | collective-permute-done | bytes 262176 | tf_op jit(solution)/shard_map/ppermute | solution.py:281
  190.7 3.3 %collective-permute-done.24 = f32[256,256]{1,0:T(8,128)S(1)} collective-permute-done((f32[256,256]{1,0:T(8,128)S(1)}, f32[256,256]{1,0:T(8,128)S(1)}, u32[]{:S(2)}, u32[]{:S(2)}) %collective-permute-start.24) | collective-permute-done | bytes 262176 | tf_op jit(solution)/shard_map/ppermute | solution.py:281
  198.3 9.6 %stencil.3.field = f32[16,256,256]{2,1,0:T(8,128)} custom-call(f32[1]{0:T(128)S(6)} %div.3.inverse, f32[16,256,256]{2,1,0:T(8,128)S(1)} %get-tuple-element.37.field.here.below.above, f32[16,256,256]{2,1,0:T(8,128)S(1)} %get-tuple-element.37.field.here.below.above, f32[16,256,256]{2,1,0:T(8,128)S(1)} %get-tuple-element.37.field.here.below.above, ...), custom_call_target="tpu_custom_call" | custom-call | flops 16777216 | bytes 12582912 | tf_op jit(solution)/shard_map/stencil/pallas_call | solution.py:246
  207.9 4.4 %below.3 = (f32[16,256,256]{2,1,0:T(8,128)}, f32[256,256]{1,0:T(8,128)}) custom-call(s32[6]{0:T(128)S(1)} %pad_add_fusion.table, f32[4,256,256]{2,1,0:T(8,128)S(1)} %bitcast.83, f32[4,256,256]{2,1,0:T(8,128)S(1)} %bitcast.87, f32[16,256,256]{2,1,0:T(8,128)S(1)} %bitcast.79, f32[16,256,256]{2,1,0:T(8,128)} %stencil.3.field, ...), custom_call_target="tpu_custom_call", output_to_operand_aliasing={{0}: (4, {})} | custom-call | flops 805306368 | bytes 5242880 | tf_op jit(solution)/shard_map/below/pallas_call | solution.py:139
  (125 shorter events, 72.9 us)
Async XLA Ops:
  7.7 82.8 %collective-permute-start.30 = (f32[6,256,256]{2,1,0:T(8,128)S(1)}, f32[6,256,256]{2,1,0:T(8,128)S(1)}, u32[]{:S(2)}, u32[]{:S(2)}) collective-permute-start(f32[6,256,256]{2,1,0:T(8,128)S(1)} %get-tuple-element.34), channel_id=1, source_target_pairs={{0,1},{1,0},{2,3},{3,2},{4,5},{5,4},{6,7},{7,6},{8,9},{9,8},{10,11... | collective-permute-start | bytes 4718600 | tf_op jit(solution)/shard_map/ppermute | solution.py:289
  7.8 12.1 %collective-permute-start.4 = (f32[256,256]{1,0:T(8,128)S(1)}, f32[256,256]{1,0:T(8,128)S(1)}, u32[]{:S(2)}, u32[]{:S(2)}) collective-permute-start(f32[256,256]{1,0:T(8,128)S(1)} %get-tuple-element.46), channel_id=1, source_target_pairs={{0,16},{1,17},{2,18},{3,19},{4,20},{5,21},{6,22},{7,23},{8,24},{9,... | collective-permute-start | bytes 786440 | tf_op jit(solution)/shard_map/ppermute | solution.py:285
  11.9 11.5 %collective-permute-start.5 = (f32[256,256]{1,0:T(8,128)S(1)}, f32[256,256]{1,0:T(8,128)S(1)}, u32[]{:S(2)}, u32[]{:S(2)}) collective-permute-start(f32[256,256]{1,0:T(8,128)S(1)} %get-tuple-element.46), channel_id=1, source_target_pairs={{0,24},{1,25},{2,26},{3,27},{4,28},{5,29},{6,30},{7,31},{8,16},{9,... | collective-permute-start | bytes 786440 | tf_op jit(solution)/shard_map/ppermute | solution.py:285
  19.9 37.0 %collective-permute-start.6 = (f32[256,256]{1,0:T(8,128)S(1)}, f32[256,256]{1,0:T(8,128)S(1)}, u32[]{:S(2)}, u32[]{:S(2)}) collective-permute-start(f32[256,256]{1,0:T(8,128)S(1)} %collective-permute-done.4.refs_0_), channel_id=1, source_target_pairs={{0,6},{1,7},{2,0},{3,1},{4,2},{5,3},{6,4},{7,5},{8,14},{9,15},{10,... | collective-permute-start | bytes 786440 | tf_op jit(solution)/shard_map/ppermute | solution.py:281
  23.4 33.6 %collective-permute-start.7 = (f32[256,256]{1,0:T(8,128)S(1)}, f32[256,256]{1,0:T(8,128)S(1)}, u32[]{:S(2)}, u32[]{:S(2)}) collective-permute-start(f32[256,256]{1,0:T(8,128)S(1)} %collective-permute-done.5.refs_1_), channel_id=1, source_target_pairs={{0,6},{1,7},{2,0},{3,1},{4,2},{5,3},{6,4},{7,5},{8,14},{9,15},{10,... | collective-permute-start | bytes 786440 | tf_op jit(solution)/shard_map/ppermute | solution.py:281
  26.5 31.0 %collective-permute-start.8 = (f32[256,256]{1,0:T(8,128)S(1)}, f32[256,256]{1,0:T(8,128)S(1)}, u32[]{:S(2)}, u32[]{:S(2)}) collective-permute-start(f32[256,256]{1,0:T(8,128)S(1)} %collective-permute-done.4.refs_0_), channel_id=1, source_target_pairs={{0,2},{1,3},{2,4},{3,5},{4,6},{5,7},{6,0},{7,1},{8,10},{9,11},{10,... | collective-permute-start | bytes 786440 | tf_op jit(solution)/shard_map/ppermute | solution.py:281
  57.4 11.2 %collective-permute-start.9 = (f32[256,256]{1,0:T(8,128)S(1)}, f32[256,256]{1,0:T(8,128)S(1)}, u32[]{:S(2)}, u32[]{:S(2)}) collective-permute-start(f32[256,256]{1,0:T(8,128)S(1)} %collective-permute-done.8.refs_6_), channel_id=1, source_target_pairs={{0,2},{1,3},{2,4},{3,5},{4,6},{5,7},{6,0},{7,1},{8,10},{9,11},{10,... | collective-permute-start | bytes 786440 | tf_op jit(solution)/shard_map/ppermute | solution.py:281
  71.5 19.1 %collective-permute-start.32 = (f32[2,256,256]{2,1,0:T(8,128)S(1)}, f32[2,256,256]{2,1,0:T(8,128)S(1)}, u32[]{:S(2)}, u32[]{:S(2)}) collective-permute-start(f32[2,256,256]{2,1,0:T(8,128)S(1)} %get-tuple-element.35), channel_id=1, source_target_pairs={{0,1},{1,0},{2,3},{3,2},{4,5},{5,4},{6,7},{7,6},{8,9},{9,8},{10,11... | collective-permute-start | bytes 1572872 | tf_op jit(solution)/shard_map/ppermute | solution.py:289
  90.1 29.5 %collective-permute-start.20 = (f32[6,256,256]{2,1,0:T(8,128)S(1)}, f32[6,256,256]{2,1,0:T(8,128)S(1)}, u32[]{:S(2)}, u32[]{:S(2)}) collective-permute-start(f32[6,256,256]{2,1,0:T(8,128)S(1)} %get-tuple-element.31), channel_id=1, source_target_pairs={{0,1},{1,0},{2,3},{3,2},{4,5},{5,4},{6,7},{7,6},{8,9},{9,8},{10,11... | collective-permute-start | bytes 4718600 | tf_op jit(solution)/shard_map/ppermute | solution.py:289
  92.9 10.4 %collective-permute-start.38 = (f32[256,256]{1,0:T(8,128)S(1)}, f32[256,256]{1,0:T(8,128)S(1)}, u32[]{:S(2)}, u32[]{:S(2)}) collective-permute-start(f32[256,256]{1,0:T(8,128)S(1)} %get-tuple-element.60), channel_id=1, source_target_pairs={{0,2},{1,3},{2,4},{3,5},{4,6},{5,7},{6,0},{7,1},{8,10},{9,11},{10,... | collective-permute-start | bytes 786440 | tf_op jit(solution)/shard_map/ppermute | solution.py:281
  92.9 14.8 %collective-permute-start.33 = (f32[256,256]{1,0:T(8,128)S(1)}, f32[256,256]{1,0:T(8,128)S(1)}, u32[]{:S(2)}, u32[]{:S(2)}) collective-permute-start(f32[256,256]{1,0:T(8,128)S(1)} %get-tuple-element.56), channel_id=1, source_target_pairs={{0,2},{1,3},{2,4},{3,5},{4,6},{5,7},{6,0},{7,1},{8,10},{9,11},{10,... | collective-permute-start | bytes 786440 | tf_op jit(solution)/shard_map/ppermute | solution.py:281
  102.5 17.0 %collective-permute-start.22 = (f32[2,256,256]{2,1,0:T(8,128)S(1)}, f32[2,256,256]{2,1,0:T(8,128)S(1)}, u32[]{:S(2)}, u32[]{:S(2)}) collective-permute-start(f32[2,256,256]{2,1,0:T(8,128)S(1)} %get-tuple-element.32), channel_id=1, source_target_pairs={{0,1},{1,0},{2,3},{3,2},{4,5},{5,4},{6,7},{7,6},{8,9},{9,8},{10,11... | collective-permute-start | bytes 1572872 | tf_op jit(solution)/shard_map/ppermute | solution.py:289
  109.5 13.4 %collective-permute-start.39 = (f32[256,256]{1,0:T(8,128)S(1)}, f32[256,256]{1,0:T(8,128)S(1)}, u32[]{:S(2)}, u32[]{:S(2)}) collective-permute-start(f32[256,256]{1,0:T(8,128)S(1)} %get-tuple-element.47), channel_id=1, source_target_pairs={{16,8},{17,9},{18,10},{19,11},{20,12},{21,13},{22,14},{23,15},{24,... | collective-permute-start | bytes 786440 | tf_op jit(solution)/shard_map/ppermute | solution.py:285
  119.7 28.3 %collective-permute-start.26 = (f32[256,256]{1,0:T(8,128)S(1)}, f32[256,256]{1,0:T(8,128)S(1)}, u32[]{:S(2)}, u32[]{:S(2)}) collective-permute-start(f32[256,256]{1,0:T(8,128)S(1)} %get-tuple-element.57), channel_id=1, source_target_pairs={{0,6},{1,7},{2,0},{3,1},{4,2},{5,3},{6,4},{7,5},{8,14},{9,15},{10,... | collective-permute-start | bytes 786440 | tf_op jit(solution)/shard_map/ppermute | solution.py:281
  130.8 15.6 %collective-permute-start.40 = (f32[16,256]{1,0:T(8,128)S(1)}, f32[16,256]{1,0:T(8,128)S(1)}, u32[]{:S(2)}, u32[]{:S(2)}) collective-permute-start(f32[16,256]{1,0:T(8,128)S(1)} %get-tuple-element.38), channel_id=1, source_target_pairs={{0,4},{1,5},{2,6},{3,7},{4,8},{5,9},{6,10},{7,11},{8,12},{9,13},{1... | collective-permute-start | bytes 49160 | tf_op jit(solution)/shard_map/ppermute | solution.py:272
  140.6 16.5 %collective-permute-start.44 = (f32[256,256]{1,0:T(8,128)S(1)}, f32[256,256]{1,0:T(8,128)S(1)}, u32[]{:S(2)}, u32[]{:S(2)}) collective-permute-start(f32[256,256]{1,0:T(8,128)S(1)} %get-tuple-element.42), channel_id=1, source_target_pairs={{0,16},{1,17},{2,18},{3,19},{4,20},{5,21},{6,22},{7,23},{8,24},{9,... | collective-permute-start | bytes 786440 | tf_op jit(solution)/shard_map/ppermute | solution.py:285
  144.5 13.3 %collective-permute-start.45 = (f32[256,256]{1,0:T(8,128)S(1)}, f32[256,256]{1,0:T(8,128)S(1)}, u32[]{:S(2)}, u32[]{:S(2)}) collective-permute-start(f32[256,256]{1,0:T(8,128)S(1)} %get-tuple-element.42), channel_id=1, source_target_pairs={{0,24},{1,25},{2,26},{3,27},{4,28},{5,29},{6,30},{7,31},{8,16},{9,... | collective-permute-start | bytes 786440 | tf_op jit(solution)/shard_map/ppermute | solution.py:285
  146.4 12.6 %collective-permute-start.28 = (f32[256,256]{1,0:T(8,128)S(1)}, f32[256,256]{1,0:T(8,128)S(1)}, u32[]{:S(2)}, u32[]{:S(2)}) collective-permute-start(f32[256,256]{1,0:T(8,128)S(1)} %get-tuple-element.62), channel_id=1, source_target_pairs={{0,2},{1,3},{2,4},{3,5},{4,6},{5,7},{6,0},{7,1},{8,10},{9,11},{10,... | collective-permute-start | bytes 786440 | tf_op jit(solution)/shard_map/ppermute | solution.py:281
  149.4 12.8 %collective-permute-start.23 = (f32[256,256]{1,0:T(8,128)S(1)}, f32[256,256]{1,0:T(8,128)S(1)}, u32[]{:S(2)}, u32[]{:S(2)}) collective-permute-start(f32[256,256]{1,0:T(8,128)S(1)} %get-tuple-element.58), channel_id=1, source_target_pairs={{0,2},{1,3},{2,4},{3,5},{4,6},{5,7},{6,0},{7,1},{8,10},{9,11},{10,... | collective-permute-start | bytes 786440 | tf_op jit(solution)/shard_map/ppermute | solution.py:281
  157.0 13.0 %collective-permute-start.46 = (f32[256,256]{1,0:T(8,128)S(1)}, f32[256,256]{1,0:T(8,128)S(1)}, u32[]{:S(2)}, u32[]{:S(2)}) collective-permute-start(f32[256,256]{1,0:T(8,128)S(1)} %collective-permute-done.44.refs_0_), channel_id=1, source_target_pairs={{0,6},{1,7},{2,0},{3,1},{4,2},{5,3},{6,4},{7,5},{8,14},{9,15},{10,... | collective-permute-start | bytes 786440 | tf_op jit(solution)/shard_map/ppermute | solution.py:281
  157.8 13.6 %collective-permute-start.48 = (f32[256,256]{1,0:T(8,128)S(1)}, f32[256,256]{1,0:T(8,128)S(1)}, u32[]{:S(2)}, u32[]{:S(2)}) collective-permute-start(f32[256,256]{1,0:T(8,128)S(1)} %collective-permute-done.44.refs_0_), channel_id=1, source_target_pairs={{0,2},{1,3},{2,4},{3,5},{4,6},{5,7},{6,0},{7,1},{8,10},{9,11},{10,... | collective-permute-start | bytes 786440 | tf_op jit(solution)/shard_map/ppermute | solution.py:281
  159.1 16.5 %collective-permute-start.27 = (f32[256,256]{1,0:T(8,128)S(1)}, f32[256,256]{1,0:T(8,128)S(1)}, u32[]{:S(2)}, u32[]{:S(2)}) collective-permute-start(f32[256,256]{1,0:T(8,128)S(1)} %fusion.17), channel_id=1, source_target_pairs={{0,6},{1,7},{2,0},{3,1},{4,2},{5,3},{6,4},{7,5},{8,14},{9,15},{10,... | collective-permute-start | bytes 786440 | tf_op jit(solution)/shard_map/ppermute | solution.py:281
  162.2 19.0 %collective-permute-start.47 = (f32[256,256]{1,0:T(8,128)S(1)}, f32[256,256]{1,0:T(8,128)S(1)}, u32[]{:S(2)}, u32[]{:S(2)}) collective-permute-start(f32[256,256]{1,0:T(8,128)S(1)} %collective-permute-done.45.refs_1_), channel_id=1, source_target_pairs={{0,6},{1,7},{2,0},{3,1},{4,2},{5,3},{6,4},{7,5},{8,14},{9,15},{10,... | collective-permute-start | bytes 786440 | tf_op jit(solution)/shard_map/ppermute | solution.py:281
  164.4 19.7 %collective-permute-start.51 = (f32[256,256]{1,0:T(8,128)S(1)}, f32[256,256]{1,0:T(8,128)S(1)}, u32[]{:S(2)}, u32[]{:S(2)}) collective-permute-start(f32[256,256]{1,0:T(8,128)S(1)} %collective-permute-done.45.refs_1_), channel_id=1, source_target_pairs={{0,2},{1,3},{2,4},{3,5},{4,6},{5,7},{6,0},{7,1},{8,10},{9,11},{10,... | collective-permute-start | bytes 786440 | tf_op jit(solution)/shard_map/ppermute | solution.py:281
  170.0 14.1 %collective-permute-start.52 = (f32[256,256]{1,0:T(8,128)S(1)}, f32[256,256]{1,0:T(8,128)S(1)}, u32[]{:S(2)}, u32[]{:S(2)}) collective-permute-start(f32[256,256]{1,0:T(8,128)S(1)} %collective-permute-done.44.refs_0_), channel_id=1, source_target_pairs={{0,1},{1,0},{2,3},{3,2},{4,5},{5,4},{6,7},{7,6},{8,9},{9,8},{10,11... | collective-permute-start | bytes 786440 | tf_op jit(solution)/shard_map/ppermute | solution.py:289
  171.4 12.8 %collective-permute-start.53 = (f32[256,256]{1,0:T(8,128)S(1)}, f32[256,256]{1,0:T(8,128)S(1)}, u32[]{:S(2)}, u32[]{:S(2)}) collective-permute-start(f32[256,256]{1,0:T(8,128)S(1)} %collective-permute-done.45.refs_1_), channel_id=1, source_target_pairs={{0,1},{1,0},{2,3},{3,2},{4,5},{5,4},{6,7},{7,6},{8,9},{9,8},{10,11... | collective-permute-start | bytes 786440 | tf_op jit(solution)/shard_map/ppermute | solution.py:289
  185.6 10.7 %collective-permute-start.58 = (f32[256,256]{1,0:T(8,128)S(1)}, f32[256,256]{1,0:T(8,128)S(1)}, u32[]{:S(2)}, u32[]{:S(2)}) collective-permute-start(f32[256,256]{1,0:T(8,128)S(1)} %collective-permute-done.48.refs_6_), channel_id=1, source_target_pairs={{0,1},{1,0},{2,3},{3,2},{4,5},{5,4},{6,7},{7,6},{8,9},{9,8},{10,11... | collective-permute-start | bytes 786440 | tf_op jit(solution)/shard_map/ppermute | solution.py:289
  190.2 17.7 %collective-permute-start.59 = (f32[256,256]{1,0:T(8,128)S(1)}, f32[256,256]{1,0:T(8,128)S(1)}, u32[]{:S(2)}, u32[]{:S(2)}) collective-permute-start(f32[256,256]{1,0:T(8,128)S(1)} %collective-permute-done.51.refs_7_), channel_id=1, source_target_pairs={{0,1},{1,0},{2,3},{3,2},{4,5},{5,4},{6,7},{7,6},{8,9},{9,8},{10,11... | collective-permute-start | bytes 786440 | tf_op jit(solution)/shard_map/ppermute | solution.py:289
  190.2 17.7 %collective-permute-start.56 = (f32[256,256]{1,0:T(8,128)S(1)}, f32[256,256]{1,0:T(8,128)S(1)}, u32[]{:S(2)}, u32[]{:S(2)}) collective-permute-start(f32[256,256]{1,0:T(8,128)S(1)} %collective-permute-done.49.refs_4_), channel_id=1, source_target_pairs={{0,1},{1,0},{2,3},{3,2},{4,5},{5,4},{6,7},{7,6},{8,9},{9,8},{10,11... | collective-permute-start | bytes 786440 | tf_op jit(solution)/shard_map/ppermute | solution.py:289
  194.0 13.9 %collective-permute-start.57 = (f32[256,256]{1,0:T(8,128)S(1)}, f32[256,256]{1,0:T(8,128)S(1)}, u32[]{:S(2)}, u32[]{:S(2)}) collective-permute-start(f32[256,256]{1,0:T(8,128)S(1)} %collective-permute-done.50.refs_5_), channel_id=1, source_target_pairs={{0,1},{1,0},{2,3},{3,2},{4,5},{5,4},{6,7},{7,6},{8,9},{9,8},{10,11... | collective-permute-start | bytes 786440 | tf_op jit(solution)/shard_map/ppermute | solution.py:289
  194.1 18.2 %collective-permute-start.29 = (f32[256,256]{1,0:T(8,128)S(1)}, f32[256,256]{1,0:T(8,128)S(1)}, u32[]{:S(2)}, u32[]{:S(2)}) collective-permute-start(f32[256,256]{1,0:T(8,128)S(1)} %get-tuple-element.51), channel_id=1, source_target_pairs={{16,8},{17,9},{18,10},{19,11},{20,12},{21,13},{22,14},{23,15},{24,... | collective-permute-start | bytes 786440 | tf_op jit(solution)/shard_map/ppermute | solution.py:285
  196.4 16.1 %collective-permute-start.25 = (f32[256,256]{1,0:T(8,128)S(1)}, f32[256,256]{1,0:T(8,128)S(1)}, u32[]{:S(2)}, u32[]{:S(2)}) collective-permute-start(f32[256,256]{1,0:T(8,128)S(1)} %fusion.27), channel_id=1, source_target_pairs={{16,0},{17,1},{18,2},{19,3},{20,4},{21,5},{22,6},{23,7},{24,8},{25... | collective-permute-start | bytes 786440 | tf_op jit(solution)/shard_map/ppermute | solution.py:285
  (36 other events, 364.0 us)

commit v2 on v1

--- a/solution.py
+++ b/solution.py
@@ -65,29 +65,23 @@
     return core_step, y_step, x_step
 
 
-def pieces_kernel(table, px, py, bottom, first, rest, keep):
-    first[...] = jnp.zeros_like(first)
-    rest[...] = jnp.zeros_like(rest)
+def pieces_kernel(table, px, py, bottom, give, keep):
+    give[...] = jnp.zeros_like(give)
     keep[...] = jnp.zeros_like(keep)
     plane = split(bottom[...])
     for k in range(4):
         left = product(split(px[k]), plane, ((0,), (0,)))
         piece = product(split(left), split(py[k]), ((1,), (0,)))
         core_step, y_step, x_step = relative(table, k)
+        slot = y_step * 2 + x_step
 
         @pl.when(core_step == 0)
         def _():
-            slot = y_step * 2 + x_step
             keep[slot] = keep[slot] + piece
 
-        @pl.when((core_step == 1) & (y_step == 2))
+        @pl.when(core_step == 1)
         def _():
-            first[x_step] = first[x_step] + piece
-
-        @pl.when((core_step == 1) & (y_step != 2))
-        def _():
-            slot = jnp.minimum(y_step, 2) * 2 + x_step
-            rest[slot] = rest[slot] + piece
+            give[slot] = give[slot] + piece
 
 
 def full(shape):
@@ -104,32 +98,29 @@
 def pieces_of(table, px, py, bottom):
     return pl.pallas_call(
         pieces_kernel,
-        out_shape=(plane_shape(2), plane_shape(6), plane_shape(8)),
+        out_shape=(plane_shape(8), plane_shape(8)),
         in_specs=[SMEM_SPEC] + [pl.BlockSpec(memory_space=pltpu.VMEM)] * 3,
-        out_specs=[pl.BlockSpec(memory_space=pltpu.VMEM)] * 3,
+        out_specs=[pl.BlockSpec(memory_space=pltpu.VMEM)] * 2,
         compiler_params=pltpu.CompilerParams(vmem_limit_bytes=24 * MIB),
         cost_estimate=pl.CostEstimate(flops=8 * 6 * W**3, bytes_accessed=7 * MIB, transcendentals=0),
         name="pieces",
     )(table, px, py, bottom)
 
 
-def below_kernel(table, px, py, speed, field, *refs):
-    tops, (out, bottom, picked, sems) = refs[:16], refs[16:]
+def below_kernel(table, px, py, speed, field, tops, out, bottom, picked, sems):
+    def fetch(k):
+        source, tile = table[k], table[4]
+        x_step = ((source >> 3) ^ (tile >> 3)) & 1
+        return pltpu.make_async_copy(tops.at[(source & 7) * 2 + x_step], picked.at[k], sems.at[k])
+
     for k in range(4):
-        core_step, y_step, x_step = relative(table, k)
-        slot = core_step * 8 + y_step * 2 + x_step
-        for j in range(16):
-
-            @pl.when(slot == j)
-            def _():
-                pltpu.make_async_copy(tops[j], picked.at[k], sems.at[k]).start()
-
+        fetch(k).start()
     total = jnp.zeros((W, W), F32)
     for k in range(4):
-        pltpu.make_async_copy(tops[0], picked.at[k], sems.at[k]).wait()
+        fetch(k).wait()
         left = product(split(px[k]), split(picked[k]), ((1,), (0,)))
         total = total + product(split(left), split(py[k]), ((1,), (1,)))
-    new = field[0] + TIME_STEP * (total + speed[0] * total)
+    new = field[0] + TIME_STEP * (total + speed[...] * total)
     out[0] = new
     bottom[...] = new
 
@@ -140,15 +131,15 @@
         below_kernel,
         grid=(1,),
         out_shape=(plane_shape(NZ), plane_shape()),
-        in_specs=[SMEM_SPEC, full((4, W, W)), full((4, W, W)), plane0, plane0]
-        + [pl.BlockSpec(memory_space=pl.ANY)] * 16,
+        in_specs=[SMEM_SPEC, full((4, W, W)), full((4, W, W)), full((W, W)), plane0]
+        + [pl.BlockSpec(memory_space=pltpu.HBM)],
         out_specs=[plane0, full((W, W))],
         scratch_shapes=[pltpu.VMEM((4, W, W), F32), pltpu.SemaphoreType.DMA((4,))],
         input_output_aliases={4: 0},
-        compiler_params=pltpu.CompilerParams(vmem_limit_bytes=24 * MIB),
+        compiler_params=pltpu.CompilerParams(vmem_limit_bytes=53 * MIB),
         cost_estimate=pl.CostEstimate(flops=8 * 6 * W**3, bytes_accessed=5 * MIB, transcendentals=0),
         name="below",
-    )(table, px, py, speed, field, *tops)
+    )(table, px, py, speed, field, tops)
 
 
 def above_kernel(table, straight, flipped, field, out, top):
@@ -168,7 +159,7 @@
         in_specs=[SMEM_SPEC, full((W, W)), full((W, W)), last],
         out_specs=[last, full((W, W))],
         input_output_aliases={3: 0},
-        compiler_params=pltpu.CompilerParams(vmem_limit_bytes=8 * MIB),
+        compiler_params=pltpu.CompilerParams(vmem_limit_bytes=53 * MIB),
         cost_estimate=pl.CostEstimate(flops=3 * W * W, bytes_accessed=MIB, transcendentals=0),
         name="above",
     )(table, straight, flipped, field)
@@ -204,7 +195,7 @@
         in_specs=[pl.BlockSpec((1, W, W), lambda z: (z, 0, 0))],
         out_specs=[full((NZ, W))] * 4,
         scratch_shapes=[pltpu.VMEM((W, 128), F32)] * 2,
-        compiler_params=pltpu.CompilerParams(vmem_limit_bytes=8 * MIB),
+        compiler_params=pltpu.CompilerParams(vmem_limit_bytes=53 * MIB),
         cost_estimate=pl.CostEstimate(flops=NZ * W * W, bytes_accessed=4 * MIB, transcendentals=0),
         name="rims",
     )(field)
@@ -261,7 +252,7 @@
         ],
         out_specs=pl.BlockSpec((1, W, W), lambda z: (z, 0, 0)),
         scratch_shapes=[pltpu.VMEM((W, 128), F32)] * 2,
-        compiler_params=pltpu.CompilerParams(vmem_limit_bytes=16 * MIB),
+        compiler_params=pltpu.CompilerParams(vmem_limit_bytes=53 * MIB),
         cost_estimate=pl.CostEstimate(flops=16 * NZ * W * W, bytes_accessed=12 * MIB, transcendentals=0),
         name="stencil",
     )(inverse, field, field, field, speed, inlets, *halos)
@@ -289,31 +280,22 @@
     return lax.ppermute(value, "tile", OTHER_CORE)
 
 
+BY_HALF = [list(range(8)), list(range(8, 16))]
+
+
 def gather_tops(top):
-    mine = send_lift(top, 1, False)
-    flip = send_lift(top, 1, True)
-    left_mine = send_y(mine, 1)
-    right_flip = send_y(flip, -1)
-    left_flip = send_y(flip, 1)
-    right_mine = send_y(mine, -1)
-    far_mine = send_y(left_mine, 1)
-    far_flip = send_y(right_flip, -1)
-    near = [mine, flip, right_mine, right_flip, far_mine, far_flip, left_mine, left_flip]
-    return near + [other_core(value) for value in near]
-
-
-def reduce_pieces(first, rest, keep):
-    first = other_core(first)
-    rest = other_core(rest)
-    far_mine = send_y(keep[4] + first[0], 1)
-    far_flip = send_y(keep[5] + first[1], -1)
-    right_flip = send_y(keep[3] + rest[3], 1)
-    left_mine = send_y(keep[6] + rest[4], -1)
-    right_mine = send_y(keep[2] + rest[2] + far_mine, 1)
-    left_flip = send_y(keep[7] + rest[5] + far_flip, -1)
-    mine = keep[0] + rest[0] + left_mine + right_mine
-    flip = keep[1] + rest[1] + left_flip + right_flip
-    return send_lift(mine, -1, False), send_lift(flip, -1, True)
+    pair = jnp.stack([send_lift(top, 1, False), send_lift(top, 1, True)])
+    return lax.all_gather(pair, "tile", axis_index_groups=BY_HALF, axis=0, tiled=True)
+
+
+def reduce_pieces(give, keep):
+    slots = keep + other_core(give)
+    far_mine = send_y(slots[4], 1)
+    far_flip = send_y(slots[5], -1)
+    right = jnp.stack([slots[2] + far_mine, slots[3]])
+    left = jnp.stack([slots[6], slots[7] + far_flip])
+    total = slots[0:2] + send_y(right, 1) + send_y(left, -1)
+    return send_lift(total[0], -1, False), send_lift(total[1], -1, True)
 
 
 def on_device(oxygen, velocity, spacing, inlets, proj_x, proj_y, sources):
@@ -332,7 +314,7 @@
         parts = reduce_pieces(*pieces_of(table, px, py, bottom))
         halos = exchange_rims(field)
         field = stencil(inverse, field, speed, inlets, halos)
-        field, bottom = below_update(table, px, py, speed, field, tops)
+        field, bottom = below_update(table, px, py, speed[0], field, tops)
         field, top = above_update(table, *parts, field)
     return field.reshape(1, NZ, 1, W, W)
 

time: 217 us -> 234 us (1.078)
  the two profiles are of different devices: /device:TPU:6 before, /device:TPU:101 now
where the time goes in v2:
time: 234 us; the launch traced here: 232 us
  waiting for transfers between devices  74.2 us (32%)
  Pallas kernels  70.7 us (30%)
  starting transfers between devices  67 us (29%)
  between operations  14.5 us (6%)
  other arithmetic  3.01 us (1%)
  local copies, waits for them, and re-layouts  2.45 us (1%)
    ppermute x8, waiting for transfers between devices, send_y(): return lax.ppermute(value, 'tile', along_y(steps))  41 us
    pallas_call x2, Pallas kernels, stencil(): pl.pallas_call(stencil_kernel, grid=(NZ,), out_shape=plane_shape(NZ), in_...  30.6 us
    ppermute x8, waiting for transfers between devices, send_lift(): return lax.ppermute(value, ('lift', 'tile'), to_lift(steps, flip))  22.5 us
    ppermute x8, starting transfers between devices, send_lift(): return lax.ppermute(value, ('lift', 'tile'), to_lift(steps, flip))  21 us
    pallas_call x2, Pallas kernels, rims_of(): pl.pallas_call(rims_kernel, grid=(NZ,), out_shape=(rim,) * 4, in_specs=[p...  18.6 us
    ppermute x8, starting transfers between devices, send_y(): return lax.ppermute(value, 'tile', along_y(steps))  12.9 us
    ppermute x2, starting transfers between devices, exchange_rims(): lax.ppermute(row_low, 'tile', [(t + TCOL, t) for t in range(TILES - TCOL)])  11.7 us
    pallas_call x2, Pallas kernels, below_update(): pl.pallas_call(below_kernel, grid=(1,), out_shape=(plane_shape(NZ), plane...  10.9 us
  transfers between devices with their start and end apart: 28, of which 13 were waited for; matrix products, arithmetic and copies ran while one was open for 1% of the time, Pallas kernels for 29%

profile of v2, /device:TPU:101, one launch (start us, length us, event | category | flops | bytes accessed | tf_op | source)
XLA Modules:
  0.0 231.9 jit_solution(16944497192753775535)
XLA Ops:
  7.8 2.2 collective-permute-start.5
  9.9 2.0 collective-permute-start.4
  11.9 7.8 %collective-permute-done.5 = f32[256,256]{1,0:T(8,128)S(1)} collective-permute-done((f32[256,256]{1,0:T(8,128)S(1)}, f32[256,256]{1,0:T(8,128)S(1)}, u32[]{:S(2)}, u32[]{:S(2)}) %collective-permute-start.5) | collective-permute-done | bytes 262176 | tf_op jit(solution)/shard_map/ppermute | solution.py:276
  19.7 3.4 %collective-permute-done.4 = f32[256,256]{1,0:T(8,128)S(1)} collective-permute-done((f32[256,256]{1,0:T(8,128)S(1)}, f32[256,256]{1,0:T(8,128)S(1)}, u32[]{:S(2)}, u32[]{:S(2)}) %collective-permute-start.4) | collective-permute-done | bytes 262176 | tf_op jit(solution)/shard_map/ppermute | solution.py:276
  24.1 3.4 %pieces.3 = (f32[8,256,256]{2,1,0:T(8,128)S(1)}, f32[8,256,256]{2,1,0:T(8,128)S(1)}) custom-call(s32[6]{0:T(128)S(1)} %pad_add_fusion.table, f32[4,256,256]{2,1,0:T(8,128)S(1)} %bitcast.72, f32[4,256,256]{2,1,0:T(8,128)S(1)} %bitcast.76, f32[256,256]{1,0:T(8,128)S(1)} %get-tuple-element.41.bottom), custom_call_target="tpu_custom_call" | custom-call | flops 805306368 | bytes 7340032 | tf_op jit(solution)/shard_map/pieces/pallas_call | solution.py:99
  29.4 3.8 %collective-permute-done.13 = f32[8,256,256]{2,1,0:T(8,128)S(1)} collective-permute-done((f32[8,256,256]{2,1,0:T(8,128)S(1)}, f32[8,256,256]{2,1,0:T(8,128)S(1)}, u32[]{:S(2)}, u32[]{:S(2)}) %collective-permute-start.13) | collective-permute-done | bytes 2097184 | tf_op jit(solution)/shard_map/ppermute | solution.py:280
  36.6 8.3 %collective-permute-done.14 = f32[256,256]{1,0:T(8,128)S(1)} collective-permute-done((f32[256,256]{1,0:T(8,128)S(1)}, f32[256,256]{1,0:T(8,128)S(1)}, u32[]{:S(2)}, u32[]{:S(2)}) %collective-permute-start.14) | collective-permute-done | bytes 262176 | tf_op jit(solution)/shard_map/ppermute | solution.py:272
  44.9 2.5 %collective-permute-done.16 = f32[256,256]{1,0:T(8,128)S(1)} collective-permute-done((f32[256,256]{1,0:T(8,128)S(1)}, f32[256,256]{1,0:T(8,128)S(1)}, u32[]{:S(2)}, u32[]{:S(2)}) %collective-permute-start.16) | collective-permute-done | bytes 262176 | tf_op jit(solution)/shard_map/ppermute | solution.py:272
  47.5 3.6 %collective-permute-start.17 = (f32[2,256,256]{2,1,0:T(8,128)S(1)}, f32[2,256,256]{2,1,0:T(8,128)S(1)}, u32[]{:S(2)}, u32[]{:S(2)}) collective-permute-start(f32[2,256,256]{2,1,0:T(8,128)S(1)} %pad_maximum_fusion.4), channel_id=1, source_target_pairs={{0,6},{1,7},{2,0},{3,1},{4,2},{5,3},{6,4},{7,5},{8,14},{9,15},{10,... | collective-permute-start | bytes 1572872 | tf_op jit(solution)/shard_map/ppermute | solution.py:272
  51.2 9.3 %rims.2 = (f32[16,256]{1,0:T(8,128)S(1)}, f32[16,256]{1,0:T(8,128)S(1)}, f32[16,256]{1,0:T(8,128)S(1)}, f32[16,256]{1,0:T(8,128)S(1)}) custom-call(f32[16,256,256]{2,1,0:T(8,128)} %bitcast.80), custom_call_target="tpu_custom_call" | custom-call | flops 1048576 | bytes 4194304 | tf_op jit(solution)/shard_map/rims/pallas_call | solution.py:191
  60.6 3.2 %collective-permute-start = (f32[16,256]{1,0:T(8,128)S(1)}, f32[16,256]{1,0:T(8,128)S(1)}, u32[]{:S(2)}, u32[]{:S(2)}) collective-permute-start(f32[16,256]{1,0:T(8,128)S(1)} %get-tuple-element.23), channel_id=1, source_target_pairs={{0,4},{1,5},{2,6},{3,7},{4,8},{5,9},{6,10},{7,11},{8,12},{9,13},{1... | collective-permute-start | bytes 49160 | tf_op jit(solution)/shard_map/ppermute | solution.py:263
  63.7 6.1 %collective-permute-start.1 = (f32[16,256]{1,0:T(8,128)S(1)}, f32[16,256]{1,0:T(8,128)S(1)}, u32[]{:S(2)}, u32[]{:S(2)}) collective-permute-start(f32[16,256]{1,0:T(8,128)S(1)} %get-tuple-element.24), channel_id=1, source_target_pairs={{4,0},{5,1},{6,2},{7,3},{8,4},{9,5},{10,6},{11,7},{12,8},{13,9},{1... | collective-permute-start | bytes 49160 | tf_op jit(solution)/shard_map/ppermute | solution.py:264
  69.9 3.8 %collective-permute-start.2 = (f32[16,256]{1,0:T(8,128)S(1)}, f32[16,256]{1,0:T(8,128)S(1)}, u32[]{:S(2)}, u32[]{:S(2)}) collective-permute-start(f32[16,256]{1,0:T(8,128)S(1)} %get-tuple-element.25), channel_id=1, source_target_pairs={{0,1},{1,2},{2,3},{4,5},{5,6},{6,7},{8,9},{9,10},{10,11},{12,13},{... | collective-permute-start | bytes 49160 | tf_op jit(solution)/shard_map/ppermute | solution.py:266
  81.4 15.4 %stencil.2.field = f32[16,256,256]{2,1,0:T(8,128)} custom-call(f32[1]{0:T(128)S(6)} %div.3.inverse, f32[16,256,256]{2,1,0:T(8,128)} %bitcast.81, f32[16,256,256]{2,1,0:T(8,128)} %bitcast.82, f32[16,256,256]{2,1,0:T(8,128)} %bitcast.83, f32[16,256,256]{2,1,0:T(8,128)} %bitcast.84, s32[256,256]{1,0:T(8,128)S(1)} %bitcast.78, ...), custom_call_target="tpu_custom_call" | custom-call | flops 16777216 | bytes 12582912 | tf_op jit(solution)/shard_map/stencil/pallas_call | solution.py:237
  96.8 5.4 %below.2 = (f32[16,256,256]{2,1,0:T(8,128)}, f32[256,256]{1,0:T(8,128)S(1)}) custom-call(s32[6]{0:T(128)S(1)} %pad_add_fusion.table, f32[4,256,256]{2,1,0:T(8,128)} %bitcast.70, f32[4,256,256]{2,1,0:T(8,128)} %bitcast.74, f32[256,256]{1,0:T(8,128)S(1)} %slice_bitcast_fusion.14.speed, f32[16,256,256]{2,1,0:T(8,128)} %stencil.2.field, ...), custom_call_target="tpu_custom_call", output_to_operand_aliasing={{0}: (4, {})} | custom-call | flops 805306368 | bytes 5242880 | tf_op jit(solution)/shard_map/below/pallas_call | solution.py:130
  104.1 3.4 %collective-permute-start.25 = (f32[256,256]{1,0:T(8,128)S(1)}, f32[256,256]{1,0:T(8,128)S(1)}, u32[]{:S(2)}, u32[]{:S(2)}) collective-permute-start(f32[256,256]{1,0:T(8,128)S(1)} %get-tuple-element.38), channel_id=1, source_target_pairs={{0,24},{1,25},{2,26},{3,27},{4,28},{5,29},{6,30},{7,31},{8,16},{9,... | collective-permute-start | bytes 786440 | tf_op jit(solution)/shard_map/ppermute | solution.py:276
  109.4 6.5 %collective-permute-done.25 = f32[256,256]{1,0:T(8,128)S(1)} collective-permute-done((f32[256,256]{1,0:T(8,128)S(1)}, f32[256,256]{1,0:T(8,128)S(1)}, u32[]{:S(2)}, u32[]{:S(2)}) %collective-permute-start.25) | collective-permute-done | bytes 262176 | tf_op jit(solution)/shard_map/ppermute | solution.py:276
  115.9 4.8 %collective-permute-done.24 = f32[256,256]{1,0:T(8,128)S(1)} collective-permute-done((f32[256,256]{1,0:T(8,128)S(1)}, f32[256,256]{1,0:T(8,128)S(1)}, u32[]{:S(2)}, u32[]{:S(2)}) %collective-permute-start.24) | collective-permute-done | bytes 262176 | tf_op jit(solution)/shard_map/ppermute | solution.py:276
  121.6 3.4 %pieces.2 = (f32[8,256,256]{2,1,0:T(8,128)S(1)}, f32[8,256,256]{2,1,0:T(8,128)S(1)}) custom-call(s32[6]{0:T(128)S(1)} %pad_add_fusion.table, f32[4,256,256]{2,1,0:T(8,128)S(1)} %bitcast.73, f32[4,256,256]{2,1,0:T(8,128)S(1)} %bitcast.77, f32[256,256]{1,0:T(8,128)S(1)} %get-tuple-element.27.bottom), custom_call_target="tpu_custom_call" | custom-call | flops 805306368 | bytes 7340032 | tf_op jit(solution)/shard_map/pieces/pallas_call | solution.py:99
  125.7 3.8 %collective-permute-done.6 = f32[8,256,256]{2,1,0:T(8,128)S(1)} collective-permute-done((f32[8,256,256]{2,1,0:T(8,128)S(1)}, f32[8,256,256]{2,1,0:T(8,128)S(1)}, u32[]{:S(2)}, u32[]{:S(2)}) %collective-permute-start.6) | collective-permute-done | bytes 2097184 | tf_op jit(solution)/shard_map/ppermute | solution.py:280
  132.6 8.1 %collective-permute-done.7 = f32[256,256]{1,0:T(8,128)S(1)} collective-permute-done((f32[256,256]{1,0:T(8,128)S(1)}, f32[256,256]{1,0:T(8,128)S(1)}, u32[]{:S(2)}, u32[]{:S(2)}) %collective-permute-start.7) | collective-permute-done | bytes 262176 | tf_op jit(solution)/shard_map/ppermute | solution.py:272
  142.7 3.6 %collective-permute-start.10 = (f32[2,256,256]{2,1,0:T(8,128)S(1)}, f32[2,256,256]{2,1,0:T(8,128)S(1)}, u32[]{:S(2)}, u32[]{:S(2)}) collective-permute-start(f32[2,256,256]{2,1,0:T(8,128)S(1)} %pad_maximum_fusion.2), channel_id=1, source_target_pairs={{0,6},{1,7},{2,0},{3,1},{4,2},{5,3},{6,4},{7,5},{8,14},{9,15},{10,... | collective-permute-start | bytes 1572872 | tf_op jit(solution)/shard_map/ppermute | solution.py:272
  146.4 20.1 %collective-permute-done.10 = f32[2,256,256]{2,1,0:T(8,128)S(1)} collective-permute-done((f32[2,256,256]{2,1,0:T(8,128)S(1)}, f32[2,256,256]{2,1,0:T(8,128)S(1)}, u32[]{:S(2)}, u32[]{:S(2)}) %collective-permute-start.10) | collective-permute-done | bytes 524320 | tf_op jit(solution)/shard_map/ppermute | solution.py:272
  166.8 2.1 collective-permute-start.11
  168.9 5.7 %collective-permute-start.12 = (f32[256,256]{1,0:T(8,128)S(1)}, f32[256,256]{1,0:T(8,128)S(1)}, u32[]{:S(2)}, u32[]{:S(2)}) collective-permute-start(f32[256,256]{1,0:T(8,128)S(1)} %get-tuple-element.57), channel_id=1, source_target_pairs={{16,8},{17,9},{18,10},{19,11},{20,12},{21,13},{22,14},{23,15},{24,... | collective-permute-start | bytes 786440 | tf_op jit(solution)/shard_map/ppermute | solution.py:276
  174.6 9.2 %rims.3 = (f32[16,256]{1,0:T(8,128)S(1)}, f32[16,256]{1,0:T(8,128)S(1)}, f32[16,256]{1,0:T(8,128)S(1)}, f32[16,256]{1,0:T(8,128)S(1)}) custom-call(f32[16,256,256]{2,1,0:T(8,128)} %get-tuple-element.33.field.here.below.above), custom_call_target="tpu_custom_call" | custom-call | flops 1048576 | bytes 4194304 | tf_op jit(solution)/shard_map/rims/pallas_call | solution.py:191
  183.8 3.6 %collective-permute-start.20 = (f32[16,256]{1,0:T(8,128)S(1)}, f32[16,256]{1,0:T(8,128)S(1)}, u32[]{:S(2)}, u32[]{:S(2)}) collective-permute-start(f32[16,256]{1,0:T(8,128)S(1)} %get-tuple-element.34), channel_id=1, source_target_pairs={{0,4},{1,5},{2,6},{3,7},{4,8},{5,9},{6,10},{7,11},{8,12},{9,13},{1... | collective-permute-start | bytes 49160 | tf_op jit(solution)/shard_map/ppermute | solution.py:263
  187.4 5.6 %collective-permute-start.21 = (f32[16,256]{1,0:T(8,128)S(1)}, f32[16,256]{1,0:T(8,128)S(1)}, u32[]{:S(2)}, u32[]{:S(2)}) collective-permute-start(f32[16,256]{1,0:T(8,128)S(1)} %get-tuple-element.35), channel_id=1, source_target_pairs={{4,0},{5,1},{6,2},{7,3},{8,4},{9,5},{10,6},{11,7},{12,8},{13,9},{1... | collective-permute-start | bytes 49160 | tf_op jit(solution)/shard_map/ppermute | solution.py:264
  193.0 4.3 %collective-permute-start.22 = (f32[16,256]{1,0:T(8,128)S(1)}, f32[16,256]{1,0:T(8,128)S(1)}, u32[]{:S(2)}, u32[]{:S(2)}) collective-permute-start(f32[16,256]{1,0:T(8,128)S(1)} %get-tuple-element.36), channel_id=1, source_target_pairs={{0,1},{1,2},{2,3},{4,5},{5,6},{6,7},{8,9},{9,10},{10,11},{12,13},{... | collective-permute-start | bytes 49160 | tf_op jit(solution)/shard_map/ppermute | solution.py:266
  199.3 3.1 %collective-permute-done.23.y_high = f32[16,256]{1,0:T(8,128)S(1)} collective-permute-done((f32[16,256]{1,0:T(8,128)S(1)}, f32[16,256]{1,0:T(8,128)S(1)}, u32[]{:S(2)}, u32[]{:S(2)}) %collective-permute-start.23) | collective-permute-done | bytes 16416 | tf_op jit(solution)/shard_map/ppermute | solution.py:267
  202.4 15.3 %stencil.3.field = f32[16,256,256]{2,1,0:T(8,128)} custom-call(f32[1]{0:T(128)S(6)} %div.3.inverse, f32[16,256,256]{2,1,0:T(8,128)} %get-tuple-element.33.field.here.below.above, f32[16,256,256]{2,1,0:T(8,128)} %get-tuple-element.33.field.here.below.above, f32[16,256,256]{2,1,0:T(8,128)} %get-tuple-element.33.field.here.below.above, ...), custom_call_target="tpu_custom_call" | custom-call | flops 16777216 | bytes 12582912 | tf_op jit(solution)/shard_map/stencil/pallas_call | solution.py:237
  217.7 5.5 %below.3 = (f32[16,256,256]{2,1,0:T(8,128)}, f32[256,256]{1,0:T(8,128)}) custom-call(s32[6]{0:T(128)S(1)} %pad_add_fusion.table, f32[4,256,256]{2,1,0:T(8,128)} %bitcast.71, f32[4,256,256]{2,1,0:T(8,128)} %bitcast.75, f32[256,256]{1,0:T(8,128)S(1)} %slice_bitcast_fusion.14.speed, f32[16,256,256]{2,1,0:T(8,128)} %stencil.3.field, ...), custom_call_target="tpu_custom_call", output_to_operand_aliasing={{0}: (4, {})} | custom-call | flops 805306368 | bytes 5242880 | tf_op jit(solution)/shard_map/below/pallas_call | solution.py:130
  (68 shorter events, 29.2 us)
Async XLA Ops:
  6.5 17.6 %copy-start.2 = (f32[1,1,4,256,256]{4,3,2,1,0:T(8,128)S(1)}, f32[1,1,4,256,256]{4,3,2,1,0:T(8,128)}, u32[]{:S(2)}) copy-start(f32[1,1,4,256,256]{4,3,2,1,0:T(8,128)} %param.12) | copy-start | bytes 3145732
  6.5 90.2 %all-gather.3.cloned.1.call-start = ((), (), s32[]{:S(2)}) async-start(), calls=%async_computation | async-start | bytes 4718592 | tf_op jit(solution)/shard_map/all_gather | solution.py:288
  7.8 12.0 %collective-permute-start.5 = (f32[256,256]{1,0:T(8,128)S(1)}, f32[256,256]{1,0:T(8,128)S(1)}, u32[]{:S(2)}, u32[]{:S(2)}) collective-permute-start(f32[256,256]{1,0:T(8,128)S(1)} %get-tuple-element.42), channel_id=1, source_target_pairs={{0,24},{1,25},{2,26},{3,27},{4,28},{5,29},{6,30},{7,31},{8,16},{9,... | collective-permute-start | bytes 786440 | tf_op jit(solution)/shard_map/ppermute | solution.py:276
  9.9 13.2 %collective-permute-start.4 = (f32[256,256]{1,0:T(8,128)S(1)}, f32[256,256]{1,0:T(8,128)S(1)}, u32[]{:S(2)}, u32[]{:S(2)}) collective-permute-start(f32[256,256]{1,0:T(8,128)S(1)} %get-tuple-element.42), channel_id=1, source_target_pairs={{0,16},{1,17},{2,18},{3,19},{4,20},{5,21},{6,22},{7,23},{8,24},{9,... | collective-permute-start | bytes 786440 | tf_op jit(solution)/shard_map/ppermute | solution.py:276
  24.0 193.7 %all-gather.5.cloned.1.call-start = ((), (), s32[]{:S(2)}) async-start(), calls=%async_computation.1 | async-start | bytes 4718592 | tf_op jit(solution)/shard_map/all_gather | solution.py:288
  27.6 5.6 %collective-permute-start.13 = (f32[8,256,256]{2,1,0:T(8,128)S(1)}, f32[8,256,256]{2,1,0:T(8,128)S(1)}, u32[]{:S(2)}, u32[]{:S(2)}) collective-permute-start(f32[8,256,256]{2,1,0:T(8,128)S(1)} %get-tuple-element.31), channel_id=1, source_target_pairs={{0,1},{1,0},{2,3},{3,2},{4,5},{5,4},{6,7},{7,6},{8,9},{9,8},{10,11... | collective-permute-start | bytes 6291464 | tf_op jit(solution)/shard_map/ppermute | solution.py:280
  33.7 11.2 %collective-permute-start.14 = (f32[256,256]{1,0:T(8,128)S(1)}, f32[256,256]{1,0:T(8,128)S(1)}, u32[]{:S(2)}, u32[]{:S(2)}) collective-permute-start(f32[256,256]{1,0:T(8,128)S(1)} %get-tuple-element.45), channel_id=1, source_target_pairs={{0,2},{1,3},{2,4},{3,5},{4,6},{5,7},{6,0},{7,1},{8,10},{9,11},{10,... | collective-permute-start | bytes 786440 | tf_op jit(solution)/shard_map/ppermute | solution.py:272
  35.1 12.3 %collective-permute-start.16 = (f32[256,256]{1,0:T(8,128)S(1)}, f32[256,256]{1,0:T(8,128)S(1)}, u32[]{:S(2)}, u32[]{:S(2)}) collective-permute-start(f32[256,256]{1,0:T(8,128)S(1)} %get-tuple-element.46), channel_id=1, source_target_pairs={{0,6},{1,7},{2,0},{3,1},{4,2},{5,3},{6,4},{7,5},{8,14},{9,15},{10,... | collective-permute-start | bytes 786440 | tf_op jit(solution)/shard_map/ppermute | solution.py:272
  47.5 26.2 %collective-permute-start.17 = (f32[2,256,256]{2,1,0:T(8,128)S(1)}, f32[2,256,256]{2,1,0:T(8,128)S(1)}, u32[]{:S(2)}, u32[]{:S(2)}) collective-permute-start(f32[2,256,256]{2,1,0:T(8,128)S(1)} %pad_maximum_fusion.4), channel_id=1, source_target_pairs={{0,6},{1,7},{2,0},{3,1},{4,2},{5,3},{6,4},{7,5},{8,14},{9,15},{10,... | collective-permute-start | bytes 1572872 | tf_op jit(solution)/shard_map/ppermute | solution.py:272
  51.1 24.5 %collective-permute-start.15 = (f32[2,256,256]{2,1,0:T(8,128)S(1)}, f32[2,256,256]{2,1,0:T(8,128)S(1)}, u32[]{:S(2)}, u32[]{:S(2)}) collective-permute-start(f32[2,256,256]{2,1,0:T(8,128)S(1)} %pad_maximum_fusion.3), channel_id=1, source_target_pairs={{0,2},{1,3},{2,4},{3,5},{4,6},{5,7},{6,0},{7,1},{8,10},{9,11},{10,... | collective-permute-start | bytes 1572872 | tf_op jit(solution)/shard_map/ppermute | solution.py:272
  60.5 20.9 %copy-start.4 = (s32[1,1,256,256]{3,2,1,0:T(8,128)S(1)}, s32[1,1,256,256]{3,2,1,0:T(8,128)}, u32[]{:S(2)}) copy-start(s32[1,1,256,256]{3,2,1,0:T(8,128)} %param.10) | copy-start | bytes 786436
  60.6 17.2 %collective-permute-start = (f32[16,256]{1,0:T(8,128)S(1)}, f32[16,256]{1,0:T(8,128)S(1)}, u32[]{:S(2)}, u32[]{:S(2)}) collective-permute-start(f32[16,256]{1,0:T(8,128)S(1)} %get-tuple-element.23), channel_id=1, source_target_pairs={{0,4},{1,5},{2,6},{3,7},{4,8},{5,9},{6,10},{7,11},{8,12},{9,13},{1... | collective-permute-start | bytes 49160 | tf_op jit(solution)/shard_map/ppermute | solution.py:263
  63.7 17.6 %collective-permute-start.1 = (f32[16,256]{1,0:T(8,128)S(1)}, f32[16,256]{1,0:T(8,128)S(1)}, u32[]{:S(2)}, u32[]{:S(2)}) collective-permute-start(f32[16,256]{1,0:T(8,128)S(1)} %get-tuple-element.24), channel_id=1, source_target_pairs={{4,0},{5,1},{6,2},{7,3},{8,4},{9,5},{10,6},{11,7},{12,8},{13,9},{1... | collective-permute-start | bytes 49160 | tf_op jit(solution)/shard_map/ppermute | solution.py:264
  69.9 11.5 %collective-permute-start.2 = (f32[16,256]{1,0:T(8,128)S(1)}, f32[16,256]{1,0:T(8,128)S(1)}, u32[]{:S(2)}, u32[]{:S(2)}) collective-permute-start(f32[16,256]{1,0:T(8,128)S(1)} %get-tuple-element.25), channel_id=1, source_target_pairs={{0,1},{1,2},{2,3},{4,5},{5,6},{6,7},{8,9},{9,10},{10,11},{12,13},{... | collective-permute-start | bytes 49160 | tf_op jit(solution)/shard_map/ppermute | solution.py:266
  73.8 7.6 %collective-permute-start.3 = (f32[16,256]{1,0:T(8,128)S(1)}, f32[16,256]{1,0:T(8,128)S(1)}, u32[]{:S(2)}, u32[]{:S(2)}) collective-permute-start(f32[16,256]{1,0:T(8,128)S(1)} %get-tuple-element.26), channel_id=1, source_target_pairs={{1,0},{2,1},{3,2},{5,4},{6,5},{7,6},{9,8},{10,9},{11,10},{13,12},{... | collective-permute-start | bytes 49160 | tf_op jit(solution)/shard_map/ppermute | solution.py:267
  75.8 26.3 %collective-permute-start.18 = (f32[256,256]{1,0:T(8,128)S(1)}, f32[256,256]{1,0:T(8,128)S(1)}, u32[]{:S(2)}, u32[]{:S(2)}) collective-permute-start(f32[256,256]{1,0:T(8,128)S(1)} %get-tuple-element.56), channel_id=1, source_target_pairs={{16,0},{17,1},{18,2},{19,3},{20,4},{21,5},{22,6},{23,7},{24,8},{25... | collective-permute-start | bytes 786440 | tf_op jit(solution)/shard_map/ppermute | solution.py:276
  77.8 24.4 %collective-permute-start.19 = (f32[256,256]{1,0:T(8,128)S(1)}, f32[256,256]{1,0:T(8,128)S(1)}, u32[]{:S(2)}, u32[]{:S(2)}) collective-permute-start(f32[256,256]{1,0:T(8,128)S(1)} %get-tuple-element.55), channel_id=1, source_target_pairs={{16,8},{17,9},{18,10},{19,11},{20,12},{21,13},{22,14},{23,15},{24,... | collective-permute-start | bytes 786440 | tf_op jit(solution)/shard_map/ppermute | solution.py:276
  102.2 19.4 %copy-start.1 = (f32[1,1,4,256,256]{4,3,2,1,0:T(8,128)S(1)}, f32[1,1,4,256,256]{4,3,2,1,0:T(8,128)}, u32[]{:S(2)}) copy-start(f32[1,1,4,256,256]{4,3,2,1,0:T(8,128)} %param.11) | copy-start | bytes 3145732
  102.2 19.4 %copy-start.3 = (f32[1,1,4,256,256]{4,3,2,1,0:T(8,128)S(1)}, f32[1,1,4,256,256]{4,3,2,1,0:T(8,128)}, u32[]{:S(2)}) copy-start(f32[1,1,4,256,256]{4,3,2,1,0:T(8,128)} %param.12) | copy-start | bytes 3145732
  104.1 11.8 %collective-permute-start.25 = (f32[256,256]{1,0:T(8,128)S(1)}, f32[256,256]{1,0:T(8,128)S(1)}, u32[]{:S(2)}, u32[]{:S(2)}) collective-permute-start(f32[256,256]{1,0:T(8,128)S(1)} %get-tuple-element.38), channel_id=1, source_target_pairs={{0,24},{1,25},{2,26},{3,27},{4,28},{5,29},{6,30},{7,31},{8,16},{9,... | collective-permute-start | bytes 786440 | tf_op jit(solution)/shard_map/ppermute | solution.py:276
  107.5 13.2 %collective-permute-start.24 = (f32[256,256]{1,0:T(8,128)S(1)}, f32[256,256]{1,0:T(8,128)S(1)}, u32[]{:S(2)}, u32[]{:S(2)}) collective-permute-start(f32[256,256]{1,0:T(8,128)S(1)} %get-tuple-element.38), channel_id=1, source_target_pairs={{0,16},{1,17},{2,18},{3,19},{4,20},{5,21},{6,22},{7,23},{8,24},{9,... | collective-permute-start | bytes 786440 | tf_op jit(solution)/shard_map/ppermute | solution.py:276
  125.0 4.4 %collective-permute-start.6 = (f32[8,256,256]{2,1,0:T(8,128)S(1)}, f32[8,256,256]{2,1,0:T(8,128)S(1)}, u32[]{:S(2)}, u32[]{:S(2)}) collective-permute-start(f32[8,256,256]{2,1,0:T(8,128)S(1)} %get-tuple-element.29), channel_id=1, source_target_pairs={{0,1},{1,0},{2,3},{3,2},{4,5},{5,4},{6,7},{7,6},{8,9},{9,8},{10,11... | collective-permute-start | bytes 6291464 | tf_op jit(solution)/shard_map/ppermute | solution.py:280
  129.9 10.8 %collective-permute-start.7 = (f32[256,256]{1,0:T(8,128)S(1)}, f32[256,256]{1,0:T(8,128)S(1)}, u32[]{:S(2)}, u32[]{:S(2)}) collective-permute-start(f32[256,256]{1,0:T(8,128)S(1)} %get-tuple-element.51), channel_id=1, source_target_pairs={{0,2},{1,3},{2,4},{3,5},{4,6},{5,7},{6,0},{7,1},{8,10},{9,11},{10,... | collective-permute-start | bytes 786440 | tf_op jit(solution)/shard_map/ppermute | solution.py:272
  130.9 11.7 %collective-permute-start.9 = (f32[256,256]{1,0:T(8,128)S(1)}, f32[256,256]{1,0:T(8,128)S(1)}, u32[]{:S(2)}, u32[]{:S(2)}) collective-permute-start(f32[256,256]{1,0:T(8,128)S(1)} %get-tuple-element.52), channel_id=1, source_target_pairs={{0,6},{1,7},{2,0},{3,1},{4,2},{5,3},{6,4},{7,5},{8,14},{9,15},{10,... | collective-permute-start | bytes 786440 | tf_op jit(solution)/shard_map/ppermute | solution.py:272
  142.7 23.8 %collective-permute-start.10 = (f32[2,256,256]{2,1,0:T(8,128)S(1)}, f32[2,256,256]{2,1,0:T(8,128)S(1)}, u32[]{:S(2)}, u32[]{:S(2)}) collective-permute-start(f32[2,256,256]{2,1,0:T(8,128)S(1)} %pad_maximum_fusion.2), channel_id=1, source_target_pairs={{0,6},{1,7},{2,0},{3,1},{4,2},{5,3},{6,4},{7,5},{8,14},{9,15},{10,... | collective-permute-start | bytes 1572872 | tf_op jit(solution)/shard_map/ppermute | solution.py:272
  146.3 20.3 %collective-permute-start.8 = (f32[2,256,256]{2,1,0:T(8,128)S(1)}, f32[2,256,256]{2,1,0:T(8,128)S(1)}, u32[]{:S(2)}, u32[]{:S(2)}) collective-permute-start(f32[2,256,256]{2,1,0:T(8,128)S(1)} %pad_maximum_fusion.1), channel_id=1, source_target_pairs={{0,2},{1,3},{2,4},{3,5},{4,6},{5,7},{6,0},{7,1},{8,10},{9,11},{10,... | collective-permute-start | bytes 1572872 | tf_op jit(solution)/shard_map/ppermute | solution.py:272
  166.8 56.4 %collective-permute-start.11 = (f32[256,256]{1,0:T(8,128)S(1)}, f32[256,256]{1,0:T(8,128)S(1)}, u32[]{:S(2)}, u32[]{:S(2)}) collective-permute-start(f32[256,256]{1,0:T(8,128)S(1)} %get-tuple-element.58), channel_id=1, source_target_pairs={{16,0},{17,1},{18,2},{19,3},{20,4},{21,5},{22,6},{23,7},{24,8},{25... | collective-permute-start | bytes 786440 | tf_op jit(solution)/shard_map/ppermute | solution.py:276
  168.9 54.3 %collective-permute-start.12 = (f32[256,256]{1,0:T(8,128)S(1)}, f32[256,256]{1,0:T(8,128)S(1)}, u32[]{:S(2)}, u32[]{:S(2)}) collective-permute-start(f32[256,256]{1,0:T(8,128)S(1)} %get-tuple-element.57), channel_id=1, source_target_pairs={{16,8},{17,9},{18,10},{19,11},{20,12},{21,13},{22,14},{23,15},{24,... | collective-permute-start | bytes 786440 | tf_op jit(solution)/shard_map/ppermute | solution.py:276
  183.8 13.5 %collective-permute-start.20 = (f32[16,256]{1,0:T(8,128)S(1)}, f32[16,256]{1,0:T(8,128)S(1)}, u32[]{:S(2)}, u32[]{:S(2)}) collective-permute-start(f32[16,256]{1,0:T(8,128)S(1)} %get-tuple-element.34), channel_id=1, source_target_pairs={{0,4},{1,5},{2,6},{3,7},{4,8},{5,9},{6,10},{7,11},{8,12},{9,13},{1... | collective-permute-start | bytes 49160 | tf_op jit(solution)/shard_map/ppermute | solution.py:263
  187.4 11.8 %collective-permute-start.21 = (f32[16,256]{1,0:T(8,128)S(1)}, f32[16,256]{1,0:T(8,128)S(1)}, u32[]{:S(2)}, u32[]{:S(2)}) collective-permute-start(f32[16,256]{1,0:T(8,128)S(1)} %get-tuple-element.35), channel_id=1, source_target_pairs={{4,0},{5,1},{6,2},{7,3},{8,4},{9,5},{10,6},{11,7},{12,8},{13,9},{1... | collective-permute-start | bytes 49160 | tf_op jit(solution)/shard_map/ppermute | solution.py:264
  193.0 6.2 %collective-permute-start.22 = (f32[16,256]{1,0:T(8,128)S(1)}, f32[16,256]{1,0:T(8,128)S(1)}, u32[]{:S(2)}, u32[]{:S(2)}) collective-permute-start(f32[16,256]{1,0:T(8,128)S(1)} %get-tuple-element.36), channel_id=1, source_target_pairs={{0,1},{1,2},{2,3},{4,5},{5,6},{6,7},{8,9},{9,10},{10,11},{12,13},{... | collective-permute-start | bytes 49160 | tf_op jit(solution)/shard_map/ppermute | solution.py:266
  197.3 5.1 %collective-permute-start.23 = (f32[16,256]{1,0:T(8,128)S(1)}, f32[16,256]{1,0:T(8,128)S(1)}, u32[]{:S(2)}, u32[]{:S(2)}) collective-permute-start(f32[16,256]{1,0:T(8,128)S(1)} %get-tuple-element.37), channel_id=1, source_target_pairs={{1,0},{2,1},{3,2},{5,4},{6,5},{7,6},{9,8},{10,9},{11,10},{13,12},{... | collective-permute-start | bytes 49160 | tf_op jit(solution)/shard_map/ppermute | solution.py:267
  (2 other events, 35.1 us)
Sparse Core Ops, SparseCore 0:
  24.1 47.1 all-gather.2
  121.7 45.9 all-gather.4

commit v3 on v0

v3 whole, which is shorter than its diff:
```python
import jax
import jax.numpy as jnp
from jax import lax
from jax.experimental import pallas as pl
from jax.experimental.pallas import tpu as pltpu
from jax.sharding import PartitionSpec as P

TCOL = 4
LIFTS = 8
TILES = 16
NZ = 16
W = 256
H = W // 2
TIME_STEP = 0.1
INJECT_RATE = 2.0
AMBIENT = 1.0
F32 = jnp.float32
BF16 = jnp.bfloat16
MIB = 1 << 20


def tile_of(x_half, y, core):
    return x_half * 8 + (y % 4) * 2 + core


def coords(tile):
    return tile // 8, (tile // 2) % 4, tile % 2


def along_y(steps):
    return [(t, tile_of(coords(t)[0], coords(t)[1] + steps, coords(t)[2])) for t in range(TILES)]


OTHER_CORE = [(t, t ^ 1) for t in range(TILES)]
OTHER_HALF = [(t, t ^ 8) for t in range(TILES)]
BY_HALF = [list(range(8)), list(range(8, 16))]


def to_lift(steps, flip):
    pairs = []
    for lift in range(LIFTS):
        if 0 <= lift + steps < LIFTS:
            for t in range(TILES):
                pairs.append((lift * TILES + t, (lift + steps) * TILES + (t ^ (8 if flip else 0))))
    return pairs


def send_y(value, steps):
    return lax.ppermute(value, "tile", along_y(steps))


def send_lift(value, steps, flip):
    return lax.ppermute(value, ("lift", "tile"), to_lift(steps, flip))


def split(value):
    high = value.astype(BF16)
    return high, (value - high.astype(F32)).astype(BF16)


def product(a, b, dims):
    def one(u, v):
        return lax.dot_general(u, v, (dims, ((), ())), preferred_element_type=F32)

    return one(a[0], b[0]) + (one(a[0], b[1]) + one(a[1], b[0]))


SMEM_SPEC = pl.BlockSpec(memory_space=pltpu.SMEM)
VMEM_SPEC = pl.BlockSpec(memory_space=pltpu.VMEM)


def planes(*count):
    return jax.ShapeDtypeStruct((*count, W, W), F32)


def cost(flops, mib):
    return pl.CostEstimate(flops=flops, bytes_accessed=mib * MIB, transcendentals=0)


def pieces_kernel(table, px, py, bottom, give, keep):
    give[...] = jnp.zeros_like(give)
    keep[...] = jnp.zeros_like(keep)
    plane = split(bottom[...])
    for k in range(4):
        left = product(split(px[k]), plane, ((0,), (0,)))
        piece = product(split(left), split(py[k]), ((1,), (0,)))
        source, tile = table[k], table[4]
        x_step = ((source >> 3) ^ (tile >> 3)) & 1
        y_step = ((source >> 1) - (tile >> 1)) & 3
        core_step = (source ^ tile) & 1
        place = jnp.where(y_step == 2, 0, jnp.where(y_step == 3, 3, y_step + 1))
        slot = x_step * 4 + place

        @pl.when(core_step == 0)
        def _():
            keep[slot] = keep[slot] + piece

        @pl.when(core_step == 1)
        def _():
            give[slot] = give[slot] + piece


def pieces_of(table, px, py, bottom):
    return pl.pallas_call(
        pieces_kernel,
        out_shape=(planes(8), planes(8)),
        in_specs=[SMEM_SPEC] + [VMEM_SPEC] * 3,
        out_specs=[VMEM_SPEC] * 2,
        compiler_params=pltpu.CompilerParams(vmem_limit_bytes=24 * MIB),
        cost_estimate=cost(8 * 6 * W**3, 7),
        name="pieces",
    )(table, px, py, bottom)


def below_kernel(table, px, py, speed, field, tops, out, picked, sems):
    def fetch(k):
        source, tile = table[k], table[4]
        x_step = ((source >> 3) ^ (tile >> 3)) & 1
        return pltpu.make_async_copy(tops.at[(source & 7) * 2 + x_step], picked.at[k], sems.at[k])

    for k in range(4):
        fetch(k).start()
    total = jnp.zeros((W, W), F32)
    for k in range(4):
        fetch(k).wait()
        left = product(split(px[k]), split(picked[k]), ((1,), (0,)))
        total = total + product(split(left), split(py[k]), ((1,), (1,)))
    total = jnp.where(table[5] == 1, total, 0.0)
    out[...] = field[...] + TIME_STEP * (total + speed[...] * total)


def below_update(table, px, py, speed, plane, tops):
    return pl.pallas_call(
        below_kernel,
        out_shape=planes(),
        in_specs=[SMEM_SPEC] + [VMEM_SPEC] * 4 + [pl.BlockSpec(memory_space=pltpu.HBM)],
        out_specs=VMEM_SPEC,
        scratch_shapes=[pltpu.VMEM((4, W, W), F32), pltpu.SemaphoreType.DMA((4,))],
        compiler_params=pltpu.CompilerParams(vmem_limit_bytes=16 * MIB),
        cost_estimate=cost(8 * 6 * W**3, 5),
        name="below",
    )(table, px, py, speed, plane, tops)


def rims_kernel(field, bottom, top, row_low, row_high, col_low, col_high):
    lane = lax.broadcasted_iota(jnp.int32, (W, 128), 1)
    low = jnp.zeros((W, 128), F32)
    high = jnp.zeros((W, 128), F32)
    for z in range(NZ):
        ref = bottom if z == 0 else top if z == NZ - 1 else field.at[z]
        row_low[z : z + 1, :] = ref[0:1, :]
        row_high[z : z + 1, :] = ref[W - 1 : W, :]
        low = jnp.where(lane == z, ref[:, 0:1], low)
        high = jnp.where(lane == z, ref[:, W - 1 : W], high)
    col_low[...] = low.T[:NZ]
    col_high[...] = high.T[:NZ]


def rims_of(field, bottom, top):
    rim = jax.ShapeDtypeStruct((NZ, W), F32)
    return pl.pallas_call(
        rims_kernel,
        out_shape=(rim,) * 4,
        in_specs=[VMEM_SPEC] * 3,
        out_specs=[VMEM_SPEC] * 4,
        compiler_params=pltpu.CompilerParams(vmem_limit_bytes=16 * MIB),
        cost_estimate=cost(NZ * W * W, 4),
        name="rims",
    )(field, bottom, top)


def stencil_kernel(inverse, field, bottom, top, speed, inlets, x_low, x_high, y_low, y_high, out, low, high):
    pad = jnp.zeros((128 - NZ, W), F32)
    low[...] = jnp.concatenate([y_low[...], pad], axis=0).T
    high[...] = jnp.concatenate([y_high[...], pad], axis=0).T
    scale = inverse[0]

    def update(z, here, under, over):
        pick = lax.broadcasted_iota(jnp.int32, (W, 128), 1) == z
        col_low = jnp.sum(jnp.where(pick, low[...], 0.0), axis=1, keepdims=True)
        col_high = jnp.sum(jnp.where(pick, high[...], 0.0), axis=1, keepdims=True)
        row = lax.broadcasted_iota(jnp.int32, (W, W), 0)
        lane = lax.broadcasted_iota(jnp.int32, (W, W), 1)
        beside = jnp.where(row == 0, x_low[pl.ds(z, 1), :], pltpu.roll(here, 1, 0))
        beside = beside + jnp.where(row == W - 1, x_high[pl.ds(z, 1), :], pltpu.roll(here, W - 1, 0))
        beside = beside + jnp.where(lane == 0, col_low, pltpu.roll(here, 1, 1))
        beside = beside + jnp.where(lane == W - 1, col_high, pltpu.roll(here, W - 1, 1))
        lapl = (beside - 4.0 * here) * scale
        change = lapl + over + under - 2.0 * here - speed[z] * (here - under)
        return here + TIME_STEP * change

    zero = jnp.zeros((W, W), F32)
    first = bottom[...]
    inject = INJECT_RATE * inlets[...].astype(F32)
    out[0] = update(0, first, zero, field[1]) + TIME_STEP * (inject * (1.0 - first))
    out[1] = update(1, field[1], first, field[2])

    def middle(z, carry):
        out[z] = update(z, field[z], field[z - 1], field[z + 1])
        return carry

    lax.fori_loop(2, NZ - 2, middle, 0)
    out[NZ - 2] = update(NZ - 2, field[NZ - 2], field[NZ - 3], top[...])
    out[NZ - 1] = update(NZ - 1, top[...], field[NZ - 2], zero)


def stencil(inverse, field, bottom, top, speed, inlets, halos):
    return pl.pallas_call(
        stencil_kernel,
        out_shape=planes(NZ),
        in_specs=[SMEM_SPEC] + [VMEM_SPEC] * 9,
        out_specs=VMEM_SPEC,
        scratch_shapes=[pltpu.VMEM((W, 128), F32)] * 2,
        compiler_params=pltpu.CompilerParams(vmem_limit_bytes=24 * MIB),
        cost_estimate=cost(16 * NZ * W * W, 12),
        name="stencil",
    )(inverse, field, bottom, top, speed, inlets, *halos)


def place_kernel(bottom, top, field, out, sems):
    copies = [
        pltpu.make_async_copy(bottom, out.at[0], sems.at[0]),
        pltpu.make_async_copy(top, out.at[NZ - 1], sems.at[1]),
    ]
    for copy in copies:
        copy.start()
    for copy in copies:
        copy.wait()


def place_ends(bottom, top, field):
    return pl.pallas_call(
        place_kernel,
        out_shape=planes(NZ),
        in_specs=[VMEM_SPEC] * 2 + [pl.BlockSpec(memory_space=pl.ANY)],
        out_specs=pl.BlockSpec(memory_space=pl.ANY),
        scratch_shapes=[pltpu.SemaphoreType.DMA((2,))],
        input_output_aliases={2: 0},
        cost_estimate=cost(1, 1),
        name="place_ends",
    )(bottom, top, field)


def exchange_rims(rims):
    row_low, row_high, col_low, col_high = rims
    x_low = lax.ppermute(row_high, "tile", [(t, t + TCOL) for t in range(TILES - TCOL)])
    x_high = lax.ppermute(row_low, "tile", [(t + TCOL, t) for t in range(TILES - TCOL)])
    inside = [t for t in range(TILES) if t % TCOL < TCOL - 1]
    y_low = lax.ppermute(col_high, "tile", [(t, t + 1) for t in inside])
    y_high = lax.ppermute(col_low, "tile", [(t + 1, t) for t in inside])
    return x_low, x_high, y_low, y_high


def climb(plane):
    return send_lift(plane, 1, False), send_lift(plane, 1, True)


def gather_pair(mine, flip):
    return lax.all_gather(jnp.stack([mine, flip]), "tile", axis_index_groups=BY_HALF, axis=0, tiled=True)


def reduce_pieces(give, keep):
    taken = lax.ppermute(give, "tile", OTHER_CORE)
    far = lax.ppermute(keep[4] + taken[4], "tile", OTHER_HALF)
    rest = lax.ppermute(keep[5:8] + taken[5:8], "tile", OTHER_HALF)
    far = far + (keep[0] + taken[0])
    from_left = send_y(far[:H], 1)
    from_right = send_y(far[H:], -1)
    mine = rest + (keep[1:4] + taken[1:4])
    right = jnp.concatenate([mine[1, :H] + from_left, mine[1, H:]])
    left = jnp.concatenate([mine[2, :H], mine[2, H:] + from_right])
    return mine[0] + (send_y(right, 1) + send_y(left, -1))


def on_device(oxygen, velocity, spacing, inlets, proj_x, proj_y, sources):
    field = oxygen.reshape(NZ, W, W)
    speed = velocity.reshape(NZ, W, W)
    inlets = inlets.reshape(W, W)
    px = proj_x.reshape(4, W, W)
    py = proj_y.reshape(4, W, W)
    inverse = 1.0 / (spacing * spacing)
    tile = lax.axis_index("tile").astype(jnp.int32)
    lift = lax.axis_index("lift")
    has_below = (lift > 0).astype(jnp.int32)
    is_top = lift == LIFTS - 1
    table = jnp.concatenate([sources.reshape(4) & (TILES - 1), tile[None], has_below[None]])
    speed_low = speed[0]
    bottom, top = field[0], field[NZ - 1]

    def with_above(plane, ghost):
        return plane + TIME_STEP * jnp.where(is_top, AMBIENT, send_lift(ghost, -1, False))

    mine, flip = climb(top)
    tops = gather_pair(mine, flip)
    ghost = reduce_pieces(*pieces_of(table, px, py, bottom))
    halos = exchange_rims(rims_of(field, bottom, top))
    field = stencil(inverse, field, bottom, top, speed, inlets, halos)
    mine, flip = climb(field[NZ - 1])
    bottom = below_update(table, px, py, speed_low, field[0], tops)
    tops = gather_pair(
        mine + TIME_STEP * ghost, flip + TIME_STEP * lax.ppermute(ghost, "tile", OTHER_HALF)
    )
    top = with_above(field[NZ - 1], ghost)
    ghost = reduce_pieces(*pieces_of(table, px, py, bottom))
    halos = exchange_rims(rims_of(field, bottom, top))
    field = stencil(inverse, field, bottom, top, speed, inlets, halos)
    bottom = below_update(table, px, py, speed_low, field[0], tops)
    top = with_above(field[NZ - 1], ghost)
    return place_ends(bottom, top, field).reshape(1, NZ, 1, W, W)


def solution(mesh):
    return jax.shard_map(
        on_device,
        mesh=mesh,
        in_specs=(
            P("lift", None, "tile", None, None),
            P("lift", None, "tile", None, None),
            P("lift"),
            P("lift", "tile", None, None),
            P("lift", "tile", None, None, None),
            P("lift", "tile", None, None, None),
            P("lift", "tile", None),
        ),
        out_specs=P("lift", None, "tile", None, None),
        check_vma=False,
    )
```

time: 527 us -> 203 us (0.39)
  waiting for transfers between devices: 358 us -> 62.4 us
  local copies, waits for them, and re-layouts: 66.6 us -> 12.8 us
  Pallas kernels: 0 us -> 32 us
  starting transfers between devices: 42.4 us -> 70.7 us
  matrix products: 23 us -> 0 us
  other arithmetic: 21.5 us -> 8.52 us
    ppermute x12 -> x29, waiting for transfers between devices: 358 us -> 62.3 us  [the longest x2 29.7 us: reduce_pieces(): far = lax.ppermute(keep[4] + taken[4], 'tile', OTHER_HALF)]
    pallas_call x0 -> x9, Pallas kernels: none -> 32 us  [the longest x2 15 us: stencil(): pl.pallas_call(stencil_kernel, out_shape=planes(NZ), in_specs=[SMEM_SPEC]...]
    ppermute x12 -> x29, starting transfers between devices: 42.3 us -> 70.7 us  [the longest x6 22.2 us: send_lift(): return lax.ppermute(value, ('lift', 'tile'), to_lift(steps, flip))]
    dot_general x10 -> x0, matrix products: 23 us -> none  [the longest x4 7.82 us: on_device(): jnp.einsum('kba,bc,kcd->kad', blocks_x, bottom_plane, blocks_y, precision...]
    slice x7 -> x2, local copies, waits for them, and re-layouts: 16.6 us -> 0.04 us  [reduce_pieces(): from_right = send_y(far[H:], -1)]
    sub x2 -> x0, other arithmetic: 15.3 us -> none  [on_device(): change = lapl + over + under - 2.0 * field - speed * (field - under)]
    broadcast_in_dim x9 -> x0, local copies, waits for them, and re-layouts: 13.3 us -> none  [the longest x1 5.34 us: on_device(): return field[None, :, None]]
    dot_general x2 -> x0, local copies, waits for them, and re-layouts: 10.6 us -> none  [on_device(): outgoing = jnp.einsum('ks,kad->sad', onehot, pieces, precision=HIGHEST)]
  transfers between devices with their start and end apart: 16 -> 31, of which waited for: 5 -> 13; matrix products, arithmetic and copies ran while one was open for 13% -> 4% of each run, Pallas kernels for 0% -> 15%
where the time goes in v3:
time: 203 us; the launch traced here: 201 us
  starting transfers between devices  70.7 us (35%)
  waiting for transfers between devices  62.4 us (31%)
  Pallas kernels  32 us (16%)
  between operations  14.7 us (7%)
  local copies, waits for them, and re-layouts  12.8 us (6%)
  other arithmetic  8.52 us (4%)
    ppermute x2, waiting for transfers between devices, reduce_pieces(): far = lax.ppermute(keep[4] + taken[4], 'tile', OTHER_HALF)  29.7 us
    ppermute x6, starting transfers between devices, send_lift(): return lax.ppermute(value, ('lift', 'tile'), to_lift(steps, flip))  22.2 us
    ppermute x6, waiting for transfers between devices, send_lift(): return lax.ppermute(value, ('lift', 'tile'), to_lift(steps, flip))  16.6 us
    pallas_call x2, Pallas kernels, stencil(): pl.pallas_call(stencil_kernel, out_shape=planes(NZ), in_specs=[SMEM_SPEC]...  15 us
    ppermute x8, starting transfers between devices, send_y(): return lax.ppermute(value, 'tile', along_y(steps))  14.5 us
    ppermute x2, starting transfers between devices, exchange_rims(): lax.ppermute(row_low, 'tile', [(t + TCOL, t) for t in range(TILES - TCOL)])  12.5 us
    unnamed x30, local copies, waits for them, and re-layouts  9.57 us
    ppermute x8, waiting for transfers between devices, send_y(): return lax.ppermute(value, 'tile', along_y(steps))  8.09 us
  transfers between devices with their start and end apart: 31, of which 13 were waited for; matrix products, arithmetic and copies ran while one was open for 4% of the time, Pallas kernels for 15%

profile of v3, /device:TPU:6, one launch (start us, length us, event | category | flops | bytes accessed | tf_op | source)
XLA Modules:
  0.0 201.1 jit_solution(15134214393143810447)
XLA Ops:
  7.8 3.7 %collective-permute-start.5 = (f32[256,256]{1,0:T(8,128)S(1)}, f32[256,256]{1,0:T(8,128)S(1)}, u32[]{:S(2)}, u32[]{:S(2)}) collective-permute-start(f32[256,256]{1,0:T(8,128)S(1)} %get-tuple-element.33.top), channel_id=1, source_target_pairs={{0,24},{1,25},{2,26},{3,27},{4,28},{5,29},{6,30},{7,31},{8,16},{9,... | collective-permute-start | bytes 786440 | tf_op jit(solution)/shard_map/ppermute | solution.py:53
  11.5 2.8 %collective-permute-start.4 = (f32[256,256]{1,0:T(8,128)S(1)}, f32[256,256]{1,0:T(8,128)S(1)}, u32[]{:S(2)}, u32[]{:S(2)}) collective-permute-start(f32[256,256]{1,0:T(8,128)S(1)} %get-tuple-element.33.top), channel_id=1, source_target_pairs={{0,16},{1,17},{2,18},{3,19},{4,20},{5,21},{6,22},{7,23},{8,24},{9,... | collective-permute-start | bytes 786440 | tf_op jit(solution)/shard_map/ppermute | solution.py:53
  14.3 4.6 %collective-permute-done.5 = f32[256,256]{1,0:T(8,128)S(1)} collective-permute-done((f32[256,256]{1,0:T(8,128)S(1)}, f32[256,256]{1,0:T(8,128)S(1)}, u32[]{:S(2)}, u32[]{:S(2)}) %collective-permute-start.5) | collective-permute-done | bytes 262176 | tf_op jit(solution)/shard_map/ppermute | solution.py:53
  18.9 4.1 %collective-permute-done.4 = f32[256,256]{1,0:T(8,128)S(1)} collective-permute-done((f32[256,256]{1,0:T(8,128)S(1)}, f32[256,256]{1,0:T(8,128)S(1)}, u32[]{:S(2)}, u32[]{:S(2)}) %collective-permute-start.4) | collective-permute-done | bytes 262176 | tf_op jit(solution)/shard_map/ppermute | solution.py:53
  24.0 3.4 %pieces.2 = (f32[8,256,256]{2,1,0:T(8,128)S(1)}, f32[8,256,256]{2,1,0:T(8,128)S(1)}) custom-call(s32[6]{0:T(128)S(1)} %pad_add_fusion.table, f32[4,256,256]{2,1,0:T(8,128)S(1)} %bitcast.85, f32[4,256,256]{2,1,0:T(8,128)S(1)} %bitcast.89, f32[256,256]{1,0:T(8,128)S(1)} %get-tuple-element.34.bottom), custom_call_target="tpu_custom_call" | custom-call | flops 805306368 | bytes 7340032 | tf_op jit(solution)/shard_map/pieces/pallas_call | solution.py:104
  27.5 2.2 %copy-done.2 = f32[1,16,1,256,256]{4,3,2,1,0:T(8,128)S(1)} copy-done((f32[1,16,1,256,256]{4,3,2,1,0:T(8,128)S(1)}, f32[1,16,1,256,256]{4,3,2,1,0:T(8,128)}, u32[]{:S(2)}) %copy-start.2) | copy-done | bytes 4194328
  31.0 5.2 %collective-permute-start = (f32[16,256]{1,0:T(8,128)S(1)}, f32[16,256]{1,0:T(8,128)S(1)}, u32[]{:S(2)}, u32[]{:S(2)}) collective-permute-start(f32[16,256]{1,0:T(8,128)S(1)} %get-tuple-element.17), channel_id=1, source_target_pairs={{0,4},{1,5},{2,6},{3,7},{4,8},{5,9},{6,10},{7,11},{8,12},{9,13},{1... | collective-permute-start | bytes 49160 | tf_op jit(solution)/shard_map/ppermute | solution.py:246
  36.2 4.7 %collective-permute-start.1 = (f32[16,256]{1,0:T(8,128)S(1)}, f32[16,256]{1,0:T(8,128)S(1)}, u32[]{:S(2)}, u32[]{:S(2)}) collective-permute-start(f32[16,256]{1,0:T(8,128)S(1)} %get-tuple-element.18), channel_id=1, source_target_pairs={{4,0},{5,1},{6,2},{7,3},{8,4},{9,5},{10,6},{11,7},{12,8},{13,9},{1... | collective-permute-start | bytes 49160 | tf_op jit(solution)/shard_map/ppermute | solution.py:247
  44.3 3.6 %collective-permute-start.8 = (f32[256,256]{1,0:T(8,128)S(1)}, f32[256,256]{1,0:T(8,128)S(1)}, u32[]{:S(2)}, u32[]{:S(2)}) collective-permute-start(f32[256,256]{1,0:T(8,128)S(1)} %fusion.9), channel_id=1, source_target_pairs={{0,8},{1,9},{2,10},{3,11},{4,12},{5,13},{6,14},{7,15},{8,0},{9,1},... | collective-permute-start | bytes 786440 | tf_op jit(solution)/shard_map/ppermute | solution.py:264
  48.7 2.3 %copy-done.4 = f32[1,16,1,256,256]{4,3,2,1,0:T(8,128)S(1)} copy-done((f32[1,16,1,256,256]{4,3,2,1,0:T(8,128)S(1)}, f32[1,16,1,256,256]{4,3,2,1,0:T(8,128)}, u32[]{:S(2)}) %copy-start.4) | copy-done | bytes 4194328
  50.9 6.5 %stencil.2.field = f32[16,256,256]{2,1,0:T(8,128)S(1)} custom-call(f32[1]{0:T(128)S(6)} %div.3.inverse, f32[16,256,256]{2,1,0:T(8,128)S(1)} %bitcast.82, f32[256,256]{1,0:T(8,128)S(1)} %get-tuple-element.34.bottom, f32[256,256]{1,0:T(8,128)S(1)} %get-tuple-element.33.top, f32[16,256,256]{2,1,0:T(8,128)S(1)} %bitcast.83, s32[256,256]{1,0:T(8,128)S(1)} %bitcast.93, ...), custom_call_target="tpu_custom_call" | custom-call | flops 16777216 | bytes 12582912 | tf_op jit(solution)/shard_map/stencil/pallas_call | solution.py:208
  57.5 5.3 %collective-permute-start.18 = (f32[256,256]{1,0:T(8,128)S(1)}, f32[256,256]{1,0:T(8,128)S(1)}, u32[]{:S(2)}, u32[]{:S(2)}) collective-permute-start(f32[256,256]{1,0:T(8,128)S(1)} %get-tuple-element.31), channel_id=1, source_target_pairs={{0,16},{1,17},{2,18},{3,19},{4,20},{5,21},{6,22},{7,23},{8,24},{9,... | collective-permute-start | bytes 786440 | tf_op jit(solution)/shard_map/ppermute | solution.py:53
  62.9 7.4 %collective-permute-done.8 = f32[256,256]{1,0:T(8,128)S(1)} collective-permute-done((f32[256,256]{1,0:T(8,128)S(1)}, f32[256,256]{1,0:T(8,128)S(1)}, u32[]{:S(2)}, u32[]{:S(2)}) %collective-permute-start.8) | collective-permute-done | bytes 262176 | tf_op jit(solution)/shard_map/ppermute | solution.py:264
  70.4 4.7 %collective-permute-start.11 = (f32[128,256]{1,0:T(8,128)S(1)}, f32[128,256]{1,0:T(8,128)S(1)}, u32[]{:S(2)}, u32[]{:S(2)}) collective-permute-start(f32[128,256]{1,0:T(8,128)S(1)} %get-tuple-element.45), channel_id=1, source_target_pairs={{0,6},{1,7},{2,0},{3,1},{4,2},{5,3},{6,4},{7,5},{8,14},{9,15},{10,... | collective-permute-start | bytes 393224 | tf_op jit(solution)/shard_map/ppermute | solution.py:49
  76.3 2.7 %collective-permute-done.11 = f32[128,256]{1,0:T(8,128)S(1)} collective-permute-done((f32[128,256]{1,0:T(8,128)S(1)}, f32[128,256]{1,0:T(8,128)S(1)}, u32[]{:S(2)}, u32[]{:S(2)}) %collective-permute-start.11) | collective-permute-done | bytes 131104 | tf_op jit(solution)/shard_map/ppermute | solution.py:49
  79.0 2.3 %collective-permute-done.9 = f32[128,256]{1,0:T(8,128)S(1)} collective-permute-done((f32[128,256]{1,0:T(8,128)S(1)}, f32[128,256]{1,0:T(8,128)S(1)}, u32[]{:S(2)}, u32[]{:S(2)}) %collective-permute-start.9) | collective-permute-done | bytes 131104 | tf_op jit(solution)/shard_map/ppermute | solution.py:49
  81.7 3.0 %collective-permute-start.12 = (f32[256,256]{1,0:T(8,128)S(1)}, f32[256,256]{1,0:T(8,128)S(1)}, u32[]{:S(2)}, u32[]{:S(2)}) collective-permute-start(f32[256,256]{1,0:T(8,128)S(1)} %pad_maximum_fusion.3), channel_id=1, source_target_pairs={{0,6},{1,7},{2,0},{3,1},{4,2},{5,3},{6,4},{7,5},{8,14},{9,15},{10,... | collective-permute-start | bytes 786440 | tf_op jit(solution)/shard_map/ppermute | solution.py:49
  84.7 6.5 %collective-permute-start.19 = (f32[256,256]{1,0:T(8,128)S(1)}, f32[256,256]{1,0:T(8,128)S(1)}, u32[]{:S(2)}, u32[]{:S(2)}) collective-permute-start(f32[256,256]{1,0:T(8,128)S(1)} %get-tuple-element.31), channel_id=1, source_target_pairs={{0,24},{1,25},{2,26},{3,27},{4,28},{5,29},{6,30},{7,31},{8,16},{9,... | collective-permute-start | bytes 786440 | tf_op jit(solution)/shard_map/ppermute | solution.py:53
  92.4 4.9 %collective-permute-done.19 = f32[256,256]{1,0:T(8,128)S(1)} collective-permute-done((f32[256,256]{1,0:T(8,128)S(1)}, f32[256,256]{1,0:T(8,128)S(1)}, u32[]{:S(2)}, u32[]{:S(2)}) %collective-permute-start.19) | collective-permute-done | bytes 262176 | tf_op jit(solution)/shard_map/ppermute | solution.py:53
  101.2 2.2 %copy-done.8 = f32[16,256,256]{2,1,0:T(8,128)S(1)} copy-done((f32[16,256,256]{2,1,0:T(8,128)S(1)}, f32[16,256,256]{2,1,0:T(8,128)}, u32[]{:S(2)}) %copy-start.8) | copy-done | bytes 4194328
  103.4 2.8 %below.2.bottom = f32[256,256]{1,0:T(8,128)S(1)} custom-call(s32[6]{0:T(128)S(1)} %pad_add_fusion.table, f32[4,256,256]{2,1,0:T(8,128)S(1)} %bitcast.86, f32[4,256,256]{2,1,0:T(8,128)S(1)} %bitcast.90, f32[256,256]{1,0:T(8,128)S(1)} %slice_bitcast_fusion.8.speed, f32[256,256]{1,0:T(8,128)S(1)} %get-tuple-element.32.field, f32[16,256,256]{2,1,0:T(8,128)S(1)} %copy-done.8), custom_call_target="tpu_custom_call" | custom-call | flops 805306368 | bytes 5242880 | tf_op jit(solution)/shard_map/below/pallas_call | solution.py:133
  106.2 3.6 %pieces.3 = (f32[8,256,256]{2,1,0:T(8,128)S(1)}, f32[8,256,256]{2,1,0:T(8,128)S(1)}) custom-call(s32[6]{0:T(128)S(1)} %pad_add_fusion.table, f32[4,256,256]{2,1,0:T(8,128)S(1)} %bitcast.87, f32[4,256,256]{2,1,0:T(8,128)S(1)} %bitcast.91, f32[256,256]{1,0:T(8,128)S(1)} %below.2.bottom), custom_call_target="tpu_custom_call" | custom-call | flops 805306368 | bytes 7340032 | tf_op jit(solution)/shard_map/pieces/pallas_call | solution.py:104
  109.9 4.1 %collective-permute-done.21 = f32[8,256,256]{2,1,0:T(8,128)S(1)} collective-permute-done((f32[8,256,256]{2,1,0:T(8,128)S(1)}, f32[8,256,256]{2,1,0:T(8,128)S(1)}, u32[]{:S(2)}, u32[]{:S(2)}) %collective-permute-start.21) | collective-permute-done | bytes 2097184 | tf_op jit(solution)/shard_map/ppermute | solution.py:263
  120.8 22.2 %collective-permute-done.23 = f32[256,256]{1,0:T(8,128)} collective-permute-done((f32[256,256]{1,0:T(8,128)S(1)}, f32[256,256]{1,0:T(8,128)}, u32[]{:S(2)}, u32[]{:S(2)}) %collective-permute-start.23) | collective-permute-done | bytes 262176 | tf_op jit(solution)/shard_map/ppermute | solution.py:264
  146.3 2.0 fusion
  149.2 2.2 %collective-permute-done.24 = f32[128,256]{1,0:T(8,128)S(1)} collective-permute-done((f32[128,256]{1,0:T(8,128)S(1)}, f32[128,256]{1,0:T(8,128)S(1)}, u32[]{:S(2)}, u32[]{:S(2)}) %collective-permute-start.24) | collective-permute-done | bytes 131104 | tf_op jit(solution)/shard_map/ppermute | solution.py:49
  151.6 3.3 %collective-permute-start.27 = (f32[256,256]{1,0:T(8,128)S(1)}, f32[256,256]{1,0:T(8,128)S(1)}, u32[]{:S(2)}, u32[]{:S(2)}) collective-permute-start(f32[256,256]{1,0:T(8,128)S(1)} %pad_maximum_fusion.5), channel_id=1, source_target_pairs={{0,6},{1,7},{2,0},{3,1},{4,2},{5,3},{6,4},{7,5},{8,14},{9,15},{10,... | collective-permute-start | bytes 786440 | tf_op jit(solution)/shard_map/ppermute | solution.py:49
  158.2 7.8 %collective-permute-start.15 = (f32[16,256]{1,0:T(8,128)S(1)}, f32[16,256]{1,0:T(8,128)S(1)}, u32[]{:S(2)}, u32[]{:S(2)}) collective-permute-start(f32[16,256]{1,0:T(8,128)S(1)} %get-tuple-element.24), channel_id=1, source_target_pairs={{4,0},{5,1},{6,2},{7,3},{8,4},{9,5},{10,6},{11,7},{12,8},{13,9},{1... | collective-permute-start | bytes 49160 | tf_op jit(solution)/shard_map/ppermute | solution.py:247
  170.4 8.5 %stencil.3.field = f32[16,256,256]{2,1,0:T(8,128)} custom-call(f32[1]{0:T(128)S(6)} %div.3.inverse, f32[16,256,256]{2,1,0:T(8,128)S(1)} %copy-done.1, f32[256,256]{1,0:T(8,128)S(1)} %below.2.bottom, f32[256,256]{1,0:T(8,128)S(1)} %multiply_add_fusion.top, f32[16,256,256]{2,1,0:T(8,128)S(1)} %bitcast.84, s32[256,256]{1,0:T(8,128)S(1)} %bitcast.94, ...), custom_call_target="tpu_custom_call" | custom-call | flops 16777216 | bytes 12582912 | tf_op jit(solution)/shard_map/stencil/pallas_call | solution.py:208
  181.9 2.2 %copy-done.9 = f32[16,256,256]{2,1,0:T(8,128)S(1)} copy-done((f32[16,256,256]{2,1,0:T(8,128)S(1)}, f32[16,256,256]{2,1,0:T(8,128)}, u32[]{:S(2)}) %copy-start.9) | copy-done | bytes 4194328
  184.1 2.8 %below.3.bottom = f32[256,256]{1,0:T(8,128)S(1)} custom-call(s32[6]{0:T(128)S(1)} %pad_add_fusion.table, f32[4,256,256]{2,1,0:T(8,128)S(1)} %bitcast.88, f32[4,256,256]{2,1,0:T(8,128)S(1)} %bitcast.92, f32[256,256]{1,0:T(8,128)S(1)} %slice_bitcast_fusion.8.speed, f32[256,256]{1,0:T(8,128)S(1)} %slice_bitcast_fusion.2.field, f32[16,256,256]{2,1,0:T(8,128)S(1)} %copy-done.9), custom_call_target="tpu_custom_call" | custom-call | flops 805306368 | bytes 5242880 | tf_op jit(solution)/shard_map/below/pallas_call | solution.py:133
  187.6 3.1 %collective-permute-done.28 = f32[256,256]{1,0:T(8,128)S(1)} collective-permute-done((f32[256,256]{1,0:T(8,128)S(1)}, f32[256,256]{1,0:T(8,128)S(1)}, u32[]{:S(2)}, u32[]{:S(2)}) %collective-permute-start.28) | collective-permute-done | bytes 262176 | tf_op jit(solution)/shard_map/ppermute | solution.py:53
  (102 shorter events, 39.8 us)
Async XLA Ops:
  6.5 94.7 %all-gather.3.cloned.1.call-start = ((), (), s32[]{:S(2)}) async-start(), calls=%async_computation | async-start | bytes 4718592 | tf_op jit(solution)/shard_map/all_gather | solution.py:259
  7.8 11.2 %collective-permute-start.5 = (f32[256,256]{1,0:T(8,128)S(1)}, f32[256,256]{1,0:T(8,128)S(1)}, u32[]{:S(2)}, u32[]{:S(2)}) collective-permute-start(f32[256,256]{1,0:T(8,128)S(1)} %get-tuple-element.33.top), channel_id=1, source_target_pairs={{0,24},{1,25},{2,26},{3,27},{4,28},{5,29},{6,30},{7,31},{8,16},{9,... | collective-permute-start | bytes 786440 | tf_op jit(solution)/shard_map/ppermute | solution.py:53
  11.5 11.5 %collective-permute-start.4 = (f32[256,256]{1,0:T(8,128)S(1)}, f32[256,256]{1,0:T(8,128)S(1)}, u32[]{:S(2)}, u32[]{:S(2)}) collective-permute-start(f32[256,256]{1,0:T(8,128)S(1)} %get-tuple-element.33.top), channel_id=1, source_target_pairs={{0,16},{1,17},{2,18},{3,19},{4,20},{5,21},{6,22},{7,23},{8,24},{9,... | collective-permute-start | bytes 786440 | tf_op jit(solution)/shard_map/ppermute | solution.py:53
  23.8 158.1 %all-gather.5.cloned.1.call-start = ((), (), s32[]{:S(2)}) async-start(), calls=%async_computation.1 | async-start | bytes 4718592 | tf_op jit(solution)/shard_map/all_gather | solution.py:259
  27.4 16.6 %collective-permute-start.6 = (f32[8,256,256]{2,1,0:T(8,128)S(1)}, f32[8,256,256]{2,1,0:T(8,128)S(1)}, u32[]{:S(2)}, u32[]{:S(2)}) collective-permute-start(f32[8,256,256]{2,1,0:T(8,128)S(1)} %get-tuple-element.22), channel_id=1, source_target_pairs={{0,1},{1,0},{2,3},{3,2},{4,5},{5,4},{6,7},{7,6},{8,9},{9,8},{10,11... | collective-permute-start | bytes 6291464 | tf_op jit(solution)/shard_map/ppermute | solution.py:263
  29.7 18.9 %copy-start.3 = (f32[1,16,1,256,256]{4,3,2,1,0:T(8,128)S(1)}, f32[1,16,1,256,256]{4,3,2,1,0:T(8,128)}, u32[]{:S(2)}) copy-start(f32[1,16,1,256,256]{4,3,2,1,0:T(8,128)} %param.7) | copy-start | bytes 12582916
  31.0 13.3 %collective-permute-start = (f32[16,256]{1,0:T(8,128)S(1)}, f32[16,256]{1,0:T(8,128)S(1)}, u32[]{:S(2)}, u32[]{:S(2)}) collective-permute-start(f32[16,256]{1,0:T(8,128)S(1)} %get-tuple-element.17), channel_id=1, source_target_pairs={{0,4},{1,5},{2,6},{3,7},{4,8},{5,9},{6,10},{7,11},{8,12},{9,13},{1... | collective-permute-start | bytes 49160 | tf_op jit(solution)/shard_map/ppermute | solution.py:246
  36.2 12.4 %collective-permute-start.1 = (f32[16,256]{1,0:T(8,128)S(1)}, f32[16,256]{1,0:T(8,128)S(1)}, u32[]{:S(2)}, u32[]{:S(2)}) collective-permute-start(f32[16,256]{1,0:T(8,128)S(1)} %get-tuple-element.18), channel_id=1, source_target_pairs={{4,0},{5,1},{6,2},{7,3},{8,4},{9,5},{10,6},{11,7},{12,8},{13,9},{1... | collective-permute-start | bytes 49160 | tf_op jit(solution)/shard_map/ppermute | solution.py:247
  40.9 7.7 %collective-permute-start.2 = (f32[16,256]{1,0:T(8,128)S(1)}, f32[16,256]{1,0:T(8,128)S(1)}, u32[]{:S(2)}, u32[]{:S(2)}) collective-permute-start(f32[16,256]{1,0:T(8,128)S(1)} %get-tuple-element.19), channel_id=1, source_target_pairs={{0,1},{1,2},{2,3},{4,5},{5,6},{6,7},{8,9},{9,10},{10,11},{12,13},{... | collective-permute-start | bytes 49160 | tf_op jit(solution)/shard_map/ppermute | solution.py:249
  42.7 5.9 %collective-permute-start.3 = (f32[16,256]{1,0:T(8,128)S(1)}, f32[16,256]{1,0:T(8,128)S(1)}, u32[]{:S(2)}, u32[]{:S(2)}) collective-permute-start(f32[16,256]{1,0:T(8,128)S(1)} %get-tuple-element.20), channel_id=1, source_target_pairs={{1,0},{2,1},{3,2},{5,4},{6,5},{7,6},{9,8},{10,9},{11,10},{13,12},{... | collective-permute-start | bytes 49160 | tf_op jit(solution)/shard_map/ppermute | solution.py:250
  44.2 31.9 %collective-permute-start.7 = (f32[3,256,256]{2,1,0:T(8,128)S(1)}, f32[3,256,256]{2,1,0:T(8,128)S(1)}, u32[]{:S(2)}, u32[]{:S(2)}) collective-permute-start(f32[3,256,256]{2,1,0:T(8,128)S(1)} %slice_add_fusion.3), channel_id=1, source_target_pairs={{0,8},{1,9},{2,10},{3,11},{4,12},{5,13},{6,14},{7,15},{8,0},{9,1},... | collective-permute-start | bytes 2359304 | tf_op jit(solution)/shard_map/ppermute | solution.py:265
  44.3 26.0 %collective-permute-start.8 = (f32[256,256]{1,0:T(8,128)S(1)}, f32[256,256]{1,0:T(8,128)S(1)}, u32[]{:S(2)}, u32[]{:S(2)}) collective-permute-start(f32[256,256]{1,0:T(8,128)S(1)} %fusion.9), channel_id=1, source_target_pairs={{0,8},{1,9},{2,10},{3,11},{4,12},{5,13},{6,14},{7,15},{8,0},{9,1},... | collective-permute-start | bytes 786440 | tf_op jit(solution)/shard_map/ppermute | solution.py:264
  57.5 33.7 %collective-permute-start.18 = (f32[256,256]{1,0:T(8,128)S(1)}, f32[256,256]{1,0:T(8,128)S(1)}, u32[]{:S(2)}, u32[]{:S(2)}) collective-permute-start(f32[256,256]{1,0:T(8,128)S(1)} %get-tuple-element.31), channel_id=1, source_target_pairs={{0,16},{1,17},{2,18},{3,19},{4,20},{5,21},{6,22},{7,23},{8,24},{9,... | collective-permute-start | bytes 786440 | tf_op jit(solution)/shard_map/ppermute | solution.py:53
  70.4 8.6 %collective-permute-start.11 = (f32[128,256]{1,0:T(8,128)S(1)}, f32[128,256]{1,0:T(8,128)S(1)}, u32[]{:S(2)}, u32[]{:S(2)}) collective-permute-start(f32[128,256]{1,0:T(8,128)S(1)} %get-tuple-element.45), channel_id=1, source_target_pairs={{0,6},{1,7},{2,0},{3,1},{4,2},{5,3},{6,4},{7,5},{8,14},{9,15},{10,... | collective-permute-start | bytes 393224 | tf_op jit(solution)/shard_map/ppermute | solution.py:49
  75.0 6.2 %collective-permute-start.9 = (f32[128,256]{1,0:T(8,128)S(1)}, f32[128,256]{1,0:T(8,128)S(1)}, u32[]{:S(2)}, u32[]{:S(2)}) collective-permute-start(f32[128,256]{1,0:T(8,128)S(1)} %get-tuple-element.46), channel_id=1, source_target_pairs={{0,2},{1,3},{2,4},{3,5},{4,6},{5,7},{6,0},{7,1},{8,10},{9,11},{10,... | collective-permute-start | bytes 393224 | tf_op jit(solution)/shard_map/ppermute | solution.py:49
  81.3 9.9 %collective-permute-start.10 = (f32[256,256]{1,0:T(8,128)S(1)}, f32[256,256]{1,0:T(8,128)S(1)}, u32[]{:S(2)}, u32[]{:S(2)}) collective-permute-start(f32[256,256]{1,0:T(8,128)S(1)} %pad_maximum_fusion.2), channel_id=1, source_target_pairs={{0,2},{1,3},{2,4},{3,5},{4,6},{5,7},{6,0},{7,1},{8,10},{9,11},{10,... | collective-permute-start | bytes 786440 | tf_op jit(solution)/shard_map/ppermute | solution.py:49
  81.7 9.6 %collective-permute-start.12 = (f32[256,256]{1,0:T(8,128)S(1)}, f32[256,256]{1,0:T(8,128)S(1)}, u32[]{:S(2)}, u32[]{:S(2)}) collective-permute-start(f32[256,256]{1,0:T(8,128)S(1)} %pad_maximum_fusion.3), channel_id=1, source_target_pairs={{0,6},{1,7},{2,0},{3,1},{4,2},{5,3},{6,4},{7,5},{8,14},{9,15},{10,... | collective-permute-start | bytes 786440 | tf_op jit(solution)/shard_map/ppermute | solution.py:49
  84.7 12.7 %collective-permute-start.19 = (f32[256,256]{1,0:T(8,128)S(1)}, f32[256,256]{1,0:T(8,128)S(1)}, u32[]{:S(2)}, u32[]{:S(2)}) collective-permute-start(f32[256,256]{1,0:T(8,128)S(1)} %get-tuple-element.31), channel_id=1, source_target_pairs={{0,24},{1,25},{2,26},{3,27},{4,28},{5,29},{6,30},{7,31},{8,16},{9,... | collective-permute-start | bytes 786440 | tf_op jit(solution)/shard_map/ppermute | solution.py:53
  91.3 8.0 %collective-permute-start.20 = (f32[256,256]{1,0:T(8,128)S(1)}, f32[256,256]{1,0:T(8,128)S(1)}, u32[]{:S(2)}, u32[]{:S(2)}) collective-permute-start(f32[256,256]{1,0:T(8,128)S(1)} %get-tuple-element.30), channel_id=1, source_target_pairs={{0,8},{1,9},{2,10},{3,11},{4,12},{5,13},{6,14},{7,15},{8,0},{9,1},... | collective-permute-start | bytes 786440 | tf_op jit(solution)/shard_map/ppermute | solution.py:301
  109.8 4.2 %collective-permute-start.21 = (f32[8,256,256]{2,1,0:T(8,128)S(1)}, f32[8,256,256]{2,1,0:T(8,128)S(1)}, u32[]{:S(2)}, u32[]{:S(2)}) collective-permute-start(f32[8,256,256]{2,1,0:T(8,128)S(1)} %get-tuple-element.28), channel_id=1, source_target_pairs={{0,1},{1,0},{2,3},{3,2},{4,5},{5,4},{6,7},{7,6},{8,9},{9,8},{10,11... | collective-permute-start | bytes 6291464 | tf_op jit(solution)/shard_map/ppermute | solution.py:263
  115.2 31.1 %collective-permute-start.22 = (f32[3,256,256]{2,1,0:T(8,128)}, f32[3,256,256]{2,1,0:T(8,128)}, u32[]{:S(2)}, u32[]{:S(2)}) collective-permute-start(f32[3,256,256]{2,1,0:T(8,128)} %slice_add_fusion.1), channel_id=1, source_target_pairs={{0,8},{1,9},{2,10},{3,11},{4,12},{5,13},{6,14},{7,15},{8,0},{9,1},... | collective-permute-start | bytes 2359304 | tf_op jit(solution)/shard_map/ppermute | solution.py:265
  117.0 26.0 %collective-permute-start.23 = (f32[256,256]{1,0:T(8,128)S(1)}, f32[256,256]{1,0:T(8,128)}, u32[]{:S(2)}, u32[]{:S(2)}) collective-permute-start(f32[256,256]{1,0:T(8,128)S(1)} %fusion.4), channel_id=1, source_target_pairs={{0,8},{1,9},{2,10},{3,11},{4,12},{5,13},{6,14},{7,15},{8,0},{9,1},... | collective-permute-start | bytes 786440 | tf_op jit(solution)/shard_map/ppermute | solution.py:264
  118.8 36.1 %collective-permute-start.13 = (f32[256,256]{1,0:T(8,128)S(1)}, f32[256,256]{1,0:T(8,128)S(1)}, u32[]{:S(2)}, u32[]{:S(2)}) collective-permute-start(f32[256,256]{1,0:T(8,128)S(1)} %get-tuple-element.30), channel_id=1, source_target_pairs={{16,0},{17,1},{18,2},{19,3},{20,4},{21,5},{22,6},{23,7},{24,8},{25... | collective-permute-start | bytes 786440 | tf_op jit(solution)/shard_map/ppermute | solution.py:53
  144.2 5.0 %collective-permute-start.26 = (f32[128,256]{1,0:T(8,128)S(1)}, f32[128,256]{1,0:T(8,128)S(1)}, u32[]{:S(2)}, u32[]{:S(2)}) collective-permute-start(f32[128,256]{1,0:T(8,128)S(1)} %get-tuple-element.43), channel_id=1, source_target_pairs={{0,6},{1,7},{2,0},{3,1},{4,2},{5,3},{6,4},{7,5},{8,14},{9,15},{10,... | collective-permute-start | bytes 393224 | tf_op jit(solution)/shard_map/ppermute | solution.py:49
  145.3 6.2 %collective-permute-start.24 = (f32[128,256]{1,0:T(8,128)S(1)}, f32[128,256]{1,0:T(8,128)S(1)}, u32[]{:S(2)}, u32[]{:S(2)}) collective-permute-start(f32[128,256]{1,0:T(8,128)S(1)} %get-tuple-element.44), channel_id=1, source_target_pairs={{0,2},{1,3},{2,4},{3,5},{4,6},{5,7},{6,0},{7,1},{8,10},{9,11},{10,... | collective-permute-start | bytes 393224 | tf_op jit(solution)/shard_map/ppermute | solution.py:49
  151.5 27.4 %collective-permute-start.25 = (f32[256,256]{1,0:T(8,128)S(1)}, f32[256,256]{1,0:T(8,128)S(1)}, u32[]{:S(2)}, u32[]{:S(2)}) collective-permute-start(f32[256,256]{1,0:T(8,128)S(1)} %pad_maximum_fusion.4), channel_id=1, source_target_pairs={{0,2},{1,3},{2,4},{3,5},{4,6},{5,7},{6,0},{7,1},{8,10},{9,11},{10,... | collective-permute-start | bytes 786440 | tf_op jit(solution)/shard_map/ppermute | solution.py:49
  151.6 27.3 %collective-permute-start.27 = (f32[256,256]{1,0:T(8,128)S(1)}, f32[256,256]{1,0:T(8,128)S(1)}, u32[]{:S(2)}, u32[]{:S(2)}) collective-permute-start(f32[256,256]{1,0:T(8,128)S(1)} %pad_maximum_fusion.5), channel_id=1, source_target_pairs={{0,6},{1,7},{2,0},{3,1},{4,2},{5,3},{6,4},{7,5},{8,14},{9,15},{10,... | collective-permute-start | bytes 786440 | tf_op jit(solution)/shard_map/ppermute | solution.py:49
  156.3 11.1 %collective-permute-start.14 = (f32[16,256]{1,0:T(8,128)S(1)}, f32[16,256]{1,0:T(8,128)S(1)}, u32[]{:S(2)}, u32[]{:S(2)}) collective-permute-start(f32[16,256]{1,0:T(8,128)S(1)} %get-tuple-element.23), channel_id=1, source_target_pairs={{0,4},{1,5},{2,6},{3,7},{4,8},{5,9},{6,10},{7,11},{8,12},{9,13},{1... | collective-permute-start | bytes 49160 | tf_op jit(solution)/shard_map/ppermute | solution.py:246
  158.2 10.4 %collective-permute-start.15 = (f32[16,256]{1,0:T(8,128)S(1)}, f32[16,256]{1,0:T(8,128)S(1)}, u32[]{:S(2)}, u32[]{:S(2)}) collective-permute-start(f32[16,256]{1,0:T(8,128)S(1)} %get-tuple-element.24), channel_id=1, source_target_pairs={{4,0},{5,1},{6,2},{7,3},{8,4},{9,5},{10,6},{11,7},{12,8},{13,9},{1... | collective-permute-start | bytes 49160 | tf_op jit(solution)/shard_map/ppermute | solution.py:247
  166.0 2.6 %collective-permute-start.16 = (f32[16,256]{1,0:T(8,128)S(1)}, f32[16,256]{1,0:T(8,128)S(1)}, u32[]{:S(2)}, u32[]{:S(2)}) collective-permute-start(f32[16,256]{1,0:T(8,128)S(1)} %get-tuple-element.25), channel_id=1, source_target_pairs={{0,1},{1,2},{2,3},{4,5},{5,6},{6,7},{8,9},{9,10},{10,11},{12,13},{... | collective-permute-start | bytes 49160 | tf_op jit(solution)/shard_map/ppermute | solution.py:249
  167.4 3.1 %collective-permute-start.17 = (f32[16,256]{1,0:T(8,128)S(1)}, f32[16,256]{1,0:T(8,128)S(1)}, u32[]{:S(2)}, u32[]{:S(2)}) collective-permute-start(f32[16,256]{1,0:T(8,128)S(1)} %get-tuple-element.26), channel_id=1, source_target_pairs={{1,0},{2,1},{3,2},{5,4},{6,5},{7,6},{9,8},{10,9},{11,10},{13,12},{... | collective-permute-start | bytes 49160 | tf_op jit(solution)/shard_map/ppermute | solution.py:250
  179.0 11.7 %collective-permute-start.28 = (f32[256,256]{1,0:T(8,128)S(1)}, f32[256,256]{1,0:T(8,128)S(1)}, u32[]{:S(2)}, u32[]{:S(2)}) collective-permute-start(f32[256,256]{1,0:T(8,128)S(1)} %fusion.5), channel_id=1, source_target_pairs={{16,0},{17,1},{18,2},{19,3},{20,4},{21,5},{22,6},{23,7},{24,8},{25... | collective-permute-start | bytes 786440 | tf_op jit(solution)/shard_map/ppermute | solution.py:53
  (14 other events, 133.6 us)
Sparse Core Ops, SparseCore 0:
  24.0 36.0 all-gather.2
  100.3 33.5 all-gather.4

commit v4 on v3

--- a/solution.py
+++ b/solution.py
@@ -73,8 +73,10 @@
     return jax.ShapeDtypeStruct((*count, W, W), F32)
 
 
-def cost(flops, mib):
-    return pl.CostEstimate(flops=flops, bytes_accessed=mib * MIB, transcendentals=0)
+MARK = jax.ShapeDtypeStruct((8, 128), F32)
+
+
+SMALL = pl.CostEstimate(flops=1024, bytes_accessed=1024, transcendentals=0)
 
 
 def pieces_kernel(table, px, py, bottom, give, keep):
@@ -88,8 +90,7 @@
         x_step = ((source >> 3) ^ (tile >> 3)) & 1
         y_step = ((source >> 1) - (tile >> 1)) & 3
         core_step = (source ^ tile) & 1
-        place = jnp.where(y_step == 2, 0, jnp.where(y_step == 3, 3, y_step + 1))
-        slot = x_step * 4 + place
+        slot = x_step * 4 + y_step
 
         @pl.when(core_step == 0)
         def _():
@@ -107,12 +108,12 @@
         in_specs=[SMEM_SPEC] + [VMEM_SPEC] * 3,
         out_specs=[VMEM_SPEC] * 2,
         compiler_params=pltpu.CompilerParams(vmem_limit_bytes=24 * MIB),
-        cost_estimate=cost(8 * 6 * W**3, 7),
+        cost_estimate=SMALL,
         name="pieces",
     )(table, px, py, bottom)
 
 
-def below_kernel(table, px, py, speed, field, tops, out, picked, sems):
+def from_below(table, px, py, tops, picked, sems):
     def fetch(k):
         source, tile = table[k], table[4]
         x_step = ((source >> 3) ^ (tile >> 3)) & 1
@@ -125,24 +126,66 @@
         fetch(k).wait()
         left = product(split(px[k]), split(picked[k]), ((1,), (0,)))
         total = total + product(split(left), split(py[k]), ((1,), (1,)))
-    total = jnp.where(table[5] == 1, total, 0.0)
+    return jnp.where(table[5] == 1, total, 0.0)
+
+
+def below_kernel(mark, table, px, py, speed, field, tops, out, picked, sems):
+    total = from_below(table, px, py, tops, picked, sems)
     out[...] = field[...] + TIME_STEP * (total + speed[...] * total)
 
 
-def below_update(table, px, py, speed, plane, tops):
+def below_update(mark, table, px, py, speed, plane, tops):
     return pl.pallas_call(
         below_kernel,
         out_shape=planes(),
-        in_specs=[SMEM_SPEC] + [VMEM_SPEC] * 4 + [pl.BlockSpec(memory_space=pltpu.HBM)],
+        in_specs=[SMEM_SPEC] * 2 + [VMEM_SPEC] * 4 + [pl.BlockSpec(memory_space=pltpu.HBM)],
         out_specs=VMEM_SPEC,
         scratch_shapes=[pltpu.VMEM((4, W, W), F32), pltpu.SemaphoreType.DMA((4,))],
-        compiler_params=pltpu.CompilerParams(vmem_limit_bytes=16 * MIB),
-        cost_estimate=cost(8 * 6 * W**3, 5),
+        compiler_params=pltpu.CompilerParams(vmem_limit_bytes=50 * MIB),
+        cost_estimate=SMALL,
         name="below",
-    )(table, px, py, speed, plane, tops)
-
-
-def rims_kernel(field, bottom, top, row_low, row_high, col_low, col_high):
+    )(mark, table, px, py, speed, plane, tops)
+
+
+def ends_kernel(table, px, py, speed, ghost, tops, field, out, picked, ends, sems):
+    def end(i, back):
+        plane = (0, NZ - 1)[i]
+        if back:
+            return pltpu.make_async_copy(ends.at[i], out.at[plane], sems.at[4 + i])
+        return pltpu.make_async_copy(field.at[plane], ends.at[i], sems.at[4 + i])
+
+    end(0, False).start()
+    end(1, False).start()
+    end(1, False).wait()
+    ends[1] = ends[1] + TIME_STEP * jnp.where(table[6] == 1, AMBIENT, ghost[...])
+    end(1, True).start()
+    total = from_below(table, px, py, tops, picked, sems)
+    end(0, False).wait()
+    ends[0] = ends[0] + TIME_STEP * (total + speed[...] * total)
+    end(0, True).start()
+    end(1, True).wait()
+    end(0, True).wait()
+
+
+def fix_ends(table, px, py, speed, ghost, tops, field):
+    return pl.pallas_call(
+        ends_kernel,
+        out_shape=planes(NZ),
+        in_specs=[SMEM_SPEC] + [VMEM_SPEC] * 4 + [pl.BlockSpec(memory_space=pltpu.HBM)] * 2,
+        out_specs=pl.BlockSpec(memory_space=pltpu.HBM),
+        scratch_shapes=[
+            pltpu.VMEM((4, W, W), F32),
+            pltpu.VMEM((2, W, W), F32),
+            pltpu.SemaphoreType.DMA((6,)),
+        ],
+        input_output_aliases={6: 0},
+        compiler_params=pltpu.CompilerParams(vmem_limit_bytes=50 * MIB),
+        cost_estimate=SMALL,
+        name="fix_ends",
+    )(table, px, py, speed, ghost, tops, field)
+
+
+def rims_kernel(mark, field, bottom, top, row_low, row_high, col_low, col_high):
     lane = lax.broadcasted_iota(jnp.int32, (W, 128), 1)
     low = jnp.zeros((W, 128), F32)
     high = jnp.zeros((W, 128), F32)
@@ -156,20 +199,21 @@
     col_high[...] = high.T[:NZ]
 
 
-def rims_of(field, bottom, top):
+def rims_of(mark, field, bottom, top):
     rim = jax.ShapeDtypeStruct((NZ, W), F32)
     return pl.pallas_call(
         rims_kernel,
         out_shape=(rim,) * 4,
-        in_specs=[VMEM_SPEC] * 3,
+        in_specs=[SMEM_SPEC] + [VMEM_SPEC] * 3,
         out_specs=[VMEM_SPEC] * 4,
         compiler_params=pltpu.CompilerParams(vmem_limit_bytes=16 * MIB),
-        cost_estimate=cost(NZ * W * W, 4),
+        cost_estimate=SMALL,
         name="rims",
-    )(field, bottom, top)
-
-
-def stencil_kernel(inverse, field, bottom, top, speed, inlets, x_low, x_high, y_low, y_high, out, low, high):
+    )(mark, field, bottom, top)
+
+
+def stencil_kernel(inverse, field, bottom, top, speed, inlets, x_low, x_high, y_low, y_high, out, mark, low, high):
+    mark[...] = jnp.zeros_like(mark)
     pad = jnp.zeros((128 - NZ, W), F32)
     low[...] = jnp.concatenate([y_low[...], pad], axis=0).T
     high[...] = jnp.concatenate([y_high[...], pad], axis=0).T
@@ -207,38 +251,14 @@
 def stencil(inverse, field, bottom, top, speed, inlets, halos):
     return pl.pallas_call(
         stencil_kernel,
-        out_shape=planes(NZ),
+        out_shape=(planes(NZ), MARK),
         in_specs=[SMEM_SPEC] + [VMEM_SPEC] * 9,
-        out_specs=VMEM_SPEC,
+        out_specs=[VMEM_SPEC] * 2,
         scratch_shapes=[pltpu.VMEM((W, 128), F32)] * 2,
         compiler_params=pltpu.CompilerParams(vmem_limit_bytes=24 * MIB),
-        cost_estimate=cost(16 * NZ * W * W, 12),
+        cost_estimate=SMALL,
         name="stencil",
     )(inverse, field, bottom, top, speed, inlets, *halos)
-
-
-def place_kernel(bottom, top, field, out, sems):
-    copies = [
-        pltpu.make_async_copy(bottom, out.at[0], sems.at[0]),
-        pltpu.make_async_copy(top, out.at[NZ - 1], sems.at[1]),
-    ]
-    for copy in copies:
-        copy.start()
-    for copy in copies:
-        copy.wait()
-
-
-def place_ends(bottom, top, field):
-    return pl.pallas_call(
-        place_kernel,
-        out_shape=planes(NZ),
-        in_specs=[VMEM_SPEC] * 2 + [pl.BlockSpec(memory_space=pl.ANY)],
-        out_specs=pl.BlockSpec(memory_space=pl.ANY),
-        scratch_shapes=[pltpu.SemaphoreType.DMA((2,))],
-        input_output_aliases={2: 0},
-        cost_estimate=cost(1, 1),
-        name="place_ends",
-    )(bottom, top, field)
 
 
 def exchange_rims(rims):
@@ -259,17 +279,22 @@
     return lax.all_gather(jnp.stack([mine, flip]), "tile", axis_index_groups=BY_HALF, axis=0, tiled=True)
 
 
-def reduce_pieces(give, keep):
+def zero_of(value):
+    return 0.0 * value[(0,) * value.ndim]
+
+
+def reduce_cores(give, keep):
     taken = lax.ppermute(give, "tile", OTHER_CORE)
-    far = lax.ppermute(keep[4] + taken[4], "tile", OTHER_HALF)
-    rest = lax.ppermute(keep[5:8] + taken[5:8], "tile", OTHER_HALF)
-    far = far + (keep[0] + taken[0])
-    from_left = send_y(far[:H], 1)
-    from_right = send_y(far[H:], -1)
-    mine = rest + (keep[1:4] + taken[1:4])
-    right = jnp.concatenate([mine[1, :H] + from_left, mine[1, H:]])
-    left = jnp.concatenate([mine[2, :H], mine[2, H:] + from_right])
-    return mine[0] + (send_y(right, 1) + send_y(left, -1))
+    slots = keep + taken
+    return slots[4:8], slots[0:4], zero_of(slots)
+
+
+def reduce_halves(give):
+    return lax.ppermute(give, "tile", OTHER_HALF)
+
+
+def reduce_ring(slots):
+    return slots[0], send_y(slots[1], 1), send_y(slots[2], 2), send_y(slots[3], -1)
 
 
 def on_device(oxygen, velocity, spacing, inlets, proj_x, proj_y, sources):
@@ -283,30 +308,38 @@
     lift = lax.axis_index("lift")
     has_below = (lift > 0).astype(jnp.int32)
     is_top = lift == LIFTS - 1
-    table = jnp.concatenate([sources.reshape(4) & (TILES - 1), tile[None], has_below[None]])
+    table = jnp.concatenate([sources.reshape(4) & (TILES - 1), tile[None], has_below[None], is_top[None].astype(jnp.int32)])
     speed_low = speed[0]
     bottom, top = field[0], field[NZ - 1]
 
-    def with_above(plane, ghost):
-        return plane + TIME_STEP * jnp.where(is_top, AMBIENT, send_lift(ghost, -1, False))
-
     mine, flip = climb(top)
-    tops = gather_pair(mine, flip)
-    ghost = reduce_pieces(*pieces_of(table, px, py, bottom))
-    halos = exchange_rims(rims_of(field, bottom, top))
-    field = stencil(inverse, field, bottom, top, speed, inlets, halos)
-    mine, flip = climb(field[NZ - 1])
-    bottom = below_update(table, px, py, speed_low, field[0], tops)
-    tops = gather_pair(
-        mine + TIME_STEP * ghost, flip + TIME_STEP * lax.ppermute(ghost, "tile", OTHER_HALF)
-    )
-    top = with_above(field[NZ - 1], ghost)
-    ghost = reduce_pieces(*pieces_of(table, px, py, bottom))
-    halos = exchange_rims(rims_of(field, bottom, top))
-    field = stencil(inverse, field, bottom, top, speed, inlets, halos)
-    bottom = below_update(table, px, py, speed_low, field[0], tops)
-    top = with_above(field[NZ - 1], ghost)
-    return place_ends(bottom, top, field).reshape(1, NZ, 1, W, W)
+    give, keep = pieces_of(table, px, py, bottom)
+    give, keep, mark = reduce_cores(give, keep)
+    tops = gather_pair(mine + mark, flip + mark)
+    got = reduce_halves(give)
+    rims = rims_of(mark[None], field, bottom, top)
+    field, mark = stencil(inverse, field, bottom, top, speed, inlets, exchange_rims(rims))
+    low, high = field[0], field[NZ - 1]
+    mine, flip = climb(high)
+    slots = keep + got + zero_of(mark)
+    own, *parts = reduce_ring(slots)
+    bottom = below_update(zero_of(slots)[None], table, px, py, speed_low, low, tops)
+    give, keep = pieces_of(table, px, py, bottom)
+    give, keep, mark = reduce_cores(give, keep)
+    got_near = reduce_halves(give[0:2])
+    ghost = own + (parts[0] + parts[1] + parts[2]) + (mark + zero_of(got_near))
+    other_ghost = lax.ppermute(ghost, "tile", OTHER_HALF)
+    tops = gather_pair(mine + TIME_STEP * ghost, flip + TIME_STEP * other_ghost)
+    ghost_above = jnp.where(is_top, AMBIENT, send_lift(ghost, -1, False))
+    top = high + TIME_STEP * ghost_above
+    got_far = reduce_halves(give[2:4])
+    rims = rims_of(mark[None], field, bottom, top)
+    field, mark = stencil(inverse, field, bottom, top, speed, inlets, exchange_rims(rims))
+    near, far = keep[0:2] + got_near, keep[2:4] + got_far + zero_of(mark)
+    own, *parts = reduce_ring([near[0], near[1], far[0], far[1]])
+    ghost = send_lift(own + (parts[0] + parts[1] + parts[2]), -1, False)
+    field = fix_ends(table, px, py, speed_low, ghost, tops, field)
+    return field.reshape(1, NZ, 1, W, W)
 
 
 def solution(mesh):

time: 203 us -> 224 us (1.10)
  waiting for transfers between devices: 62.4 us -> 86 us
  starting transfers between devices: 70.7 us -> 61.1 us
  local copies, waits for them, and re-layouts: 12.8 us -> 19 us
  between operations: 14.7 us -> 20.1 us
  other arithmetic: 8.52 us -> 4.78 us
    ppermute x6, waiting for transfers between devices: 16.6 us -> 50.1 us  [send_lift(): return lax.ppermute(value, ('lift', 'tile'), to_lift(steps, flip))]
    ppermute x7 -> x6, waiting for transfers between devices: 35.8 us -> 9.44 us  [the longest x3 5.29 us: reduce_halves(): return lax.ppermute(give, 'tile', OTHER_HALF)]
    ppermute x2, waiting for transfers between devices: 0.01 us -> 9.23 us  [exchange_rims(): lax.ppermute(row_high, 'tile', [(t, t + TCOL) for t in range(TILES - TCOL)])]
    ppermute x8 -> x6, waiting for transfers between devices: 8.09 us -> 13.7 us  [send_y(): return lax.ppermute(value, 'tile', along_y(steps))]
    ppermute x8 -> x6, starting transfers between devices: 14.5 us -> 9.06 us  [send_y(): return lax.ppermute(value, 'tile', along_y(steps))]
    add x13 -> x6, other arithmetic: 6.55 us -> 2.11 us  [the longest x1 0.99 us: on_device(): top = high + TIME_STEP * ghost_above]
    slice x2 -> x8, local copies, waits for them, and re-layouts: 0.04 us -> 4.39 us  [the longest x6 3.31 us: zero_of(): return 0.0 * value[(0,) * value.ndim]]
    ppermute x2, starting transfers between devices: 7.14 us -> 10.4 us  [exchange_rims(): lax.ppermute(row_high, 'tile', [(t, t + TCOL) for t in range(TILES - TCOL)])]
  transfers between devices with their start and end apart: 31 -> 28, of which waited for: 13 -> 12; matrix products, arithmetic and copies ran while one was open for 4% -> 3% of each run, Pallas kernels for 15% -> 7%
where the time goes in v4:
time: 224 us; the launch traced here: 223 us
  waiting for transfers between devices  86 us (38%)
  starting transfers between devices  61.1 us (27%)
  Pallas kernels  32.5 us (15%)
  between operations  20.1 us (9%)
  local copies, waits for them, and re-layouts  19 us (8%)
  other arithmetic  4.78 us (2%)
    ppermute x6, waiting for transfers between devices, send_lift(): return lax.ppermute(value, ('lift', 'tile'), to_lift(steps, flip))  50.1 us
    ppermute x6, starting transfers between devices, send_lift(): return lax.ppermute(value, ('lift', 'tile'), to_lift(steps, flip))  19.9 us
    pallas_call x2, Pallas kernels, stencil(): pl.pallas_call(stencil_kernel, out_shape=(planes(NZ), MARK), in_specs=[SM...  13.9 us
    ppermute x6, waiting for transfers between devices, send_y(): return lax.ppermute(value, 'tile', along_y(steps))  13.7 us
    unnamed x42, local copies, waits for them, and re-layouts  12.4 us
    ppermute x2, starting transfers between devices, exchange_rims(): lax.ppermute(row_high, 'tile', [(t, t + TCOL) for t in range(TILES - TCOL)])  10.4 us
    ppermute x2, starting transfers between devices, exchange_rims(): lax.ppermute(row_low, 'tile', [(t + TCOL, t) for t in range(TILES - TCOL)])  9.24 us
    ppermute x2, waiting for transfers between devices, exchange_rims(): lax.ppermute(row_high, 'tile', [(t, t + TCOL) for t in range(TILES - TCOL)])  9.23 us
  transfers between devices with their start and end apart: 28, of which 12 were waited for; matrix products, arithmetic and copies ran while one was open for 3% of the time, Pallas kernels for 7%

profile of v4, /device:TPU:6, one launch (start us, length us, event | category | flops | bytes accessed | tf_op | source)
XLA Modules:
  0.0 223.4 jit_solution(14801649334824073724)
XLA Ops:
  10.8 3.4 %pieces.2 = (f32[8,256,256]{2,1,0:T(8,128)S(1)}, f32[8,256,256]{2,1,0:T(8,128)S(1)}) custom-call(s32[7]{0:T(128)S(1)} %pad_add_fusion.table, f32[4,256,256]{2,1,0:T(8,128)S(1)} %bitcast.67, f32[4,256,256]{2,1,0:T(8,128)S(1)} %bitcast.71, f32[256,256]{1,0:T(8,128)S(1)} %get-tuple-element.42.bottom), custom_call_target="tpu_custom_call" | custom-call | flops 1024 | bytes 1024 | tf_op jit(solution)/shard_map/pieces/pallas_call | solution.py:105
  14.3 3.7 %collective-permute-start.7 = (f32[256,256]{1,0:T(8,128)S(1)}, f32[256,256]{1,0:T(8,128)S(1)}, u32[]{:S(2)}, u32[]{:S(2)}) collective-permute-start(f32[256,256]{1,0:T(8,128)S(1)} %get-tuple-element.41.top), channel_id=1, source_target_pairs={{0,24},{1,25},{2,26},{3,27},{4,28},{5,29},{6,30},{7,31},{8,16},{9,... | collective-permute-start | bytes 786440 | tf_op jit(solution)/shard_map/ppermute | solution.py:53
  18.1 2.8 %collective-permute-start.6 = (f32[256,256]{1,0:T(8,128)S(1)}, f32[256,256]{1,0:T(8,128)S(1)}, u32[]{:S(2)}, u32[]{:S(2)}) collective-permute-start(f32[256,256]{1,0:T(8,128)S(1)} %get-tuple-element.41.top), channel_id=1, source_target_pairs={{0,16},{1,17},{2,18},{3,19},{4,20},{5,21},{6,22},{7,23},{8,24},{9,... | collective-permute-start | bytes 786440 | tf_op jit(solution)/shard_map/ppermute | solution.py:53
  22.6 3.5 %collective-permute-done.7 = f32[256,256]{1,0:T(8,128)S(1)} collective-permute-done((f32[256,256]{1,0:T(8,128)S(1)}, f32[256,256]{1,0:T(8,128)S(1)}, u32[]{:S(2)}, u32[]{:S(2)}) %collective-permute-start.7) | collective-permute-done | bytes 262176 | tf_op jit(solution)/shard_map/ppermute | solution.py:53
  26.1 4.0 %collective-permute-done.6 = f32[256,256]{1,0:T(8,128)S(1)} collective-permute-done((f32[256,256]{1,0:T(8,128)S(1)}, f32[256,256]{1,0:T(8,128)S(1)}, u32[]{:S(2)}, u32[]{:S(2)}) %collective-permute-start.6) | collective-permute-done | bytes 262176 | tf_op jit(solution)/shard_map/ppermute | solution.py:53
  31.2 2.4 %collective-permute-start.1 = (f32[4,256,256]{2,1,0:T(8,128)S(1)}, f32[4,256,256]{2,1,0:T(8,128)S(1)}, u32[]{:S(2)}, u32[]{:S(2)}) collective-permute-start(f32[4,256,256]{2,1,0:T(8,128)S(1)} %slice.110), channel_id=1, source_target_pairs={{0,8},{1,9},{2,10},{3,11},{4,12},{5,13},{6,14},{7,15},{8,0},{9,1},... | collective-permute-start | bytes 3145736 | tf_op jit(solution)/shard_map/ppermute | solution.py:293
  37.1 5.1 %collective-permute-start.2 = (f32[16,256]{1,0:T(8,128)S(1)}, f32[16,256]{1,0:T(8,128)S(1)}, u32[]{:S(2)}, u32[]{:S(2)}) collective-permute-start(f32[16,256]{1,0:T(8,128)S(1)} %get-tuple-element.23), channel_id=1, source_target_pairs={{0,4},{1,5},{2,6},{3,7},{4,8},{5,9},{6,10},{7,11},{8,12},{9,13},{1... | collective-permute-start | bytes 49160 | tf_op jit(solution)/shard_map/ppermute | solution.py:266
  42.2 4.6 %collective-permute-start.3 = (f32[16,256]{1,0:T(8,128)S(1)}, f32[16,256]{1,0:T(8,128)S(1)}, u32[]{:S(2)}, u32[]{:S(2)}) collective-permute-start(f32[16,256]{1,0:T(8,128)S(1)} %get-tuple-element.24), channel_id=1, source_target_pairs={{4,0},{5,1},{6,2},{7,3},{8,4},{9,5},{10,6},{11,7},{12,8},{13,9},{1... | collective-permute-start | bytes 49160 | tf_op jit(solution)/shard_map/ppermute | solution.py:267
  51.1 9.2 %collective-permute-done.2.x_low = f32[16,256]{1,0:T(8,128)S(1)} collective-permute-done((f32[16,256]{1,0:T(8,128)S(1)}, f32[16,256]{1,0:T(8,128)S(1)}, u32[]{:S(2)}, u32[]{:S(2)}) %collective-permute-start.2) | collective-permute-done | bytes 16416 | tf_op jit(solution)/shard_map/ppermute | solution.py:266
  60.4 2.3 %copy-done.5 = f32[1,16,1,256,256]{4,3,2,1,0:T(8,128)S(1)} copy-done((f32[1,16,1,256,256]{4,3,2,1,0:T(8,128)S(1)}, f32[1,16,1,256,256]{4,3,2,1,0:T(8,128)}, u32[]{:S(2)}) %copy-start.5) | copy-done | bytes 4194328
  62.7 5.9 %stencil.2 = (f32[16,256,256]{2,1,0:T(8,128)S(1)}, f32[8,128]{1,0:T(8,128)S(1)}) custom-call(f32[1]{0:T(128)S(6)} %div.3.inverse, f32[16,256,256]{2,1,0:T(8,128)S(1)} %bitcast.64, f32[256,256]{1,0:T(8,128)S(1)} %get-tuple-element.42.bottom, f32[256,256]{1,0:T(8,128)S(1)} %get-tuple-element.41.top, f32[16,256,256]{2,1,0:T(8,128)S(1)} %bitcast.65, ...), custom_call_target="tpu_custom_call" | custom-call | flops 1024 | bytes 1024 | tf_op jit(solution)/shard_map/stencil/pallas_call | solution.py:252
  74.0 3.6 %below.1.bottom = f32[256,256]{1,0:T(8,128)S(1)} custom-call(f32[1]{0:T(128)} %bitcast.14.mark, s32[7]{0:T(128)S(1)} %pad_add_fusion.table, f32[4,256,256]{2,1,0:T(8,128)S(1)} %bitcast.68, f32[4,256,256]{2,1,0:T(8,128)S(1)} %bitcast.72, f32[256,256]{1,0:T(8,128)S(1)} %slice_bitcast_fusion.12.speed, f32[256,256]{1,0:T(8,128)S(1)} %get-tuple-element.40.field, ...), custom_call_target="tpu_custom_call" | custom-call | flops 1024 | bytes 1024 | tf_op jit(solution)/shard_map/below/pallas_call | solution.py:138
  77.6 3.4 %pieces.3 = (f32[8,256,256]{2,1,0:T(8,128)S(1)}, f32[8,256,256]{2,1,0:T(8,128)S(1)}) custom-call(s32[7]{0:T(128)S(1)} %pad_add_fusion.table, f32[4,256,256]{2,1,0:T(8,128)S(1)} %bitcast.69, f32[4,256,256]{2,1,0:T(8,128)S(1)} %bitcast.73, f32[256,256]{1,0:T(8,128)S(1)} %below.1.bottom), custom_call_target="tpu_custom_call" | custom-call | flops 1024 | bytes 1024 | tf_op jit(solution)/shard_map/pieces/pallas_call | solution.py:105
  81.1 4.1 %collective-permute-done.8 = f32[8,256,256]{2,1,0:T(8,128)S(1)} collective-permute-done((f32[8,256,256]{2,1,0:T(8,128)S(1)}, f32[8,256,256]{2,1,0:T(8,128)S(1)}, u32[]{:S(2)}, u32[]{:S(2)}) %collective-permute-start.8) | collective-permute-done | bytes 2097184 | tf_op jit(solution)/shard_map/ppermute | solution.py:287
  86.6 5.2 %collective-permute-start.23 = (f32[256,256]{1,0:T(8,128)S(1)}, f32[256,256]{1,0:T(8,128)S(1)}, u32[]{:S(2)}, u32[]{:S(2)}) collective-permute-start(f32[256,256]{1,0:T(8,128)S(1)} %get-tuple-element.39), channel_id=1, source_target_pairs={{0,16},{1,17},{2,18},{3,19},{4,20},{5,21},{6,22},{7,23},{8,24},{9,... | collective-permute-start | bytes 786440 | tf_op jit(solution)/shard_map/ppermute | solution.py:53
  91.9 2.8 %collective-permute-start.14 = (f32[256,256]{1,0:T(8,128)S(1)}, f32[256,256]{1,0:T(8,128)S(1)}, u32[]{:S(2)}, u32[]{:S(2)}) collective-permute-start(f32[256,256]{1,0:T(8,128)S(1)} %get-tuple-element.48), channel_id=1, source_target_pairs={{0,6},{1,7},{2,0},{3,1},{4,2},{5,3},{6,4},{7,5},{8,14},{9,15},{10,... | collective-permute-start | bytes 786440 | tf_op jit(solution)/shard_map/ppermute | solution.py:49
  97.6 5.3 %collective-permute-done.9 = f32[2,256,256]{2,1,0:T(8,128)S(1)} collective-permute-done((f32[2,256,256]{2,1,0:T(8,128)S(1)}, f32[2,256,256]{2,1,0:T(8,128)S(1)}, u32[]{:S(2)}, u32[]{:S(2)}) %collective-permute-start.9) | collective-permute-done | bytes 524320 | tf_op jit(solution)/shard_map/ppermute | solution.py:293
  102.9 4.3 %collective-permute-start.24 = (f32[256,256]{1,0:T(8,128)S(1)}, f32[256,256]{1,0:T(8,128)S(1)}, u32[]{:S(2)}, u32[]{:S(2)}) collective-permute-start(f32[256,256]{1,0:T(8,128)S(1)} %get-tuple-element.39), channel_id=1, source_target_pairs={{0,24},{1,25},{2,26},{3,27},{4,28},{5,29},{6,30},{7,31},{8,16},{9,... | collective-permute-start | bytes 786440 | tf_op jit(solution)/shard_map/ppermute | solution.py:53
  109.3 2.3 %collective-permute-start.25 = (f32[256,256]{1,0:T(8,128)S(1)}, f32[256,256]{1,0:T(8,128)S(1)}, u32[]{:S(2)}, u32[]{:S(2)}) collective-permute-start(f32[256,256]{1,0:T(8,128)S(1)} %get-tuple-element.38), channel_id=1, source_target_pairs={{0,8},{1,9},{2,10},{3,11},{4,12},{5,13},{6,14},{7,15},{8,0},{9,1},... | collective-permute-start | bytes 786440 | tf_op jit(solution)/shard_map/ppermute | solution.py:331
  111.6 17.4 %collective-permute-done.24 = f32[256,256]{1,0:T(8,128)S(1)} collective-permute-done((f32[256,256]{1,0:T(8,128)S(1)}, f32[256,256]{1,0:T(8,128)S(1)}, u32[]{:S(2)}, u32[]{:S(2)}) %collective-permute-start.24) | collective-permute-done | bytes 262176 | tf_op jit(solution)/shard_map/ppermute | solution.py:53
  129.9 2.4 %collective-permute-start.11 = (f32[2,256,256]{2,1,0:T(8,128)}, f32[2,256,256]{2,1,0:T(8,128)S(1)}, u32[]{:S(2)}, u32[]{:S(2)}) collective-permute-start(f32[2,256,256]{2,1,0:T(8,128)} %get-tuple-element.45), channel_id=1, source_target_pairs={{0,8},{1,9},{2,10},{3,11},{4,12},{5,13},{6,14},{7,15},{8,0},{9,1},... | collective-permute-start | bytes 1572872 | tf_op jit(solution)/shard_map/ppermute | solution.py:293
  134.2 16.5 %collective-permute-done.15 = f32[256,256]{1,0:T(8,128)S(1)} collective-permute-done((f32[256,256]{1,0:T(8,128)}, f32[256,256]{1,0:T(8,128)S(1)}, u32[]{:S(2)}, u32[]{:S(2)}) %collective-permute-start.15) | collective-permute-done | bytes 262176 | tf_op jit(solution)/shard_map/ppermute | solution.py:53
  151.7 2.3 %copy-done.1 = f32[16,256,256]{2,1,0:T(8,128)S(1)} copy-done((f32[16,256,256]{2,1,0:T(8,128)S(1)}, f32[16,256,256]{2,1,0:T(8,128)}, u32[]{:S(2)}) %copy-start.1) | copy-done | bytes 4194328
  155.3 5.3 %collective-permute-start.16 = (f32[16,256]{1,0:T(8,128)S(1)}, f32[16,256]{1,0:T(8,128)S(1)}, u32[]{:S(2)}, u32[]{:S(2)}) collective-permute-start(f32[16,256]{1,0:T(8,128)S(1)} %get-tuple-element.31), channel_id=1, source_target_pairs={{0,4},{1,5},{2,6},{3,7},{4,8},{5,9},{6,10},{7,11},{8,12},{9,13},{1... | collective-permute-start | bytes 49160 | tf_op jit(solution)/shard_map/ppermute | solution.py:266
  160.6 4.6 %collective-permute-start.17 = (f32[16,256]{1,0:T(8,128)S(1)}, f32[16,256]{1,0:T(8,128)S(1)}, u32[]{:S(2)}, u32[]{:S(2)}) collective-permute-start(f32[16,256]{1,0:T(8,128)S(1)} %get-tuple-element.32), channel_id=1, source_target_pairs={{4,0},{5,1},{6,2},{7,3},{8,4},{9,5},{10,6},{11,7},{12,8},{13,9},{1... | collective-permute-start | bytes 49160 | tf_op jit(solution)/shard_map/ppermute | solution.py:267
  167.8 3.3 %collective-permute-done.19.y_high = f32[16,256]{1,0:T(8,128)S(1)} collective-permute-done((f32[16,256]{1,0:T(8,128)S(1)}, f32[16,256]{1,0:T(8,128)S(1)}, u32[]{:S(2)}, u32[]{:S(2)}) %collective-permute-start.19) | collective-permute-done | bytes 16416 | tf_op jit(solution)/shard_map/ppermute | solution.py:270
  173.3 7.9 %stencil.3 = (f32[16,256,256]{2,1,0:T(8,128)}, f32[8,128]{1,0:T(8,128)S(1)}) custom-call(f32[1]{0:T(128)S(6)} %div.3.inverse, f32[16,256,256]{2,1,0:T(8,128)S(1)} %copy-done.2, f32[256,256]{1,0:T(8,128)S(1)} %below.1.bottom, f32[256,256]{1,0:T(8,128)S(1)} %multiply_add_fusion.top, f32[16,256,256]{2,1,0:T(8,128)S(1)} %bitcast.66, s32[256,256]{1,0:T(8,128)S(1)} %bitcast.76, ...), custom_call_target="tpu_custom_call" | custom-call | flops 1024 | bytes 1024 | tf_op jit(solution)/shard_map/stencil/pallas_call | solution.py:252
  182.6 3.0 %collective-permute-start.21 = (f32[256,256]{1,0:T(8,128)S(1)}, f32[256,256]{1,0:T(8,128)S(1)}, u32[]{:S(2)}, u32[]{:S(2)}) collective-permute-start(f32[256,256]{1,0:T(8,128)S(1)} %get-tuple-element.51), channel_id=1, source_target_pairs={{0,6},{1,7},{2,0},{3,1},{4,2},{5,3},{6,4},{7,5},{8,14},{9,15},{10,... | collective-permute-start | bytes 786440 | tf_op jit(solution)/shard_map/ppermute | solution.py:49
  187.3 4.5 %collective-permute-done.21 = f32[256,256]{1,0:T(8,128)S(1)} collective-permute-done((f32[256,256]{1,0:T(8,128)S(1)}, f32[256,256]{1,0:T(8,128)S(1)}, u32[]{:S(2)}, u32[]{:S(2)}) %collective-permute-start.21) | collective-permute-done | bytes 262176 | tf_op jit(solution)/shard_map/ppermute | solution.py:49
  191.8 8.5 %collective-permute-done.10 = f32[256,256]{1,0:T(8,128)S(1)} collective-permute-done((f32[256,256]{1,0:T(8,128)S(1)}, f32[256,256]{1,0:T(8,128)S(1)}, u32[]{:S(2)}, u32[]{:S(2)}) %collective-permute-start.10) | collective-permute-done | bytes 262176 | tf_op jit(solution)/shard_map/ppermute | solution.py:49
  202.3 8.7 %collective-permute-done.22.ghost = f32[256,256]{1,0:T(8,128)S(1)} collective-permute-done((f32[256,256]{1,0:T(8,128)S(1)}, f32[256,256]{1,0:T(8,128)S(1)}, u32[]{:S(2)}, u32[]{:S(2)}) %collective-permute-start.22) | collective-permute-done | bytes 262176 | tf_op jit(solution)/shard_map/ppermute | solution.py:53
  211.0 5.5 %fix_ends.1 = f32[16,256,256]{2,1,0:T(8,128)} custom-call(s32[7]{0:T(128)S(1)} %pad_add_fusion.table, f32[4,256,256]{2,1,0:T(8,128)S(1)} %bitcast.70, f32[4,256,256]{2,1,0:T(8,128)S(1)} %bitcast.74, f32[256,256]{1,0:T(8,128)S(1)} %slice_bitcast_fusion.12.speed, f32[256,256]{1,0:T(8,128)S(1)} %collective-permute-done.22.ghost, ...), custom_call_target="tpu_custom_call", output_to_operand_aliasing={{}: (6, {})} | custom-call | flops 1024 | bytes 1024 | tf_op jit(solution)/shard_map/fix_ends/pallas_call | solution.py:171
  (104 shorter events, 35.1 us)
Async XLA Ops:
  6.5 67.4 %all-gather.3.cloned.1.call-start = ((), (), s32[]{:S(2)}) async-start(), calls=%async_computation | async-start | bytes 4718592 | tf_op jit(solution)/shard_map/all_gather | solution.py:279
  14.2 6.7 %collective-permute-start = (f32[8,256,256]{2,1,0:T(8,128)S(1)}, f32[8,256,256]{2,1,0:T(8,128)S(1)}, u32[]{:S(2)}, u32[]{:S(2)}) collective-permute-start(f32[8,256,256]{2,1,0:T(8,128)S(1)} %get-tuple-element.22), channel_id=1, source_target_pairs={{0,1},{1,0},{2,3},{3,2},{4,5},{5,4},{6,7},{7,6},{8,9},{9,8},{10,11... | collective-permute-start | bytes 6291464 | tf_op jit(solution)/shard_map/ppermute | solution.py:287
  14.3 11.8 %collective-permute-start.7 = (f32[256,256]{1,0:T(8,128)S(1)}, f32[256,256]{1,0:T(8,128)S(1)}, u32[]{:S(2)}, u32[]{:S(2)}) collective-permute-start(f32[256,256]{1,0:T(8,128)S(1)} %get-tuple-element.41.top), channel_id=1, source_target_pairs={{0,24},{1,25},{2,26},{3,27},{4,28},{5,29},{6,30},{7,31},{8,16},{9,... | collective-permute-start | bytes 786440 | tf_op jit(solution)/shard_map/ppermute | solution.py:53
  18.1 12.1 %collective-permute-start.6 = (f32[256,256]{1,0:T(8,128)S(1)}, f32[256,256]{1,0:T(8,128)S(1)}, u32[]{:S(2)}, u32[]{:S(2)}) collective-permute-start(f32[256,256]{1,0:T(8,128)S(1)} %get-tuple-element.41.top), channel_id=1, source_target_pairs={{0,16},{1,17},{2,18},{3,19},{4,20},{5,21},{6,22},{7,23},{8,24},{9,... | collective-permute-start | bytes 786440 | tf_op jit(solution)/shard_map/ppermute | solution.py:53
  31.1 29.3 %copy-start.11 = (s32[1,1,256,256]{3,2,1,0:T(8,128)S(1)}, s32[1,1,256,256]{3,2,1,0:T(8,128)}, u32[]{:S(2)}) copy-start(s32[1,1,256,256]{3,2,1,0:T(8,128)} %param.10) | copy-start | bytes 786436
  31.1 179.9 %all-gather.5.cloned.1.call-start = ((), (), s32[]{:S(2)}) async-start(), calls=%async_computation.1 | async-start | bytes 4718592 | tf_op jit(solution)/shard_map/all_gather | solution.py:279
  31.2 40.2 %collective-permute-start.1 = (f32[4,256,256]{2,1,0:T(8,128)S(1)}, f32[4,256,256]{2,1,0:T(8,128)S(1)}, u32[]{:S(2)}, u32[]{:S(2)}) collective-permute-start(f32[4,256,256]{2,1,0:T(8,128)S(1)} %slice.110), channel_id=1, source_target_pairs={{0,8},{1,9},{2,10},{3,11},{4,12},{5,13},{6,14},{7,15},{8,0},{9,1},... | collective-permute-start | bytes 3145736 | tf_op jit(solution)/shard_map/ppermute | solution.py:293
  35.8 24.6 %copy-start.4 = (f32[1,16,1,256,256]{4,3,2,1,0:T(8,128)S(1)}, f32[1,16,1,256,256]{4,3,2,1,0:T(8,128)}, u32[]{:S(2)}) copy-start(f32[1,16,1,256,256]{4,3,2,1,0:T(8,128)} %param.7) | copy-start | bytes 12582916
  37.1 23.3 %collective-permute-start.2 = (f32[16,256]{1,0:T(8,128)S(1)}, f32[16,256]{1,0:T(8,128)S(1)}, u32[]{:S(2)}, u32[]{:S(2)}) collective-permute-start(f32[16,256]{1,0:T(8,128)S(1)} %get-tuple-element.23), channel_id=1, source_target_pairs={{0,4},{1,5},{2,6},{3,7},{4,8},{5,9},{6,10},{7,11},{8,12},{9,13},{1... | collective-permute-start | bytes 49160 | tf_op jit(solution)/shard_map/ppermute | solution.py:266
  42.2 18.1 %collective-permute-start.3 = (f32[16,256]{1,0:T(8,128)S(1)}, f32[16,256]{1,0:T(8,128)S(1)}, u32[]{:S(2)}, u32[]{:S(2)}) collective-permute-start(f32[16,256]{1,0:T(8,128)S(1)} %get-tuple-element.24), channel_id=1, source_target_pairs={{4,0},{5,1},{6,2},{7,3},{8,4},{9,5},{10,6},{11,7},{12,8},{13,9},{1... | collective-permute-start | bytes 49160 | tf_op jit(solution)/shard_map/ppermute | solution.py:267
  46.9 13.5 %collective-permute-start.4 = (f32[16,256]{1,0:T(8,128)S(1)}, f32[16,256]{1,0:T(8,128)S(1)}, u32[]{:S(2)}, u32[]{:S(2)}) collective-permute-start(f32[16,256]{1,0:T(8,128)S(1)} %get-tuple-element.25), channel_id=1, source_target_pairs={{0,1},{1,2},{2,3},{4,5},{5,6},{6,7},{8,9},{9,10},{10,11},{12,13},{... | collective-permute-start | bytes 49160 | tf_op jit(solution)/shard_map/ppermute | solution.py:269
  48.2 12.2 %collective-permute-start.5 = (f32[16,256]{1,0:T(8,128)S(1)}, f32[16,256]{1,0:T(8,128)S(1)}, u32[]{:S(2)}, u32[]{:S(2)}) collective-permute-start(f32[16,256]{1,0:T(8,128)S(1)} %get-tuple-element.26), channel_id=1, source_target_pairs={{1,0},{2,1},{3,2},{5,4},{6,5},{7,6},{9,8},{10,9},{11,10},{13,12},{... | collective-permute-start | bytes 49160 | tf_op jit(solution)/shard_map/ppermute | solution.py:270
  81.0 4.2 %collective-permute-start.8 = (f32[8,256,256]{2,1,0:T(8,128)S(1)}, f32[8,256,256]{2,1,0:T(8,128)S(1)}, u32[]{:S(2)}, u32[]{:S(2)}) collective-permute-start(f32[8,256,256]{2,1,0:T(8,128)S(1)} %get-tuple-element.30), channel_id=1, source_target_pairs={{0,1},{1,0},{2,3},{3,2},{4,5},{5,4},{6,7},{7,6},{8,9},{9,8},{10,11... | collective-permute-start | bytes 6291464 | tf_op jit(solution)/shard_map/ppermute | solution.py:287
  86.6 16.3 %collective-permute-start.9 = (f32[2,256,256]{2,1,0:T(8,128)S(1)}, f32[2,256,256]{2,1,0:T(8,128)S(1)}, u32[]{:S(2)}, u32[]{:S(2)}) collective-permute-start(f32[2,256,256]{2,1,0:T(8,128)S(1)} %get-tuple-element.46), channel_id=1, source_target_pairs={{0,8},{1,9},{2,10},{3,11},{4,12},{5,13},{6,14},{7,15},{8,0},{9,1},... | collective-permute-start | bytes 1572872 | tf_op jit(solution)/shard_map/ppermute | solution.py:293
  86.6 21.7 %collective-permute-start.23 = (f32[256,256]{1,0:T(8,128)S(1)}, f32[256,256]{1,0:T(8,128)S(1)}, u32[]{:S(2)}, u32[]{:S(2)}) collective-permute-start(f32[256,256]{1,0:T(8,128)S(1)} %get-tuple-element.39), channel_id=1, source_target_pairs={{0,16},{1,17},{2,18},{3,19},{4,20},{5,21},{6,22},{7,23},{8,24},{9,... | collective-permute-start | bytes 786440 | tf_op jit(solution)/shard_map/ppermute | solution.py:53
  91.9 16.4 %collective-permute-start.14 = (f32[256,256]{1,0:T(8,128)S(1)}, f32[256,256]{1,0:T(8,128)S(1)}, u32[]{:S(2)}, u32[]{:S(2)}) collective-permute-start(f32[256,256]{1,0:T(8,128)S(1)} %get-tuple-element.48), channel_id=1, source_target_pairs={{0,6},{1,7},{2,0},{3,1},{4,2},{5,3},{6,4},{7,5},{8,14},{9,15},{10,... | collective-permute-start | bytes 786440 | tf_op jit(solution)/shard_map/ppermute | solution.py:49
  94.8 14.3 %collective-permute-start.12 = (f32[256,256]{1,0:T(8,128)S(1)}, f32[256,256]{1,0:T(8,128)S(1)}, u32[]{:S(2)}, u32[]{:S(2)}) collective-permute-start(f32[256,256]{1,0:T(8,128)S(1)} %get-tuple-element.49), channel_id=1, source_target_pairs={{0,2},{1,3},{2,4},{3,5},{4,6},{5,7},{6,0},{7,1},{8,10},{9,11},{10,... | collective-permute-start | bytes 786440 | tf_op jit(solution)/shard_map/ppermute | solution.py:49
  94.8 14.3 %collective-permute-start.13 = (f32[256,256]{1,0:T(8,128)S(1)}, f32[256,256]{1,0:T(8,128)S(1)}, u32[]{:S(2)}, u32[]{:S(2)}) collective-permute-start(f32[256,256]{1,0:T(8,128)S(1)} %get-tuple-element.47), channel_id=1, source_target_pairs={{0,4},{1,5},{2,6},{3,7},{4,0},{5,1},{6,2},{7,3},{8,12},{9,13},{10,... | collective-permute-start | bytes 786440 | tf_op jit(solution)/shard_map/ppermute | solution.py:49
  102.9 26.1 %collective-permute-start.24 = (f32[256,256]{1,0:T(8,128)S(1)}, f32[256,256]{1,0:T(8,128)S(1)}, u32[]{:S(2)}, u32[]{:S(2)}) collective-permute-start(f32[256,256]{1,0:T(8,128)S(1)} %get-tuple-element.39), channel_id=1, source_target_pairs={{0,24},{1,25},{2,26},{3,27},{4,28},{5,29},{6,30},{7,31},{8,16},{9,... | collective-permute-start | bytes 786440 | tf_op jit(solution)/shard_map/ppermute | solution.py:53
  109.2 19.8 %copy-start.20 = (f32[256,256]{1,0:T(8,128)}, f32[256,256]{1,0:T(8,128)S(1)}, u32[]{:S(2)}) copy-start(f32[256,256]{1,0:T(8,128)S(1)} %get-tuple-element.38) | copy-start | bytes 786436
  109.3 19.7 %collective-permute-start.25 = (f32[256,256]{1,0:T(8,128)S(1)}, f32[256,256]{1,0:T(8,128)S(1)}, u32[]{:S(2)}, u32[]{:S(2)}) collective-permute-start(f32[256,256]{1,0:T(8,128)S(1)} %get-tuple-element.38), channel_id=1, source_target_pairs={{0,8},{1,9},{2,10},{3,11},{4,12},{5,13},{6,14},{7,15},{8,0},{9,1},... | collective-permute-start | bytes 786440 | tf_op jit(solution)/shard_map/ppermute | solution.py:331
  129.9 52.5 %collective-permute-start.11 = (f32[2,256,256]{2,1,0:T(8,128)}, f32[2,256,256]{2,1,0:T(8,128)S(1)}, u32[]{:S(2)}, u32[]{:S(2)}) collective-permute-start(f32[2,256,256]{2,1,0:T(8,128)} %get-tuple-element.45), channel_id=1, source_target_pairs={{0,8},{1,9},{2,10},{3,11},{4,12},{5,13},{6,14},{7,15},{8,0},{9,1},... | collective-permute-start | bytes 1572872 | tf_op jit(solution)/shard_map/ppermute | solution.py:293
  132.3 18.4 %collective-permute-start.15 = (f32[256,256]{1,0:T(8,128)}, f32[256,256]{1,0:T(8,128)S(1)}, u32[]{:S(2)}, u32[]{:S(2)}) collective-permute-start(f32[256,256]{1,0:T(8,128)} %copy-done.20), channel_id=1, source_target_pairs={{16,0},{17,1},{18,2},{19,3},{20,4},{21,5},{22,6},{23,7},{24,8},{25... | collective-permute-start | bytes 786440 | tf_op jit(solution)/shard_map/ppermute | solution.py:53
  154.0 17.2 %copy-start.2 = (f32[16,256,256]{2,1,0:T(8,128)S(1)}, f32[16,256,256]{2,1,0:T(8,128)}, u32[]{:S(2)}) copy-start(f32[16,256,256]{2,1,0:T(8,128)} %copy-done) | copy-start | bytes 12582916
  155.3 12.5 %collective-permute-start.16 = (f32[16,256]{1,0:T(8,128)S(1)}, f32[16,256]{1,0:T(8,128)S(1)}, u32[]{:S(2)}, u32[]{:S(2)}) collective-permute-start(f32[16,256]{1,0:T(8,128)S(1)} %get-tuple-element.31), channel_id=1, source_target_pairs={{0,4},{1,5},{2,6},{3,7},{4,8},{5,9},{6,10},{7,11},{8,12},{9,13},{1... | collective-permute-start | bytes 49160 | tf_op jit(solution)/shard_map/ppermute | solution.py:266
  160.6 7.2 %collective-permute-start.17 = (f32[16,256]{1,0:T(8,128)S(1)}, f32[16,256]{1,0:T(8,128)S(1)}, u32[]{:S(2)}, u32[]{:S(2)}) collective-permute-start(f32[16,256]{1,0:T(8,128)S(1)} %get-tuple-element.32), channel_id=1, source_target_pairs={{4,0},{5,1},{6,2},{7,3},{8,4},{9,5},{10,6},{11,7},{12,8},{13,9},{1... | collective-permute-start | bytes 49160 | tf_op jit(solution)/shard_map/ppermute | solution.py:267
  165.2 2.6 %collective-permute-start.18 = (f32[16,256]{1,0:T(8,128)S(1)}, f32[16,256]{1,0:T(8,128)S(1)}, u32[]{:S(2)}, u32[]{:S(2)}) collective-permute-start(f32[16,256]{1,0:T(8,128)S(1)} %get-tuple-element.33), channel_id=1, source_target_pairs={{0,1},{1,2},{2,3},{4,5},{5,6},{6,7},{8,9},{9,10},{10,11},{12,13},{... | collective-permute-start | bytes 49160 | tf_op jit(solution)/shard_map/ppermute | solution.py:269
  166.5 4.7 %collective-permute-start.19 = (f32[16,256]{1,0:T(8,128)S(1)}, f32[16,256]{1,0:T(8,128)S(1)}, u32[]{:S(2)}, u32[]{:S(2)}) collective-permute-start(f32[16,256]{1,0:T(8,128)S(1)} %get-tuple-element.34), channel_id=1, source_target_pairs={{1,0},{2,1},{3,2},{5,4},{6,5},{7,6},{9,8},{10,9},{11,10},{13,12},{... | collective-permute-start | bytes 49160 | tf_op jit(solution)/shard_map/ppermute | solution.py:270
  182.6 9.2 %collective-permute-start.21 = (f32[256,256]{1,0:T(8,128)S(1)}, f32[256,256]{1,0:T(8,128)S(1)}, u32[]{:S(2)}, u32[]{:S(2)}) collective-permute-start(f32[256,256]{1,0:T(8,128)S(1)} %get-tuple-element.51), channel_id=1, source_target_pairs={{0,6},{1,7},{2,0},{3,1},{4,2},{5,3},{6,4},{7,5},{8,14},{9,15},{10,... | collective-permute-start | bytes 786440 | tf_op jit(solution)/shard_map/ppermute | solution.py:49
  185.6 14.7 %collective-permute-start.10 = (f32[256,256]{1,0:T(8,128)S(1)}, f32[256,256]{1,0:T(8,128)S(1)}, u32[]{:S(2)}, u32[]{:S(2)}) collective-permute-start(f32[256,256]{1,0:T(8,128)S(1)} %slice_bitcast_fusion.6), channel_id=1, source_target_pairs={{0,2},{1,3},{2,4},{3,5},{4,6},{5,7},{6,0},{7,1},{8,10},{9,11},{10,... | collective-permute-start | bytes 786440 | tf_op jit(solution)/shard_map/ppermute | solution.py:49
  185.7 14.6 %collective-permute-start.20 = (f32[256,256]{1,0:T(8,128)S(1)}, f32[256,256]{1,0:T(8,128)S(1)}, u32[]{:S(2)}, u32[]{:S(2)}) collective-permute-start(f32[256,256]{1,0:T(8,128)S(1)} %get-tuple-element.50), channel_id=1, source_target_pairs={{0,4},{1,5},{2,6},{3,7},{4,0},{5,1},{6,2},{7,3},{8,12},{9,13},{10,... | collective-permute-start | bytes 786440 | tf_op jit(solution)/shard_map/ppermute | solution.py:49
  200.4 10.6 %collective-permute-start.22 = (f32[256,256]{1,0:T(8,128)S(1)}, f32[256,256]{1,0:T(8,128)S(1)}, u32[]{:S(2)}, u32[]{:S(2)}) collective-permute-start(f32[256,256]{1,0:T(8,128)S(1)} %fusion.4), channel_id=1, source_target_pairs={{16,0},{17,1},{18,2},{19,3},{20,4},{21,5},{22,6},{23,7},{24,8},{25... | collective-permute-start | bytes 786440 | tf_op jit(solution)/shard_map/ppermute | solution.py:53
  (17 other events, 92.0 us)
Sparse Core Ops, SparseCore 0:
  31.2 36.2 all-gather.2
  130.0 31.3 all-gather.4

commit v5 on v4

--- a/solution.py
+++ b/solution.py
@@ -314,8 +314,9 @@
 
     mine, flip = climb(top)
     give, keep = pieces_of(table, px, py, bottom)
+    mark = zero_of(keep)
+    tops = gather_pair(mine + mark, flip + mark)
     give, keep, mark = reduce_cores(give, keep)
-    tops = gather_pair(mine + mark, flip + mark)
     got = reduce_halves(give)
     rims = rims_of(mark[None], field, bottom, top)
     field, mark = stencil(inverse, field, bottom, top, speed, inlets, exchange_rims(rims))
@@ -323,21 +324,22 @@
     mine, flip = climb(high)
     slots = keep + got + zero_of(mark)
     own, *parts = reduce_ring(slots)
-    bottom = below_update(zero_of(slots)[None], table, px, py, speed_low, low, tops)
-    give, keep = pieces_of(table, px, py, bottom)
+    mark = zero_of(slots) + zero_of(mine) + zero_of(flip)
+    bottom = below_update(mark[None], table, px, py, speed_low, low, tops)
+    ghost = own + (parts[0] + parts[1] + parts[2])
+    other_ghost = lax.ppermute(ghost, "tile", OTHER_HALF)
+    ghost_above = jnp.where(is_top, AMBIENT, send_lift(ghost, -1, False))
+    give, keep = pieces_of(table, px, py, bottom + zero_of(ghost))
+    mark = zero_of(keep)
+    tops = gather_pair(mine + TIME_STEP * ghost + mark, flip + TIME_STEP * other_ghost)
+    top = high + TIME_STEP * ghost_above
     give, keep, mark = reduce_cores(give, keep)
-    got_near = reduce_halves(give[0:2])
-    ghost = own + (parts[0] + parts[1] + parts[2]) + (mark + zero_of(got_near))
-    other_ghost = lax.ppermute(ghost, "tile", OTHER_HALF)
-    tops = gather_pair(mine + TIME_STEP * ghost, flip + TIME_STEP * other_ghost)
-    ghost_above = jnp.where(is_top, AMBIENT, send_lift(ghost, -1, False))
-    top = high + TIME_STEP * ghost_above
-    got_far = reduce_halves(give[2:4])
-    rims = rims_of(mark[None], field, bottom, top)
-    field, mark = stencil(inverse, field, bottom, top, speed, inlets, exchange_rims(rims))
-    near, far = keep[0:2] + got_near, keep[2:4] + got_far + zero_of(mark)
-    own, *parts = reduce_ring([near[0], near[1], far[0], far[1]])
-    ghost = send_lift(own + (parts[0] + parts[1] + parts[2]), -1, False)
+    got = reduce_halves(give + zero_of(ghost_above))
+    halos = exchange_rims(rims_of(mark[None], field, bottom, top))
+    field, mark = stencil(inverse, field, bottom, top, speed, inlets, halos)
+    own, *parts = reduce_ring(keep + got + sum(zero_of(halo) for halo in halos))
+    ghost = own + (parts[0] + parts[1] + parts[2]) + zero_of(mark)
+    ghost = send_lift(ghost, -1, False)
     field = fix_ends(table, px, py, speed_low, ghost, tops, field)
     return field.reshape(1, NZ, 1, W, W)
 

time: 224 us -> 198 us (0.88); the launches traced: 223 us -> 194 us
  waiting for transfers between devices: 86 us -> 51 us
  between operations: 20.1 us -> 25.9 us
  other arithmetic: 4.78 us -> 8.94 us
  local copies, waits for them, and re-layouts: 19 us -> 16 us
    ppermute x6, waiting for transfers between devices: 50.1 us -> 20.2 us  [send_lift(): return lax.ppermute(value, ('lift', 'tile'), to_lift(steps, flip))]
    ppermute x2, waiting for transfers between devices: 9.23 us -> 21.8 us  [exchange_rims(): lax.ppermute(row_high, 'tile', [(t, t + TCOL) for t in range(TILES - TCOL)])]
    ppermute x6, waiting for transfers between devices: 13.7 us -> 4.47 us  [send_y(): return lax.ppermute(value, 'tile', along_y(steps))]
    unnamed x42 -> x36, local copies, waits for them, and re-layouts: 12.4 us -> 6.57 us
    ppermute x3 -> x2, waiting for transfers between devices: 5.29 us -> 0.01 us  [reduce_halves(): return lax.ppermute(give, 'tile', OTHER_HALF)]
    slice x6 -> x15, local copies, waits for them, and re-layouts: 3.31 us -> 8.14 us  [zero_of(): return 0.0 * value[(0,) * value.ndim]]
    ppermute x6, starting transfers between devices: 9.06 us -> 5.55 us  [send_y(): return lax.ppermute(value, 'tile', along_y(steps))]
    ppermute x2, waiting for transfers between devices: 3.35 us -> 0.01 us  [exchange_rims(): y_high = lax.ppermute(col_low, 'tile', [(t + 1, t) for t in inside])]
  transfers between devices with their start and end apart: 28 -> 27, of which waited for: 12 -> 8; matrix products, arithmetic and copies ran while one was open for 3% -> 7% of each run, Pallas kernels for 7% -> 12%
where the time goes in v5:
time: 198 us; the launch traced here: 194 us
  starting transfers between devices  59.9 us (30%)
  waiting for transfers between devices  51 us (26%)
  Pallas kernels  32.5 us (16%)
  between operations  25.9 us (13%)
  local copies, waits for them, and re-layouts  16 us (8%)
  other arithmetic  8.94 us (5%)
    ppermute x2, waiting for transfers between devices, exchange_rims(): lax.ppermute(row_high, 'tile', [(t, t + TCOL) for t in range(TILES - TCOL)])  21.8 us
    ppermute x6, waiting for transfers between devices, send_lift(): return lax.ppermute(value, ('lift', 'tile'), to_lift(steps, flip))  20.2 us
    ppermute x6, starting transfers between devices, send_lift(): return lax.ppermute(value, ('lift', 'tile'), to_lift(steps, flip))  19.2 us
    pallas_call x2, Pallas kernels, stencil(): pl.pallas_call(stencil_kernel, out_shape=(planes(NZ), MARK), in_specs=[SM...  13.9 us
    ppermute x2, starting transfers between devices, exchange_rims(): lax.ppermute(row_low, 'tile', [(t + TCOL, t) for t in range(TILES - TCOL)])  10.5 us
    ppermute x2, starting transfers between devices, exchange_rims(): lax.ppermute(row_high, 'tile', [(t, t + TCOL) for t in range(TILES - TCOL)])  9.1 us
    slice x15, local copies, waits for them, and re-layouts, zero_of(): return 0.0 * value[(0,) * value.ndim]  8.14 us
    pallas_call x2, Pallas kernels, pieces_of(): pl.pallas_call(pieces_kernel, out_shape=(planes(8), planes(8)), in_specs=...  6.86 us
  transfers between devices with their start and end apart: 27, of which 8 were waited for; matrix products, arithmetic and copies ran while one was open for 7% of the time, Pallas kernels for 12%

profile of v5, /device:TPU:6, one launch (start us, length us, event | category | flops | bytes accessed | tf_op | source)
XLA Modules:
  0.0 194.3 jit_solution(3873352573922038138)
XLA Ops:
  7.6 3.7 %collective-permute-start.9 = (f32[256,256]{1,0:T(8,128)S(1)}, f32[256,256]{1,0:T(8,128)S(1)}, u32[]{:S(2)}, u32[]{:S(2)}) collective-permute-start(f32[256,256]{1,0:T(8,128)S(1)} %get-tuple-element.41.top), channel_id=1, source_target_pairs={{0,24},{1,25},{2,26},{3,27},{4,28},{5,29},{6,30},{7,31},{8,16},{9,... | collective-permute-start | bytes 786440 | tf_op jit(solution)/shard_map/ppermute | solution.py:53
  11.4 2.8 %collective-permute-start.8 = (f32[256,256]{1,0:T(8,128)S(1)}, f32[256,256]{1,0:T(8,128)S(1)}, u32[]{:S(2)}, u32[]{:S(2)}) collective-permute-start(f32[256,256]{1,0:T(8,128)S(1)} %get-tuple-element.41.top), channel_id=1, source_target_pairs={{0,16},{1,17},{2,18},{3,19},{4,20},{5,21},{6,22},{7,23},{8,24},{9,... | collective-permute-start | bytes 786440 | tf_op jit(solution)/shard_map/ppermute | solution.py:53
  17.4 3.4 %pieces.2 = (f32[8,256,256]{2,1,0:T(8,128)S(1)}, f32[8,256,256]{2,1,0:T(8,128)S(1)}) custom-call(s32[7]{0:T(128)S(1)} %pad_add_fusion.table, f32[4,256,256]{2,1,0:T(8,128)S(1)} %bitcast.72, f32[4,256,256]{2,1,0:T(8,128)S(1)} %bitcast.76, f32[256,256]{1,0:T(8,128)S(1)} %get-tuple-element.42.bottom), custom_call_target="tpu_custom_call" | custom-call | flops 1024 | bytes 1024 | tf_op jit(solution)/shard_map/pieces/pallas_call | solution.py:105
  24.5 4.4 %collective-permute-done = f32[8,256,256]{2,1,0:T(8,128)S(1)} collective-permute-done((f32[8,256,256]{2,1,0:T(8,128)}, f32[8,256,256]{2,1,0:T(8,128)S(1)}, u32[]{:S(2)}, u32[]{:S(2)}) %collective-permute-start) | collective-permute-done | bytes 2097184 | tf_op jit(solution)/shard_map/ppermute | solution.py:287
  28.9 1.9 add.105
  30.9 3.4 %collective-permute-start.1 = (f32[4,256,256]{2,1,0:T(8,128)S(1)}, f32[4,256,256]{2,1,0:T(8,128)S(1)}, u32[]{:S(2)}, u32[]{:S(2)}) collective-permute-start(f32[4,256,256]{2,1,0:T(8,128)S(1)} %slice.132), channel_id=1, source_target_pairs={{0,8},{1,9},{2,10},{3,11},{4,12},{5,13},{6,14},{7,15},{8,0},{9,1},... | collective-permute-start | bytes 3145736 | tf_op jit(solution)/shard_map/ppermute | solution.py:293
  36.7 5.1 %collective-permute-start.2 = (f32[16,256]{1,0:T(8,128)S(1)}, f32[16,256]{1,0:T(8,128)S(1)}, u32[]{:S(2)}, u32[]{:S(2)}) collective-permute-start(f32[16,256]{1,0:T(8,128)S(1)} %get-tuple-element.23), channel_id=1, source_target_pairs={{0,4},{1,5},{2,6},{3,7},{4,8},{5,9},{6,10},{7,11},{8,12},{9,13},{1... | collective-permute-start | bytes 49160 | tf_op jit(solution)/shard_map/ppermute | solution.py:266
  41.8 4.6 %collective-permute-start.3 = (f32[16,256]{1,0:T(8,128)S(1)}, f32[16,256]{1,0:T(8,128)S(1)}, u32[]{:S(2)}, u32[]{:S(2)}) collective-permute-start(f32[16,256]{1,0:T(8,128)S(1)} %get-tuple-element.24), channel_id=1, source_target_pairs={{4,0},{5,1},{6,2},{7,3},{8,4},{9,5},{10,6},{11,7},{12,8},{13,9},{1... | collective-permute-start | bytes 49160 | tf_op jit(solution)/shard_map/ppermute | solution.py:267
  49.8 10.9 %collective-permute-done.2.x_low = f32[16,256]{1,0:T(8,128)S(1)} collective-permute-done((f32[16,256]{1,0:T(8,128)S(1)}, f32[16,256]{1,0:T(8,128)S(1)}, u32[]{:S(2)}, u32[]{:S(2)}) %collective-permute-start.2) | collective-permute-done | bytes 16416 | tf_op jit(solution)/shard_map/ppermute | solution.py:266
  60.8 5.9 %stencil.2 = (f32[16,256,256]{2,1,0:T(8,128)S(1)}, f32[8,128]{1,0:T(8,128)S(1)}) custom-call(f32[1]{0:T(128)S(6)} %div.3.inverse, f32[16,256,256]{2,1,0:T(8,128)S(1)} %bitcast.69, f32[256,256]{1,0:T(8,128)S(1)} %get-tuple-element.42.bottom, f32[256,256]{1,0:T(8,128)S(1)} %get-tuple-element.41.top, f32[16,256,256]{2,1,0:T(8,128)S(1)} %bitcast.70, ...), custom_call_target="tpu_custom_call" | custom-call | flops 1024 | bytes 1024 | tf_op jit(solution)/shard_map/stencil/pallas_call | solution.py:252
  69.8 2.0 %collective-permute-start.10 = (f32[256,256]{1,0:T(8,128)S(1)}, f32[256,256]{1,0:T(8,128)S(1)}, u32[]{:S(2)}, u32[]{:S(2)}) collective-permute-start(f32[256,256]{1,0:T(8,128)S(1)} %get-tuple-element.48), channel_id=1, source_target_pairs={{0,2},{1,3},{2,4},{3,5},{4,6},{5,7},{6,0},{7,1},{8,10},{9,11},{10,... | collective-permute-start | bytes 786440 | tf_op jit(solution)/shard_map/ppermute | solution.py:49
  72.6 4.6 %collective-permute-start.6 = (f32[256,256]{1,0:T(8,128)S(1)}, f32[256,256]{1,0:T(8,128)S(1)}, u32[]{:S(2)}, u32[]{:S(2)}) collective-permute-start(f32[256,256]{1,0:T(8,128)S(1)} %get-tuple-element.40), channel_id=1, source_target_pairs={{0,16},{1,17},{2,18},{3,19},{4,20},{5,21},{6,22},{7,23},{8,24},{9,... | collective-permute-start | bytes 786440 | tf_op jit(solution)/shard_map/ppermute | solution.py:53
  77.2 4.2 %collective-permute-start.7 = (f32[256,256]{1,0:T(8,128)S(1)}, f32[256,256]{1,0:T(8,128)S(1)}, u32[]{:S(2)}, u32[]{:S(2)}) collective-permute-start(f32[256,256]{1,0:T(8,128)S(1)} %get-tuple-element.40), channel_id=1, source_target_pairs={{0,24},{1,25},{2,26},{3,27},{4,28},{5,29},{6,30},{7,31},{8,16},{9,... | collective-permute-start | bytes 786440 | tf_op jit(solution)/shard_map/ppermute | solution.py:53
  81.4 2.6 %collective-permute-done.10 = f32[256,256]{1,0:T(8,128)S(1)} collective-permute-done((f32[256,256]{1,0:T(8,128)S(1)}, f32[256,256]{1,0:T(8,128)S(1)}, u32[]{:S(2)}, u32[]{:S(2)}) %collective-permute-start.10) | collective-permute-done | bytes 262176 | tf_op jit(solution)/shard_map/ppermute | solution.py:49
  84.1 3.9 %collective-permute-start.24 = (f32[256,256]{1,0:T(8,128)S(1)}, f32[256,256]{1,0:T(8,128)}, u32[]{:S(2)}, u32[]{:S(2)}) collective-permute-start(f32[256,256]{1,0:T(8,128)S(1)} %fusion.4), channel_id=1, source_target_pairs={{0,8},{1,9},{2,10},{3,11},{4,12},{5,13},{6,14},{7,15},{8,0},{9,1},... | collective-permute-start | bytes 786440 | tf_op jit(solution)/shard_map/ppermute | solution.py:330
  89.3 2.7 %collective-permute-done.7 = f32[256,256]{1,0:T(8,128)S(1)} collective-permute-done((f32[256,256]{1,0:T(8,128)S(1)}, f32[256,256]{1,0:T(8,128)S(1)}, u32[]{:S(2)}, u32[]{:S(2)}) %collective-permute-start.7) | collective-permute-done | bytes 262176 | tf_op jit(solution)/shard_map/ppermute | solution.py:53
  95.6 3.6 %below.1.bottom = f32[256,256]{1,0:T(8,128)S(1)} custom-call(f32[1]{0:T(128)} %bitcast.18.mark, s32[7]{0:T(128)S(1)} %pad_add_fusion.table, f32[4,256,256]{2,1,0:T(8,128)S(1)} %bitcast.73, f32[4,256,256]{2,1,0:T(8,128)S(1)} %bitcast.77, f32[256,256]{1,0:T(8,128)S(1)} %slice_bitcast_fusion.12.speed, f32[256,256]{1,0:T(8,128)S(1)} %get-tuple-element.39.field, ...), custom_call_target="tpu_custom_call" | custom-call | flops 1024 | bytes 1024 | tf_op jit(solution)/shard_map/below/pallas_call | solution.py:138
  100.3 3.4 %pieces.3 = (f32[8,256,256]{2,1,0:T(8,128)S(1)}, f32[8,256,256]{2,1,0:T(8,128)S(1)}) custom-call(s32[7]{0:T(128)S(1)} %pad_add_fusion.table, f32[4,256,256]{2,1,0:T(8,128)S(1)} %bitcast.74, f32[4,256,256]{2,1,0:T(8,128)S(1)} %bitcast.78, f32[256,256]{1,0:T(8,128)S(1)} %broadcast_add_fusion.bottom), custom_call_target="tpu_custom_call" | custom-call | flops 1024 | bytes 1024 | tf_op jit(solution)/shard_map/pieces/pallas_call | solution.py:105
  103.7 1.4 copy-done.12
  108.9 1.9 collective-permute-start.14
  110.8 10.3 %collective-permute-done.14 = f32[256,256]{1,0:T(8,128)S(1)} collective-permute-done((f32[256,256]{1,0:T(8,128)S(1)}, f32[256,256]{1,0:T(8,128)S(1)}, u32[]{:S(2)}, u32[]{:S(2)}) %collective-permute-start.14) | collective-permute-done | bytes 262176 | tf_op jit(solution)/shard_map/ppermute | solution.py:53
  123.3 2.1 %add.119 = f32[8,256,256]{2,1,0:T(8,128)S(1)} add(f32[8,256,256]{2,1,0:T(8,128)} %copy-done.9, f32[8,256,256]{2,1,0:T(8,128)S(1)} %collective-permute-done.13) | non-fusion elementwise | flops 524288 | bytes 6291456 | tf_op jit(solution)/shard_map/add | solution.py:288
  125.4 2.7 %collective-permute-start.15 = (f32[4,256,256]{2,1,0:T(8,128)S(1)}, f32[4,256,256]{2,1,0:T(8,128)S(1)}, u32[]{:S(2)}, u32[]{:S(2)}) collective-permute-start(f32[4,256,256]{2,1,0:T(8,128)S(1)} %slice_add_fusion), channel_id=1, source_target_pairs={{0,8},{1,9},{2,10},{3,11},{4,12},{5,13},{6,14},{7,15},{8,0},{9,1},... | collective-permute-start | bytes 3145736 | tf_op jit(solution)/shard_map/ppermute | solution.py:293
  130.6 4.0 %collective-permute-start.16 = (f32[16,256]{1,0:T(8,128)S(1)}, f32[16,256]{1,0:T(8,128)S(1)}, u32[]{:S(2)}, u32[]{:S(2)}) collective-permute-start(f32[16,256]{1,0:T(8,128)S(1)} %get-tuple-element.31), channel_id=1, source_target_pairs={{0,4},{1,5},{2,6},{3,7},{4,8},{5,9},{6,10},{7,11},{8,12},{9,13},{1... | collective-permute-start | bytes 49160 | tf_op jit(solution)/shard_map/ppermute | solution.py:266
  134.6 5.9 %collective-permute-start.17 = (f32[16,256]{1,0:T(8,128)S(1)}, f32[16,256]{1,0:T(8,128)S(1)}, u32[]{:S(2)}, u32[]{:S(2)}) collective-permute-start(f32[16,256]{1,0:T(8,128)S(1)} %get-tuple-element.32), channel_id=1, source_target_pairs={{4,0},{5,1},{6,2},{7,3},{8,4},{9,5},{10,6},{11,7},{12,8},{13,9},{1... | collective-permute-start | bytes 49160 | tf_op jit(solution)/shard_map/ppermute | solution.py:267
  143.1 10.9 %collective-permute-done.16.x_low = f32[16,256]{1,0:T(8,128)S(1)} collective-permute-done((f32[16,256]{1,0:T(8,128)S(1)}, f32[16,256]{1,0:T(8,128)S(1)}, u32[]{:S(2)}, u32[]{:S(2)}) %collective-permute-start.16) | collective-permute-done | bytes 16416 | tf_op jit(solution)/shard_map/ppermute | solution.py:266
  159.0 2.0 %collective-permute-start.20 = (f32[256,256]{1,0:T(8,128)S(1)}, f32[256,256]{1,0:T(8,128)S(1)}, u32[]{:S(2)}, u32[]{:S(2)}) collective-permute-start(f32[256,256]{1,0:T(8,128)S(1)} %get-tuple-element.45), channel_id=1, source_target_pairs={{0,2},{1,3},{2,4},{3,5},{4,6},{5,7},{6,0},{7,1},{8,10},{9,11},{10,... | collective-permute-start | bytes 786440 | tf_op jit(solution)/shard_map/ppermute | solution.py:49
  161.7 7.9 %stencil.3 = (f32[16,256,256]{2,1,0:T(8,128)}, f32[8,128]{1,0:T(8,128)S(1)}) custom-call(f32[1]{0:T(128)S(6)} %div.3.inverse, f32[16,256,256]{2,1,0:T(8,128)S(1)} %copy-done.1, f32[256,256]{1,0:T(8,128)S(1)} %below.1.bottom, f32[256,256]{1,0:T(8,128)S(1)} %get-tuple-element.37.top, f32[16,256,256]{2,1,0:T(8,128)S(1)} %bitcast.71, s32[256,256]{1,0:T(8,128)S(1)} %bitcast.81, ...), custom_call_target="tpu_custom_call" | custom-call | flops 1024 | bytes 1024 | tf_op jit(solution)/shard_map/stencil/pallas_call | solution.py:252
  170.8 1.9 collective-permute-done.20
  172.7 1.9 collective-permute-start.23
  174.7 7.2 %collective-permute-done.23.ghost = f32[256,256]{1,0:T(8,128)S(1)} collective-permute-done((f32[256,256]{1,0:T(8,128)S(1)}, f32[256,256]{1,0:T(8,128)S(1)}, u32[]{:S(2)}, u32[]{:S(2)}) %collective-permute-start.23) | collective-permute-done | bytes 262176 | tf_op jit(solution)/shard_map/ppermute | solution.py:53
  181.9 5.5 %fix_ends.1 = f32[16,256,256]{2,1,0:T(8,128)} custom-call(s32[7]{0:T(128)S(1)} %pad_add_fusion.table, f32[4,256,256]{2,1,0:T(8,128)S(1)} %bitcast.75, f32[4,256,256]{2,1,0:T(8,128)S(1)} %bitcast.79, f32[256,256]{1,0:T(8,128)S(1)} %slice_bitcast_fusion.12.speed, f32[256,256]{1,0:T(8,128)S(1)} %collective-permute-done.23.ghost, ...), custom_call_target="tpu_custom_call", output_to_operand_aliasing={{}: (6, {})} | custom-call | flops 1024 | bytes 1024 | tf_op jit(solution)/shard_map/fix_ends/pallas_call | solution.py:171
  (106 shorter events, 29.4 us)
Async XLA Ops:
  6.5 89.0 %all-gather.3.cloned.1.call-start = ((), (), s32[]{:S(2)}) async-start(), calls=%async_computation | async-start | bytes 4718592 | tf_op jit(solution)/shard_map/all_gather | solution.py:279
  7.6 15.8 %collective-permute-start.9 = (f32[256,256]{1,0:T(8,128)S(1)}, f32[256,256]{1,0:T(8,128)S(1)}, u32[]{:S(2)}, u32[]{:S(2)}) collective-permute-start(f32[256,256]{1,0:T(8,128)S(1)} %get-tuple-element.41.top), channel_id=1, source_target_pairs={{0,24},{1,25},{2,26},{3,27},{4,28},{5,29},{6,30},{7,31},{8,16},{9,... | collective-permute-start | bytes 786440 | tf_op jit(solution)/shard_map/ppermute | solution.py:53
  11.4 12.1 %collective-permute-start.8 = (f32[256,256]{1,0:T(8,128)S(1)}, f32[256,256]{1,0:T(8,128)S(1)}, u32[]{:S(2)}, u32[]{:S(2)}) collective-permute-start(f32[256,256]{1,0:T(8,128)S(1)} %get-tuple-element.41.top), channel_id=1, source_target_pairs={{0,16},{1,17},{2,18},{3,19},{4,20},{5,21},{6,22},{7,23},{8,24},{9,... | collective-permute-start | bytes 786440 | tf_op jit(solution)/shard_map/ppermute | solution.py:53
  24.4 157.5 %all-gather.5.cloned.1.call-start = ((), (), s32[]{:S(2)}) async-start(), calls=%async_computation.1 | async-start | bytes 4718592 | tf_op jit(solution)/shard_map/all_gather | solution.py:279
  24.4 4.5 %collective-permute-start = (f32[8,256,256]{2,1,0:T(8,128)}, f32[8,256,256]{2,1,0:T(8,128)S(1)}, u32[]{:S(2)}, u32[]{:S(2)}) collective-permute-start(f32[8,256,256]{2,1,0:T(8,128)} %copy-done.13), channel_id=1, source_target_pairs={{0,1},{1,0},{2,3},{3,2},{4,5},{5,4},{6,7},{7,6},{8,9},{9,8},{10,11... | collective-permute-start | bytes 6291464 | tf_op jit(solution)/shard_map/ppermute | solution.py:287
  30.7 30.0 %copy-start.3 = (f32[1,16,1,256,256]{4,3,2,1,0:T(8,128)S(1)}, f32[1,16,1,256,256]{4,3,2,1,0:T(8,128)}, u32[]{:S(2)}) copy-start(f32[1,16,1,256,256]{4,3,2,1,0:T(8,128)} %param.8) | copy-start | bytes 12582916
  30.8 30.0 %copy-start.11 = (s32[1,1,256,256]{3,2,1,0:T(8,128)S(1)}, s32[1,1,256,256]{3,2,1,0:T(8,128)}, u32[]{:S(2)}) copy-start(s32[1,1,256,256]{3,2,1,0:T(8,128)} %param.10) | copy-start | bytes 786436
  30.9 38.6 %collective-permute-start.1 = (f32[4,256,256]{2,1,0:T(8,128)S(1)}, f32[4,256,256]{2,1,0:T(8,128)S(1)}, u32[]{:S(2)}, u32[]{:S(2)}) collective-permute-start(f32[4,256,256]{2,1,0:T(8,128)S(1)} %slice.132), channel_id=1, source_target_pairs={{0,8},{1,9},{2,10},{3,11},{4,12},{5,13},{6,14},{7,15},{8,0},{9,1},... | collective-permute-start | bytes 3145736 | tf_op jit(solution)/shard_map/ppermute | solution.py:293
  36.7 24.0 %collective-permute-start.2 = (f32[16,256]{1,0:T(8,128)S(1)}, f32[16,256]{1,0:T(8,128)S(1)}, u32[]{:S(2)}, u32[]{:S(2)}) collective-permute-start(f32[16,256]{1,0:T(8,128)S(1)} %get-tuple-element.23), channel_id=1, source_target_pairs={{0,4},{1,5},{2,6},{3,7},{4,8},{5,9},{6,10},{7,11},{8,12},{9,13},{1... | collective-permute-start | bytes 49160 | tf_op jit(solution)/shard_map/ppermute | solution.py:266
  41.8 18.9 %collective-permute-start.3 = (f32[16,256]{1,0:T(8,128)S(1)}, f32[16,256]{1,0:T(8,128)S(1)}, u32[]{:S(2)}, u32[]{:S(2)}) collective-permute-start(f32[16,256]{1,0:T(8,128)S(1)} %get-tuple-element.24), channel_id=1, source_target_pairs={{4,0},{5,1},{6,2},{7,3},{8,4},{9,5},{10,6},{11,7},{12,8},{13,9},{1... | collective-permute-start | bytes 49160 | tf_op jit(solution)/shard_map/ppermute | solution.py:267
  46.5 14.2 %collective-permute-start.4 = (f32[16,256]{1,0:T(8,128)S(1)}, f32[16,256]{1,0:T(8,128)S(1)}, u32[]{:S(2)}, u32[]{:S(2)}) collective-permute-start(f32[16,256]{1,0:T(8,128)S(1)} %get-tuple-element.25), channel_id=1, source_target_pairs={{0,1},{1,2},{2,3},{4,5},{5,6},{6,7},{8,9},{9,10},{10,11},{12,13},{... | collective-permute-start | bytes 49160 | tf_op jit(solution)/shard_map/ppermute | solution.py:269
  47.8 12.9 %collective-permute-start.5 = (f32[16,256]{1,0:T(8,128)S(1)}, f32[16,256]{1,0:T(8,128)S(1)}, u32[]{:S(2)}, u32[]{:S(2)}) collective-permute-start(f32[16,256]{1,0:T(8,128)S(1)} %get-tuple-element.26), channel_id=1, source_target_pairs={{1,0},{2,1},{3,2},{5,4},{6,5},{7,6},{9,8},{10,9},{11,10},{13,12},{... | collective-permute-start | bytes 49160 | tf_op jit(solution)/shard_map/ppermute | solution.py:270
  66.7 28.8 %copy-start.6 = (f32[1,1,4,256,256]{4,3,2,1,0:T(8,128)S(1)}, f32[1,1,4,256,256]{4,3,2,1,0:T(8,128)}, u32[]{:S(2)}) copy-start(f32[1,1,4,256,256]{4,3,2,1,0:T(8,128)} %param.11) | copy-start | bytes 3145732
  66.7 28.8 %copy-start.8 = (f32[1,1,4,256,256]{4,3,2,1,0:T(8,128)S(1)}, f32[1,1,4,256,256]{4,3,2,1,0:T(8,128)}, u32[]{:S(2)}) copy-start(f32[1,1,4,256,256]{4,3,2,1,0:T(8,128)} %param.12) | copy-start | bytes 3145732
  69.7 11.7 %collective-permute-start.12 = (f32[256,256]{1,0:T(8,128)S(1)}, f32[256,256]{1,0:T(8,128)S(1)}, u32[]{:S(2)}, u32[]{:S(2)}) collective-permute-start(f32[256,256]{1,0:T(8,128)S(1)} %get-tuple-element.47), channel_id=1, source_target_pairs={{0,6},{1,7},{2,0},{3,1},{4,2},{5,3},{6,4},{7,5},{8,14},{9,15},{10,... | collective-permute-start | bytes 786440 | tf_op jit(solution)/shard_map/ppermute | solution.py:49
  69.8 14.2 %collective-permute-start.10 = (f32[256,256]{1,0:T(8,128)S(1)}, f32[256,256]{1,0:T(8,128)S(1)}, u32[]{:S(2)}, u32[]{:S(2)}) collective-permute-start(f32[256,256]{1,0:T(8,128)S(1)} %get-tuple-element.48), channel_id=1, source_target_pairs={{0,2},{1,3},{2,4},{3,5},{4,6},{5,7},{6,0},{7,1},{8,10},{9,11},{10,... | collective-permute-start | bytes 786440 | tf_op jit(solution)/shard_map/ppermute | solution.py:49
  71.8 12.2 %collective-permute-start.11 = (f32[256,256]{1,0:T(8,128)S(1)}, f32[256,256]{1,0:T(8,128)S(1)}, u32[]{:S(2)}, u32[]{:S(2)}) collective-permute-start(f32[256,256]{1,0:T(8,128)S(1)} %get-tuple-element.46), channel_id=1, source_target_pairs={{0,4},{1,5},{2,6},{3,7},{4,0},{5,1},{6,2},{7,3},{8,12},{9,13},{10,... | collective-permute-start | bytes 786440 | tf_op jit(solution)/shard_map/ppermute | solution.py:49
  72.6 15.4 %collective-permute-start.6 = (f32[256,256]{1,0:T(8,128)S(1)}, f32[256,256]{1,0:T(8,128)S(1)}, u32[]{:S(2)}, u32[]{:S(2)}) collective-permute-start(f32[256,256]{1,0:T(8,128)S(1)} %get-tuple-element.40), channel_id=1, source_target_pairs={{0,16},{1,17},{2,18},{3,19},{4,20},{5,21},{6,22},{7,23},{8,24},{9,... | collective-permute-start | bytes 786440 | tf_op jit(solution)/shard_map/ppermute | solution.py:53
  77.2 14.8 %collective-permute-start.7 = (f32[256,256]{1,0:T(8,128)S(1)}, f32[256,256]{1,0:T(8,128)S(1)}, u32[]{:S(2)}, u32[]{:S(2)}) collective-permute-start(f32[256,256]{1,0:T(8,128)S(1)} %get-tuple-element.40), channel_id=1, source_target_pairs={{0,24},{1,25},{2,26},{3,27},{4,28},{5,29},{6,30},{7,31},{8,16},{9,... | collective-permute-start | bytes 786440 | tf_op jit(solution)/shard_map/ppermute | solution.py:53
  84.1 15.2 %collective-permute-start.24 = (f32[256,256]{1,0:T(8,128)S(1)}, f32[256,256]{1,0:T(8,128)}, u32[]{:S(2)}, u32[]{:S(2)}) collective-permute-start(f32[256,256]{1,0:T(8,128)S(1)} %fusion.4), channel_id=1, source_target_pairs={{0,8},{1,9},{2,10},{3,11},{4,12},{5,13},{6,14},{7,15},{8,0},{9,1},... | collective-permute-start | bytes 786440 | tf_op jit(solution)/shard_map/ppermute | solution.py:330
  108.6 14.7 %collective-permute-start.13 = (f32[8,256,256]{2,1,0:T(8,128)}, f32[8,256,256]{2,1,0:T(8,128)S(1)}, u32[]{:S(2)}, u32[]{:S(2)}) collective-permute-start(f32[8,256,256]{2,1,0:T(8,128)} %copy-done.12), channel_id=1, source_target_pairs={{0,1},{1,0},{2,3},{3,2},{4,5},{5,4},{6,7},{7,6},{8,9},{9,8},{10,11... | collective-permute-start | bytes 6291464 | tf_op jit(solution)/shard_map/ppermute | solution.py:287
  108.9 12.3 %collective-permute-start.14 = (f32[256,256]{1,0:T(8,128)S(1)}, f32[256,256]{1,0:T(8,128)S(1)}, u32[]{:S(2)}, u32[]{:S(2)}) collective-permute-start(f32[256,256]{1,0:T(8,128)S(1)} %fusion.4), channel_id=1, source_target_pairs={{16,0},{17,1},{18,2},{19,3},{20,4},{21,5},{22,6},{23,7},{24,8},{25... | collective-permute-start | bytes 786440 | tf_op jit(solution)/shard_map/ppermute | solution.py:53
  125.4 33.3 %collective-permute-start.15 = (f32[4,256,256]{2,1,0:T(8,128)S(1)}, f32[4,256,256]{2,1,0:T(8,128)S(1)}, u32[]{:S(2)}, u32[]{:S(2)}) collective-permute-start(f32[4,256,256]{2,1,0:T(8,128)S(1)} %slice_add_fusion), channel_id=1, source_target_pairs={{0,8},{1,9},{2,10},{3,11},{4,12},{5,13},{6,14},{7,15},{8,0},{9,1},... | collective-permute-start | bytes 3145736 | tf_op jit(solution)/shard_map/ppermute | solution.py:293
  129.3 32.3 %copy-start.4 = (f32[1,16,1,256,256]{4,3,2,1,0:T(8,128)S(1)}, f32[1,16,1,256,256]{4,3,2,1,0:T(8,128)}, u32[]{:S(2)}) copy-start(f32[1,16,1,256,256]{4,3,2,1,0:T(8,128)} %param.8) | copy-start | bytes 12582916
  130.6 23.4 %collective-permute-start.16 = (f32[16,256]{1,0:T(8,128)S(1)}, f32[16,256]{1,0:T(8,128)S(1)}, u32[]{:S(2)}, u32[]{:S(2)}) collective-permute-start(f32[16,256]{1,0:T(8,128)S(1)} %get-tuple-element.31), channel_id=1, source_target_pairs={{0,4},{1,5},{2,6},{3,7},{4,8},{5,9},{6,10},{7,11},{8,12},{9,13},{1... | collective-permute-start | bytes 49160 | tf_op jit(solution)/shard_map/ppermute | solution.py:266
  134.6 19.9 %collective-permute-start.17 = (f32[16,256]{1,0:T(8,128)S(1)}, f32[16,256]{1,0:T(8,128)S(1)}, u32[]{:S(2)}, u32[]{:S(2)}) collective-permute-start(f32[16,256]{1,0:T(8,128)S(1)} %get-tuple-element.32), channel_id=1, source_target_pairs={{4,0},{5,1},{6,2},{7,3},{8,4},{9,5},{10,6},{11,7},{12,8},{13,9},{1... | collective-permute-start | bytes 49160 | tf_op jit(solution)/shard_map/ppermute | solution.py:267
  140.5 15.8 %collective-permute-start.18 = (f32[16,256]{1,0:T(8,128)S(1)}, f32[16,256]{1,0:T(8,128)S(1)}, u32[]{:S(2)}, u32[]{:S(2)}) collective-permute-start(f32[16,256]{1,0:T(8,128)S(1)} %get-tuple-element.33), channel_id=1, source_target_pairs={{0,1},{1,2},{2,3},{4,5},{5,6},{6,7},{8,9},{9,10},{10,11},{12,13},{... | collective-permute-start | bytes 49160 | tf_op jit(solution)/shard_map/ppermute | solution.py:269
  141.8 15.7 %collective-permute-start.19 = (f32[16,256]{1,0:T(8,128)S(1)}, f32[16,256]{1,0:T(8,128)S(1)}, u32[]{:S(2)}, u32[]{:S(2)}) collective-permute-start(f32[16,256]{1,0:T(8,128)S(1)} %get-tuple-element.34), channel_id=1, source_target_pairs={{1,0},{2,1},{3,2},{5,4},{6,5},{7,6},{9,8},{10,9},{11,10},{13,12},{... | collective-permute-start | bytes 49160 | tf_op jit(solution)/shard_map/ppermute | solution.py:270
  158.9 11.9 %collective-permute-start.22 = (f32[256,256]{1,0:T(8,128)S(1)}, f32[256,256]{1,0:T(8,128)S(1)}, u32[]{:S(2)}, u32[]{:S(2)}) collective-permute-start(f32[256,256]{1,0:T(8,128)S(1)} %get-tuple-element.44), channel_id=1, source_target_pairs={{0,6},{1,7},{2,0},{3,1},{4,2},{5,3},{6,4},{7,5},{8,14},{9,15},{10,... | collective-permute-start | bytes 786440 | tf_op jit(solution)/shard_map/ppermute | solution.py:49
  159.0 13.7 %collective-permute-start.20 = (f32[256,256]{1,0:T(8,128)S(1)}, f32[256,256]{1,0:T(8,128)S(1)}, u32[]{:S(2)}, u32[]{:S(2)}) collective-permute-start(f32[256,256]{1,0:T(8,128)S(1)} %get-tuple-element.45), channel_id=1, source_target_pairs={{0,2},{1,3},{2,4},{3,5},{4,6},{5,7},{6,0},{7,1},{8,10},{9,11},{10,... | collective-permute-start | bytes 786440 | tf_op jit(solution)/shard_map/ppermute | solution.py:49
  161.0 11.7 %collective-permute-start.21 = (f32[256,256]{1,0:T(8,128)S(1)}, f32[256,256]{1,0:T(8,128)S(1)}, u32[]{:S(2)}, u32[]{:S(2)}) collective-permute-start(f32[256,256]{1,0:T(8,128)S(1)} %get-tuple-element.43), channel_id=1, source_target_pairs={{0,4},{1,5},{2,6},{3,7},{4,0},{5,1},{6,2},{7,3},{8,12},{9,13},{10,... | collective-permute-start | bytes 786440 | tf_op jit(solution)/shard_map/ppermute | solution.py:49
  172.7 9.2 %collective-permute-start.23 = (f32[256,256]{1,0:T(8,128)S(1)}, f32[256,256]{1,0:T(8,128)S(1)}, u32[]{:S(2)}, u32[]{:S(2)}) collective-permute-start(f32[256,256]{1,0:T(8,128)S(1)} %fusion.3), channel_id=1, source_target_pairs={{16,0},{17,1},{18,2},{19,3},{20,4},{21,5},{22,6},{23,7},{24,8},{25... | collective-permute-start | bytes 786440 | tf_op jit(solution)/shard_map/ppermute | solution.py:53
  (13 other events, 55.9 us)
Sparse Core Ops, SparseCore 0:
  24.5 35.3 all-gather.2
  108.7 35.1 all-gather.4

commit v6 on v4

--- a/solution.py
+++ b/solution.py
@@ -37,12 +37,11 @@
 
 
 def to_lift(steps, flip):
-    pairs = []
-    for lift in range(LIFTS):
-        if 0 <= lift + steps < LIFTS:
-            for t in range(TILES):
-                pairs.append((lift * TILES + t, (lift + steps) * TILES + (t ^ (8 if flip else 0))))
-    return pairs
+    return [
+        (lift * TILES + t, (lift + steps) % LIFTS * TILES + (t ^ (8 if flip else 0)))
+        for lift in range(LIFTS)
+        for t in range(TILES)
+    ]
 
 
 def send_y(value, steps):
@@ -79,7 +78,9 @@
 SMALL = pl.CostEstimate(flops=1024, bytes_accessed=1024, transcendentals=0)
 
 
-def pieces_kernel(table, px, py, bottom, give, keep):
+def pieces_kernel(table, px, py, bottom, *refs):
+    give, keep, mark = refs[-3:]
+    mark[...] = jnp.zeros_like(mark)
     give[...] = jnp.zeros_like(give)
     keep[...] = jnp.zeros_like(keep)
     plane = split(bottom[...])
@@ -101,16 +102,60 @@
             give[slot] = give[slot] + piece
 
 
-def pieces_of(table, px, py, bottom):
+ANY_SPEC = pl.BlockSpec(memory_space=pl.ANY)
+
+
+def pieces_of(table, px, py, bottom, *earlier):
     return pl.pallas_call(
         pieces_kernel,
-        out_shape=(planes(8), planes(8)),
-        in_specs=[SMEM_SPEC] + [VMEM_SPEC] * 3,
-        out_specs=[VMEM_SPEC] * 2,
+        out_shape=(planes(8), planes(8), MARK),
+        in_specs=[SMEM_SPEC] + [VMEM_SPEC] * 3 + [ANY_SPEC] * len(earlier),
+        out_specs=[VMEM_SPEC] * 3,
         compiler_params=pltpu.CompilerParams(vmem_limit_bytes=24 * MIB),
         cost_estimate=SMALL,
         name="pieces",
-    )(table, px, py, bottom)
+    )(table, px, py, bottom, *earlier)
+
+
+def small_kernel(body, name, out_shape, inputs, earlier=()):
+    count = len(inputs)
+
+    def kernel(*refs):
+        body(*refs[:count], *refs[count + len(earlier) :])
+
+    return pl.pallas_call(
+        kernel,
+        out_shape=out_shape,
+        in_specs=[VMEM_SPEC] * count + [ANY_SPEC] * len(earlier),
+        out_specs=jax.tree.map(lambda _: VMEM_SPEC, out_shape),
+        compiler_params=pltpu.CompilerParams(vmem_limit_bytes=16 * MIB),
+        cost_estimate=SMALL,
+        name=name,
+    )(*inputs, *earlier)
+
+
+def pair_body(mine, flip, out):
+    out[0] = mine[...]
+    out[1] = flip[...]
+
+
+def new_pair_body(mine, flip, ghost, other, out):
+    out[0] = mine[...] + TIME_STEP * ghost[...]
+    out[1] = flip[...] + TIME_STEP * other[...]
+
+
+def cores_body(keep, taken, give_half, keep_half):
+    keep_half[...] = keep[0:4] + taken[0:4]
+    give_half[...] = keep[4:8] + taken[4:8]
+
+
+def halves_body(keep, got, *outs):
+    for i in range(4):
+        outs[i][...] = keep[i] + got[i]
+
+
+def ghost_body(own, a, b, c, out):
+    out[...] = own[...] + (a[...] + b[...] + c[...])
 
 
 def from_below(table, px, py, tops, picked, sems):
@@ -129,22 +174,23 @@
     return jnp.where(table[5] == 1, total, 0.0)
 
 
-def below_kernel(mark, table, px, py, speed, field, tops, out, picked, sems):
+def below_kernel(table, px, py, speed, field, tops, *refs):
+    out, picked, sems = refs[-3:]
     total = from_below(table, px, py, tops, picked, sems)
     out[...] = field[...] + TIME_STEP * (total + speed[...] * total)
 
 
-def below_update(mark, table, px, py, speed, plane, tops):
+def below_update(table, px, py, speed, plane, tops, *earlier):
     return pl.pallas_call(
         below_kernel,
         out_shape=planes(),
-        in_specs=[SMEM_SPEC] * 2 + [VMEM_SPEC] * 4 + [pl.BlockSpec(memory_space=pltpu.HBM)],
+        in_specs=[SMEM_SPEC] + [VMEM_SPEC] * 4 + [pl.BlockSpec(memory_space=pltpu.HBM)] + [ANY_SPEC] * len(earlier),
         out_specs=VMEM_SPEC,
         scratch_shapes=[pltpu.VMEM((4, W, W), F32), pltpu.SemaphoreType.DMA((4,))],
         compiler_params=pltpu.CompilerParams(vmem_limit_bytes=50 * MIB),
         cost_estimate=SMALL,
         name="below",
-    )(mark, table, px, py, speed, plane, tops)
+    )(table, px, py, speed, plane, tops, *earlier)
 
 
 def ends_kernel(table, px, py, speed, ghost, tops, field, out, picked, ends, sems):
@@ -185,7 +231,8 @@
     )(table, px, py, speed, ghost, tops, field)
 
 
-def rims_kernel(mark, field, bottom, top, row_low, row_high, col_low, col_high):
+def rims_kernel(field, bottom, top, *refs):
+    row_low, row_high, col_low, col_high = refs[-4:]
     lane = lax.broadcasted_iota(jnp.int32, (W, 128), 1)
     low = jnp.zeros((W, 128), F32)
     high = jnp.zeros((W, 128), F32)
@@ -199,24 +246,24 @@
     col_high[...] = high.T[:NZ]
 
 
-def rims_of(mark, field, bottom, top):
+def rims_of(field, bottom, top, *earlier):
     rim = jax.ShapeDtypeStruct((NZ, W), F32)
     return pl.pallas_call(
         rims_kernel,
         out_shape=(rim,) * 4,
-        in_specs=[SMEM_SPEC] + [VMEM_SPEC] * 3,
+        in_specs=[VMEM_SPEC] * 3 + [ANY_SPEC] * len(earlier),
         out_specs=[VMEM_SPEC] * 4,
         compiler_params=pltpu.CompilerParams(vmem_limit_bytes=16 * MIB),
         cost_estimate=SMALL,
         name="rims",
-    )(mark, field, bottom, top)
-
-
-def stencil_kernel(inverse, field, bottom, top, speed, inlets, x_low, x_high, y_low, y_high, out, mark, low, high):
+    )(field, bottom, top, *earlier)
+
+
+def stencil_kernel(inverse, inside, field, bottom, top, speed, inlets, x_low, x_high, y_low, y_high, out, mark, low, high):
     mark[...] = jnp.zeros_like(mark)
     pad = jnp.zeros((128 - NZ, W), F32)
-    low[...] = jnp.concatenate([y_low[...], pad], axis=0).T
-    high[...] = jnp.concatenate([y_high[...], pad], axis=0).T
+    low[...] = jnp.concatenate([jnp.where(inside[2] == 1, y_low[...], 0.0), pad], axis=0).T
+    high[...] = jnp.concatenate([jnp.where(inside[3] == 1, y_high[...], 0.0), pad], axis=0).T
     scale = inverse[0]
 
     def update(z, here, under, over):
@@ -225,8 +272,10 @@
         col_high = jnp.sum(jnp.where(pick, high[...], 0.0), axis=1, keepdims=True)
         row = lax.broadcasted_iota(jnp.int32, (W, W), 0)
         lane = lax.broadcasted_iota(jnp.int32, (W, W), 1)
-        beside = jnp.where(row == 0, x_low[pl.ds(z, 1), :], pltpu.roll(here, 1, 0))
-        beside = beside + jnp.where(row == W - 1, x_high[pl.ds(z, 1), :], pltpu.roll(here, W - 1, 0))
+        row_low = jnp.where(inside[0] == 1, x_low[pl.ds(z, 1), :], 0.0)
+        row_high = jnp.where(inside[1] == 1, x_high[pl.ds(z, 1), :], 0.0)
+        beside = jnp.where(row == 0, row_low, pltpu.roll(here, 1, 0))
+        beside = beside + jnp.where(row == W - 1, row_high, pltpu.roll(here, W - 1, 0))
         beside = beside + jnp.where(lane == 0, col_low, pltpu.roll(here, 1, 1))
         beside = beside + jnp.where(lane == W - 1, col_high, pltpu.roll(here, W - 1, 1))
         lapl = (beside - 4.0 * here) * scale
@@ -248,26 +297,27 @@
     out[NZ - 1] = update(NZ - 1, top[...], field[NZ - 2], zero)
 
 
-def stencil(inverse, field, bottom, top, speed, inlets, halos):
+def stencil(inverse, inside, field, bottom, top, speed, inlets, halos):
     return pl.pallas_call(
         stencil_kernel,
         out_shape=(planes(NZ), MARK),
-        in_specs=[SMEM_SPEC] + [VMEM_SPEC] * 9,
+        in_specs=[SMEM_SPEC] * 2 + [VMEM_SPEC] * 9,
         out_specs=[VMEM_SPEC] * 2,
         scratch_shapes=[pltpu.VMEM((W, 128), F32)] * 2,
         compiler_params=pltpu.CompilerParams(vmem_limit_bytes=24 * MIB),
         cost_estimate=SMALL,
         name="stencil",
-    )(inverse, field, bottom, top, speed, inlets, *halos)
+    )(inverse, inside, field, bottom, top, speed, inlets, *halos)
 
 
 def exchange_rims(rims):
     row_low, row_high, col_low, col_high = rims
-    x_low = lax.ppermute(row_high, "tile", [(t, t + TCOL) for t in range(TILES - TCOL)])
-    x_high = lax.ppermute(row_low, "tile", [(t + TCOL, t) for t in range(TILES - TCOL)])
-    inside = [t for t in range(TILES) if t % TCOL < TCOL - 1]
-    y_low = lax.ppermute(col_high, "tile", [(t, t + 1) for t in inside])
-    y_high = lax.ppermute(col_low, "tile", [(t + 1, t) for t in inside])
+    up = [(t, (t + TCOL) % TILES) for t in range(TILES)]
+    right = [(t, t - t % TCOL + (t + 1) % TCOL) for t in range(TILES)]
+    x_low = lax.ppermute(row_high, "tile", up)
+    x_high = lax.ppermute(row_low, "tile", [(d, s) for s, d in up])
+    y_low = lax.ppermute(col_high, "tile", right)
+    y_high = lax.ppermute(col_low, "tile", [(d, s) for s, d in right])
     return x_low, x_high, y_low, y_high
 
 
@@ -275,26 +325,26 @@
     return send_lift(plane, 1, False), send_lift(plane, 1, True)
 
 
-def gather_pair(mine, flip):
-    return lax.all_gather(jnp.stack([mine, flip]), "tile", axis_index_groups=BY_HALF, axis=0, tiled=True)
-
-
-def zero_of(value):
-    return 0.0 * value[(0,) * value.ndim]
-
-
-def reduce_cores(give, keep):
+def gather_pair(pair):
+    return lax.all_gather(pair, "tile", axis_index_groups=BY_HALF, axis=0, tiled=True)
+
+
+def reduce_cores(give, keep, *earlier):
     taken = lax.ppermute(give, "tile", OTHER_CORE)
-    slots = keep + taken
-    return slots[4:8], slots[0:4], zero_of(slots)
+    return small_kernel(cores_body, "cores_sum", (planes(4), planes(4)), (keep, taken), earlier)
 
 
 def reduce_halves(give):
     return lax.ppermute(give, "tile", OTHER_HALF)
 
 
-def reduce_ring(slots):
-    return slots[0], send_y(slots[1], 1), send_y(slots[2], 2), send_y(slots[3], -1)
+def reduce_ring(keep, got, *earlier):
+    own, *others = small_kernel(halves_body, "halves_sum", (planes(),) * 4, (keep, got), earlier)
+    return own, *(send_y(part, step) for part, step in zip(others, (1, 2, -1)))
+
+
+def ghost_sum(parts, *earlier):
+    return small_kernel(ghost_body, "ghost_sum", planes(), parts, earlier)
 
 
 def on_device(oxygen, velocity, spacing, inlets, proj_x, proj_y, sources):
@@ -309,35 +359,34 @@
     has_below = (lift > 0).astype(jnp.int32)
     is_top = lift == LIFTS - 1
     table = jnp.concatenate([sources.reshape(4) & (TILES - 1), tile[None], has_below[None], is_top[None].astype(jnp.int32)])
+    inside = jnp.stack([tile >= TCOL, tile < TILES - TCOL, tile % TCOL > 0, tile % TCOL < TCOL - 1]).astype(jnp.int32)
     speed_low = speed[0]
     bottom, top = field[0], field[NZ - 1]
 
     mine, flip = climb(top)
-    give, keep = pieces_of(table, px, py, bottom)
-    give, keep, mark = reduce_cores(give, keep)
-    tops = gather_pair(mine + mark, flip + mark)
+    give, keep, mark = pieces_of(table, px, py, bottom)
+    tops = gather_pair(small_kernel(pair_body, "pair", planes(2), (mine, flip), (mark,)))
+    give, keep = reduce_cores(give, keep)
     got = reduce_halves(give)
-    rims = rims_of(mark[None], field, bottom, top)
-    field, mark = stencil(inverse, field, bottom, top, speed, inlets, exchange_rims(rims))
+    halos = exchange_rims(rims_of(field, bottom, top, give))
+    field, mark = stencil(inverse, inside, field, bottom, top, speed, inlets, halos)
     low, high = field[0], field[NZ - 1]
     mine, flip = climb(high)
-    slots = keep + got + zero_of(mark)
-    own, *parts = reduce_ring(slots)
-    bottom = below_update(zero_of(slots)[None], table, px, py, speed_low, low, tops)
-    give, keep = pieces_of(table, px, py, bottom)
-    give, keep, mark = reduce_cores(give, keep)
-    got_near = reduce_halves(give[0:2])
-    ghost = own + (parts[0] + parts[1] + parts[2]) + (mark + zero_of(got_near))
+    parts = reduce_ring(keep, got, mark)
+    bottom = below_update(table, px, py, speed_low, low, tops, parts[0], mine, flip)
+    ghost = ghost_sum(parts)
     other_ghost = lax.ppermute(ghost, "tile", OTHER_HALF)
-    tops = gather_pair(mine + TIME_STEP * ghost, flip + TIME_STEP * other_ghost)
     ghost_above = jnp.where(is_top, AMBIENT, send_lift(ghost, -1, False))
+    give, keep, mark = pieces_of(table, px, py, bottom, ghost)
+    pair = small_kernel(new_pair_body, "new_pair", planes(2), (mine, flip, ghost, other_ghost), (mark,))
+    tops = gather_pair(pair)
     top = high + TIME_STEP * ghost_above
-    got_far = reduce_halves(give[2:4])
-    rims = rims_of(mark[None], field, bottom, top)
-    field, mark = stencil(inverse, field, bottom, top, speed, inlets, exchange_rims(rims))
-    near, far = keep[0:2] + got_near, keep[2:4] + got_far + zero_of(mark)
-    own, *parts = reduce_ring([near[0], near[1], far[0], far[1]])
-    ghost = send_lift(own + (parts[0] + parts[1] + parts[2]), -1, False)
+    give, keep = reduce_cores(give, keep, top)
+    got = reduce_halves(give)
+    halos = exchange_rims(rims_of(field, bottom, top, give))
+    field, mark = stencil(inverse, inside, field, bottom, top, speed, inlets, halos)
+    parts = reduce_ring(keep, got, *halos)
+    ghost = send_lift(ghost_sum(parts, mark), -1, False)
     field = fix_ends(table, px, py, speed_low, ghost, tops, field)
     return field.reshape(1, NZ, 1, W, W)
 

time: 224 us -> 184 us (0.82); the launches traced: 223 us -> 181 us
  waiting for transfers between devices: 86 us -> 55.1 us
  starting transfers between devices: 61.1 us -> 48.5 us
  Pallas kernels: 32.5 us -> 41.3 us
  between operations: 20.1 us -> 14.4 us
  other arithmetic: 4.78 us -> 1.84 us
    ppermute x6, waiting for transfers between devices: 50.1 us -> 10.9 us  [send_lift(): return lax.ppermute(value, ('lift', 'tile'), to_lift(steps, flip))]
    ppermute x8, waiting for transfers between devices: 12.6 us -> 32.7 us  [the longest x2 32.7 us: exchange_rims(): x_low = lax.ppermute(row_high, 'tile', up)]
    ppermute x8, starting transfers between devices: 24.8 us -> 15.4 us  [the longest x2 6.38 us: exchange_rims(): x_high = lax.ppermute(row_low, 'tile', [(d, s) for s, d in up])]
    pallas_call x5 -> x13, Pallas kernels: 13 us -> 19.7 us  [the longest x2 6.89 us: pieces_of(): pl.pallas_call(pieces_kernel, out_shape=(planes(8), planes(8), MARK), in_...]
    ppermute x6, waiting for transfers between devices: 13.7 us -> 7.06 us  [send_y(): return lax.ppermute(value, 'tile', along_y(steps))]
    unnamed x42 -> x44, local copies, waits for them, and re-layouts: 12.4 us -> 18 us
    ppermute x3 -> x2, waiting for transfers between devices: 5.29 us -> 0.01 us  [reduce_halves(): return lax.ppermute(give, 'tile', OTHER_HALF)]
    slice x8 -> x0, local copies, waits for them, and re-layouts: 4.39 us -> none  [the longest x6 3.31 us: zero_of(): return 0.0 * value[(0,) * value.ndim]]
  transfers between devices with their start and end apart: 28 -> 27, of which waited for: 12 -> 10; matrix products, arithmetic and copies ran while one was open for 3% -> 1% of each run, Pallas kernels for 7% -> 18%
where the time goes in v6:
time: 184 us; the launch traced here: 181 us
  waiting for transfers between devices  55.1 us (30%)
  starting transfers between devices  48.5 us (26%)
  Pallas kernels  41.3 us (22%)
  local copies, waits for them, and re-layouts  19.9 us (11%)
  between operations  14.4 us (8%)
  other arithmetic  1.84 us (1%)
    ppermute x2, waiting for transfers between devices, exchange_rims(): x_low = lax.ppermute(row_high, 'tile', up)  32.7 us
    unnamed x44, local copies, waits for them, and re-layouts  18 us
    ppermute x6, starting transfers between devices, send_lift(): return lax.ppermute(value, ('lift', 'tile'), to_lift(steps, flip))  17 us
    pallas_call x2, Pallas kernels, stencil(): pl.pallas_call(stencil_kernel, out_shape=(planes(NZ), MARK), in_specs=[SM...  16 us
    ppermute x6, waiting for transfers between devices, send_lift(): return lax.ppermute(value, ('lift', 'tile'), to_lift(steps, flip))  10.9 us
    ppermute x6, starting transfers between devices, send_y(): return lax.ppermute(value, 'tile', along_y(steps))  7.27 us
    ppermute x6, waiting for transfers between devices, send_y(): return lax.ppermute(value, 'tile', along_y(steps))  7.06 us
    pallas_call x2, Pallas kernels, pieces_of(): pl.pallas_call(pieces_kernel, out_shape=(planes(8), planes(8), MARK), in_...  6.89 us
  transfers between devices with their start and end apart: 27, of which 10 were waited for; matrix products, arithmetic and copies ran while one was open for 1% of the time, Pallas kernels for 18%

profile of v6, /device:TPU:6, one launch (start us, length us, event | category | flops | bytes accessed | tf_op | source)
XLA Modules:
  0.0 180.9 jit_solution(16006463023319011369)
XLA Ops:
  7.6 2.3 %collective-permute-start.5 = (f32[256,256]{1,0:T(8,128)S(1)}, f32[256,256]{1,0:T(8,128)S(1)}, u32[]{:S(2)}, u32[]{:S(2)}) collective-permute-start(f32[256,256]{1,0:T(8,128)S(1)} %get-tuple-element.67.top), channel_id=1, source_target_pairs={{0,16},{1,17},{2,18},{3,19},{4,20},{5,21},{6,22},{7,23},{8,24},{9,... | collective-permute-start | bytes 786440 | tf_op jit(solution)/shard_map/ppermute | solution.py:52
  14.2 3.4 %pieces.2 = (f32[8,256,256]{2,1,0:T(8,128)S(1)}, f32[8,256,256]{2,1,0:T(8,128)S(1)}, f32[8,128]{1,0:T(8,128)S(1)}) custom-call(s32[7]{0:T(128)S(1)} %pad_add_fusion.table, f32[4,256,256]{2,1,0:T(8,128)S(1)} %bitcast.33, f32[4,256,256]{2,1,0:T(8,128)S(1)} %bitcast.37, f32[256,256]{1,0:T(8,128)S(1)} %get-tuple-element.68.bottom), custom_call_target="tpu_custom_call" | custom-call | flops 1024 | bytes 1024 | tf_op jit(solution)/shard_map/pieces/pallas_call | solution.py:109
  20.1 4.4 %collective-permute-done.refs_1_ = f32[8,256,256]{2,1,0:T(8,128)S(1)} collective-permute-done((f32[8,256,256]{2,1,0:T(8,128)}, f32[8,256,256]{2,1,0:T(8,128)S(1)}, u32[]{:S(2)}, u32[]{:S(2)}) %collective-permute-start) | collective-permute-done | bytes 2097184 | tf_op jit(solution)/shard_map/ppermute | solution.py:333
  26.6 3.9 %collective-permute-start.7 = (f32[4,256,256]{2,1,0:T(8,128)}, f32[4,256,256]{2,1,0:T(8,128)}, u32[]{:S(2)}, u32[]{:S(2)}) collective-permute-start(f32[4,256,256]{2,1,0:T(8,128)} %get-tuple-element.37.refs_0_), channel_id=1, source_target_pairs={{0,8},{1,9},{2,10},{3,11},{4,12},{5,13},{6,14},{7,15},{8,0},{9,1},... | collective-permute-start | bytes 3145736 | tf_op jit(solution)/shard_map/ppermute | solution.py:338
  30.5 2.2 %copy-done.2 = f32[1,16,1,256,256]{4,3,2,1,0:T(8,128)S(1)} copy-done((f32[1,16,1,256,256]{4,3,2,1,0:T(8,128)S(1)}, f32[1,16,1,256,256]{4,3,2,1,0:T(8,128)}, u32[]{:S(2)}) %copy-start.2) | copy-done | bytes 4194328
  34.0 3.2 %collective-permute-start.1 = (f32[16,256]{1,0:T(8,128)S(1)}, f32[16,256]{1,0:T(8,128)S(1)}, u32[]{:S(2)}, u32[]{:S(2)}) collective-permute-start(f32[16,256]{1,0:T(8,128)S(1)} %get-tuple-element.38), channel_id=1, source_target_pairs={{0,4},{1,5},{2,6},{3,7},{4,8},{5,9},{6,10},{7,11},{8,12},{9,13},{1... | collective-permute-start | bytes 49160 | tf_op jit(solution)/shard_map/ppermute | solution.py:317
  37.2 2.7 %collective-permute-start.2 = (f32[16,256]{1,0:T(8,128)S(1)}, f32[16,256]{1,0:T(8,128)S(1)}, u32[]{:S(2)}, u32[]{:S(2)}) collective-permute-start(f32[16,256]{1,0:T(8,128)S(1)} %get-tuple-element.39), channel_id=1, source_target_pairs={{4,0},{5,1},{6,2},{7,3},{8,4},{9,5},{10,6},{11,7},{12,8},{13,9},{1... | collective-permute-start | bytes 49160 | tf_op jit(solution)/shard_map/ppermute | solution.py:318
  40.0 1.7 collective-permute-start.4
  42.5 14.8 %collective-permute-done.1.x_low = f32[16,256]{1,0:T(8,128)S(1)} collective-permute-done((f32[16,256]{1,0:T(8,128)S(1)}, f32[16,256]{1,0:T(8,128)S(1)}, u32[]{:S(2)}, u32[]{:S(2)}) %collective-permute-start.1) | collective-permute-done | bytes 16416 | tf_op jit(solution)/shard_map/ppermute | solution.py:317
  57.3 2.2 %copy-done.4 = f32[1,16,1,256,256]{4,3,2,1,0:T(8,128)S(1)} copy-done((f32[1,16,1,256,256]{4,3,2,1,0:T(8,128)S(1)}, f32[1,16,1,256,256]{4,3,2,1,0:T(8,128)}, u32[]{:S(2)}) %copy-start.4) | copy-done | bytes 4194328
  59.5 7.0 %stencil.2 = (f32[16,256,256]{2,1,0:T(8,128)S(1)}, f32[8,128]{1,0:T(8,128)S(1)}) custom-call(f32[1]{0:T(128)S(6)} %div.3.inverse, s32[4]{0:T(128)S(1)} %add_convert_fusion.inside, f32[16,256,256]{2,1,0:T(8,128)S(1)} %bitcast.30, f32[256,256]{1,0:T(8,128)S(1)} %get-tuple-element.68.bottom, f32[256,256]{1,0:T(8,128)S(1)} %get-tuple-element.67.top, ...), custom_call_target="tpu_custom_call" | custom-call | flops 1024 | bytes 1024 | tf_op jit(solution)/shard_map/stencil/pallas_call | solution.py:301
  66.6 2.3 %halves_sum.2 = (f32[256,256]{1,0:T(8,128)S(1)}, f32[256,256]{1,0:T(8,128)S(1)}, f32[256,256]{1,0:T(8,128)S(1)}, f32[256,256]{1,0:T(8,128)S(1)}) custom-call(f32[4,256,256]{2,1,0:T(8,128)S(1)} %copy-done.14, f32[4,256,256]{2,1,0:T(8,128)} %collective-permute-done.7.refs_1_, f32[8,128]{1,0:T(8,128)S(1)} %get-tuple-element.45.refs_2_), custom_call_target="tpu_custom_call" | custom-call | flops 1024 | bytes 1024 | tf_op jit(solution)/shard_map/halves_sum/pallas_call | solution.py:126
  69.7 1.9 %collective-permute-start.11 = (f32[256,256]{1,0:T(8,128)S(1)}, f32[256,256]{1,0:T(8,128)S(1)}, u32[]{:S(2)}, u32[]{:S(2)}) collective-permute-start(f32[256,256]{1,0:T(8,128)S(1)} %get-tuple-element.48), channel_id=1, source_target_pairs={{0,4},{1,5},{2,6},{3,7},{4,0},{5,1},{6,2},{7,3},{8,12},{9,13},{10,... | collective-permute-start | bytes 786440 | tf_op jit(solution)/shard_map/ppermute | solution.py:48
  73.2 4.5 %collective-permute-start.8 = (f32[256,256]{1,0:T(8,128)S(1)}, f32[256,256]{1,0:T(8,128)S(1)}, u32[]{:S(2)}, u32[]{:S(2)}) collective-permute-start(f32[256,256]{1,0:T(8,128)S(1)} %get-tuple-element.65), channel_id=1, source_target_pairs={{0,16},{1,17},{2,18},{3,19},{4,20},{5,21},{6,22},{7,23},{8,24},{9,... | collective-permute-start | bytes 786440 | tf_op jit(solution)/shard_map/ppermute | solution.py:52
  78.2 5.0 %collective-permute-done.10.refs_1_ = f32[256,256]{1,0:T(8,128)S(1)} collective-permute-done((f32[256,256]{1,0:T(8,128)S(1)}, f32[256,256]{1,0:T(8,128)S(1)}, u32[]{:S(2)}, u32[]{:S(2)}) %collective-permute-start.10) | collective-permute-done | bytes 262176 | tf_op jit(solution)/shard_map/ppermute | solution.py:48
  84.0 3.1 %collective-permute-start.24 = (f32[256,256]{1,0:T(8,128)S(1)}, f32[256,256]{1,0:T(8,128)}, u32[]{:S(2)}, u32[]{:S(2)}) collective-permute-start(f32[256,256]{1,0:T(8,128)S(1)} %ghost_sum.2.refs_0_.refs_2_), channel_id=1, source_target_pairs={{0,8},{1,9},{2,10},{3,11},{4,12},{5,13},{6,14},{7,15},{8,0},{9,1},... | collective-permute-start | bytes 786440 | tf_op jit(solution)/shard_map/ppermute | solution.py:378
  91.4 3.6 %below.1.bottom = f32[256,256]{1,0:T(8,128)S(1)} custom-call(s32[7]{0:T(128)S(1)} %pad_add_fusion.table, f32[4,256,256]{2,1,0:T(8,128)S(1)} %bitcast.34, f32[4,256,256]{2,1,0:T(8,128)S(1)} %bitcast.38, f32[256,256]{1,0:T(8,128)S(1)} %slice_bitcast_fusion.4.speed, f32[256,256]{1,0:T(8,128)S(1)} %copy-done.19, ...), custom_call_target="tpu_custom_call" | custom-call | flops 1024 | bytes 1024 | tf_op jit(solution)/shard_map/below/pallas_call | solution.py:184
  95.1 3.4 %pieces.3 = (f32[8,256,256]{2,1,0:T(8,128)S(1)}, f32[8,256,256]{2,1,0:T(8,128)S(1)}, f32[8,128]{1,0:T(8,128)S(1)}) custom-call(s32[7]{0:T(128)S(1)} %pad_add_fusion.table, f32[4,256,256]{2,1,0:T(8,128)S(1)} %bitcast.35, f32[4,256,256]{2,1,0:T(8,128)S(1)} %bitcast.39, f32[256,256]{1,0:T(8,128)S(1)} %below.1.bottom, f32[256,256]{1,0:T(8,128)S(1)} %ghost_sum.2.refs_0_.refs_2_), custom_call_target="tpu_custom_call" | custom-call | flops 1024 | bytes 1024 | tf_op jit(solution)/shard_map/pieces/pallas_call | solution.py:109
  101.3 1.8 %new_pair.1 = f32[2,256,256]{2,1,0:T(8,128)} custom-call(f32[256,256]{1,0:T(8,128)S(1)} %copy-done.16, f32[256,256]{1,0:T(8,128)S(1)} %copy-done.18, f32[256,256]{1,0:T(8,128)S(1)} %ghost_sum.2.refs_0_.refs_2_, f32[256,256]{1,0:T(8,128)} %collective-permute-done.24.refs_3_, f32[8,128]{1,0:T(8,128)S(1)} %get-tuple-element.63.refs_4_), custom_call_target="tpu_custom_call" | custom-call | flops 1024 | bytes 1024 | tf_op jit(solution)/shard_map/new_pair/pallas_call | solution.py:126
  103.2 5.7 %collective-permute-start.14 = (f32[256,256]{1,0:T(8,128)S(1)}, f32[256,256]{1,0:T(8,128)S(1)}, u32[]{:S(2)}, u32[]{:S(2)}) collective-permute-start(f32[256,256]{1,0:T(8,128)S(1)} %ghost_sum.2.refs_0_.refs_2_), channel_id=1, source_target_pairs={{0,112},{1,113},{2,114},{3,115},{4,116},{5,117},{6,118},{7,119},{8... | collective-permute-start | bytes 786440 | tf_op jit(solution)/shard_map/ppermute | solution.py:52
  109.0 6.2 %collective-permute-done.14 = f32[256,256]{1,0:T(8,128)S(1)} collective-permute-done((f32[256,256]{1,0:T(8,128)S(1)}, f32[256,256]{1,0:T(8,128)S(1)}, u32[]{:S(2)}, u32[]{:S(2)}) %collective-permute-start.14) | collective-permute-done | bytes 262176 | tf_op jit(solution)/shard_map/ppermute | solution.py:52
  116.2 1.9 %copy-done.11 = f32[8,256,256]{2,1,0:T(8,128)S(1)} copy-done((f32[8,256,256]{2,1,0:T(8,128)S(1)}, f32[8,256,256]{2,1,0:T(8,128)}, u32[]{:S(2)}) %copy-start.11) | copy-done | bytes 2097176
  118.3 1.4 collective-permute-start.15
  121.0 2.3 %collective-permute-start.16 = (f32[16,256]{1,0:T(8,128)S(1)}, f32[16,256]{1,0:T(8,128)S(1)}, u32[]{:S(2)}, u32[]{:S(2)}) collective-permute-start(f32[16,256]{1,0:T(8,128)S(1)} %get-tuple-element.54), channel_id=1, source_target_pairs={{0,4},{1,5},{2,6},{3,7},{4,8},{5,9},{6,10},{7,11},{8,12},{9,13},{1... | collective-permute-start | bytes 49160 | tf_op jit(solution)/shard_map/ppermute | solution.py:317
  123.4 3.6 %collective-permute-start.17 = (f32[16,256]{1,0:T(8,128)S(1)}, f32[16,256]{1,0:T(8,128)S(1)}, u32[]{:S(2)}, u32[]{:S(2)}) collective-permute-start(f32[16,256]{1,0:T(8,128)S(1)} %get-tuple-element.55), channel_id=1, source_target_pairs={{4,0},{5,1},{6,2},{7,3},{8,4},{9,5},{10,6},{11,7},{12,8},{13,9},{1... | collective-permute-start | bytes 49160 | tf_op jit(solution)/shard_map/ppermute | solution.py:318
  127.0 1.7 collective-permute-start.19
  128.8 17.9 %collective-permute-done.16.refs_2_.x_low = f32[16,256]{1,0:T(8,128)S(1)} collective-permute-done((f32[16,256]{1,0:T(8,128)S(1)}, f32[16,256]{1,0:T(8,128)S(1)}, u32[]{:S(2)}, u32[]{:S(2)}) %collective-permute-start.16) | collective-permute-done | bytes 16416 | tf_op jit(solution)/shard_map/ppermute | solution.py:317
  146.9 2.5 %collective-permute-start.21 = (f32[256,256]{1,0:T(8,128)S(1)}, f32[256,256]{1,0:T(8,128)S(1)}, u32[]{:S(2)}, u32[]{:S(2)}) collective-permute-start(f32[256,256]{1,0:T(8,128)S(1)} %get-tuple-element.60), channel_id=1, source_target_pairs={{0,4},{1,5},{2,6},{3,7},{4,0},{5,1},{6,2},{7,3},{8,12},{9,13},{10,... | collective-permute-start | bytes 786440 | tf_op jit(solution)/shard_map/ppermute | solution.py:48
  150.6 9.0 %stencil.3 = (f32[16,256,256]{2,1,0:T(8,128)}, f32[8,128]{1,0:T(8,128)S(1)}) custom-call(f32[1]{0:T(128)S(6)} %div.3.inverse, s32[4]{0:T(128)S(1)} %add_convert_fusion.inside, f32[16,256,256]{2,1,0:T(8,128)S(1)} %copy-done.1, f32[256,256]{1,0:T(8,128)S(1)} %below.1.bottom, f32[256,256]{1,0:T(8,128)S(1)} %multiply_add_fusion.refs_2_.top, ...), custom_call_target="tpu_custom_call" | custom-call | flops 1024 | bytes 1024 | tf_op jit(solution)/shard_map/stencil/pallas_call | solution.py:301
  161.0 2.9 %collective-permute-start.23 = (f32[256,256]{1,0:T(8,128)S(1)}, f32[256,256]{1,0:T(8,128)S(1)}, u32[]{:S(2)}, u32[]{:S(2)}) collective-permute-start(f32[256,256]{1,0:T(8,128)S(1)} %ghost_sum.3), channel_id=1, source_target_pairs={{0,112},{1,113},{2,114},{3,115},{4,116},{5,117},{6,118},{7,119},{8... | collective-permute-start | bytes 786440 | tf_op jit(solution)/shard_map/ppermute | solution.py:52
  163.9 4.6 %collective-permute-done.23.ghost = f32[256,256]{1,0:T(8,128)S(1)} collective-permute-done((f32[256,256]{1,0:T(8,128)S(1)}, f32[256,256]{1,0:T(8,128)S(1)}, u32[]{:S(2)}, u32[]{:S(2)}) %collective-permute-start.23) | collective-permute-done | bytes 262176 | tf_op jit(solution)/shard_map/ppermute | solution.py:52
  168.5 5.6 %fix_ends.1 = f32[16,256,256]{2,1,0:T(8,128)} custom-call(s32[7]{0:T(128)S(1)} %pad_add_fusion.table, f32[4,256,256]{2,1,0:T(8,128)S(1)} %bitcast.36, f32[4,256,256]{2,1,0:T(8,128)S(1)} %bitcast.40, f32[256,256]{1,0:T(8,128)S(1)} %slice_bitcast_fusion.4.speed, f32[256,256]{1,0:T(8,128)S(1)} %collective-permute-done.23.ghost, ...), custom_call_target="tpu_custom_call", output_to_operand_aliasing={{}: (6, {})} | custom-call | flops 1024 | bytes 1024 | tf_op jit(solution)/shard_map/fix_ends/pallas_call | solution.py:217
  (91 shorter events, 27.5 us)
Async XLA Ops:
  6.5 82.0 %all-gather.3.cloned.1.call-start = ((), (), s32[]{:S(2)}) async-start(), calls=%async_computation | async-start | bytes 4718592 | tf_op jit(solution)/shard_map/all_gather | solution.py:329
  7.6 11.5 %collective-permute-start.5 = (f32[256,256]{1,0:T(8,128)S(1)}, f32[256,256]{1,0:T(8,128)S(1)}, u32[]{:S(2)}, u32[]{:S(2)}) collective-permute-start(f32[256,256]{1,0:T(8,128)S(1)} %get-tuple-element.67.top), channel_id=1, source_target_pairs={{0,16},{1,17},{2,18},{3,19},{4,20},{5,21},{6,22},{7,23},{8,24},{9,... | collective-permute-start | bytes 786440 | tf_op jit(solution)/shard_map/ppermute | solution.py:52
  9.9 9.3 %collective-permute-start.6 = (f32[256,256]{1,0:T(8,128)S(1)}, f32[256,256]{1,0:T(8,128)S(1)}, u32[]{:S(2)}, u32[]{:S(2)}) collective-permute-start(f32[256,256]{1,0:T(8,128)S(1)} %get-tuple-element.67.top), channel_id=1, source_target_pairs={{0,24},{1,25},{2,26},{3,27},{4,28},{5,29},{6,30},{7,31},{8,16},{9,... | collective-permute-start | bytes 786440 | tf_op jit(solution)/shard_map/ppermute | solution.py:52
  20.0 148.5 %all-gather.5.cloned.1.call-start = ((), (), s32[]{:S(2)}) async-start(), calls=%async_computation.1 | async-start | bytes 4718592 | tf_op jit(solution)/shard_map/all_gather | solution.py:329
  20.0 4.5 %collective-permute-start = (f32[8,256,256]{2,1,0:T(8,128)}, f32[8,256,256]{2,1,0:T(8,128)S(1)}, u32[]{:S(2)}, u32[]{:S(2)}) collective-permute-start(f32[8,256,256]{2,1,0:T(8,128)} %copy-done.21), channel_id=1, source_target_pairs={{0,1},{1,0},{2,3},{3,2},{4,5},{5,4},{6,7},{7,6},{8,9},{9,8},{10,11... | collective-permute-start | bytes 6291464 | tf_op jit(solution)/shard_map/ppermute | solution.py:333
  24.5 32.8 %copy-start.12 = (s32[1,1,256,256]{3,2,1,0:T(8,128)S(1)}, s32[1,1,256,256]{3,2,1,0:T(8,128)}, u32[]{:S(2)}) copy-start(s32[1,1,256,256]{3,2,1,0:T(8,128)} %param.10) | copy-start | bytes 786436
  26.6 39.9 %collective-permute-start.7 = (f32[4,256,256]{2,1,0:T(8,128)}, f32[4,256,256]{2,1,0:T(8,128)}, u32[]{:S(2)}, u32[]{:S(2)}) collective-permute-start(f32[4,256,256]{2,1,0:T(8,128)} %get-tuple-element.37.refs_0_), channel_id=1, source_target_pairs={{0,8},{1,9},{2,10},{3,11},{4,12},{5,13},{6,14},{7,15},{8,0},{9,1},... | collective-permute-start | bytes 3145736 | tf_op jit(solution)/shard_map/ppermute | solution.py:338
  32.7 24.6 %copy-start.3 = (f32[1,16,1,256,256]{4,3,2,1,0:T(8,128)S(1)}, f32[1,16,1,256,256]{4,3,2,1,0:T(8,128)}, u32[]{:S(2)}) copy-start(f32[1,16,1,256,256]{4,3,2,1,0:T(8,128)} %param.7) | copy-start | bytes 12582916
  34.0 23.3 %collective-permute-start.1 = (f32[16,256]{1,0:T(8,128)S(1)}, f32[16,256]{1,0:T(8,128)S(1)}, u32[]{:S(2)}, u32[]{:S(2)}) collective-permute-start(f32[16,256]{1,0:T(8,128)S(1)} %get-tuple-element.38), channel_id=1, source_target_pairs={{0,4},{1,5},{2,6},{3,7},{4,8},{5,9},{6,10},{7,11},{8,12},{9,13},{1... | collective-permute-start | bytes 49160 | tf_op jit(solution)/shard_map/ppermute | solution.py:317
  37.2 20.0 %collective-permute-start.2 = (f32[16,256]{1,0:T(8,128)S(1)}, f32[16,256]{1,0:T(8,128)S(1)}, u32[]{:S(2)}, u32[]{:S(2)}) collective-permute-start(f32[16,256]{1,0:T(8,128)S(1)} %get-tuple-element.39), channel_id=1, source_target_pairs={{4,0},{5,1},{6,2},{7,3},{8,4},{9,5},{10,6},{11,7},{12,8},{13,9},{1... | collective-permute-start | bytes 49160 | tf_op jit(solution)/shard_map/ppermute | solution.py:318
  40.0 17.3 %collective-permute-start.3 = (f32[16,256]{1,0:T(8,128)S(1)}, f32[16,256]{1,0:T(8,128)S(1)}, u32[]{:S(2)}, u32[]{:S(2)}) collective-permute-start(f32[16,256]{1,0:T(8,128)S(1)} %get-tuple-element.40), channel_id=1, source_target_pairs={{0,1},{1,2},{2,3},{3,0},{4,5},{5,6},{6,7},{7,4},{8,9},{9,10},{10,1... | collective-permute-start | bytes 49160 | tf_op jit(solution)/shard_map/ppermute | solution.py:319
  40.0 17.3 %collective-permute-start.4 = (f32[16,256]{1,0:T(8,128)S(1)}, f32[16,256]{1,0:T(8,128)S(1)}, u32[]{:S(2)}, u32[]{:S(2)}) collective-permute-start(f32[16,256]{1,0:T(8,128)S(1)} %get-tuple-element.41), channel_id=1, source_target_pairs={{1,0},{2,1},{3,2},{0,3},{5,4},{6,5},{7,6},{4,7},{9,8},{10,9},{11,1... | collective-permute-start | bytes 49160 | tf_op jit(solution)/shard_map/ppermute | solution.py:320
  66.5 22.1 %copy-start.7 = (f32[1,1,4,256,256]{4,3,2,1,0:T(8,128)S(1)}, f32[1,1,4,256,256]{4,3,2,1,0:T(8,128)}, u32[]{:S(2)}) copy-start(f32[1,1,4,256,256]{4,3,2,1,0:T(8,128)} %param.11) | copy-start | bytes 3145732
  66.5 22.0 %copy-start.9 = (f32[1,1,4,256,256]{4,3,2,1,0:T(8,128)S(1)}, f32[1,1,4,256,256]{4,3,2,1,0:T(8,128)}, u32[]{:S(2)}) copy-start(f32[1,1,4,256,256]{4,3,2,1,0:T(8,128)} %param.12) | copy-start | bytes 3145732
  68.9 14.4 %collective-permute-start.10 = (f32[256,256]{1,0:T(8,128)S(1)}, f32[256,256]{1,0:T(8,128)S(1)}, u32[]{:S(2)}, u32[]{:S(2)}) collective-permute-start(f32[256,256]{1,0:T(8,128)S(1)} %get-tuple-element.47), channel_id=1, source_target_pairs={{0,2},{1,3},{2,4},{3,5},{4,6},{5,7},{6,0},{7,1},{8,10},{9,11},{10,... | collective-permute-start | bytes 786440 | tf_op jit(solution)/shard_map/ppermute | solution.py:48
  69.7 13.6 %collective-permute-start.11 = (f32[256,256]{1,0:T(8,128)S(1)}, f32[256,256]{1,0:T(8,128)S(1)}, u32[]{:S(2)}, u32[]{:S(2)}) collective-permute-start(f32[256,256]{1,0:T(8,128)S(1)} %get-tuple-element.48), channel_id=1, source_target_pairs={{0,4},{1,5},{2,6},{3,7},{4,0},{5,1},{6,2},{7,3},{8,12},{9,13},{10,... | collective-permute-start | bytes 786440 | tf_op jit(solution)/shard_map/ppermute | solution.py:48
  71.5 12.4 %collective-permute-start.12 = (f32[256,256]{1,0:T(8,128)S(1)}, f32[256,256]{1,0:T(8,128)S(1)}, u32[]{:S(2)}, u32[]{:S(2)}) collective-permute-start(f32[256,256]{1,0:T(8,128)S(1)} %get-tuple-element.49), channel_id=1, source_target_pairs={{0,6},{1,7},{2,0},{3,1},{4,2},{5,3},{6,4},{7,5},{8,14},{9,15},{10,... | collective-permute-start | bytes 786440 | tf_op jit(solution)/shard_map/ppermute | solution.py:48
  73.2 14.0 %collective-permute-start.8 = (f32[256,256]{1,0:T(8,128)S(1)}, f32[256,256]{1,0:T(8,128)S(1)}, u32[]{:S(2)}, u32[]{:S(2)}) collective-permute-start(f32[256,256]{1,0:T(8,128)S(1)} %get-tuple-element.65), channel_id=1, source_target_pairs={{0,16},{1,17},{2,18},{3,19},{4,20},{5,21},{6,22},{7,23},{8,24},{9,... | collective-permute-start | bytes 786440 | tf_op jit(solution)/shard_map/ppermute | solution.py:52
  77.7 10.1 %collective-permute-start.9 = (f32[256,256]{1,0:T(8,128)S(1)}, f32[256,256]{1,0:T(8,128)S(1)}, u32[]{:S(2)}, u32[]{:S(2)}) collective-permute-start(f32[256,256]{1,0:T(8,128)S(1)} %get-tuple-element.65), channel_id=1, source_target_pairs={{0,24},{1,25},{2,26},{3,27},{4,28},{5,29},{6,30},{7,31},{8,16},{9,... | collective-permute-start | bytes 786440 | tf_op jit(solution)/shard_map/ppermute | solution.py:52
  84.0 17.3 %collective-permute-start.24 = (f32[256,256]{1,0:T(8,128)S(1)}, f32[256,256]{1,0:T(8,128)}, u32[]{:S(2)}, u32[]{:S(2)}) collective-permute-start(f32[256,256]{1,0:T(8,128)S(1)} %ghost_sum.2.refs_0_.refs_2_), channel_id=1, source_target_pairs={{0,8},{1,9},{2,10},{3,11},{4,12},{5,13},{6,14},{7,15},{8,0},{9,1},... | collective-permute-start | bytes 786440 | tf_op jit(solution)/shard_map/ppermute | solution.py:378
  103.1 13.0 %collective-permute-start.13 = (f32[8,256,256]{2,1,0:T(8,128)}, f32[8,256,256]{2,1,0:T(8,128)S(1)}, u32[]{:S(2)}, u32[]{:S(2)}) collective-permute-start(f32[8,256,256]{2,1,0:T(8,128)} %copy-done.20), channel_id=1, source_target_pairs={{0,1},{1,0},{2,3},{3,2},{4,5},{5,4},{6,7},{7,6},{8,9},{9,8},{10,11... | collective-permute-start | bytes 6291464 | tf_op jit(solution)/shard_map/ppermute | solution.py:333
  103.2 11.9 %collective-permute-start.14 = (f32[256,256]{1,0:T(8,128)S(1)}, f32[256,256]{1,0:T(8,128)S(1)}, u32[]{:S(2)}, u32[]{:S(2)}) collective-permute-start(f32[256,256]{1,0:T(8,128)S(1)} %ghost_sum.2.refs_0_.refs_2_), channel_id=1, source_target_pairs={{0,112},{1,113},{2,114},{3,115},{4,116},{5,117},{6,118},{7,119},{8... | collective-permute-start | bytes 786440 | tf_op jit(solution)/shard_map/ppermute | solution.py:52
  118.3 32.3 %copy-start.5 = (f32[1,16,1,256,256]{4,3,2,1,0:T(8,128)S(1)}, f32[1,16,1,256,256]{4,3,2,1,0:T(8,128)}, u32[]{:S(2)}) copy-start(f32[1,16,1,256,256]{4,3,2,1,0:T(8,128)} %param.8) | copy-start | bytes 12582916
  118.3 28.3 %collective-permute-start.15 = (f32[4,256,256]{2,1,0:T(8,128)S(1)}, f32[4,256,256]{2,1,0:T(8,128)S(1)}, u32[]{:S(2)}, u32[]{:S(2)}) collective-permute-start(f32[4,256,256]{2,1,0:T(8,128)S(1)} %get-tuple-element.53.refs_0_), channel_id=1, source_target_pairs={{0,8},{1,9},{2,10},{3,11},{4,12},{5,13},{6,14},{7,15},{8,0},{9,1},... | collective-permute-start | bytes 3145736 | tf_op jit(solution)/shard_map/ppermute | solution.py:338
  121.0 25.6 %collective-permute-start.16 = (f32[16,256]{1,0:T(8,128)S(1)}, f32[16,256]{1,0:T(8,128)S(1)}, u32[]{:S(2)}, u32[]{:S(2)}) collective-permute-start(f32[16,256]{1,0:T(8,128)S(1)} %get-tuple-element.54), channel_id=1, source_target_pairs={{0,4},{1,5},{2,6},{3,7},{4,8},{5,9},{6,10},{7,11},{8,12},{9,13},{1... | collective-permute-start | bytes 49160 | tf_op jit(solution)/shard_map/ppermute | solution.py:317
  123.4 23.3 %collective-permute-start.17 = (f32[16,256]{1,0:T(8,128)S(1)}, f32[16,256]{1,0:T(8,128)S(1)}, u32[]{:S(2)}, u32[]{:S(2)}) collective-permute-start(f32[16,256]{1,0:T(8,128)S(1)} %get-tuple-element.55), channel_id=1, source_target_pairs={{4,0},{5,1},{6,2},{7,3},{8,4},{9,5},{10,6},{11,7},{12,8},{13,9},{1... | collective-permute-start | bytes 49160 | tf_op jit(solution)/shard_map/ppermute | solution.py:318
  127.0 19.6 %collective-permute-start.18 = (f32[16,256]{1,0:T(8,128)S(1)}, f32[16,256]{1,0:T(8,128)S(1)}, u32[]{:S(2)}, u32[]{:S(2)}) collective-permute-start(f32[16,256]{1,0:T(8,128)S(1)} %get-tuple-element.56), channel_id=1, source_target_pairs={{0,1},{1,2},{2,3},{3,0},{4,5},{5,6},{6,7},{7,4},{8,9},{9,10},{10,1... | collective-permute-start | bytes 49160 | tf_op jit(solution)/shard_map/ppermute | solution.py:319
  127.0 19.6 %collective-permute-start.19 = (f32[16,256]{1,0:T(8,128)S(1)}, f32[16,256]{1,0:T(8,128)S(1)}, u32[]{:S(2)}, u32[]{:S(2)}) collective-permute-start(f32[16,256]{1,0:T(8,128)S(1)} %get-tuple-element.57), channel_id=1, source_target_pairs={{1,0},{2,1},{3,2},{0,3},{5,4},{6,5},{7,6},{4,7},{9,8},{10,9},{11,1... | collective-permute-start | bytes 49160 | tf_op jit(solution)/shard_map/ppermute | solution.py:320
  146.8 13.6 %collective-permute-start.20 = (f32[256,256]{1,0:T(8,128)S(1)}, f32[256,256]{1,0:T(8,128)S(1)}, u32[]{:S(2)}, u32[]{:S(2)}) collective-permute-start(f32[256,256]{1,0:T(8,128)S(1)} %get-tuple-element.59), channel_id=1, source_target_pairs={{0,2},{1,3},{2,4},{3,5},{4,6},{5,7},{6,0},{7,1},{8,10},{9,11},{10,... | collective-permute-start | bytes 786440 | tf_op jit(solution)/shard_map/ppermute | solution.py:48
  146.9 13.5 %collective-permute-start.21 = (f32[256,256]{1,0:T(8,128)S(1)}, f32[256,256]{1,0:T(8,128)S(1)}, u32[]{:S(2)}, u32[]{:S(2)}) collective-permute-start(f32[256,256]{1,0:T(8,128)S(1)} %get-tuple-element.60), channel_id=1, source_target_pairs={{0,4},{1,5},{2,6},{3,7},{4,0},{5,1},{6,2},{7,3},{8,12},{9,13},{10,... | collective-permute-start | bytes 786440 | tf_op jit(solution)/shard_map/ppermute | solution.py:48
  149.3 11.6 %collective-permute-start.22 = (f32[256,256]{1,0:T(8,128)S(1)}, f32[256,256]{1,0:T(8,128)S(1)}, u32[]{:S(2)}, u32[]{:S(2)}) collective-permute-start(f32[256,256]{1,0:T(8,128)S(1)} %get-tuple-element.61), channel_id=1, source_target_pairs={{0,6},{1,7},{2,0},{3,1},{4,2},{5,3},{6,4},{7,5},{8,14},{9,15},{10,... | collective-permute-start | bytes 786440 | tf_op jit(solution)/shard_map/ppermute | solution.py:48
  161.0 7.5 %collective-permute-start.23 = (f32[256,256]{1,0:T(8,128)S(1)}, f32[256,256]{1,0:T(8,128)S(1)}, u32[]{:S(2)}, u32[]{:S(2)}) collective-permute-start(f32[256,256]{1,0:T(8,128)S(1)} %ghost_sum.3), channel_id=1, source_target_pairs={{0,112},{1,113},{2,114},{3,115},{4,116},{5,117},{6,118},{7,119},{8... | collective-permute-start | bytes 786440 | tf_op jit(solution)/shard_map/ppermute | solution.py:52
  (17 other events, 47.6 us)
Sparse Core Ops, SparseCore 0:
  20.1 37.9 all-gather.2
  103.3 35.6 all-gather.4

commit v7 on v6

--- a/solution.py
+++ b/solution.py
@@ -144,14 +144,22 @@
     out[1] = flip[...] + TIME_STEP * other[...]
 
 
-def cores_body(keep, taken, give_half, keep_half):
+def cores_body(keep, taken, give_near, give_far, keep_half):
+    keep_half[...] = keep[0:4] + taken[0:4]
+    give_near[...] = keep[4:6] + taken[4:6]
+    give_far[...] = keep[6:8] + taken[6:8]
+
+
+def whole_cores_body(keep, taken, give_half, keep_half):
     keep_half[...] = keep[0:4] + taken[0:4]
     give_half[...] = keep[4:8] + taken[4:8]
 
 
-def halves_body(keep, got, *outs):
+def halves_body(keep, *refs):
+    outs = refs[-4:]
+    got = [ref.at[i] for ref in refs[:-4] for i in range(ref.shape[0])]
     for i in range(4):
-        outs[i][...] = keep[i] + got[i]
+        outs[i][...] = keep[i] + got[i][...]
 
 
 def ghost_body(own, a, b, c, out):
@@ -174,61 +182,91 @@
     return jnp.where(table[5] == 1, total, 0.0)
 
 
-def below_kernel(table, px, py, speed, field, tops, *refs):
-    out, picked, sems = refs[-3:]
+def ends_copies(field, speed, ends, sems):
+    return [
+        pltpu.make_async_copy(field.at[0], ends.at[0], sems.at[4]),
+        pltpu.make_async_copy(speed.at[0], ends.at[1], sems.at[5]),
+    ]
+
+
+def below_value(table, px, py, field, speed, tops, picked, ends, sems):
+    copies = ends_copies(field, speed, ends, sems)
+    for copy in copies:
+        copy.start()
     total = from_below(table, px, py, tops, picked, sems)
-    out[...] = field[...] + TIME_STEP * (total + speed[...] * total)
-
-
-def below_update(table, px, py, speed, plane, tops, *earlier):
+    for copy in copies:
+        copy.wait()
+    return ends[0] + TIME_STEP * (total + ends[1] * total)
+
+
+def below_kernel(table, px, py, field, speed, tops, *refs):
+    out, *scratch = refs[-4:]
+    out[...] = below_value(table, px, py, field, speed, tops, *scratch)
+
+
+BELOW_SCRATCH = [
+    pltpu.VMEM((4, W, W), F32),
+    pltpu.VMEM((2, W, W), F32),
+    pltpu.SemaphoreType.DMA((7,)),
+]
+
+
+def below_update(table, px, py, field, speed, tops, *earlier):
     return pl.pallas_call(
         below_kernel,
         out_shape=planes(),
-        in_specs=[SMEM_SPEC] + [VMEM_SPEC] * 4 + [pl.BlockSpec(memory_space=pltpu.HBM)] + [ANY_SPEC] * len(earlier),
+        in_specs=[SMEM_SPEC] + [VMEM_SPEC] * 2 + [ANY_SPEC] * (3 + len(earlier)),
         out_specs=VMEM_SPEC,
-        scratch_shapes=[pltpu.VMEM((4, W, W), F32), pltpu.SemaphoreType.DMA((4,))],
+        scratch_shapes=BELOW_SCRATCH,
         compiler_params=pltpu.CompilerParams(vmem_limit_bytes=50 * MIB),
         cost_estimate=SMALL,
         name="below",
-    )(table, px, py, speed, plane, tops, *earlier)
-
-
-def ends_kernel(table, px, py, speed, ghost, tops, field, out, picked, ends, sems):
-    def end(i, back):
-        plane = (0, NZ - 1)[i]
-        if back:
-            return pltpu.make_async_copy(ends.at[i], out.at[plane], sems.at[4 + i])
-        return pltpu.make_async_copy(field.at[plane], ends.at[i], sems.at[4 + i])
-
-    end(0, False).start()
-    end(1, False).start()
-    end(1, False).wait()
-    ends[1] = ends[1] + TIME_STEP * jnp.where(table[6] == 1, AMBIENT, ghost[...])
-    end(1, True).start()
-    total = from_below(table, px, py, tops, picked, sems)
-    end(0, False).wait()
-    ends[0] = ends[0] + TIME_STEP * (total + speed[...] * total)
-    end(0, True).start()
-    end(1, True).wait()
-    end(0, True).wait()
-
-
-def fix_ends(table, px, py, speed, ghost, tops, field):
-    return pl.pallas_call(
-        ends_kernel,
+    )(table, px, py, field, speed, tops, *earlier)
+
+
+def fix_bottom_kernel(table, px, py, speed, tops, field, out, picked, ends, sems):
+    ends[0] = below_value(table, px, py, field, speed, tops, picked, ends, sems)
+    copy = pltpu.make_async_copy(ends.at[0], out.at[0], sems.at[6])
+    copy.start()
+    copy.wait()
+
+
+def fix_bottom(table, px, py, speed, tops, field):
+    return pl.pallas_call(
+        fix_bottom_kernel,
         out_shape=planes(NZ),
-        in_specs=[SMEM_SPEC] + [VMEM_SPEC] * 4 + [pl.BlockSpec(memory_space=pltpu.HBM)] * 2,
+        in_specs=[SMEM_SPEC] + [VMEM_SPEC] * 2 + [ANY_SPEC] * 2 + [pl.BlockSpec(memory_space=pltpu.HBM)],
         out_specs=pl.BlockSpec(memory_space=pltpu.HBM),
-        scratch_shapes=[
-            pltpu.VMEM((4, W, W), F32),
-            pltpu.VMEM((2, W, W), F32),
-            pltpu.SemaphoreType.DMA((6,)),
-        ],
-        input_output_aliases={6: 0},
+        scratch_shapes=BELOW_SCRATCH,
+        input_output_aliases={5: 0},
         compiler_params=pltpu.CompilerParams(vmem_limit_bytes=50 * MIB),
         cost_estimate=SMALL,
-        name="fix_ends",
-    )(table, px, py, speed, ghost, tops, field)
+        name="fix_bottom",
+    )(table, px, py, speed, tops, field)
+
+
+def fix_top_kernel(table, ghost, field, out, plane, sems):
+    fetch = pltpu.make_async_copy(field.at[NZ - 1], plane, sems.at[0])
+    fetch.start()
+    fetch.wait()
+    plane[...] = plane[...] + TIME_STEP * jnp.where(table[6] == 1, AMBIENT, ghost[...])
+    store = pltpu.make_async_copy(plane, out.at[NZ - 1], sems.at[1])
+    store.start()
+    store.wait()
+
+
+def fix_top(table, ghost, field):
+    return pl.pallas_call(
+        fix_top_kernel,
+        out_shape=planes(NZ),
+        in_specs=[SMEM_SPEC, VMEM_SPEC, pl.BlockSpec(memory_space=pltpu.HBM)],
+        out_specs=pl.BlockSpec(memory_space=pltpu.HBM),
+        scratch_shapes=[pltpu.VMEM((W, W), F32), pltpu.SemaphoreType.DMA((2,))],
+        input_output_aliases={2: 0},
+        compiler_params=pltpu.CompilerParams(vmem_limit_bytes=8 * MIB),
+        cost_estimate=SMALL,
+        name="fix_top",
+    )(table, ghost, field)
 
 
 def rims_kernel(field, bottom, top, *refs):
@@ -259,7 +297,12 @@
     )(field, bottom, top, *earlier)
 
 
-def stencil_kernel(inverse, inside, field, bottom, top, speed, inlets, x_low, x_high, y_low, y_high, out, mark, low, high):
+def stencil_kernel(inverse, inside, field, bottom, top, speed, inlets, x_low, x_high, y_low, y_high, out, mark, low, high, fast, sems):
+    def fetch(z):
+        return pltpu.make_async_copy(speed.at[z], fast.at[z], sems.at[z])
+
+    for z in range(NZ):
+        fetch(z).start()
     mark[...] = jnp.zeros_like(mark)
     pad = jnp.zeros((128 - NZ, W), F32)
     low[...] = jnp.concatenate([jnp.where(inside[2] == 1, y_low[...], 0.0), pad], axis=0).T
@@ -267,6 +310,7 @@
     scale = inverse[0]
 
     def update(z, here, under, over):
+        fetch(z).wait()
         pick = lax.broadcasted_iota(jnp.int32, (W, 128), 1) == z
         col_low = jnp.sum(jnp.where(pick, low[...], 0.0), axis=1, keepdims=True)
         col_high = jnp.sum(jnp.where(pick, high[...], 0.0), axis=1, keepdims=True)
@@ -279,7 +323,7 @@
         beside = beside + jnp.where(lane == 0, col_low, pltpu.roll(here, 1, 1))
         beside = beside + jnp.where(lane == W - 1, col_high, pltpu.roll(here, W - 1, 1))
         lapl = (beside - 4.0 * here) * scale
-        change = lapl + over + under - 2.0 * here - speed[z] * (here - under)
+        change = lapl + over + under - 2.0 * here - fast[z] * (here - under)
         return here + TIME_STEP * change
 
     zero = jnp.zeros((W, W), F32)
@@ -301,9 +345,10 @@
     return pl.pallas_call(
         stencil_kernel,
         out_shape=(planes(NZ), MARK),
-        in_specs=[SMEM_SPEC] * 2 + [VMEM_SPEC] * 9,
+        in_specs=[SMEM_SPEC] * 2 + [VMEM_SPEC] * 3 + [ANY_SPEC] + [VMEM_SPEC] * 5,
         out_specs=[VMEM_SPEC] * 2,
-        scratch_shapes=[pltpu.VMEM((W, 128), F32)] * 2,
+        scratch_shapes=[pltpu.VMEM((W, 128), F32)] * 2
+        + [pltpu.VMEM((NZ, W, W), F32), pltpu.SemaphoreType.DMA((NZ,))],
         compiler_params=pltpu.CompilerParams(vmem_limit_bytes=24 * MIB),
         cost_estimate=SMALL,
         name="stencil",
@@ -329,9 +374,10 @@
     return lax.all_gather(pair, "tile", axis_index_groups=BY_HALF, axis=0, tiled=True)
 
 
-def reduce_cores(give, keep, *earlier):
+def reduce_cores(give, keep, body, *counts, earlier=()):
     taken = lax.ppermute(give, "tile", OTHER_CORE)
-    return small_kernel(cores_body, "cores_sum", (planes(4), planes(4)), (keep, taken), earlier)
+    shapes = tuple(planes(count) for count in (*counts, 4))
+    return small_kernel(body, "cores_sum", shapes, (keep, taken), earlier)
 
 
 def reduce_halves(give):
@@ -339,7 +385,7 @@
 
 
 def reduce_ring(keep, got, *earlier):
-    own, *others = small_kernel(halves_body, "halves_sum", (planes(),) * 4, (keep, got), earlier)
+    own, *others = small_kernel(halves_body, "halves_sum", (planes(),) * 4, (keep, *got), earlier)
     return own, *(send_y(part, step) for part, step in zip(others, (1, 2, -1)))
 
 
@@ -360,34 +406,37 @@
     is_top = lift == LIFTS - 1
     table = jnp.concatenate([sources.reshape(4) & (TILES - 1), tile[None], has_below[None], is_top[None].astype(jnp.int32)])
     inside = jnp.stack([tile >= TCOL, tile < TILES - TCOL, tile % TCOL > 0, tile % TCOL < TCOL - 1]).astype(jnp.int32)
-    speed_low = speed[0]
     bottom, top = field[0], field[NZ - 1]
 
     mine, flip = climb(top)
-    give, keep, mark = pieces_of(table, px, py, bottom)
-    tops = gather_pair(small_kernel(pair_body, "pair", planes(2), (mine, flip), (mark,)))
-    give, keep = reduce_cores(give, keep)
+    rims = rims_of(field, bottom, top)
+    halos = exchange_rims(rims)
+    pair = small_kernel(pair_body, "pair", planes(2), (mine, flip), (rims[0],))
+    tops = gather_pair(pair)
+    give, keep, mark = pieces_of(table, px, py, bottom, pair)
+    give, keep = reduce_cores(give, keep, whole_cores_body, 4, earlier=halos)
     got = reduce_halves(give)
-    halos = exchange_rims(rims_of(field, bottom, top, give))
     field, mark = stencil(inverse, inside, field, bottom, top, speed, inlets, halos)
-    low, high = field[0], field[NZ - 1]
+    high = field[NZ - 1]
     mine, flip = climb(high)
-    parts = reduce_ring(keep, got, mark)
-    bottom = below_update(table, px, py, speed_low, low, tops, parts[0], mine, flip)
-    ghost = ghost_sum(parts)
-    other_ghost = lax.ppermute(ghost, "tile", OTHER_HALF)
+    parts = reduce_ring(keep, [got], mark)
+    bottom = below_update(table, px, py, field, speed, tops, parts[0])
+    give, keep, mark = pieces_of(table, px, py, bottom, mine, flip)
+    give_near, give_far, keep = reduce_cores(give, keep, cores_body, 2, 2)
+    ghost = ghost_sum(parts, give_near, mine, flip)
+    got_near = reduce_halves(give_near)
+    other_ghost = reduce_halves(ghost)
     ghost_above = jnp.where(is_top, AMBIENT, send_lift(ghost, -1, False))
-    give, keep, mark = pieces_of(table, px, py, bottom, ghost)
-    pair = small_kernel(new_pair_body, "new_pair", planes(2), (mine, flip, ghost, other_ghost), (mark,))
+    pair = small_kernel(new_pair_body, "new_pair", planes(2), (mine, flip, ghost, other_ghost), (got_near,))
     tops = gather_pair(pair)
     top = high + TIME_STEP * ghost_above
-    give, keep = reduce_cores(give, keep, top)
-    got = reduce_halves(give)
-    halos = exchange_rims(rims_of(field, bottom, top, give))
+    got_far = reduce_halves(give_far)
+    halos = exchange_rims(rims_of(field, bottom, top))
     field, mark = stencil(inverse, inside, field, bottom, top, speed, inlets, halos)
-    parts = reduce_ring(keep, got, *halos)
+    parts = reduce_ring(keep, [got_near, got_far], *halos)
     ghost = send_lift(ghost_sum(parts, mark), -1, False)
-    field = fix_ends(table, px, py, speed_low, ghost, tops, field)
+    field = fix_bottom(table, px, py, speed, tops, field)
+    field = fix_top(table, ghost, field)
     return field.reshape(1, NZ, 1, W, W)
 
 

time: 184 us -> 183 us (level)
  Pallas kernels: 41.3 us -> 43.8 us
  starting transfers between devices: 48.5 us -> 46.2 us
    ppermute x2, waiting for transfers between devices: 32.7 us -> 0.01 us  [exchange_rims(): x_low = lax.ppermute(row_high, 'tile', up)]
    ppermute x2 -> x4, waiting for transfers between devices: 0.01 us -> 16.5 us  [reduce_halves(): return lax.ppermute(give, 'tile', OTHER_HALF)]
    ppermute x6, waiting for transfers between devices: 10.9 us -> 25.1 us  [send_lift(): return lax.ppermute(value, ('lift', 'tile'), to_lift(steps, flip))]
    ppermute x6, starting transfers between devices: 7.27 us -> 14.8 us  [send_y(): return lax.ppermute(value, 'tile', along_y(steps))]
    ppermute x6, starting transfers between devices: 17 us -> 10.9 us  [send_lift(): return lax.ppermute(value, ('lift', 'tile'), to_lift(steps, flip))]
    ppermute x2, waiting for transfers between devices: 4.36 us -> 0.01 us  [reduce_cores(): taken = lax.ppermute(give, 'tile', OTHER_CORE)]
    ppermute x1 -> x0, starting transfers between devices: 3.14 us -> none  [on_device(): other_ghost = lax.ppermute(ghost, 'tile', OTHER_HALF)]
    ppermute x2, waiting for transfers between devices: 0.01 us -> 2.36 us  [exchange_rims(): x_high = lax.ppermute(row_low, 'tile', [(d, s) for s, d in up])]
  transfers between devices with their start and end apart: 27 -> 28, of which waited for: 10 -> 11; matrix products, arithmetic and copies ran while one was open for 1% -> 1% of each run, Pallas kernels for 18% -> 20%
where the time goes in v7:
time: 183 us; the launch traced here: 180 us
  waiting for transfers between devices  53.8 us (29%)
  starting transfers between devices  46.2 us (25%)
  Pallas kernels  43.8 us (24%)
  local copies, waits for them, and re-layouts  20.8 us (11%)
  between operations  14.4 us (8%)
    ppermute x6, waiting for transfers between devices, send_lift(): return lax.ppermute(value, ('lift', 'tile'), to_lift(steps, flip))  25.1 us
    unnamed x52, local copies, waits for them, and re-layouts  18.9 us
    pallas_call x2, Pallas kernels, stencil(): pl.pallas_call(stencil_kernel, out_shape=(planes(NZ), MARK), in_specs=[SM...  17.6 us
    ppermute x4, waiting for transfers between devices, reduce_halves(): return lax.ppermute(give, 'tile', OTHER_HALF)  16.5 us
    ppermute x6, starting transfers between devices, send_y(): return lax.ppermute(value, 'tile', along_y(steps))  14.8 us
    ppermute x6, starting transfers between devices, send_lift(): return lax.ppermute(value, ('lift', 'tile'), to_lift(steps, flip))  10.9 us
    ppermute x6, waiting for transfers between devices, send_y(): return lax.ppermute(value, 'tile', along_y(steps))  8.36 us
    pallas_call x2, Pallas kernels, pieces_of(): pl.pallas_call(pieces_kernel, out_shape=(planes(8), planes(8), MARK), in_...  8.23 us
  transfers between devices with their start and end apart: 28, of which 11 were waited for; matrix products, arithmetic and copies ran while one was open for 1% of the time, Pallas kernels for 20%

profile of v7, /device:TPU:6, one launch (start us, length us, event | category | flops | bytes accessed | tf_op | source)
XLA Modules:
  0.0 180.0 jit_solution(16962748401008625532)
XLA Ops:
  7.7 1.9 %collective-permute-start.5 = (f32[256,256]{1,0:T(8,128)S(1)}, f32[256,256]{1,0:T(8,128)S(1)}, u32[]{:S(2)}, u32[]{:S(2)}) collective-permute-start(f32[256,256]{1,0:T(8,128)S(1)} %get-tuple-element.63.top), channel_id=1, source_target_pairs={{0,24},{1,25},{2,26},{3,27},{4,28},{5,29},{6,30},{7,31},{8,16},{9,... | collective-permute-start | bytes 786440 | tf_op jit(solution)/shard_map/ppermute | solution.py:52
  10.5 2.2 %copy-done.5 = f32[1,16,1,256,256]{4,3,2,1,0:T(8,128)S(1)} copy-done((f32[1,16,1,256,256]{4,3,2,1,0:T(8,128)S(1)}, f32[1,16,1,256,256]{4,3,2,1,0:T(8,128)}, u32[]{:S(2)}) %copy-start.5) | copy-done | bytes 4194328
  14.0 3.1 %collective-permute-done.5.refs_1_ = f32[256,256]{1,0:T(8,128)S(1)} collective-permute-done((f32[256,256]{1,0:T(8,128)S(1)}, f32[256,256]{1,0:T(8,128)S(1)}, u32[]{:S(2)}, u32[]{:S(2)}) %collective-permute-start.5) | collective-permute-done | bytes 262176 | tf_op jit(solution)/shard_map/ppermute | solution.py:52
  17.0 3.4 %collective-permute-done.4.refs_0_ = f32[256,256]{1,0:T(8,128)S(1)} collective-permute-done((f32[256,256]{1,0:T(8,128)S(1)}, f32[256,256]{1,0:T(8,128)S(1)}, u32[]{:S(2)}, u32[]{:S(2)}) %collective-permute-start.4) | collective-permute-done | bytes 262176 | tf_op jit(solution)/shard_map/ppermute | solution.py:52
  21.4 4.0 %pieces.2 = (f32[8,256,256]{2,1,0:T(8,128)S(1)}, f32[8,256,256]{2,1,0:T(8,128)S(1)}, f32[8,128]{1,0:T(8,128)}) custom-call(s32[7]{0:T(128)S(1)} %pad_add_fusion.table, f32[4,256,256]{2,1,0:T(8,128)S(1)} %bitcast.31, f32[4,256,256]{2,1,0:T(8,128)S(1)} %bitcast.35, f32[256,256]{1,0:T(8,128)S(1)} %get-tuple-element.64.bottom, f32[2,256,256]{2,1,0:T(8,128)} %pair.1.refs_0_), custom_call_target="tpu_custom_call" | custom-call | flops 1024 | bytes 1024 | tf_op jit(solution)/shard_map/pieces/pallas_call | solution.py:109
  25.5 3.2 %collective-permute-start = (f32[16,256]{1,0:T(8,128)S(1)}, f32[16,256]{1,0:T(8,128)S(1)}, u32[]{:S(2)}, u32[]{:S(2)}) collective-permute-start(f32[16,256]{1,0:T(8,128)S(1)} %get-tuple-element.34), channel_id=1, source_target_pairs={{0,4},{1,5},{2,6},{3,7},{4,8},{5,9},{6,10},{7,11},{8,12},{9,13},{1... | collective-permute-start | bytes 49160 | tf_op jit(solution)/shard_map/ppermute | solution.py:362
  30.4 3.0 %collective-permute-start.1 = (f32[16,256]{1,0:T(8,128)S(1)}, f32[16,256]{1,0:T(8,128)S(1)}, u32[]{:S(2)}, u32[]{:S(2)}) collective-permute-start(f32[16,256]{1,0:T(8,128)S(1)} %get-tuple-element.35.refs_2_), channel_id=1, source_target_pairs={{4,0},{5,1},{6,2},{7,3},{8,4},{9,5},{10,6},{11,7},{12,8},{13,9},{1... | collective-permute-start | bytes 49160 | tf_op jit(solution)/shard_map/ppermute | solution.py:363
  33.4 2.2 %collective-permute-done.1.x_high.refs_3_ = f32[16,256]{1,0:T(8,128)S(1)} collective-permute-done((f32[16,256]{1,0:T(8,128)S(1)}, f32[16,256]{1,0:T(8,128)S(1)}, u32[]{:S(2)}, u32[]{:S(2)}) %collective-permute-start.1) | collective-permute-done | bytes 16416 | tf_op jit(solution)/shard_map/ppermute | solution.py:363
  37.9 3.0 %collective-permute-start.7 = (f32[4,256,256]{2,1,0:T(8,128)}, f32[4,256,256]{2,1,0:T(8,128)}, u32[]{:S(2)}, u32[]{:S(2)}) collective-permute-start(f32[4,256,256]{2,1,0:T(8,128)} %get-tuple-element.42), channel_id=1, source_target_pairs={{0,8},{1,9},{2,10},{3,11},{4,12},{5,13},{6,14},{7,15},{8,0},{9,1},... | collective-permute-start | bytes 3145736 | tf_op jit(solution)/shard_map/ppermute | solution.py:384
  41.7 2.3 %copy-done = f32[1,16,1,256,256]{4,3,2,1,0:T(8,128)S(1)} copy-done((f32[1,16,1,256,256]{4,3,2,1,0:T(8,128)S(1)}, f32[1,16,1,256,256]{4,3,2,1,0:T(8,128)}, u32[]{:S(2)}) %copy-start) | copy-done | bytes 4194328
  44.0 2.3 %copy-done.6 = f32[1,16,1,256,256]{4,3,2,1,0:T(8,128)S(1)} copy-done((f32[1,16,1,256,256]{4,3,2,1,0:T(8,128)S(1)}, f32[1,16,1,256,256]{4,3,2,1,0:T(8,128)}, u32[]{:S(2)}) %copy-start.6) | copy-done | bytes 4194328
  46.2 7.8 %stencil.2 = (f32[16,256,256]{2,1,0:T(8,128)S(1)}, f32[8,128]{1,0:T(8,128)S(1)}) custom-call(f32[1]{0:T(128)S(6)} %div.3.inverse, s32[4]{0:T(128)S(1)} %add_convert_fusion.inside, f32[16,256,256]{2,1,0:T(8,128)S(1)} %bitcast.30, f32[256,256]{1,0:T(8,128)S(1)} %get-tuple-element.64.bottom, f32[256,256]{1,0:T(8,128)S(1)} %get-tuple-element.63.top, ...), custom_call_target="tpu_custom_call" | custom-call | flops 1024 | bytes 1024 | tf_op jit(solution)/shard_map/stencil/pallas_call | solution.py:345
  54.0 2.0 %copy-done.2 = f32[16,256,256]{2,1,0:T(8,128)} copy-done((f32[16,256,256]{2,1,0:T(8,128)}, f32[16,256,256]{2,1,0:T(8,128)S(1)}, u32[]{:S(2)}) %copy-start.2) | copy-done | bytes 4194328
  56.8 3.8 %collective-permute-start.9 = (f32[256,256]{1,0:T(8,128)}, f32[256,256]{1,0:T(8,128)S(1)}, u32[]{:S(2)}, u32[]{:S(2)}) collective-permute-start(f32[256,256]{1,0:T(8,128)} %slice_bitcast_fusion), channel_id=1, source_target_pairs={{0,24},{1,25},{2,26},{3,27},{4,28},{5,29},{6,30},{7,31},{8,16},{9,... | collective-permute-start | bytes 786440 | tf_op jit(solution)/shard_map/ppermute | solution.py:52
  60.6 5.2 %collective-permute-done.7.refs_1_ = f32[4,256,256]{2,1,0:T(8,128)} collective-permute-done((f32[4,256,256]{2,1,0:T(8,128)}, f32[4,256,256]{2,1,0:T(8,128)}, u32[]{:S(2)}, u32[]{:S(2)}) %collective-permute-start.7) | collective-permute-done | bytes 1048608 | tf_op jit(solution)/shard_map/ppermute | solution.py:384
  69.3 3.8 %below.1.bottom = f32[256,256]{1,0:T(8,128)S(1)} custom-call(s32[7]{0:T(128)S(1)} %pad_add_fusion.table, f32[4,256,256]{2,1,0:T(8,128)S(1)} %bitcast.32, f32[4,256,256]{2,1,0:T(8,128)S(1)} %bitcast.36, f32[16,256,256]{2,1,0:T(8,128)} %copy-done.2, f32[16,256,256]{2,1,0:T(8,128)} %bitcast.25, f32[16,256,256]{2,1,0:T(8,128)} %all-gather.3.cloned.1.call-done.tops, ...), custom_call_target="tpu_custom_call" | custom-call | flops 1024 | bytes 1024 | tf_op jit(solution)/shard_map/below/pallas_call | solution.py:215
  73.2 4.2 %pieces.3 = (f32[8,256,256]{2,1,0:T(8,128)S(1)}, f32[8,256,256]{2,1,0:T(8,128)S(1)}, f32[8,128]{1,0:T(8,128)}) custom-call(s32[7]{0:T(128)S(1)} %pad_add_fusion.table, f32[4,256,256]{2,1,0:T(8,128)S(1)} %bitcast.33, f32[4,256,256]{2,1,0:T(8,128)S(1)} %bitcast.37, f32[256,256]{1,0:T(8,128)S(1)} %below.1.bottom, ...), custom_call_target="tpu_custom_call" | custom-call | flops 1024 | bytes 1024 | tf_op jit(solution)/shard_map/pieces/pallas_call | solution.py:109
  77.4 7.0 %collective-permute-start.14 = (f32[256,256]{1,0:T(8,128)S(1)}, f32[256,256]{1,0:T(8,128)S(1)}, u32[]{:S(2)}, u32[]{:S(2)}) collective-permute-start(f32[256,256]{1,0:T(8,128)S(1)} %copy-done.22), channel_id=1, source_target_pairs={{0,4},{1,5},{2,6},{3,7},{4,0},{5,1},{6,2},{7,3},{8,12},{9,13},{10,... | collective-permute-start | bytes 786440 | tf_op jit(solution)/shard_map/ppermute | solution.py:48
  90.0 6.8 %collective-permute-done.14.refs_2_ = f32[256,256]{1,0:T(8,128)S(1)} collective-permute-done((f32[256,256]{1,0:T(8,128)S(1)}, f32[256,256]{1,0:T(8,128)S(1)}, u32[]{:S(2)}, u32[]{:S(2)}) %collective-permute-start.14) | collective-permute-done | bytes 262176 | tf_op jit(solution)/shard_map/ppermute | solution.py:48
  96.9 11.3 %collective-permute-done.25.refs_3_ = f32[256,256]{1,0:T(8,128)S(1)} collective-permute-done((f32[256,256]{1,0:T(8,128)S(1)}, f32[256,256]{1,0:T(8,128)S(1)}, u32[]{:S(2)}, u32[]{:S(2)}) %collective-permute-start.25) | collective-permute-done | bytes 262176 | tf_op jit(solution)/shard_map/ppermute | solution.py:384
  110.7 4.2 %collective-permute-start.16 = (f32[256,256]{1,0:T(8,128)}, f32[256,256]{1,0:T(8,128)S(1)}, u32[]{:S(2)}, u32[]{:S(2)}) collective-permute-start(f32[256,256]{1,0:T(8,128)} %copy-done.17), channel_id=1, source_target_pairs={{0,112},{1,113},{2,114},{3,115},{4,116},{5,117},{6,118},{7,119},{8... | collective-permute-start | bytes 786440 | tf_op jit(solution)/shard_map/ppermute | solution.py:52
  114.9 16.0 %collective-permute-done.16 = f32[256,256]{1,0:T(8,128)S(1)} collective-permute-done((f32[256,256]{1,0:T(8,128)}, f32[256,256]{1,0:T(8,128)S(1)}, u32[]{:S(2)}, u32[]{:S(2)}) %collective-permute-start.16) | collective-permute-done | bytes 262176 | tf_op jit(solution)/shard_map/ppermute | solution.py:52
  132.0 2.3 %copy-done.3 = f32[16,256,256]{2,1,0:T(8,128)S(1)} copy-done((f32[16,256,256]{2,1,0:T(8,128)S(1)}, f32[16,256,256]{2,1,0:T(8,128)}, u32[]{:S(2)}) %copy-start.3) | copy-done | bytes 4194328
  135.5 2.6 %collective-permute-start.17 = (f32[16,256]{1,0:T(8,128)S(1)}, f32[16,256]{1,0:T(8,128)S(1)}, u32[]{:S(2)}, u32[]{:S(2)}) collective-permute-start(f32[16,256]{1,0:T(8,128)S(1)} %get-tuple-element.53), channel_id=1, source_target_pairs={{0,4},{1,5},{2,6},{3,7},{4,8},{5,9},{6,10},{7,11},{8,12},{9,13},{1... | collective-permute-start | bytes 49160 | tf_op jit(solution)/shard_map/ppermute | solution.py:362
  138.1 3.4 %collective-permute-start.18 = (f32[16,256]{1,0:T(8,128)S(1)}, f32[16,256]{1,0:T(8,128)S(1)}, u32[]{:S(2)}, u32[]{:S(2)}) collective-permute-start(f32[16,256]{1,0:T(8,128)S(1)} %get-tuple-element.54), channel_id=1, source_target_pairs={{4,0},{5,1},{6,2},{7,3},{8,4},{9,5},{10,6},{11,7},{12,8},{13,9},{1... | collective-permute-start | bytes 49160 | tf_op jit(solution)/shard_map/ppermute | solution.py:363
  141.5 1.7 collective-permute-start.20
  145.9 4.6 %collective-permute-start.22 = (f32[256,256]{1,0:T(8,128)S(1)}, f32[256,256]{1,0:T(8,128)S(1)}, u32[]{:S(2)}, u32[]{:S(2)}) collective-permute-start(f32[256,256]{1,0:T(8,128)S(1)} %get-tuple-element.59), channel_id=1, source_target_pairs={{0,4},{1,5},{2,6},{3,7},{4,0},{5,1},{6,2},{7,3},{8,12},{9,13},{10,... | collective-permute-start | bytes 786440 | tf_op jit(solution)/shard_map/ppermute | solution.py:48
  151.5 2.2 %copy-done.4 = f32[16,256,256]{2,1,0:T(8,128)S(1)} copy-done((f32[16,256,256]{2,1,0:T(8,128)S(1)}, f32[16,256,256]{2,1,0:T(8,128)}, u32[]{:S(2)}) %copy-start.4) | copy-done | bytes 4194328
  153.7 9.8 %stencil.3 = (f32[16,256,256]{2,1,0:T(8,128)}, f32[8,128]{1,0:T(8,128)S(1)}) custom-call(f32[1]{0:T(128)S(6)} %div.3.inverse, s32[4]{0:T(128)S(1)} %add_convert_fusion.inside, f32[16,256,256]{2,1,0:T(8,128)S(1)} %copy-done.4, f32[256,256]{1,0:T(8,128)S(1)} %below.1.bottom, f32[256,256]{1,0:T(8,128)S(1)} %multiply_add_fusion.top, ...), custom_call_target="tpu_custom_call" | custom-call | flops 1024 | bytes 1024 | tf_op jit(solution)/shard_map/stencil/pallas_call | solution.py:345
  163.7 4.6 %fix_bottom.1.field = f32[16,256,256]{2,1,0:T(8,128)} custom-call(s32[7]{0:T(128)S(1)} %pad_add_fusion.table, f32[4,256,256]{2,1,0:T(8,128)S(1)} %bitcast.34, f32[4,256,256]{2,1,0:T(8,128)S(1)} %bitcast.38, f32[16,256,256]{2,1,0:T(8,128)} %bitcast.26, f32[16,256,256]{2,1,0:T(8,128)} %all-gather.5.cloned.1.call-done.tops, ...), custom_call_target="tpu_custom_call", output_to_operand_aliasing={{}: (5, {})} | custom-call | flops 1024 | bytes 1024 | tf_op jit(solution)/shard_map/fix_bottom/pallas_call | solution.py:235
  168.3 2.7 %collective-permute-done.24.ghost = f32[256,256]{1,0:T(8,128)S(1)} collective-permute-done((f32[256,256]{1,0:T(8,128)S(1)}, f32[256,256]{1,0:T(8,128)S(1)}, u32[]{:S(2)}, u32[]{:S(2)}) %collective-permute-start.24) | collective-permute-done | bytes 262176 | tf_op jit(solution)/shard_map/ppermute | solution.py:52
  170.9 2.2 %fix_top.1 = f32[16,256,256]{2,1,0:T(8,128)} custom-call(s32[7]{0:T(128)S(1)} %pad_add_fusion.table, f32[256,256]{1,0:T(8,128)S(1)} %collective-permute-done.24.ghost, f32[16,256,256]{2,1,0:T(8,128)} %fix_bottom.1.field), custom_call_target="tpu_custom_call", output_to_operand_aliasing={{}: (2, {})} | custom-call | flops 1024 | bytes 1024 | tf_op jit(solution)/shard_map/fix_top/pallas_call | solution.py:259
  (101 shorter events, 26.9 us)
Async XLA Ops:
  6.5 62.7 %all-gather.3.cloned.1.call-start = ((), (), s32[]{:S(2)}) async-start(), calls=%async_computation | async-start | bytes 4718592 | tf_op jit(solution)/shard_map/all_gather | solution.py:374
  7.7 9.3 %collective-permute-start.5 = (f32[256,256]{1,0:T(8,128)S(1)}, f32[256,256]{1,0:T(8,128)S(1)}, u32[]{:S(2)}, u32[]{:S(2)}) collective-permute-start(f32[256,256]{1,0:T(8,128)S(1)} %get-tuple-element.63.top), channel_id=1, source_target_pairs={{0,24},{1,25},{2,26},{3,27},{4,28},{5,29},{6,30},{7,31},{8,16},{9,... | collective-permute-start | bytes 786440 | tf_op jit(solution)/shard_map/ppermute | solution.py:52
  9.6 10.8 %collective-permute-start.4 = (f32[256,256]{1,0:T(8,128)S(1)}, f32[256,256]{1,0:T(8,128)S(1)}, u32[]{:S(2)}, u32[]{:S(2)}) collective-permute-start(f32[256,256]{1,0:T(8,128)S(1)} %get-tuple-element.63.top), channel_id=1, source_target_pairs={{0,16},{1,17},{2,18},{3,19},{4,20},{5,21},{6,22},{7,23},{8,24},{9,... | collective-permute-start | bytes 786440 | tf_op jit(solution)/shard_map/ppermute | solution.py:52
  20.4 21.3 %copy-start.11 = (s32[1,1,256,256]{3,2,1,0:T(8,128)S(1)}, s32[1,1,256,256]{3,2,1,0:T(8,128)}, u32[]{:S(2)}) copy-start(s32[1,1,256,256]{3,2,1,0:T(8,128)} %param.10) | copy-start | bytes 786436
  21.3 142.4 %all-gather.5.cloned.1.call-start = ((), (), s32[]{:S(2)}) async-start(), calls=%async_computation.1 | async-start | bytes 4718592 | tf_op jit(solution)/shard_map/all_gather | solution.py:374
  25.5 10.2 %collective-permute-start.6 = (f32[8,256,256]{2,1,0:T(8,128)S(1)}, f32[8,256,256]{2,1,0:T(8,128)S(1)}, u32[]{:S(2)}, u32[]{:S(2)}) collective-permute-start(f32[8,256,256]{2,1,0:T(8,128)S(1)} %get-tuple-element.40), channel_id=1, source_target_pairs={{0,1},{1,0},{2,3},{3,2},{4,5},{5,4},{6,7},{7,6},{8,9},{9,8},{10,11... | collective-permute-start | bytes 6291464 | tf_op jit(solution)/shard_map/ppermute | solution.py:378
  25.5 8.0 %collective-permute-start = (f32[16,256]{1,0:T(8,128)S(1)}, f32[16,256]{1,0:T(8,128)S(1)}, u32[]{:S(2)}, u32[]{:S(2)}) collective-permute-start(f32[16,256]{1,0:T(8,128)S(1)} %get-tuple-element.34), channel_id=1, source_target_pairs={{0,4},{1,5},{2,6},{3,7},{4,8},{5,9},{6,10},{7,11},{8,12},{9,13},{1... | collective-permute-start | bytes 49160 | tf_op jit(solution)/shard_map/ppermute | solution.py:362
  28.7 4.8 %collective-permute-start.2 = (f32[16,256]{1,0:T(8,128)S(1)}, f32[16,256]{1,0:T(8,128)S(1)}, u32[]{:S(2)}, u32[]{:S(2)}) collective-permute-start(f32[16,256]{1,0:T(8,128)S(1)} %get-tuple-element.36), channel_id=1, source_target_pairs={{0,1},{1,2},{2,3},{3,0},{4,5},{5,6},{6,7},{7,4},{8,9},{9,10},{10,1... | collective-permute-start | bytes 49160 | tf_op jit(solution)/shard_map/ppermute | solution.py:364
  28.9 4.5 %collective-permute-start.3 = (f32[16,256]{1,0:T(8,128)S(1)}, f32[16,256]{1,0:T(8,128)S(1)}, u32[]{:S(2)}, u32[]{:S(2)}) collective-permute-start(f32[16,256]{1,0:T(8,128)S(1)} %get-tuple-element.37), channel_id=1, source_target_pairs={{1,0},{2,1},{3,2},{0,3},{5,4},{6,5},{7,6},{4,7},{9,8},{10,9},{11,1... | collective-permute-start | bytes 49160 | tf_op jit(solution)/shard_map/ppermute | solution.py:365
  30.4 5.2 %collective-permute-start.1 = (f32[16,256]{1,0:T(8,128)S(1)}, f32[16,256]{1,0:T(8,128)S(1)}, u32[]{:S(2)}, u32[]{:S(2)}) collective-permute-start(f32[16,256]{1,0:T(8,128)S(1)} %get-tuple-element.35.refs_2_), channel_id=1, source_target_pairs={{4,0},{5,1},{6,2},{7,3},{8,4},{9,5},{10,6},{11,7},{12,8},{13,9},{1... | collective-permute-start | bytes 49160 | tf_op jit(solution)/shard_map/ppermute | solution.py:363
  37.9 27.9 %collective-permute-start.7 = (f32[4,256,256]{2,1,0:T(8,128)}, f32[4,256,256]{2,1,0:T(8,128)}, u32[]{:S(2)}, u32[]{:S(2)}) collective-permute-start(f32[4,256,256]{2,1,0:T(8,128)} %get-tuple-element.42), channel_id=1, source_target_pairs={{0,8},{1,9},{2,10},{3,11},{4,12},{5,13},{6,14},{7,15},{8,0},{9,1},... | collective-permute-start | bytes 3145736 | tf_op jit(solution)/shard_map/ppermute | solution.py:384
  56.8 16.4 %collective-permute-start.9 = (f32[256,256]{1,0:T(8,128)}, f32[256,256]{1,0:T(8,128)S(1)}, u32[]{:S(2)}, u32[]{:S(2)}) collective-permute-start(f32[256,256]{1,0:T(8,128)} %slice_bitcast_fusion), channel_id=1, source_target_pairs={{0,24},{1,25},{2,26},{3,27},{4,28},{5,29},{6,30},{7,31},{8,16},{9,... | collective-permute-start | bytes 786440 | tf_op jit(solution)/shard_map/ppermute | solution.py:52
  60.6 12.6 %collective-permute-start.8 = (f32[256,256]{1,0:T(8,128)}, f32[256,256]{1,0:T(8,128)S(1)}, u32[]{:S(2)}, u32[]{:S(2)}) collective-permute-start(f32[256,256]{1,0:T(8,128)} %slice_bitcast_fusion), channel_id=1, source_target_pairs={{0,16},{1,17},{2,18},{3,19},{4,20},{5,21},{6,22},{7,23},{8,24},{9,... | collective-permute-start | bytes 786440 | tf_op jit(solution)/shard_map/ppermute | solution.py:52
  73.2 23.6 %copy-start.10 = (f32[256,256]{1,0:T(8,128)S(1)}, f32[256,256]{1,0:T(8,128)}, u32[]{:S(2)}) copy-start(f32[256,256]{1,0:T(8,128)} %copy-done.9) | copy-start | bytes 786436
  77.4 8.2 %collective-permute-start.10 = (f32[8,256,256]{2,1,0:T(8,128)S(1)}, f32[8,256,256]{2,1,0:T(8,128)S(1)}, u32[]{:S(2)}, u32[]{:S(2)}) collective-permute-start(f32[8,256,256]{2,1,0:T(8,128)S(1)} %get-tuple-element.46), channel_id=1, source_target_pairs={{0,1},{1,0},{2,3},{3,2},{4,5},{5,4},{6,7},{7,6},{8,9},{9,8},{10,11... | collective-permute-start | bytes 6291464 | tf_op jit(solution)/shard_map/ppermute | solution.py:378
  77.4 12.5 %collective-permute-start.13 = (f32[256,256]{1,0:T(8,128)S(1)}, f32[256,256]{1,0:T(8,128)S(1)}, u32[]{:S(2)}, u32[]{:S(2)}) collective-permute-start(f32[256,256]{1,0:T(8,128)S(1)} %copy-done.24), channel_id=1, source_target_pairs={{0,2},{1,3},{2,4},{3,5},{4,6},{5,7},{6,0},{7,1},{8,10},{9,11},{10,... | collective-permute-start | bytes 786440 | tf_op jit(solution)/shard_map/ppermute | solution.py:48
  77.4 19.3 %collective-permute-start.14 = (f32[256,256]{1,0:T(8,128)S(1)}, f32[256,256]{1,0:T(8,128)S(1)}, u32[]{:S(2)}, u32[]{:S(2)}) collective-permute-start(f32[256,256]{1,0:T(8,128)S(1)} %copy-done.22), channel_id=1, source_target_pairs={{0,4},{1,5},{2,6},{3,7},{4,0},{5,1},{6,2},{7,3},{8,12},{9,13},{10,... | collective-permute-start | bytes 786440 | tf_op jit(solution)/shard_map/ppermute | solution.py:48
  84.4 12.3 %collective-permute-start.15 = (f32[256,256]{1,0:T(8,128)S(1)}, f32[256,256]{1,0:T(8,128)S(1)}, u32[]{:S(2)}, u32[]{:S(2)}) collective-permute-start(f32[256,256]{1,0:T(8,128)S(1)} %copy-done.20), channel_id=1, source_target_pairs={{0,6},{1,7},{2,0},{3,1},{4,2},{5,3},{6,4},{7,5},{8,14},{9,15},{10,... | collective-permute-start | bytes 786440 | tf_op jit(solution)/shard_map/ppermute | solution.py:48
  87.6 20.6 %collective-permute-start.11 = (f32[2,256,256]{2,1,0:T(8,128)S(1)}, f32[2,256,256]{2,1,0:T(8,128)S(1)}, u32[]{:S(2)}, u32[]{:S(2)}) collective-permute-start(f32[2,256,256]{2,1,0:T(8,128)S(1)} %get-tuple-element.48.refs_4_), channel_id=1, source_target_pairs={{0,8},{1,9},{2,10},{3,11},{4,12},{5,13},{6,14},{7,15},{8,0},{9,1},... | collective-permute-start | bytes 1572872 | tf_op jit(solution)/shard_map/ppermute | solution.py:384
  96.8 11.4 %collective-permute-start.25 = (f32[256,256]{1,0:T(8,128)S(1)}, f32[256,256]{1,0:T(8,128)S(1)}, u32[]{:S(2)}, u32[]{:S(2)}) collective-permute-start(f32[256,256]{1,0:T(8,128)S(1)} %ghost_sum.2.refs_2_), channel_id=1, source_target_pairs={{0,8},{1,9},{2,10},{3,11},{4,12},{5,13},{6,14},{7,15},{8,0},{9,1},... | collective-permute-start | bytes 786440 | tf_op jit(solution)/shard_map/ppermute | solution.py:384
  109.8 41.7 %copy-start.12 = (s32[1,1,256,256]{3,2,1,0:T(8,128)S(1)}, s32[1,1,256,256]{3,2,1,0:T(8,128)}, u32[]{:S(2)}) copy-start(s32[1,1,256,256]{3,2,1,0:T(8,128)} %param.10) | copy-start | bytes 786436
  109.8 41.7 %copy-start.1 = (f32[1,16,1,256,256]{4,3,2,1,0:T(8,128)S(1)}, f32[1,16,1,256,256]{4,3,2,1,0:T(8,128)}, u32[]{:S(2)}) copy-start(f32[1,16,1,256,256]{4,3,2,1,0:T(8,128)} %param.8) | copy-start | bytes 12582916
  109.8 34.9 %collective-permute-start.12 = (f32[2,256,256]{2,1,0:T(8,128)}, f32[2,256,256]{2,1,0:T(8,128)S(1)}, u32[]{:S(2)}, u32[]{:S(2)}) collective-permute-start(f32[2,256,256]{2,1,0:T(8,128)} %copy-done.18), channel_id=1, source_target_pairs={{0,8},{1,9},{2,10},{3,11},{4,12},{5,13},{6,14},{7,15},{8,0},{9,1},... | collective-permute-start | bytes 1572872 | tf_op jit(solution)/shard_map/ppermute | solution.py:384
  110.7 20.2 %collective-permute-start.16 = (f32[256,256]{1,0:T(8,128)}, f32[256,256]{1,0:T(8,128)S(1)}, u32[]{:S(2)}, u32[]{:S(2)}) collective-permute-start(f32[256,256]{1,0:T(8,128)} %copy-done.17), channel_id=1, source_target_pairs={{0,112},{1,113},{2,114},{3,115},{4,116},{5,117},{6,118},{7,119},{8... | collective-permute-start | bytes 786440 | tf_op jit(solution)/shard_map/ppermute | solution.py:52
  135.5 7.7 %collective-permute-start.17 = (f32[16,256]{1,0:T(8,128)S(1)}, f32[16,256]{1,0:T(8,128)S(1)}, u32[]{:S(2)}, u32[]{:S(2)}) collective-permute-start(f32[16,256]{1,0:T(8,128)S(1)} %get-tuple-element.53), channel_id=1, source_target_pairs={{0,4},{1,5},{2,6},{3,7},{4,8},{5,9},{6,10},{7,11},{8,12},{9,13},{1... | collective-permute-start | bytes 49160 | tf_op jit(solution)/shard_map/ppermute | solution.py:362
  138.1 5.3 %collective-permute-start.18 = (f32[16,256]{1,0:T(8,128)S(1)}, f32[16,256]{1,0:T(8,128)S(1)}, u32[]{:S(2)}, u32[]{:S(2)}) collective-permute-start(f32[16,256]{1,0:T(8,128)S(1)} %get-tuple-element.54), channel_id=1, source_target_pairs={{4,0},{5,1},{6,2},{7,3},{8,4},{9,5},{10,6},{11,7},{12,8},{13,9},{1... | collective-permute-start | bytes 49160 | tf_op jit(solution)/shard_map/ppermute | solution.py:363
  141.5 3.2 %collective-permute-start.19 = (f32[16,256]{1,0:T(8,128)S(1)}, f32[16,256]{1,0:T(8,128)S(1)}, u32[]{:S(2)}, u32[]{:S(2)}) collective-permute-start(f32[16,256]{1,0:T(8,128)S(1)} %get-tuple-element.55), channel_id=1, source_target_pairs={{0,1},{1,2},{2,3},{3,0},{4,5},{5,6},{6,7},{7,4},{8,9},{9,10},{10,1... | collective-permute-start | bytes 49160 | tf_op jit(solution)/shard_map/ppermute | solution.py:364
  141.5 3.2 %collective-permute-start.20 = (f32[16,256]{1,0:T(8,128)S(1)}, f32[16,256]{1,0:T(8,128)S(1)}, u32[]{:S(2)}, u32[]{:S(2)}) collective-permute-start(f32[16,256]{1,0:T(8,128)S(1)} %get-tuple-element.56), channel_id=1, source_target_pairs={{1,0},{2,1},{3,2},{0,3},{5,4},{6,5},{7,6},{4,7},{9,8},{10,9},{11,1... | collective-permute-start | bytes 49160 | tf_op jit(solution)/shard_map/ppermute | solution.py:365
  144.8 18.7 %collective-permute-start.21 = (f32[256,256]{1,0:T(8,128)S(1)}, f32[256,256]{1,0:T(8,128)S(1)}, u32[]{:S(2)}, u32[]{:S(2)}) collective-permute-start(f32[256,256]{1,0:T(8,128)S(1)} %get-tuple-element.58), channel_id=1, source_target_pairs={{0,2},{1,3},{2,4},{3,5},{4,6},{5,7},{6,0},{7,1},{8,10},{9,11},{10,... | collective-permute-start | bytes 786440 | tf_op jit(solution)/shard_map/ppermute | solution.py:48
  145.9 17.6 %collective-permute-start.22 = (f32[256,256]{1,0:T(8,128)S(1)}, f32[256,256]{1,0:T(8,128)S(1)}, u32[]{:S(2)}, u32[]{:S(2)}) collective-permute-start(f32[256,256]{1,0:T(8,128)S(1)} %get-tuple-element.59), channel_id=1, source_target_pairs={{0,4},{1,5},{2,6},{3,7},{4,0},{5,1},{6,2},{7,3},{8,12},{9,13},{10,... | collective-permute-start | bytes 786440 | tf_op jit(solution)/shard_map/ppermute | solution.py:48
  150.5 13.1 %collective-permute-start.23 = (f32[256,256]{1,0:T(8,128)S(1)}, f32[256,256]{1,0:T(8,128)S(1)}, u32[]{:S(2)}, u32[]{:S(2)}) collective-permute-start(f32[256,256]{1,0:T(8,128)S(1)} %get-tuple-element.60), channel_id=1, source_target_pairs={{0,6},{1,7},{2,0},{3,1},{4,2},{5,3},{6,4},{7,5},{8,14},{9,15},{10,... | collective-permute-start | bytes 786440 | tf_op jit(solution)/shard_map/ppermute | solution.py:48
  163.6 7.3 %collective-permute-start.24 = (f32[256,256]{1,0:T(8,128)S(1)}, f32[256,256]{1,0:T(8,128)S(1)}, u32[]{:S(2)}, u32[]{:S(2)}) collective-permute-start(f32[256,256]{1,0:T(8,128)S(1)} %ghost_sum.3), channel_id=1, source_target_pairs={{0,112},{1,113},{2,114},{3,115},{4,116},{5,117},{6,118},{7,119},{8... | collective-permute-start | bytes 786440 | tf_op jit(solution)/shard_map/ppermute | solution.py:52
  (22 other events, 122.7 us)
Sparse Core Ops, SparseCore 0:
  21.4 36.3 all-gather.2
  110.0 34.3 all-gather.4

commit v8 on v7

--- a/solution.py
+++ b/solution.py
@@ -409,27 +409,27 @@
     bottom, top = field[0], field[NZ - 1]
 
     mine, flip = climb(top)
-    rims = rims_of(field, bottom, top)
-    halos = exchange_rims(rims)
-    pair = small_kernel(pair_body, "pair", planes(2), (mine, flip), (rims[0],))
+    halos = exchange_rims(rims_of(field, bottom, top))
+    pair = small_kernel(pair_body, "pair", planes(2), (mine, flip), halos)
     tops = gather_pair(pair)
     give, keep, mark = pieces_of(table, px, py, bottom, pair)
-    give, keep = reduce_cores(give, keep, whole_cores_body, 4, earlier=halos)
+    give, keep = reduce_cores(give, keep, whole_cores_body, 4)
     got = reduce_halves(give)
     field, mark = stencil(inverse, inside, field, bottom, top, speed, inlets, halos)
     high = field[NZ - 1]
     mine, flip = climb(high)
     parts = reduce_ring(keep, [got], mark)
     bottom = below_update(table, px, py, field, speed, tops, parts[0])
-    give, keep, mark = pieces_of(table, px, py, bottom, mine, flip)
+    give, keep, mark = pieces_of(table, px, py, bottom, mine, flip, parts[1], parts[3])
     give_near, give_far, keep = reduce_cores(give, keep, cores_body, 2, 2)
     ghost = ghost_sum(parts, give_near, mine, flip)
     got_near = reduce_halves(give_near)
     other_ghost = reduce_halves(ghost)
-    ghost_above = jnp.where(is_top, AMBIENT, send_lift(ghost, -1, False))
-    pair = small_kernel(new_pair_body, "new_pair", planes(2), (mine, flip, ghost, other_ghost), (got_near,))
+    ghost_above = send_lift(ghost, -1, False)
+    earlier = (got_near, ghost_above)
+    pair = small_kernel(new_pair_body, "new_pair", planes(2), (mine, flip, ghost, other_ghost), earlier)
     tops = gather_pair(pair)
-    top = high + TIME_STEP * ghost_above
+    top = high + TIME_STEP * jnp.where(is_top, AMBIENT, ghost_above)
     got_far = reduce_halves(give_far)
     halos = exchange_rims(rims_of(field, bottom, top))
     field, mark = stencil(inverse, inside, field, bottom, top, speed, inlets, halos)

time: 183 us -> 175 us (0.956)
  waiting for transfers between devices: 53.8 us -> 50.3 us
  local copies, waits for them, and re-layouts: 20.8 us -> 18.3 us
    ppermute x6, waiting for transfers between devices: 25.1 us -> 13.6 us  [send_lift(): return lax.ppermute(value, ('lift', 'tile'), to_lift(steps, flip))]
    ppermute x6, waiting for transfers between devices: 8.36 us -> 14.2 us  [send_y(): return lax.ppermute(value, 'tile', along_y(steps))]
    ppermute x4, starting transfers between devices: 4.8 us -> 10.6 us  [reduce_halves(): return lax.ppermute(give, 'tile', OTHER_HALF)]
    ppermute x4, waiting for transfers between devices: 16.5 us -> 10.7 us  [reduce_halves(): return lax.ppermute(give, 'tile', OTHER_HALF)]
    ppermute x2, waiting for transfers between devices: 0.01 us -> 5.38 us  [reduce_cores(): taken = lax.ppermute(give, 'tile', OTHER_CORE)]
    ppermute x2, waiting for transfers between devices: 0.01 us -> 4.57 us  [exchange_rims(): x_low = lax.ppermute(row_high, 'tile', up)]
    ppermute x6, starting transfers between devices: 14.8 us -> 10.5 us  [send_y(): return lax.ppermute(value, 'tile', along_y(steps))]
    ppermute x6, starting transfers between devices: 10.9 us -> 8.38 us  [send_lift(): return lax.ppermute(value, ('lift', 'tile'), to_lift(steps, flip))]
  transfers between devices with their start and end apart: 28 -> 28, of which waited for: 11 -> 16; matrix products, arithmetic and copies ran while one was open for 1% -> 1% of each run, Pallas kernels for 20% -> 21%
where the time goes in v8:
time: 175 us; the launch traced here: 174 us
  waiting for transfers between devices  50.3 us (29%)
  Pallas kernels  45.3 us (26%)
  starting transfers between devices  44.4 us (25%)
  local copies, waits for them, and re-layouts  18.3 us (10%)
  between operations  14.3 us (8%)
    pallas_call x2, Pallas kernels, stencil(): pl.pallas_call(stencil_kernel, out_shape=(planes(NZ), MARK), in_specs=[SM...  17.6 us
    unnamed x48, local copies, waits for them, and re-layouts  16.4 us
    ppermute x6, waiting for transfers between devices, send_y(): return lax.ppermute(value, 'tile', along_y(steps))  14.2 us
    ppermute x6, waiting for transfers between devices, send_lift(): return lax.ppermute(value, ('lift', 'tile'), to_lift(steps, flip))  13.6 us
    ppermute x4, waiting for transfers between devices, reduce_halves(): return lax.ppermute(give, 'tile', OTHER_HALF)  10.7 us
    ppermute x4, starting transfers between devices, reduce_halves(): return lax.ppermute(give, 'tile', OTHER_HALF)  10.6 us
    ppermute x6, starting transfers between devices, send_y(): return lax.ppermute(value, 'tile', along_y(steps))  10.5 us
    ppermute x6, starting transfers between devices, send_lift(): return lax.ppermute(value, ('lift', 'tile'), to_lift(steps, flip))  8.38 us
  transfers between devices with their start and end apart: 28, of which 16 were waited for; matrix products, arithmetic and copies ran while one was open for 1% of the time, Pallas kernels for 21%

profile of v8, /device:TPU:6, one launch (start us, length us, event | category | flops | bytes accessed | tf_op | source)
XLA Modules:
  0.0 173.8 jit_solution(12020870851214712153)
XLA Ops:
  7.7 2.3 %collective-permute-start.4 = (f32[256,256]{1,0:T(8,128)S(1)}, f32[256,256]{1,0:T(8,128)S(1)}, u32[]{:S(2)}, u32[]{:S(2)}) collective-permute-start(f32[256,256]{1,0:T(8,128)S(1)} %get-tuple-element.63.top), channel_id=1, source_target_pairs={{0,16},{1,17},{2,18},{3,19},{4,20},{5,21},{6,22},{7,23},{8,24},{9,... | collective-permute-start | bytes 786440 | tf_op jit(solution)/shard_map/ppermute | solution.py:52
  11.1 2.2 %copy-done.5 = f32[1,16,1,256,256]{4,3,2,1,0:T(8,128)S(1)} copy-done((f32[1,16,1,256,256]{4,3,2,1,0:T(8,128)S(1)}, f32[1,16,1,256,256]{4,3,2,1,0:T(8,128)}, u32[]{:S(2)}) %copy-start.5) | copy-done | bytes 4194328
  14.6 3.2 %collective-permute-start = (f32[16,256]{1,0:T(8,128)S(1)}, f32[16,256]{1,0:T(8,128)S(1)}, u32[]{:S(2)}, u32[]{:S(2)}) collective-permute-start(f32[16,256]{1,0:T(8,128)S(1)} %get-tuple-element.34), channel_id=1, source_target_pairs={{0,4},{1,5},{2,6},{3,7},{4,8},{5,9},{6,10},{7,11},{8,12},{9,13},{1... | collective-permute-start | bytes 49160 | tf_op jit(solution)/shard_map/ppermute | solution.py:362
  17.8 2.7 %collective-permute-start.1 = (f32[16,256]{1,0:T(8,128)S(1)}, f32[16,256]{1,0:T(8,128)S(1)}, u32[]{:S(2)}, u32[]{:S(2)}) collective-permute-start(f32[16,256]{1,0:T(8,128)S(1)} %get-tuple-element.35), channel_id=1, source_target_pairs={{4,0},{5,1},{6,2},{7,3},{8,4},{9,5},{10,6},{11,7},{12,8},{13,9},{1... | collective-permute-start | bytes 49160 | tf_op jit(solution)/shard_map/ppermute | solution.py:363
  20.6 2.3 %collective-permute-done.x_low.refs_2_ = f32[16,256]{1,0:T(8,128)S(1)} collective-permute-done((f32[16,256]{1,0:T(8,128)S(1)}, f32[16,256]{1,0:T(8,128)S(1)}, u32[]{:S(2)}, u32[]{:S(2)}) %collective-permute-start) | collective-permute-done | bytes 16416 | tf_op jit(solution)/shard_map/ppermute | solution.py:362
  25.3 4.0 %pieces.2 = (f32[8,256,256]{2,1,0:T(8,128)S(1)}, f32[8,256,256]{2,1,0:T(8,128)S(1)}, f32[8,128]{1,0:T(8,128)}) custom-call(s32[7]{0:T(128)S(1)} %pad_add_fusion.table, f32[4,256,256]{2,1,0:T(8,128)S(1)} %bitcast.31, f32[4,256,256]{2,1,0:T(8,128)S(1)} %bitcast.35, f32[256,256]{1,0:T(8,128)S(1)} %get-tuple-element.64.bottom, f32[2,256,256]{2,1,0:T(8,128)} %pair.1.refs_0_), custom_call_target="tpu_custom_call" | custom-call | flops 1024 | bytes 1024 | tf_op jit(solution)/shard_map/pieces/pallas_call | solution.py:109
  30.6 3.8 %collective-permute-done.6.refs_1_ = f32[8,256,256]{2,1,0:T(8,128)S(1)} collective-permute-done((f32[8,256,256]{2,1,0:T(8,128)S(1)}, f32[8,256,256]{2,1,0:T(8,128)S(1)}, u32[]{:S(2)}, u32[]{:S(2)}) %collective-permute-start.6) | collective-permute-done | bytes 2097184 | tf_op jit(solution)/shard_map/ppermute | solution.py:378
  36.6 2.7 %collective-permute-start.7 = (f32[4,256,256]{2,1,0:T(8,128)}, f32[4,256,256]{2,1,0:T(8,128)}, u32[]{:S(2)}, u32[]{:S(2)}) collective-permute-start(f32[4,256,256]{2,1,0:T(8,128)} %get-tuple-element.42), channel_id=1, source_target_pairs={{0,8},{1,9},{2,10},{3,11},{4,12},{5,13},{6,14},{7,15},{8,0},{9,1},... | collective-permute-start | bytes 3145736 | tf_op jit(solution)/shard_map/ppermute | solution.py:384
  40.1 2.2 %copy-done = f32[1,16,1,256,256]{4,3,2,1,0:T(8,128)S(1)} copy-done((f32[1,16,1,256,256]{4,3,2,1,0:T(8,128)S(1)}, f32[1,16,1,256,256]{4,3,2,1,0:T(8,128)}, u32[]{:S(2)}) %copy-start) | copy-done | bytes 4194328
  42.3 2.2 %copy-done.6 = f32[1,16,1,256,256]{4,3,2,1,0:T(8,128)S(1)} copy-done((f32[1,16,1,256,256]{4,3,2,1,0:T(8,128)S(1)}, f32[1,16,1,256,256]{4,3,2,1,0:T(8,128)}, u32[]{:S(2)}) %copy-start.6) | copy-done | bytes 4194328
  44.5 7.8 %stencil.2 = (f32[16,256,256]{2,1,0:T(8,128)S(1)}, f32[8,128]{1,0:T(8,128)S(1)}) custom-call(f32[1]{0:T(128)S(6)} %div.3.inverse, s32[4]{0:T(128)S(1)} %add_convert_fusion.inside, f32[16,256,256]{2,1,0:T(8,128)S(1)} %bitcast.30, f32[256,256]{1,0:T(8,128)S(1)} %get-tuple-element.64.bottom, f32[256,256]{1,0:T(8,128)S(1)} %get-tuple-element.63.top, ...), custom_call_target="tpu_custom_call" | custom-call | flops 1024 | bytes 1024 | tf_op jit(solution)/shard_map/stencil/pallas_call | solution.py:345
  57.7 6.7 %collective-permute-done.7.refs_1_ = f32[4,256,256]{2,1,0:T(8,128)} collective-permute-done((f32[4,256,256]{2,1,0:T(8,128)}, f32[4,256,256]{2,1,0:T(8,128)}, u32[]{:S(2)}, u32[]{:S(2)}) %collective-permute-start.7) | collective-permute-done | bytes 1048608 | tf_op jit(solution)/shard_map/ppermute | solution.py:384
  64.4 2.1 %halves_sum.2 = (f32[256,256]{1,0:T(8,128)S(1)}, f32[256,256]{1,0:T(8,128)}, f32[256,256]{1,0:T(8,128)S(1)}, f32[256,256]{1,0:T(8,128)}) custom-call(f32[4,256,256]{2,1,0:T(8,128)S(1)} %copy-done.18, f32[4,256,256]{2,1,0:T(8,128)} %collective-permute-done.7.refs_1_, f32[8,128]{1,0:T(8,128)S(1)} %get-tuple-element.43.refs_2_), custom_call_target="tpu_custom_call" | custom-call | flops 1024 | bytes 1024 | tf_op jit(solution)/shard_map/halves_sum/pallas_call | solution.py:126
  68.1 2.3 %collective-permute-start.11 = (f32[256,256]{1,0:T(8,128)}, f32[256,256]{1,0:T(8,128)}, u32[]{:S(2)}, u32[]{:S(2)}) collective-permute-start(f32[256,256]{1,0:T(8,128)} %get-tuple-element.46), channel_id=1, source_target_pairs={{0,6},{1,7},{2,0},{3,1},{4,2},{5,3},{6,4},{7,5},{8,14},{9,15},{10,... | collective-permute-start | bytes 786440 | tf_op jit(solution)/shard_map/ppermute | solution.py:48
  70.5 3.8 %below.1.bottom = f32[256,256]{1,0:T(8,128)S(1)} custom-call(s32[7]{0:T(128)S(1)} %pad_add_fusion.table, f32[4,256,256]{2,1,0:T(8,128)S(1)} %bitcast.32, f32[4,256,256]{2,1,0:T(8,128)S(1)} %bitcast.36, f32[16,256,256]{2,1,0:T(8,128)} %copy-done.2, f32[16,256,256]{2,1,0:T(8,128)} %bitcast.25, f32[16,256,256]{2,1,0:T(8,128)} %all-gather.3.cloned.1.call-done.tops, ...), custom_call_target="tpu_custom_call" | custom-call | flops 1024 | bytes 1024 | tf_op jit(solution)/shard_map/below/pallas_call | solution.py:215
  75.9 4.0 %pieces.3 = (f32[8,256,256]{2,1,0:T(8,128)S(1)}, f32[8,256,256]{2,1,0:T(8,128)S(1)}, f32[8,128]{1,0:T(8,128)}) custom-call(s32[7]{0:T(128)S(1)} %pad_add_fusion.table, f32[4,256,256]{2,1,0:T(8,128)S(1)} %bitcast.33, f32[4,256,256]{2,1,0:T(8,128)S(1)} %bitcast.37, f32[256,256]{1,0:T(8,128)S(1)} %below.1.bottom, ...), custom_call_target="tpu_custom_call" | custom-call | flops 1024 | bytes 1024 | tf_op jit(solution)/shard_map/pieces/pallas_call | solution.py:109
  79.9 2.6 %collective-permute-start.15 = (f32[256,256]{1,0:T(8,128)S(1)}, f32[256,256]{1,0:T(8,128)S(1)}, u32[]{:S(2)}, u32[]{:S(2)}) collective-permute-start(f32[256,256]{1,0:T(8,128)S(1)} %copy-done.22), channel_id=1, source_target_pairs={{0,4},{1,5},{2,6},{3,7},{4,0},{5,1},{6,2},{7,3},{8,12},{9,13},{10,... | collective-permute-start | bytes 786440 | tf_op jit(solution)/shard_map/ppermute | solution.py:48
  84.3 2.8 %collective-permute-start.13 = (f32[2,256,256]{2,1,0:T(8,128)S(1)}, f32[2,256,256]{2,1,0:T(8,128)S(1)}, u32[]{:S(2)}, u32[]{:S(2)}) collective-permute-start(f32[2,256,256]{2,1,0:T(8,128)S(1)} %get-tuple-element.50.refs_4_), channel_id=1, source_target_pairs={{0,8},{1,9},{2,10},{3,11},{4,12},{5,13},{6,14},{7,15},{8,0},{9,1},... | collective-permute-start | bytes 1572872 | tf_op jit(solution)/shard_map/ppermute | solution.py:384
  87.1 3.0 %collective-permute-done.15.refs_2_ = f32[256,256]{1,0:T(8,128)S(1)} collective-permute-done((f32[256,256]{1,0:T(8,128)S(1)}, f32[256,256]{1,0:T(8,128)S(1)}, u32[]{:S(2)}, u32[]{:S(2)}) %collective-permute-start.15) | collective-permute-done | bytes 262176 | tf_op jit(solution)/shard_map/ppermute | solution.py:48
  93.5 2.3 %collective-permute-start.25 = (f32[256,256]{1,0:T(8,128)S(1)}, f32[256,256]{1,0:T(8,128)S(1)}, u32[]{:S(2)}, u32[]{:S(2)}) collective-permute-start(f32[256,256]{1,0:T(8,128)S(1)} %ghost_sum.2.refs_2_), channel_id=1, source_target_pairs={{0,8},{1,9},{2,10},{3,11},{4,12},{5,13},{6,14},{7,15},{8,0},{9,1},... | collective-permute-start | bytes 786440 | tf_op jit(solution)/shard_map/ppermute | solution.py:384
  95.7 11.3 %collective-permute-done.16.refs_5_ = f32[256,256]{1,0:T(8,128)S(1)} collective-permute-done((f32[256,256]{1,0:T(8,128)S(1)}, f32[256,256]{1,0:T(8,128)S(1)}, u32[]{:S(2)}, u32[]{:S(2)}) %collective-permute-start.16) | collective-permute-done | bytes 262176 | tf_op jit(solution)/shard_map/ppermute | solution.py:52
  107.0 4.0 %collective-permute-done.25.refs_3_ = f32[256,256]{1,0:T(8,128)S(1)} collective-permute-done((f32[256,256]{1,0:T(8,128)S(1)}, f32[256,256]{1,0:T(8,128)S(1)}, u32[]{:S(2)}, u32[]{:S(2)}) %collective-permute-start.25) | collective-permute-done | bytes 262176 | tf_op jit(solution)/shard_map/ppermute | solution.py:384
  112.7 2.8 %collective-permute-start.14 = (f32[2,256,256]{2,1,0:T(8,128)}, f32[2,256,256]{2,1,0:T(8,128)S(1)}, u32[]{:S(2)}, u32[]{:S(2)}) collective-permute-start(f32[2,256,256]{2,1,0:T(8,128)} %copy-done.20), channel_id=1, source_target_pairs={{0,8},{1,9},{2,10},{3,11},{4,12},{5,13},{6,14},{7,15},{8,0},{9,1},... | collective-permute-start | bytes 1572872 | tf_op jit(solution)/shard_map/ppermute | solution.py:384
  116.6 2.2 %copy-done.3 = f32[16,256,256]{2,1,0:T(8,128)S(1)} copy-done((f32[16,256,256]{2,1,0:T(8,128)S(1)}, f32[16,256,256]{2,1,0:T(8,128)}, u32[]{:S(2)}) %copy-start.3) | copy-done | bytes 4194328
  121.7 4.4 %collective-permute-start.18 = (f32[16,256]{1,0:T(8,128)S(1)}, f32[16,256]{1,0:T(8,128)S(1)}, u32[]{:S(2)}, u32[]{:S(2)}) collective-permute-start(f32[16,256]{1,0:T(8,128)S(1)} %get-tuple-element.54), channel_id=1, source_target_pairs={{4,0},{5,1},{6,2},{7,3},{8,4},{9,5},{10,6},{11,7},{12,8},{13,9},{1... | collective-permute-start | bytes 49160 | tf_op jit(solution)/shard_map/ppermute | solution.py:363
  127.8 2.3 %collective-permute-done.17.refs_3_.x_low = f32[16,256]{1,0:T(8,128)S(1)} collective-permute-done((f32[16,256]{1,0:T(8,128)S(1)}, f32[16,256]{1,0:T(8,128)S(1)}, u32[]{:S(2)}, u32[]{:S(2)}) %collective-permute-start.17) | collective-permute-done | bytes 16416 | tf_op jit(solution)/shard_map/ppermute | solution.py:362
  134.9 2.2 %copy-done.4 = f32[16,256,256]{2,1,0:T(8,128)S(1)} copy-done((f32[16,256,256]{2,1,0:T(8,128)S(1)}, f32[16,256,256]{2,1,0:T(8,128)}, u32[]{:S(2)}) %copy-start.4) | copy-done | bytes 4194328
  137.1 9.8 %stencil.3 = (f32[16,256,256]{2,1,0:T(8,128)}, f32[8,128]{1,0:T(8,128)S(1)}) custom-call(f32[1]{0:T(128)S(6)} %div.3.inverse, s32[4]{0:T(128)S(1)} %add_convert_fusion.inside, f32[16,256,256]{2,1,0:T(8,128)S(1)} %copy-done.4, f32[256,256]{1,0:T(8,128)S(1)} %below.1.bottom, f32[256,256]{1,0:T(8,128)S(1)} %multiply_add_fusion.top, ...), custom_call_target="tpu_custom_call" | custom-call | flops 1024 | bytes 1024 | tf_op jit(solution)/shard_map/stencil/pallas_call | solution.py:345
  147.2 9.4 %collective-permute-done.22.refs_2_ = f32[256,256]{1,0:T(8,128)S(1)} collective-permute-done((f32[256,256]{1,0:T(8,128)S(1)}, f32[256,256]{1,0:T(8,128)S(1)}, u32[]{:S(2)}, u32[]{:S(2)}) %collective-permute-start.22) | collective-permute-done | bytes 262176 | tf_op jit(solution)/shard_map/ppermute | solution.py:48
  157.9 4.5 %fix_bottom.1.field = f32[16,256,256]{2,1,0:T(8,128)} custom-call(s32[7]{0:T(128)S(1)} %pad_add_fusion.table, f32[4,256,256]{2,1,0:T(8,128)S(1)} %bitcast.34, f32[4,256,256]{2,1,0:T(8,128)S(1)} %bitcast.38, f32[16,256,256]{2,1,0:T(8,128)} %bitcast.26, f32[16,256,256]{2,1,0:T(8,128)} %all-gather.5.cloned.1.call-done.tops, ...), custom_call_target="tpu_custom_call", output_to_operand_aliasing={{}: (5, {})} | custom-call | flops 1024 | bytes 1024 | tf_op jit(solution)/shard_map/fix_bottom/pallas_call | solution.py:235
  162.5 2.3 %collective-permute-done.24.ghost = f32[256,256]{1,0:T(8,128)S(1)} collective-permute-done((f32[256,256]{1,0:T(8,128)S(1)}, f32[256,256]{1,0:T(8,128)S(1)}, u32[]{:S(2)}, u32[]{:S(2)}) %collective-permute-start.24) | collective-permute-done | bytes 262176 | tf_op jit(solution)/shard_map/ppermute | solution.py:52
  164.7 2.2 %fix_top.1 = f32[16,256,256]{2,1,0:T(8,128)} custom-call(s32[7]{0:T(128)S(1)} %pad_add_fusion.table, f32[256,256]{1,0:T(8,128)S(1)} %collective-permute-done.24.ghost, f32[16,256,256]{2,1,0:T(8,128)} %fix_bottom.1.field), custom_call_target="tpu_custom_call", output_to_operand_aliasing={{}: (2, {})} | custom-call | flops 1024 | bytes 1024 | tf_op jit(solution)/shard_map/fix_top/pallas_call | solution.py:259
  (97 shorter events, 36.9 us)
Async XLA Ops:
  6.5 63.9 %all-gather.3.cloned.1.call-start = ((), (), s32[]{:S(2)}) async-start(), calls=%async_computation | async-start | bytes 4718592 | tf_op jit(solution)/shard_map/all_gather | solution.py:374
  7.7 16.6 %collective-permute-start.4 = (f32[256,256]{1,0:T(8,128)S(1)}, f32[256,256]{1,0:T(8,128)S(1)}, u32[]{:S(2)}, u32[]{:S(2)}) collective-permute-start(f32[256,256]{1,0:T(8,128)S(1)} %get-tuple-element.63.top), channel_id=1, source_target_pairs={{0,16},{1,17},{2,18},{3,19},{4,20},{5,21},{6,22},{7,23},{8,24},{9,... | collective-permute-start | bytes 786440 | tf_op jit(solution)/shard_map/ppermute | solution.py:52
  9.9 14.3 %collective-permute-start.5 = (f32[256,256]{1,0:T(8,128)S(1)}, f32[256,256]{1,0:T(8,128)S(1)}, u32[]{:S(2)}, u32[]{:S(2)}) collective-permute-start(f32[256,256]{1,0:T(8,128)S(1)} %get-tuple-element.63.top), channel_id=1, source_target_pairs={{0,24},{1,25},{2,26},{3,27},{4,28},{5,29},{6,30},{7,31},{8,16},{9,... | collective-permute-start | bytes 786440 | tf_op jit(solution)/shard_map/ppermute | solution.py:52
  14.6 8.2 %collective-permute-start = (f32[16,256]{1,0:T(8,128)S(1)}, f32[16,256]{1,0:T(8,128)S(1)}, u32[]{:S(2)}, u32[]{:S(2)}) collective-permute-start(f32[16,256]{1,0:T(8,128)S(1)} %get-tuple-element.34), channel_id=1, source_target_pairs={{0,4},{1,5},{2,6},{3,7},{4,8},{5,9},{6,10},{7,11},{8,12},{9,13},{1... | collective-permute-start | bytes 49160 | tf_op jit(solution)/shard_map/ppermute | solution.py:362
  17.8 5.2 %collective-permute-start.1 = (f32[16,256]{1,0:T(8,128)S(1)}, f32[16,256]{1,0:T(8,128)S(1)}, u32[]{:S(2)}, u32[]{:S(2)}) collective-permute-start(f32[16,256]{1,0:T(8,128)S(1)} %get-tuple-element.35), channel_id=1, source_target_pairs={{4,0},{5,1},{6,2},{7,3},{8,4},{9,5},{10,6},{11,7},{12,8},{13,9},{1... | collective-permute-start | bytes 49160 | tf_op jit(solution)/shard_map/ppermute | solution.py:363
  20.6 3.2 %collective-permute-start.2 = (f32[16,256]{1,0:T(8,128)S(1)}, f32[16,256]{1,0:T(8,128)S(1)}, u32[]{:S(2)}, u32[]{:S(2)}) collective-permute-start(f32[16,256]{1,0:T(8,128)S(1)} %get-tuple-element.36), channel_id=1, source_target_pairs={{0,1},{1,2},{2,3},{3,0},{4,5},{5,6},{6,7},{7,4},{8,9},{9,10},{10,1... | collective-permute-start | bytes 49160 | tf_op jit(solution)/shard_map/ppermute | solution.py:364
  22.8 1.4 collective-permute-start.3
  25.2 132.7 %all-gather.5.cloned.1.call-start = ((), (), s32[]{:S(2)}) async-start(), calls=%async_computation.1 | async-start | bytes 4718592 | tf_op jit(solution)/shard_map/all_gather | solution.py:374
  29.4 5.0 %collective-permute-start.6 = (f32[8,256,256]{2,1,0:T(8,128)S(1)}, f32[8,256,256]{2,1,0:T(8,128)S(1)}, u32[]{:S(2)}, u32[]{:S(2)}) collective-permute-start(f32[8,256,256]{2,1,0:T(8,128)S(1)} %get-tuple-element.40), channel_id=1, source_target_pairs={{0,1},{1,0},{2,3},{3,2},{4,5},{5,4},{6,7},{7,6},{8,9},{9,8},{10,11... | collective-permute-start | bytes 6291464 | tf_op jit(solution)/shard_map/ppermute | solution.py:378
  36.6 27.9 %collective-permute-start.7 = (f32[4,256,256]{2,1,0:T(8,128)}, f32[4,256,256]{2,1,0:T(8,128)}, u32[]{:S(2)}, u32[]{:S(2)}) collective-permute-start(f32[4,256,256]{2,1,0:T(8,128)} %get-tuple-element.42), channel_id=1, source_target_pairs={{0,8},{1,9},{2,10},{3,11},{4,12},{5,13},{6,14},{7,15},{8,0},{9,1},... | collective-permute-start | bytes 3145736 | tf_op jit(solution)/shard_map/ppermute | solution.py:384
  55.1 19.2 %collective-permute-start.8 = (f32[256,256]{1,0:T(8,128)}, f32[256,256]{1,0:T(8,128)S(1)}, u32[]{:S(2)}, u32[]{:S(2)}) collective-permute-start(f32[256,256]{1,0:T(8,128)} %slice_bitcast_fusion), channel_id=1, source_target_pairs={{0,16},{1,17},{2,18},{3,19},{4,20},{5,21},{6,22},{7,23},{8,24},{9,... | collective-permute-start | bytes 786440 | tf_op jit(solution)/shard_map/ppermute | solution.py:52
  56.6 17.7 %collective-permute-start.9 = (f32[256,256]{1,0:T(8,128)}, f32[256,256]{1,0:T(8,128)S(1)}, u32[]{:S(2)}, u32[]{:S(2)}) collective-permute-start(f32[256,256]{1,0:T(8,128)} %slice_bitcast_fusion), channel_id=1, source_target_pairs={{0,24},{1,25},{2,26},{3,27},{4,28},{5,29},{6,30},{7,31},{8,16},{9,... | collective-permute-start | bytes 786440 | tf_op jit(solution)/shard_map/ppermute | solution.py:52
  67.2 8.6 %collective-permute-start.10 = (f32[256,256]{1,0:T(8,128)}, f32[256,256]{1,0:T(8,128)S(1)}, u32[]{:S(2)}, u32[]{:S(2)}) collective-permute-start(f32[256,256]{1,0:T(8,128)} %get-tuple-element.45), channel_id=1, source_target_pairs={{0,2},{1,3},{2,4},{3,5},{4,6},{5,7},{6,0},{7,1},{8,10},{9,11},{10,... | collective-permute-start | bytes 786440 | tf_op jit(solution)/shard_map/ppermute | solution.py:48
  68.1 7.7 %collective-permute-start.11 = (f32[256,256]{1,0:T(8,128)}, f32[256,256]{1,0:T(8,128)}, u32[]{:S(2)}, u32[]{:S(2)}) collective-permute-start(f32[256,256]{1,0:T(8,128)} %get-tuple-element.46), channel_id=1, source_target_pairs={{0,6},{1,7},{2,0},{3,1},{4,2},{5,3},{6,4},{7,5},{8,14},{9,15},{10,... | collective-permute-start | bytes 786440 | tf_op jit(solution)/shard_map/ppermute | solution.py:48
  79.9 4.2 %collective-permute-start.12 = (f32[8,256,256]{2,1,0:T(8,128)S(1)}, f32[8,256,256]{2,1,0:T(8,128)S(1)}, u32[]{:S(2)}, u32[]{:S(2)}) collective-permute-start(f32[8,256,256]{2,1,0:T(8,128)S(1)} %get-tuple-element.48), channel_id=1, source_target_pairs={{0,1},{1,0},{2,3},{3,2},{4,5},{5,4},{6,7},{7,6},{8,9},{9,8},{10,11... | collective-permute-start | bytes 6291464 | tf_op jit(solution)/shard_map/ppermute | solution.py:378
  79.9 10.2 %collective-permute-start.15 = (f32[256,256]{1,0:T(8,128)S(1)}, f32[256,256]{1,0:T(8,128)S(1)}, u32[]{:S(2)}, u32[]{:S(2)}) collective-permute-start(f32[256,256]{1,0:T(8,128)S(1)} %copy-done.22), channel_id=1, source_target_pairs={{0,4},{1,5},{2,6},{3,7},{4,0},{5,1},{6,2},{7,3},{8,12},{9,13},{10,... | collective-permute-start | bytes 786440 | tf_op jit(solution)/shard_map/ppermute | solution.py:48
  84.3 26.8 %copy-start.15 = (f32[4,256,256]{2,1,0:T(8,128)}, f32[4,256,256]{2,1,0:T(8,128)S(1)}, u32[]{:S(2)}) copy-start(f32[4,256,256]{2,1,0:T(8,128)S(1)} %get-tuple-element.49.refs_0_) | copy-start | bytes 3145732
  84.3 26.8 %copy-start.20 = (f32[2,256,256]{2,1,0:T(8,128)}, f32[2,256,256]{2,1,0:T(8,128)S(1)}, u32[]{:S(2)}) copy-start(f32[2,256,256]{2,1,0:T(8,128)S(1)} %get-tuple-element.51) | copy-start | bytes 1572868
  84.3 26.8 %collective-permute-start.13 = (f32[2,256,256]{2,1,0:T(8,128)S(1)}, f32[2,256,256]{2,1,0:T(8,128)S(1)}, u32[]{:S(2)}, u32[]{:S(2)}) collective-permute-start(f32[2,256,256]{2,1,0:T(8,128)S(1)} %get-tuple-element.50.refs_4_), channel_id=1, source_target_pairs={{0,8},{1,9},{2,10},{3,11},{4,12},{5,13},{6,14},{7,15},{8,0},{9,1},... | collective-permute-start | bytes 1572872 | tf_op jit(solution)/shard_map/ppermute | solution.py:384
  92.1 15.0 %collective-permute-start.16 = (f32[256,256]{1,0:T(8,128)S(1)}, f32[256,256]{1,0:T(8,128)S(1)}, u32[]{:S(2)}, u32[]{:S(2)}) collective-permute-start(f32[256,256]{1,0:T(8,128)S(1)} %ghost_sum.2.refs_2_), channel_id=1, source_target_pairs={{0,112},{1,113},{2,114},{3,115},{4,116},{5,117},{6,118},{7,119},{8... | collective-permute-start | bytes 786440 | tf_op jit(solution)/shard_map/ppermute | solution.py:52
  93.5 17.6 %collective-permute-start.25 = (f32[256,256]{1,0:T(8,128)S(1)}, f32[256,256]{1,0:T(8,128)S(1)}, u32[]{:S(2)}, u32[]{:S(2)}) collective-permute-start(f32[256,256]{1,0:T(8,128)S(1)} %ghost_sum.2.refs_2_), channel_id=1, source_target_pairs={{0,8},{1,9},{2,10},{3,11},{4,12},{5,13},{6,14},{7,15},{8,0},{9,1},... | collective-permute-start | bytes 786440 | tf_op jit(solution)/shard_map/ppermute | solution.py:384
  112.7 22.3 %copy-start.12 = (s32[1,1,256,256]{3,2,1,0:T(8,128)S(1)}, s32[1,1,256,256]{3,2,1,0:T(8,128)}, u32[]{:S(2)}) copy-start(s32[1,1,256,256]{3,2,1,0:T(8,128)} %param.10) | copy-start | bytes 786436
  112.7 22.2 %copy-start.1 = (f32[1,16,1,256,256]{4,3,2,1,0:T(8,128)S(1)}, f32[1,16,1,256,256]{4,3,2,1,0:T(8,128)}, u32[]{:S(2)}) copy-start(f32[1,16,1,256,256]{4,3,2,1,0:T(8,128)} %param.8) | copy-start | bytes 12582916
  112.7 17.4 %collective-permute-start.14 = (f32[2,256,256]{2,1,0:T(8,128)}, f32[2,256,256]{2,1,0:T(8,128)S(1)}, u32[]{:S(2)}, u32[]{:S(2)}) collective-permute-start(f32[2,256,256]{2,1,0:T(8,128)} %copy-done.20), channel_id=1, source_target_pairs={{0,8},{1,9},{2,10},{3,11},{4,12},{5,13},{6,14},{7,15},{8,0},{9,1},... | collective-permute-start | bytes 1572872 | tf_op jit(solution)/shard_map/ppermute | solution.py:384
  120.1 10.0 %collective-permute-start.17 = (f32[16,256]{1,0:T(8,128)S(1)}, f32[16,256]{1,0:T(8,128)S(1)}, u32[]{:S(2)}, u32[]{:S(2)}) collective-permute-start(f32[16,256]{1,0:T(8,128)S(1)} %get-tuple-element.53), channel_id=1, source_target_pairs={{0,4},{1,5},{2,6},{3,7},{4,8},{5,9},{6,10},{7,11},{8,12},{9,13},{1... | collective-permute-start | bytes 49160 | tf_op jit(solution)/shard_map/ppermute | solution.py:362
  121.7 8.5 %collective-permute-start.18 = (f32[16,256]{1,0:T(8,128)S(1)}, f32[16,256]{1,0:T(8,128)S(1)}, u32[]{:S(2)}, u32[]{:S(2)}) collective-permute-start(f32[16,256]{1,0:T(8,128)S(1)} %get-tuple-element.54), channel_id=1, source_target_pairs={{4,0},{5,1},{6,2},{7,3},{8,4},{9,5},{10,6},{11,7},{12,8},{13,9},{1... | collective-permute-start | bytes 49160 | tf_op jit(solution)/shard_map/ppermute | solution.py:363
  126.1 4.1 %collective-permute-start.19 = (f32[16,256]{1,0:T(8,128)S(1)}, f32[16,256]{1,0:T(8,128)S(1)}, u32[]{:S(2)}, u32[]{:S(2)}) collective-permute-start(f32[16,256]{1,0:T(8,128)S(1)} %get-tuple-element.55), channel_id=1, source_target_pairs={{0,1},{1,2},{2,3},{3,0},{4,5},{5,6},{6,7},{7,4},{8,9},{9,10},{10,1... | collective-permute-start | bytes 49160 | tf_op jit(solution)/shard_map/ppermute | solution.py:364
  126.1 4.1 %collective-permute-start.20 = (f32[16,256]{1,0:T(8,128)S(1)}, f32[16,256]{1,0:T(8,128)S(1)}, u32[]{:S(2)}, u32[]{:S(2)}) collective-permute-start(f32[16,256]{1,0:T(8,128)S(1)} %get-tuple-element.56), channel_id=1, source_target_pairs={{1,0},{2,1},{3,2},{0,3},{5,4},{6,5},{7,6},{4,7},{9,8},{10,9},{11,1... | collective-permute-start | bytes 49160 | tf_op jit(solution)/shard_map/ppermute | solution.py:365
  130.3 17.0 %collective-permute-start.21 = (f32[256,256]{1,0:T(8,128)S(1)}, f32[256,256]{1,0:T(8,128)S(1)}, u32[]{:S(2)}, u32[]{:S(2)}) collective-permute-start(f32[256,256]{1,0:T(8,128)S(1)} %get-tuple-element.58), channel_id=1, source_target_pairs={{0,2},{1,3},{2,4},{3,5},{4,6},{5,7},{6,0},{7,1},{8,10},{9,11},{10,... | collective-permute-start | bytes 786440 | tf_op jit(solution)/shard_map/ppermute | solution.py:48
  131.7 25.0 %collective-permute-start.22 = (f32[256,256]{1,0:T(8,128)S(1)}, f32[256,256]{1,0:T(8,128)S(1)}, u32[]{:S(2)}, u32[]{:S(2)}) collective-permute-start(f32[256,256]{1,0:T(8,128)S(1)} %get-tuple-element.59), channel_id=1, source_target_pairs={{0,4},{1,5},{2,6},{3,7},{4,0},{5,1},{6,2},{7,3},{8,12},{9,13},{10,... | collective-permute-start | bytes 786440 | tf_op jit(solution)/shard_map/ppermute | solution.py:48
  133.2 23.4 %collective-permute-start.23 = (f32[256,256]{1,0:T(8,128)S(1)}, f32[256,256]{1,0:T(8,128)S(1)}, u32[]{:S(2)}, u32[]{:S(2)}) collective-permute-start(f32[256,256]{1,0:T(8,128)S(1)} %get-tuple-element.60), channel_id=1, source_target_pairs={{0,6},{1,7},{2,0},{3,1},{4,2},{5,3},{6,4},{7,5},{8,14},{9,15},{10,... | collective-permute-start | bytes 786440 | tf_op jit(solution)/shard_map/ppermute | solution.py:48
  156.7 8.0 %collective-permute-start.24 = (f32[256,256]{1,0:T(8,128)S(1)}, f32[256,256]{1,0:T(8,128)S(1)}, u32[]{:S(2)}, u32[]{:S(2)}) collective-permute-start(f32[256,256]{1,0:T(8,128)S(1)} %ghost_sum.3), channel_id=1, source_target_pairs={{0,112},{1,113},{2,114},{3,115},{4,116},{5,117},{6,118},{7,119},{8... | collective-permute-start | bytes 786440 | tf_op jit(solution)/shard_map/ppermute | solution.py:52
  (20 other events, 155.2 us)
Sparse Core Ops, SparseCore 0:
  25.3 34.6 all-gather.2
  112.8 45.0 all-gather.4

commit v9 on v8

--- a/solution.py
+++ b/solution.py
@@ -146,8 +146,8 @@
 
 def cores_body(keep, taken, give_near, give_far, keep_half):
     keep_half[...] = keep[0:4] + taken[0:4]
-    give_near[...] = keep[4:6] + taken[4:6]
-    give_far[...] = keep[6:8] + taken[6:8]
+    give_near[...] = keep[4:5] + taken[4:5]
+    give_far[...] = keep[5:8] + taken[5:8]
 
 
 def whole_cores_body(keep, taken, give_half, keep_half):
@@ -409,11 +409,10 @@
     bottom, top = field[0], field[NZ - 1]
 
     mine, flip = climb(top)
-    halos = exchange_rims(rims_of(field, bottom, top))
-    pair = small_kernel(pair_body, "pair", planes(2), (mine, flip), halos)
-    tops = gather_pair(pair)
-    give, keep, mark = pieces_of(table, px, py, bottom, pair)
-    give, keep = reduce_cores(give, keep, whole_cores_body, 4)
+    give, keep, mark = pieces_of(table, px, py, bottom)
+    halos = exchange_rims(rims_of(field, bottom, top, mark))
+    give, keep = reduce_cores(give, keep, whole_cores_body, 4, earlier=halos)
+    tops = gather_pair(small_kernel(pair_body, "pair", planes(2), (mine, flip), (give,)))
     got = reduce_halves(give)
     field, mark = stencil(inverse, inside, field, bottom, top, speed, inlets, halos)
     high = field[NZ - 1]
@@ -421,7 +420,7 @@
     parts = reduce_ring(keep, [got], mark)
     bottom = below_update(table, px, py, field, speed, tops, parts[0])
     give, keep, mark = pieces_of(table, px, py, bottom, mine, flip, parts[1], parts[3])
-    give_near, give_far, keep = reduce_cores(give, keep, cores_body, 2, 2)
+    give_near, give_far, keep = reduce_cores(give, keep, cores_body, 1, 3)
     ghost = ghost_sum(parts, give_near, mine, flip)
     got_near = reduce_halves(give_near)
     other_ghost = reduce_halves(ghost)

time: 175 us -> 172 us (0.983)
  waiting for transfers between devices: 50.3 us -> 44.9 us
    ppermute x2, waiting for transfers between devices: 4.57 us -> 9.87 us  [exchange_rims(): x_low = lax.ppermute(row_high, 'tile', up)]
    ppermute x6, waiting for transfers between devices: 14.2 us -> 9.62 us  [send_y(): return lax.ppermute(value, 'tile', along_y(steps))]
    ppermute x6, waiting for transfers between devices: 13.6 us -> 9.59 us  [send_lift(): return lax.ppermute(value, ('lift', 'tile'), to_lift(steps, flip))]
    ppermute x2, waiting for transfers between devices: 5.38 us -> 2.09 us  [reduce_cores(): taken = lax.ppermute(give, 'tile', OTHER_CORE)]
    unnamed x48 -> x42, local copies, waits for them, and re-layouts: 16.4 us -> 17.9 us
  transfers between devices with their start and end apart: 28 -> 28, of which waited for: 16 -> 13; matrix products, arithmetic and copies ran while one was open for 1% -> 1% of each run, Pallas kernels for 21% -> 20%
where the time goes in v9:
time: 172 us; the launch traced here: 171 us
  Pallas kernels  45.2 us (26%)
  waiting for transfers between devices  44.9 us (26%)
  starting transfers between devices  44.8 us (26%)
  local copies, waits for them, and re-layouts  19.7 us (11%)
  between operations  14.3 us (8%)
  other arithmetic  1.8 us (1%)
    unnamed x42, local copies, waits for them, and re-layouts  17.9 us
    pallas_call x2, Pallas kernels, stencil(): pl.pallas_call(stencil_kernel, out_shape=(planes(NZ), MARK), in_specs=[SM...  17.8 us
    ppermute x4, starting transfers between devices, reduce_halves(): return lax.ppermute(give, 'tile', OTHER_HALF)  11.5 us
    ppermute x4, waiting for transfers between devices, reduce_halves(): return lax.ppermute(give, 'tile', OTHER_HALF)  11.1 us
    ppermute x6, starting transfers between devices, send_y(): return lax.ppermute(value, 'tile', along_y(steps))  10.7 us
    ppermute x2, waiting for transfers between devices, exchange_rims(): x_low = lax.ppermute(row_high, 'tile', up)  9.87 us
    ppermute x6, waiting for transfers between devices, send_y(): return lax.ppermute(value, 'tile', along_y(steps))  9.62 us
    ppermute x6, waiting for transfers between devices, send_lift(): return lax.ppermute(value, ('lift', 'tile'), to_lift(steps, flip))  9.59 us
  transfers between devices with their start and end apart: 28, of which 13 were waited for; matrix products, arithmetic and copies ran while one was open for 1% of the time, Pallas kernels for 20%

profile of v9, /device:TPU:6, one launch (start us, length us, event | category | flops | bytes accessed | tf_op | source)
XLA Modules:
  0.0 170.6 jit_solution(6192049761407307590)
XLA Ops:
  10.8 3.4 %pieces.2 = (f32[8,256,256]{2,1,0:T(8,128)S(1)}, f32[8,256,256]{2,1,0:T(8,128)S(1)}, f32[8,128]{1,0:T(8,128)S(1)}) custom-call(s32[7]{0:T(128)S(1)} %pad_add_fusion.table, f32[4,256,256]{2,1,0:T(8,128)S(1)} %bitcast.31, f32[4,256,256]{2,1,0:T(8,128)S(1)} %bitcast.35, f32[256,256]{1,0:T(8,128)S(1)} %get-tuple-element.66.bottom), custom_call_target="tpu_custom_call" | custom-call | flops 1024 | bytes 1024 | tf_op jit(solution)/shard_map/pieces/pallas_call | solution.py:109
  14.3 2.3 %collective-permute-start.4 = (f32[256,256]{1,0:T(8,128)S(1)}, f32[256,256]{1,0:T(8,128)S(1)}, u32[]{:S(2)}, u32[]{:S(2)}) collective-permute-start(f32[256,256]{1,0:T(8,128)S(1)} %get-tuple-element.65.top), channel_id=1, source_target_pairs={{0,16},{1,17},{2,18},{3,19},{4,20},{5,21},{6,22},{7,23},{8,24},{9,... | collective-permute-start | bytes 786440 | tf_op jit(solution)/shard_map/ppermute | solution.py:52
  17.7 2.2 %copy-done.5 = f32[1,16,1,256,256]{4,3,2,1,0:T(8,128)S(1)} copy-done((f32[1,16,1,256,256]{4,3,2,1,0:T(8,128)S(1)}, f32[1,16,1,256,256]{4,3,2,1,0:T(8,128)}, u32[]{:S(2)}) %copy-start.5) | copy-done | bytes 4194328
  21.2 3.2 %collective-permute-start = (f32[16,256]{1,0:T(8,128)S(1)}, f32[16,256]{1,0:T(8,128)S(1)}, u32[]{:S(2)}, u32[]{:S(2)}) collective-permute-start(f32[16,256]{1,0:T(8,128)S(1)} %get-tuple-element.36), channel_id=1, source_target_pairs={{0,4},{1,5},{2,6},{3,7},{4,8},{5,9},{6,10},{7,11},{8,12},{9,13},{1... | collective-permute-start | bytes 49160 | tf_op jit(solution)/shard_map/ppermute | solution.py:362
  24.5 2.7 %collective-permute-start.1 = (f32[16,256]{1,0:T(8,128)S(1)}, f32[16,256]{1,0:T(8,128)S(1)}, u32[]{:S(2)}, u32[]{:S(2)}) collective-permute-start(f32[16,256]{1,0:T(8,128)S(1)} %get-tuple-element.37), channel_id=1, source_target_pairs={{4,0},{5,1},{6,2},{7,3},{8,4},{9,5},{10,6},{11,7},{12,8},{13,9},{1... | collective-permute-start | bytes 49160 | tf_op jit(solution)/shard_map/ppermute | solution.py:363
  27.2 2.8 %collective-permute-done.x_low.refs_2_ = f32[16,256]{1,0:T(8,128)S(1)} collective-permute-done((f32[16,256]{1,0:T(8,128)S(1)}, f32[16,256]{1,0:T(8,128)S(1)}, u32[]{:S(2)}, u32[]{:S(2)}) %collective-permute-start) | collective-permute-done | bytes 16416 | tf_op jit(solution)/shard_map/ppermute | solution.py:362
  36.4 3.3 %collective-permute-start.7 = (f32[4,256,256]{2,1,0:T(8,128)}, f32[4,256,256]{2,1,0:T(8,128)}, u32[]{:S(2)}, u32[]{:S(2)}) collective-permute-start(f32[4,256,256]{2,1,0:T(8,128)} %get-tuple-element.43.refs_2_), channel_id=1, source_target_pairs={{0,8},{1,9},{2,10},{3,11},{4,12},{5,13},{6,14},{7,15},{8,0},{9,1},... | collective-permute-start | bytes 3145736 | tf_op jit(solution)/shard_map/ppermute | solution.py:384
  40.5 2.2 %copy-done = f32[1,16,1,256,256]{4,3,2,1,0:T(8,128)S(1)} copy-done((f32[1,16,1,256,256]{4,3,2,1,0:T(8,128)S(1)}, f32[1,16,1,256,256]{4,3,2,1,0:T(8,128)}, u32[]{:S(2)}) %copy-start) | copy-done | bytes 4194328
  42.7 2.2 %copy-done.6 = f32[1,16,1,256,256]{4,3,2,1,0:T(8,128)S(1)} copy-done((f32[1,16,1,256,256]{4,3,2,1,0:T(8,128)S(1)}, f32[1,16,1,256,256]{4,3,2,1,0:T(8,128)}, u32[]{:S(2)}) %copy-start.6) | copy-done | bytes 4194328
  44.9 7.9 %stencil.2 = (f32[16,256,256]{2,1,0:T(8,128)S(1)}, f32[8,128]{1,0:T(8,128)S(1)}) custom-call(f32[1]{0:T(128)S(6)} %div.3.inverse, s32[4]{0:T(128)S(1)} %add_convert_fusion.inside, f32[16,256,256]{2,1,0:T(8,128)S(1)} %bitcast.30, f32[256,256]{1,0:T(8,128)S(1)} %get-tuple-element.66.bottom, f32[256,256]{1,0:T(8,128)S(1)} %get-tuple-element.65.top, ...), custom_call_target="tpu_custom_call" | custom-call | flops 1024 | bytes 1024 | tf_op jit(solution)/shard_map/stencil/pallas_call | solution.py:345
  55.6 2.3 %collective-permute-start.9 = (f32[256,256]{1,0:T(8,128)}, f32[256,256]{1,0:T(8,128)S(1)}, u32[]{:S(2)}, u32[]{:S(2)}) collective-permute-start(f32[256,256]{1,0:T(8,128)} %slice_bitcast_fusion), channel_id=1, source_target_pairs={{0,24},{1,25},{2,26},{3,27},{4,28},{5,29},{6,30},{7,31},{8,16},{9,... | collective-permute-start | bytes 786440 | tf_op jit(solution)/shard_map/ppermute | solution.py:52
  57.8 6.6 %collective-permute-done.7.refs_1_ = f32[4,256,256]{2,1,0:T(8,128)} collective-permute-done((f32[4,256,256]{2,1,0:T(8,128)}, f32[4,256,256]{2,1,0:T(8,128)}, u32[]{:S(2)}, u32[]{:S(2)}) %collective-permute-start.7) | collective-permute-done | bytes 1048608 | tf_op jit(solution)/shard_map/ppermute | solution.py:384
  64.4 2.1 %halves_sum.2 = (f32[256,256]{1,0:T(8,128)S(1)}, f32[256,256]{1,0:T(8,128)}, f32[256,256]{1,0:T(8,128)S(1)}, f32[256,256]{1,0:T(8,128)}) custom-call(f32[4,256,256]{2,1,0:T(8,128)S(1)} %copy-done.15, f32[4,256,256]{2,1,0:T(8,128)} %collective-permute-done.7.refs_1_, f32[8,128]{1,0:T(8,128)S(1)} %get-tuple-element.45.refs_2_), custom_call_target="tpu_custom_call" | custom-call | flops 1024 | bytes 1024 | tf_op jit(solution)/shard_map/halves_sum/pallas_call | solution.py:126
  67.6 2.8 %collective-permute-start.11 = (f32[256,256]{1,0:T(8,128)}, f32[256,256]{1,0:T(8,128)}, u32[]{:S(2)}, u32[]{:S(2)}) collective-permute-start(f32[256,256]{1,0:T(8,128)} %get-tuple-element.48), channel_id=1, source_target_pairs={{0,6},{1,7},{2,0},{3,1},{4,2},{5,3},{6,4},{7,5},{8,14},{9,15},{10,... | collective-permute-start | bytes 786440 | tf_op jit(solution)/shard_map/ppermute | solution.py:48
  71.5 3.9 %below.1.bottom = f32[256,256]{1,0:T(8,128)S(1)} custom-call(s32[7]{0:T(128)S(1)} %pad_add_fusion.table, f32[4,256,256]{2,1,0:T(8,128)S(1)} %bitcast.32, f32[4,256,256]{2,1,0:T(8,128)S(1)} %bitcast.36, f32[16,256,256]{2,1,0:T(8,128)} %copy-done.2, f32[16,256,256]{2,1,0:T(8,128)} %bitcast.25, f32[16,256,256]{2,1,0:T(8,128)} %all-gather.3.cloned.1.call-done.tops, ...), custom_call_target="tpu_custom_call" | custom-call | flops 1024 | bytes 1024 | tf_op jit(solution)/shard_map/below/pallas_call | solution.py:215
  77.0 4.0 %pieces.3 = (f32[8,256,256]{2,1,0:T(8,128)S(1)}, f32[8,256,256]{2,1,0:T(8,128)S(1)}, f32[8,128]{1,0:T(8,128)}) custom-call(s32[7]{0:T(128)S(1)} %pad_add_fusion.table, f32[4,256,256]{2,1,0:T(8,128)S(1)} %bitcast.33, f32[4,256,256]{2,1,0:T(8,128)S(1)} %bitcast.37, f32[256,256]{1,0:T(8,128)S(1)} %below.1.bottom, ...), custom_call_target="tpu_custom_call" | custom-call | flops 1024 | bytes 1024 | tf_op jit(solution)/shard_map/pieces/pallas_call | solution.py:109
  85.4 2.9 %collective-permute-start.13 = (f32[1,256,256]{2,1,0:T(8,128)S(1)}, f32[1,256,256]{2,1,0:T(8,128)S(1)}, u32[]{:S(2)}, u32[]{:S(2)}) collective-permute-start(f32[1,256,256]{2,1,0:T(8,128)S(1)} %get-tuple-element.52.refs_4_), channel_id=1, source_target_pairs={{0,8},{1,9},{2,10},{3,11},{4,12},{5,13},{6,14},{7,15},{8,0},{9,1},... | collective-permute-start | bytes 786440 | tf_op jit(solution)/shard_map/ppermute | solution.py:384
  88.4 2.9 %collective-permute-done.15.refs_2_ = f32[256,256]{1,0:T(8,128)S(1)} collective-permute-done((f32[256,256]{1,0:T(8,128)S(1)}, f32[256,256]{1,0:T(8,128)S(1)}, u32[]{:S(2)}, u32[]{:S(2)}) %collective-permute-start.15) | collective-permute-done | bytes 262176 | tf_op jit(solution)/shard_map/ppermute | solution.py:48
  92.5 2.9 %collective-permute-start.25 = (f32[256,256]{1,0:T(8,128)S(1)}, f32[256,256]{1,0:T(8,128)S(1)}, u32[]{:S(2)}, u32[]{:S(2)}) collective-permute-start(f32[256,256]{1,0:T(8,128)S(1)} %ghost_sum.2.refs_2_), channel_id=1, source_target_pairs={{0,8},{1,9},{2,10},{3,11},{4,12},{5,13},{6,14},{7,15},{8,0},{9,1},... | collective-permute-start | bytes 786440 | tf_op jit(solution)/shard_map/ppermute | solution.py:384
  95.4 7.2 %collective-permute-done.16.refs_5_ = f32[256,256]{1,0:T(8,128)S(1)} collective-permute-done((f32[256,256]{1,0:T(8,128)S(1)}, f32[256,256]{1,0:T(8,128)S(1)}, u32[]{:S(2)}, u32[]{:S(2)}) %collective-permute-start.16) | collective-permute-done | bytes 262176 | tf_op jit(solution)/shard_map/ppermute | solution.py:52
  102.6 4.6 %collective-permute-done.25.refs_3_ = f32[256,256]{1,0:T(8,128)S(1)} collective-permute-done((f32[256,256]{1,0:T(8,128)S(1)}, f32[256,256]{1,0:T(8,128)S(1)}, u32[]{:S(2)}, u32[]{:S(2)}) %collective-permute-start.25) | collective-permute-done | bytes 262176 | tf_op jit(solution)/shard_map/ppermute | solution.py:384
  108.7 2.4 %collective-permute-start.14 = (f32[3,256,256]{2,1,0:T(8,128)}, f32[3,256,256]{2,1,0:T(8,128)S(1)}, u32[]{:S(2)}, u32[]{:S(2)}) collective-permute-start(f32[3,256,256]{2,1,0:T(8,128)} %copy-done.18), channel_id=1, source_target_pairs={{0,8},{1,9},{2,10},{3,11},{4,12},{5,13},{6,14},{7,15},{8,0},{9,1},... | collective-permute-start | bytes 2359304 | tf_op jit(solution)/shard_map/ppermute | solution.py:384
  112.1 2.2 %copy-done.3 = f32[16,256,256]{2,1,0:T(8,128)S(1)} copy-done((f32[16,256,256]{2,1,0:T(8,128)S(1)}, f32[16,256,256]{2,1,0:T(8,128)}, u32[]{:S(2)}) %copy-start.3) | copy-done | bytes 4194328
  117.1 4.5 %collective-permute-start.18 = (f32[16,256]{1,0:T(8,128)S(1)}, f32[16,256]{1,0:T(8,128)S(1)}, u32[]{:S(2)}, u32[]{:S(2)}) collective-permute-start(f32[16,256]{1,0:T(8,128)S(1)} %get-tuple-element.56), channel_id=1, source_target_pairs={{4,0},{5,1},{6,2},{7,3},{8,4},{9,5},{10,6},{11,7},{12,8},{13,9},{1... | collective-permute-start | bytes 49160 | tf_op jit(solution)/shard_map/ppermute | solution.py:363
  123.3 7.0 %collective-permute-done.17.refs_3_.x_low = f32[16,256]{1,0:T(8,128)S(1)} collective-permute-done((f32[16,256]{1,0:T(8,128)S(1)}, f32[16,256]{1,0:T(8,128)S(1)}, u32[]{:S(2)}, u32[]{:S(2)}) %collective-permute-start.17) | collective-permute-done | bytes 16416 | tf_op jit(solution)/shard_map/ppermute | solution.py:362
  130.5 2.6 %collective-permute-start.21 = (f32[256,256]{1,0:T(8,128)S(1)}, f32[256,256]{1,0:T(8,128)S(1)}, u32[]{:S(2)}, u32[]{:S(2)}) collective-permute-start(f32[256,256]{1,0:T(8,128)S(1)} %get-tuple-element.60), channel_id=1, source_target_pairs={{0,2},{1,3},{2,4},{3,5},{4,6},{5,7},{6,0},{7,1},{8,10},{9,11},{10,... | collective-permute-start | bytes 786440 | tf_op jit(solution)/shard_map/ppermute | solution.py:48
  135.9 2.3 %copy-done.4 = f32[16,256,256]{2,1,0:T(8,128)S(1)} copy-done((f32[16,256,256]{2,1,0:T(8,128)S(1)}, f32[16,256,256]{2,1,0:T(8,128)}, u32[]{:S(2)}) %copy-start.4) | copy-done | bytes 4194328
  138.1 9.9 %stencil.3 = (f32[16,256,256]{2,1,0:T(8,128)}, f32[8,128]{1,0:T(8,128)S(1)}) custom-call(f32[1]{0:T(128)S(6)} %div.3.inverse, s32[4]{0:T(128)S(1)} %add_convert_fusion.inside, f32[16,256,256]{2,1,0:T(8,128)S(1)} %copy-done.4, f32[256,256]{1,0:T(8,128)S(1)} %below.1.bottom, f32[256,256]{1,0:T(8,128)S(1)} %multiply_add_fusion.top, ...), custom_call_target="tpu_custom_call" | custom-call | flops 1024 | bytes 1024 | tf_op jit(solution)/shard_map/stencil/pallas_call | solution.py:345
  148.1 5.1 %collective-permute-done.22.refs_2_ = f32[256,256]{1,0:T(8,128)S(1)} collective-permute-done((f32[256,256]{1,0:T(8,128)S(1)}, f32[256,256]{1,0:T(8,128)S(1)}, u32[]{:S(2)}, u32[]{:S(2)}) %collective-permute-start.22) | collective-permute-done | bytes 262176 | tf_op jit(solution)/shard_map/ppermute | solution.py:48
  154.5 4.6 %fix_bottom.1.field = f32[16,256,256]{2,1,0:T(8,128)} custom-call(s32[7]{0:T(128)S(1)} %pad_add_fusion.table, f32[4,256,256]{2,1,0:T(8,128)S(1)} %bitcast.34, f32[4,256,256]{2,1,0:T(8,128)S(1)} %bitcast.38, f32[16,256,256]{2,1,0:T(8,128)} %bitcast.26, f32[16,256,256]{2,1,0:T(8,128)} %all-gather.5.cloned.1.call-done.tops, ...), custom_call_target="tpu_custom_call", output_to_operand_aliasing={{}: (5, {})} | custom-call | flops 1024 | bytes 1024 | tf_op jit(solution)/shard_map/fix_bottom/pallas_call | solution.py:235
  159.1 2.4 %collective-permute-done.24.ghost = f32[256,256]{1,0:T(8,128)S(1)} collective-permute-done((f32[256,256]{1,0:T(8,128)S(1)}, f32[256,256]{1,0:T(8,128)S(1)}, u32[]{:S(2)}, u32[]{:S(2)}) %collective-permute-start.24) | collective-permute-done | bytes 262176 | tf_op jit(solution)/shard_map/ppermute | solution.py:52
  161.5 2.3 %fix_top.1 = f32[16,256,256]{2,1,0:T(8,128)} custom-call(s32[7]{0:T(128)S(1)} %pad_add_fusion.table, f32[256,256]{1,0:T(8,128)S(1)} %collective-permute-done.24.ghost, f32[16,256,256]{2,1,0:T(8,128)} %fix_bottom.1.field), custom_call_target="tpu_custom_call", output_to_operand_aliasing={{}: (2, {})} | custom-call | flops 1024 | bytes 1024 | tf_op jit(solution)/shard_map/fix_top/pallas_call | solution.py:259
  (91 shorter events, 36.8 us)
Async XLA Ops:
  6.5 64.9 %all-gather.3.cloned.1.call-start = ((), (), s32[]{:S(2)}) async-start(), calls=%async_computation | async-start | bytes 4718592 | tf_op jit(solution)/shard_map/all_gather | solution.py:374
  14.2 19.0 %collective-permute-start.6 = (f32[8,256,256]{2,1,0:T(8,128)S(1)}, f32[8,256,256]{2,1,0:T(8,128)S(1)}, u32[]{:S(2)}, u32[]{:S(2)}) collective-permute-start(f32[8,256,256]{2,1,0:T(8,128)S(1)} %get-tuple-element.42), channel_id=1, source_target_pairs={{0,1},{1,0},{2,3},{3,2},{4,5},{5,4},{6,7},{7,6},{8,9},{9,8},{10,11... | collective-permute-start | bytes 6291464 | tf_op jit(solution)/shard_map/ppermute | solution.py:378
  14.3 21.1 %collective-permute-start.4 = (f32[256,256]{1,0:T(8,128)S(1)}, f32[256,256]{1,0:T(8,128)S(1)}, u32[]{:S(2)}, u32[]{:S(2)}) collective-permute-start(f32[256,256]{1,0:T(8,128)S(1)} %get-tuple-element.65.top), channel_id=1, source_target_pairs={{0,16},{1,17},{2,18},{3,19},{4,20},{5,21},{6,22},{7,23},{8,24},{9,... | collective-permute-start | bytes 786440 | tf_op jit(solution)/shard_map/ppermute | solution.py:52
  16.6 18.9 %collective-permute-start.5 = (f32[256,256]{1,0:T(8,128)S(1)}, f32[256,256]{1,0:T(8,128)S(1)}, u32[]{:S(2)}, u32[]{:S(2)}) collective-permute-start(f32[256,256]{1,0:T(8,128)S(1)} %get-tuple-element.65.top), channel_id=1, source_target_pairs={{0,24},{1,25},{2,26},{3,27},{4,28},{5,29},{6,30},{7,31},{8,16},{9,... | collective-permute-start | bytes 786440 | tf_op jit(solution)/shard_map/ppermute | solution.py:52
  21.2 8.8 %collective-permute-start = (f32[16,256]{1,0:T(8,128)S(1)}, f32[16,256]{1,0:T(8,128)S(1)}, u32[]{:S(2)}, u32[]{:S(2)}) collective-permute-start(f32[16,256]{1,0:T(8,128)S(1)} %get-tuple-element.36), channel_id=1, source_target_pairs={{0,4},{1,5},{2,6},{3,7},{4,8},{5,9},{6,10},{7,11},{8,12},{9,13},{1... | collective-permute-start | bytes 49160 | tf_op jit(solution)/shard_map/ppermute | solution.py:362
  24.5 5.6 %collective-permute-start.1 = (f32[16,256]{1,0:T(8,128)S(1)}, f32[16,256]{1,0:T(8,128)S(1)}, u32[]{:S(2)}, u32[]{:S(2)}) collective-permute-start(f32[16,256]{1,0:T(8,128)S(1)} %get-tuple-element.37), channel_id=1, source_target_pairs={{4,0},{5,1},{6,2},{7,3},{8,4},{9,5},{10,6},{11,7},{12,8},{13,9},{1... | collective-permute-start | bytes 49160 | tf_op jit(solution)/shard_map/ppermute | solution.py:363
  30.1 3.2 %collective-permute-start.2 = (f32[16,256]{1,0:T(8,128)S(1)}, f32[16,256]{1,0:T(8,128)S(1)}, u32[]{:S(2)}, u32[]{:S(2)}) collective-permute-start(f32[16,256]{1,0:T(8,128)S(1)} %get-tuple-element.38), channel_id=1, source_target_pairs={{0,1},{1,2},{2,3},{3,0},{4,5},{5,6},{6,7},{7,4},{8,9},{9,10},{10,1... | collective-permute-start | bytes 49160 | tf_op jit(solution)/shard_map/ppermute | solution.py:364
  30.1 3.2 %collective-permute-start.3 = (f32[16,256]{1,0:T(8,128)S(1)}, f32[16,256]{1,0:T(8,128)S(1)}, u32[]{:S(2)}, u32[]{:S(2)}) collective-permute-start(f32[16,256]{1,0:T(8,128)S(1)} %get-tuple-element.39), channel_id=1, source_target_pairs={{1,0},{2,1},{3,2},{0,3},{5,4},{6,5},{7,6},{4,7},{9,8},{10,9},{11,1... | collective-permute-start | bytes 49160 | tf_op jit(solution)/shard_map/ppermute | solution.py:365
  36.4 118.1 %all-gather.5.cloned.1.call-start = ((), (), s32[]{:S(2)}) async-start(), calls=%async_computation.1 | async-start | bytes 4718592 | tf_op jit(solution)/shard_map/all_gather | solution.py:374
  36.4 28.0 %collective-permute-start.7 = (f32[4,256,256]{2,1,0:T(8,128)}, f32[4,256,256]{2,1,0:T(8,128)}, u32[]{:S(2)}, u32[]{:S(2)}) collective-permute-start(f32[4,256,256]{2,1,0:T(8,128)} %get-tuple-element.43.refs_2_), channel_id=1, source_target_pairs={{0,8},{1,9},{2,10},{3,11},{4,12},{5,13},{6,14},{7,15},{8,0},{9,1},... | collective-permute-start | bytes 3145736 | tf_op jit(solution)/shard_map/ppermute | solution.py:384
  44.9 26.6 %copy-start.8 = (f32[1,1,4,256,256]{4,3,2,1,0:T(8,128)S(1)}, f32[1,1,4,256,256]{4,3,2,1,0:T(8,128)}, u32[]{:S(2)}) copy-start(f32[1,1,4,256,256]{4,3,2,1,0:T(8,128)} %param.11) | copy-start | bytes 3145732
  44.9 26.6 %copy-start.10 = (f32[1,1,4,256,256]{4,3,2,1,0:T(8,128)S(1)}, f32[1,1,4,256,256]{4,3,2,1,0:T(8,128)}, u32[]{:S(2)}) copy-start(f32[1,1,4,256,256]{4,3,2,1,0:T(8,128)} %param.12) | copy-start | bytes 3145732
  55.6 19.8 %collective-permute-start.8 = (f32[256,256]{1,0:T(8,128)}, f32[256,256]{1,0:T(8,128)S(1)}, u32[]{:S(2)}, u32[]{:S(2)}) collective-permute-start(f32[256,256]{1,0:T(8,128)} %slice_bitcast_fusion), channel_id=1, source_target_pairs={{0,16},{1,17},{2,18},{3,19},{4,20},{5,21},{6,22},{7,23},{8,24},{9,... | collective-permute-start | bytes 786440 | tf_op jit(solution)/shard_map/ppermute | solution.py:52
  55.6 19.8 %collective-permute-start.9 = (f32[256,256]{1,0:T(8,128)}, f32[256,256]{1,0:T(8,128)S(1)}, u32[]{:S(2)}, u32[]{:S(2)}) collective-permute-start(f32[256,256]{1,0:T(8,128)} %slice_bitcast_fusion), channel_id=1, source_target_pairs={{0,24},{1,25},{2,26},{3,27},{4,28},{5,29},{6,30},{7,31},{8,16},{9,... | collective-permute-start | bytes 786440 | tf_op jit(solution)/shard_map/ppermute | solution.py:52
  67.2 9.6 %collective-permute-start.10 = (f32[256,256]{1,0:T(8,128)}, f32[256,256]{1,0:T(8,128)}, u32[]{:S(2)}, u32[]{:S(2)}) collective-permute-start(f32[256,256]{1,0:T(8,128)} %get-tuple-element.47), channel_id=1, source_target_pairs={{0,2},{1,3},{2,4},{3,5},{4,6},{5,7},{6,0},{7,1},{8,10},{9,11},{10,... | collective-permute-start | bytes 786440 | tf_op jit(solution)/shard_map/ppermute | solution.py:48
  67.6 9.4 %collective-permute-start.11 = (f32[256,256]{1,0:T(8,128)}, f32[256,256]{1,0:T(8,128)}, u32[]{:S(2)}, u32[]{:S(2)}) collective-permute-start(f32[256,256]{1,0:T(8,128)} %get-tuple-element.48), channel_id=1, source_target_pairs={{0,6},{1,7},{2,0},{3,1},{4,2},{5,3},{6,4},{7,5},{8,14},{9,15},{10,... | collective-permute-start | bytes 786440 | tf_op jit(solution)/shard_map/ppermute | solution.py:48
  81.0 4.2 %collective-permute-start.12 = (f32[8,256,256]{2,1,0:T(8,128)S(1)}, f32[8,256,256]{2,1,0:T(8,128)S(1)}, u32[]{:S(2)}, u32[]{:S(2)}) collective-permute-start(f32[8,256,256]{2,1,0:T(8,128)S(1)} %get-tuple-element.50), channel_id=1, source_target_pairs={{0,1},{1,0},{2,3},{3,2},{4,5},{5,4},{6,7},{7,6},{8,9},{9,8},{10,11... | collective-permute-start | bytes 6291464 | tf_op jit(solution)/shard_map/ppermute | solution.py:378
  81.0 10.2 %collective-permute-start.15 = (f32[256,256]{1,0:T(8,128)S(1)}, f32[256,256]{1,0:T(8,128)S(1)}, u32[]{:S(2)}, u32[]{:S(2)}) collective-permute-start(f32[256,256]{1,0:T(8,128)S(1)} %copy-done.20), channel_id=1, source_target_pairs={{0,4},{1,5},{2,6},{3,7},{4,0},{5,1},{6,2},{7,3},{8,12},{9,13},{10,... | collective-permute-start | bytes 786440 | tf_op jit(solution)/shard_map/ppermute | solution.py:48
  85.4 21.7 %copy-start.18 = (f32[3,256,256]{2,1,0:T(8,128)}, f32[3,256,256]{2,1,0:T(8,128)S(1)}, u32[]{:S(2)}) copy-start(f32[3,256,256]{2,1,0:T(8,128)S(1)} %get-tuple-element.53) | copy-start | bytes 2359300
  85.4 10.0 %collective-permute-start.13 = (f32[1,256,256]{2,1,0:T(8,128)S(1)}, f32[1,256,256]{2,1,0:T(8,128)S(1)}, u32[]{:S(2)}, u32[]{:S(2)}) collective-permute-start(f32[1,256,256]{2,1,0:T(8,128)S(1)} %get-tuple-element.52.refs_4_), channel_id=1, source_target_pairs={{0,8},{1,9},{2,10},{3,11},{4,12},{5,13},{6,14},{7,15},{8,0},{9,1},... | collective-permute-start | bytes 786440 | tf_op jit(solution)/shard_map/ppermute | solution.py:384
  92.4 10.2 %collective-permute-start.16 = (f32[256,256]{1,0:T(8,128)S(1)}, f32[256,256]{1,0:T(8,128)S(1)}, u32[]{:S(2)}, u32[]{:S(2)}) collective-permute-start(f32[256,256]{1,0:T(8,128)S(1)} %ghost_sum.2.refs_2_), channel_id=1, source_target_pairs={{0,112},{1,113},{2,114},{3,115},{4,116},{5,117},{6,118},{7,119},{8... | collective-permute-start | bytes 786440 | tf_op jit(solution)/shard_map/ppermute | solution.py:52
  92.5 14.7 %collective-permute-start.25 = (f32[256,256]{1,0:T(8,128)S(1)}, f32[256,256]{1,0:T(8,128)S(1)}, u32[]{:S(2)}, u32[]{:S(2)}) collective-permute-start(f32[256,256]{1,0:T(8,128)S(1)} %ghost_sum.2.refs_2_), channel_id=1, source_target_pairs={{0,8},{1,9},{2,10},{3,11},{4,12},{5,13},{6,14},{7,15},{8,0},{9,1},... | collective-permute-start | bytes 786440 | tf_op jit(solution)/shard_map/ppermute | solution.py:384
  108.7 27.1 %copy-start.1 = (f32[1,16,1,256,256]{4,3,2,1,0:T(8,128)S(1)}, f32[1,16,1,256,256]{4,3,2,1,0:T(8,128)}, u32[]{:S(2)}) copy-start(f32[1,16,1,256,256]{4,3,2,1,0:T(8,128)} %param.8) | copy-start | bytes 12582916
  108.7 21.6 %collective-permute-start.14 = (f32[3,256,256]{2,1,0:T(8,128)}, f32[3,256,256]{2,1,0:T(8,128)S(1)}, u32[]{:S(2)}, u32[]{:S(2)}) collective-permute-start(f32[3,256,256]{2,1,0:T(8,128)} %copy-done.18), channel_id=1, source_target_pairs={{0,8},{1,9},{2,10},{3,11},{4,12},{5,13},{6,14},{7,15},{8,0},{9,1},... | collective-permute-start | bytes 2359304 | tf_op jit(solution)/shard_map/ppermute | solution.py:384
  115.6 14.7 %collective-permute-start.17 = (f32[16,256]{1,0:T(8,128)S(1)}, f32[16,256]{1,0:T(8,128)S(1)}, u32[]{:S(2)}, u32[]{:S(2)}) collective-permute-start(f32[16,256]{1,0:T(8,128)S(1)} %get-tuple-element.55), channel_id=1, source_target_pairs={{0,4},{1,5},{2,6},{3,7},{4,8},{5,9},{6,10},{7,11},{8,12},{9,13},{1... | collective-permute-start | bytes 49160 | tf_op jit(solution)/shard_map/ppermute | solution.py:362
  117.1 13.2 %collective-permute-start.18 = (f32[16,256]{1,0:T(8,128)S(1)}, f32[16,256]{1,0:T(8,128)S(1)}, u32[]{:S(2)}, u32[]{:S(2)}) collective-permute-start(f32[16,256]{1,0:T(8,128)S(1)} %get-tuple-element.56), channel_id=1, source_target_pairs={{4,0},{5,1},{6,2},{7,3},{8,4},{9,5},{10,6},{11,7},{12,8},{13,9},{1... | collective-permute-start | bytes 49160 | tf_op jit(solution)/shard_map/ppermute | solution.py:363
  121.6 8.8 %collective-permute-start.19 = (f32[16,256]{1,0:T(8,128)S(1)}, f32[16,256]{1,0:T(8,128)S(1)}, u32[]{:S(2)}, u32[]{:S(2)}) collective-permute-start(f32[16,256]{1,0:T(8,128)S(1)} %get-tuple-element.57), channel_id=1, source_target_pairs={{0,1},{1,2},{2,3},{3,0},{4,5},{5,6},{6,7},{7,4},{8,9},{9,10},{10,1... | collective-permute-start | bytes 49160 | tf_op jit(solution)/shard_map/ppermute | solution.py:364
  121.6 8.8 %collective-permute-start.20 = (f32[16,256]{1,0:T(8,128)S(1)}, f32[16,256]{1,0:T(8,128)S(1)}, u32[]{:S(2)}, u32[]{:S(2)}) collective-permute-start(f32[16,256]{1,0:T(8,128)S(1)} %get-tuple-element.58), channel_id=1, source_target_pairs={{1,0},{2,1},{3,2},{0,3},{5,4},{6,5},{7,6},{4,7},{9,8},{10,9},{11,1... | collective-permute-start | bytes 49160 | tf_op jit(solution)/shard_map/ppermute | solution.py:365
  130.5 17.6 %collective-permute-start.21 = (f32[256,256]{1,0:T(8,128)S(1)}, f32[256,256]{1,0:T(8,128)S(1)}, u32[]{:S(2)}, u32[]{:S(2)}) collective-permute-start(f32[256,256]{1,0:T(8,128)S(1)} %get-tuple-element.60), channel_id=1, source_target_pairs={{0,2},{1,3},{2,4},{3,5},{4,6},{5,7},{6,0},{7,1},{8,10},{9,11},{10,... | collective-permute-start | bytes 786440 | tf_op jit(solution)/shard_map/ppermute | solution.py:48
  133.1 20.1 %collective-permute-start.22 = (f32[256,256]{1,0:T(8,128)S(1)}, f32[256,256]{1,0:T(8,128)S(1)}, u32[]{:S(2)}, u32[]{:S(2)}) collective-permute-start(f32[256,256]{1,0:T(8,128)S(1)} %get-tuple-element.61), channel_id=1, source_target_pairs={{0,4},{1,5},{2,6},{3,7},{4,0},{5,1},{6,2},{7,3},{8,12},{9,13},{10,... | collective-permute-start | bytes 786440 | tf_op jit(solution)/shard_map/ppermute | solution.py:48
  134.8 18.4 %collective-permute-start.23 = (f32[256,256]{1,0:T(8,128)S(1)}, f32[256,256]{1,0:T(8,128)S(1)}, u32[]{:S(2)}, u32[]{:S(2)}) collective-permute-start(f32[256,256]{1,0:T(8,128)S(1)} %get-tuple-element.62), channel_id=1, source_target_pairs={{0,6},{1,7},{2,0},{3,1},{4,2},{5,3},{6,4},{7,5},{8,14},{9,15},{10,... | collective-permute-start | bytes 786440 | tf_op jit(solution)/shard_map/ppermute | solution.py:48
  153.2 8.3 %collective-permute-start.24 = (f32[256,256]{1,0:T(8,128)S(1)}, f32[256,256]{1,0:T(8,128)S(1)}, u32[]{:S(2)}, u32[]{:S(2)}) collective-permute-start(f32[256,256]{1,0:T(8,128)S(1)} %ghost_sum.3), channel_id=1, source_target_pairs={{0,112},{1,113},{2,114},{3,115},{4,116},{5,117},{6,118},{7,119},{8... | collective-permute-start | bytes 786440 | tf_op jit(solution)/shard_map/ppermute | solution.py:52
  (17 other events, 111.0 us)
Sparse Core Ops, SparseCore 0:
  36.5 34.9 all-gather.2
  108.9 41.6 all-gather.4

commit v10 on v9

--- a/solution.py
+++ b/solution.py
@@ -33,7 +33,6 @@
 
 OTHER_CORE = [(t, t ^ 1) for t in range(TILES)]
 OTHER_HALF = [(t, t ^ 8) for t in range(TILES)]
-BY_HALF = [list(range(8)), list(range(8, 16))]
 
 
 def to_lift(steps, flip):
@@ -167,16 +166,34 @@
 
 
 def from_below(table, px, py, tops, picked, sems):
-    def fetch(k):
+    def place(k):
         source, tile = table[k], table[4]
         x_step = ((source >> 3) ^ (tile >> 3)) & 1
-        return pltpu.make_async_copy(tops.at[(source & 7) * 2 + x_step], picked.at[k], sems.at[k])
+        y_step = ((source >> 1) - (tile >> 1)) & 3
+        return (source ^ tile) & 1, y_step, x_step
+
+    def fetch(plane, k):
+        return pltpu.make_async_copy(plane, picked.at[k], sems.at[k])
 
     for k in range(4):
-        fetch(k).start()
+        core_step, y_step, x_step = place(k)
+        for core in range(2):
+            pair, right, left, *far = tops[5 * core : 5 * core + 5]
+            for step, near in ((0, pair), (1, right), (3, left)):
+
+                @pl.when((core_step == core) & (y_step == step))
+                def _():
+                    fetch(near.at[x_step], k).start()
+
+            for half in range(2):
+
+                @pl.when((core_step == core) & (y_step == 2) & (x_step == half))
+                def _():
+                    fetch(far[half], k).start()
+
     total = jnp.zeros((W, W), F32)
     for k in range(4):
-        fetch(k).wait()
+        fetch(tops[3], k).wait()
         left = product(split(px[k]), split(picked[k]), ((1,), (0,)))
         total = total + product(split(left), split(py[k]), ((1,), (1,)))
     return jnp.where(table[5] == 1, total, 0.0)
@@ -199,8 +216,8 @@
     return ends[0] + TIME_STEP * (total + ends[1] * total)
 
 
-def below_kernel(table, px, py, field, speed, tops, *refs):
-    out, *scratch = refs[-4:]
+def below_kernel(table, px, py, field, speed, *refs):
+    tops, (out, *scratch) = refs[:10], refs[-4:]
     out[...] = below_value(table, px, py, field, speed, tops, *scratch)
 
 
@@ -215,16 +232,17 @@
     return pl.pallas_call(
         below_kernel,
         out_shape=planes(),
-        in_specs=[SMEM_SPEC] + [VMEM_SPEC] * 2 + [ANY_SPEC] * (3 + len(earlier)),
+        in_specs=[SMEM_SPEC] + [VMEM_SPEC] * 2 + [ANY_SPEC] * (12 + len(earlier)),
         out_specs=VMEM_SPEC,
         scratch_shapes=BELOW_SCRATCH,
         compiler_params=pltpu.CompilerParams(vmem_limit_bytes=50 * MIB),
         cost_estimate=SMALL,
         name="below",
-    )(table, px, py, field, speed, tops, *earlier)
-
-
-def fix_bottom_kernel(table, px, py, speed, tops, field, out, picked, ends, sems):
+    )(table, px, py, field, speed, *tops, *earlier)
+
+
+def fix_bottom_kernel(table, px, py, speed, *refs):
+    tops, (field, out, picked, ends, sems) = refs[:10], refs[10:]
     ends[0] = below_value(table, px, py, field, speed, tops, picked, ends, sems)
     copy = pltpu.make_async_copy(ends.at[0], out.at[0], sems.at[6])
     copy.start()
@@ -235,14 +253,14 @@
     return pl.pallas_call(
         fix_bottom_kernel,
         out_shape=planes(NZ),
-        in_specs=[SMEM_SPEC] + [VMEM_SPEC] * 2 + [ANY_SPEC] * 2 + [pl.BlockSpec(memory_space=pltpu.HBM)],
+        in_specs=[SMEM_SPEC] + [VMEM_SPEC] * 2 + [ANY_SPEC] * 11 + [pl.BlockSpec(memory_space=pltpu.HBM)],
         out_specs=pl.BlockSpec(memory_space=pltpu.HBM),
         scratch_shapes=BELOW_SCRATCH,
-        input_output_aliases={5: 0},
+        input_output_aliases={14: 0},
         compiler_params=pltpu.CompilerParams(vmem_limit_bytes=50 * MIB),
         cost_estimate=SMALL,
         name="fix_bottom",
-    )(table, px, py, speed, tops, field)
+    )(table, px, py, speed, *tops, field)
 
 
 def fix_top_kernel(table, ghost, field, out, plane, sems):
@@ -297,7 +315,9 @@
     )(field, bottom, top, *earlier)
 
 
-def stencil_kernel(inverse, inside, field, bottom, top, speed, inlets, x_low, x_high, y_low, y_high, out, mark, low, high, fast, sems):
+def stencil_kernel(inverse, inside, field, bottom, top, speed, inlets, x_low, x_high, y_low, y_high, *refs):
+    out, mark, low, high, fast, sems = refs[-6:]
+
     def fetch(z):
         return pltpu.make_async_copy(speed.at[z], fast.at[z], sems.at[z])
 
@@ -341,18 +361,18 @@
     out[NZ - 1] = update(NZ - 1, top[...], field[NZ - 2], zero)
 
 
-def stencil(inverse, inside, field, bottom, top, speed, inlets, halos):
+def stencil(inverse, inside, field, bottom, top, speed, inlets, halos, *earlier):
     return pl.pallas_call(
         stencil_kernel,
         out_shape=(planes(NZ), MARK),
-        in_specs=[SMEM_SPEC] * 2 + [VMEM_SPEC] * 3 + [ANY_SPEC] + [VMEM_SPEC] * 5,
+        in_specs=[SMEM_SPEC] * 2 + [VMEM_SPEC] * 3 + [ANY_SPEC] + [VMEM_SPEC] * 5 + [ANY_SPEC] * len(earlier),
         out_specs=[VMEM_SPEC] * 2,
         scratch_shapes=[pltpu.VMEM((W, 128), F32)] * 2
         + [pltpu.VMEM((NZ, W, W), F32), pltpu.SemaphoreType.DMA((NZ,))],
         compiler_params=pltpu.CompilerParams(vmem_limit_bytes=24 * MIB),
         cost_estimate=SMALL,
         name="stencil",
-    )(inverse, inside, field, bottom, top, speed, inlets, *halos)
+    )(inverse, inside, field, bottom, top, speed, inlets, *halos, *earlier)
 
 
 def exchange_rims(rims):
@@ -370,8 +390,22 @@
     return send_lift(plane, 1, False), send_lift(plane, 1, True)
 
 
-def gather_pair(pair):
-    return lax.all_gather(pair, "tile", axis_index_groups=BY_HALF, axis=0, tiled=True)
+def other_core(value):
+    return lax.ppermute(value, "tile", OTHER_CORE)
+
+
+def gather_near(pair):
+    return send_y(pair, -1), send_y(pair, 1)
+
+
+def far_body(right, left, mine, flip):
+    mine[...] = left[0]
+    flip[...] = right[1]
+
+
+def gather_far(near, *earlier):
+    mine, flip = small_kernel(far_body, "far_planes", (planes(), planes()), near, earlier)
+    return send_y(mine, 1), send_y(flip, -1)
 
 
 def reduce_cores(give, keep, body, *counts, earlier=()):
@@ -412,9 +446,13 @@
     give, keep, mark = pieces_of(table, px, py, bottom)
     halos = exchange_rims(rims_of(field, bottom, top, mark))
     give, keep = reduce_cores(give, keep, whole_cores_body, 4, earlier=halos)
-    tops = gather_pair(small_kernel(pair_body, "pair", planes(2), (mine, flip), (give,)))
+    pair = small_kernel(pair_body, "pair", planes(2), (mine, flip), (give,))
+    near = gather_near(pair)
     got = reduce_halves(give)
     field, mark = stencil(inverse, inside, field, bottom, top, speed, inlets, halos)
+    far = gather_far(near, mark)
+    tops = [pair, *near, *far]
+    tops = tops + [other_core(value) for value in tops]
     high = field[NZ - 1]
     mine, flip = climb(high)
     parts = reduce_ring(keep, [got], mark)
@@ -427,12 +465,15 @@
     ghost_above = send_lift(ghost, -1, False)
     earlier = (got_near, ghost_above)
     pair = small_kernel(new_pair_body, "new_pair", planes(2), (mine, flip, ghost, other_ghost), earlier)
-    tops = gather_pair(pair)
+    near = gather_near(pair)
+    far = gather_far(near)
+    tops = [pair, *near, *far]
+    tops = tops + [other_core(value) for value in tops]
     top = high + TIME_STEP * jnp.where(is_top, AMBIENT, ghost_above)
     got_far = reduce_halves(give_far)
     halos = exchange_rims(rims_of(field, bottom, top))
-    field, mark = stencil(inverse, inside, field, bottom, top, speed, inlets, halos)
-    parts = reduce_ring(keep, [got_near, got_far], *halos)
+    field, mark = stencil(inverse, inside, field, bottom, top, speed, inlets, halos, *far)
+    parts = reduce_ring(keep, [got_near, got_far], *halos, *near)
     ghost = send_lift(ghost_sum(parts, mark), -1, False)
     field = fix_bottom(table, px, py, speed, tops, field)
     field = fix_top(table, ghost, field)

time: 172 us -> 197 us (1.15)
  waiting for transfers between devices: 44.9 us -> 76.7 us
  starting transfers between devices: 44.8 us -> 62.8 us
  between operations: 14.3 us -> 1.12 us
  local copies, waits for them, and re-layouts: 19.7 us -> 11.7 us
  Pallas kernels: 45.2 us -> 42 us
    ppermute x6, waiting for transfers between devices: 9.59 us -> 30.6 us  [send_lift(): return lax.ppermute(value, ('lift', 'tile'), to_lift(steps, flip))]
    ppermute x6 -> x14, waiting for transfers between devices: 9.62 us -> 27.4 us  [send_y(): return lax.ppermute(value, 'tile', along_y(steps))]
    ppermute x6 -> x14, starting transfers between devices: 10.7 us -> 21 us  [send_y(): return lax.ppermute(value, 'tile', along_y(steps))]
    ppermute x6, starting transfers between devices: 7.06 us -> 16.2 us  [send_lift(): return lax.ppermute(value, ('lift', 'tile'), to_lift(steps, flip))]
    unnamed x42 -> x28, local copies, waits for them, and re-layouts: 17.9 us -> 10.6 us
    ppermute x4, starting transfers between devices: 11.5 us -> 7.93 us  [reduce_halves(): return lax.ppermute(give, 'tile', OTHER_HALF)]
    ppermute x4, waiting for transfers between devices: 11.1 us -> 7.65 us  [reduce_halves(): return lax.ppermute(give, 'tile', OTHER_HALF)]
    pallas_call x8 -> x10, Pallas kernels: 6.58 us -> 3.19 us  [small_kernel(): pl.pallas_call(kernel, out_shape=out_shape, in_specs=[VMEM_SPEC] * count...]
  transfers between devices with their start and end apart: 28 -> 44, of which waited for: 13 -> 15; matrix products, arithmetic and copies ran while one was open for 1% -> 0% of each run, Pallas kernels for 20% -> 16%
where the time goes in v10:
time: 197 us; the launch traced here: 195 us
  waiting for transfers between devices  76.7 us (39%)
  starting transfers between devices  62.8 us (32%)
  Pallas kernels  42 us (21%)
  local copies, waits for them, and re-layouts  11.7 us (6%)
    ppermute x6, waiting for transfers between devices, send_lift(): return lax.ppermute(value, ('lift', 'tile'), to_lift(steps, flip))  30.6 us
    ppermute x14, waiting for transfers between devices, send_y(): return lax.ppermute(value, 'tile', along_y(steps))  27.4 us
    ppermute x14, starting transfers between devices, send_y(): return lax.ppermute(value, 'tile', along_y(steps))  21 us
    pallas_call x2, Pallas kernels, stencil(): pl.pallas_call(stencil_kernel, out_shape=(planes(NZ), MARK), in_specs=[SM...  17.6 us
    ppermute x6, starting transfers between devices, send_lift(): return lax.ppermute(value, ('lift', 'tile'), to_lift(steps, flip))  16.2 us
    unnamed x28, local copies, waits for them, and re-layouts  10.6 us
    ppermute x4, starting transfers between devices, reduce_halves(): return lax.ppermute(give, 'tile', OTHER_HALF)  7.93 us
    ppermute x2, waiting for transfers between devices, exchange_rims(): x_low = lax.ppermute(row_high, 'tile', up)  7.81 us
  transfers between devices with their start and end apart: 44, of which 15 were waited for; matrix products, arithmetic and copies ran while one was open for 0% of the time, Pallas kernels for 16%

profile of v10, /device:TPU:6, one launch (start us, length us, event | category | flops | bytes accessed | tf_op | source)
XLA Modules:
  0.0 195.2 jit_solution(4426759235243135638)
XLA Ops:
  4.3 3.4 %pieces.2 = (f32[8,256,256]{2,1,0:T(8,128)S(1)}, f32[8,256,256]{2,1,0:T(8,128)S(1)}, f32[8,128]{1,0:T(8,128)S(1)}) custom-call(s32[7]{0:T(128)S(1)} %pad_add_fusion.table, f32[4,256,256]{2,1,0:T(8,128)S(1)} %bitcast.33, f32[4,256,256]{2,1,0:T(8,128)S(1)} %bitcast.37, f32[256,256]{1,0:T(8,128)S(1)} %get-tuple-element.74.bottom), custom_call_target="tpu_custom_call" | custom-call | flops 1024 | bytes 1024 | tf_op jit(solution)/shard_map/pieces/pallas_call | solution.py:108
  11.3 3.2 %collective-permute-start = (f32[16,256]{1,0:T(8,128)S(1)}, f32[16,256]{1,0:T(8,128)S(1)}, u32[]{:S(2)}, u32[]{:S(2)}) collective-permute-start(f32[16,256]{1,0:T(8,128)S(1)} %get-tuple-element.40), channel_id=1, source_target_pairs={{0,4},{1,5},{2,6},{3,7},{4,8},{5,9},{6,10},{7,11},{8,12},{9,13},{1... | collective-permute-start | bytes 49160 | tf_op jit(solution)/shard_map/ppermute | solution.py:382
  14.5 2.7 %collective-permute-start.1 = (f32[16,256]{1,0:T(8,128)S(1)}, f32[16,256]{1,0:T(8,128)S(1)}, u32[]{:S(2)}, u32[]{:S(2)}) collective-permute-start(f32[16,256]{1,0:T(8,128)S(1)} %get-tuple-element.41), channel_id=1, source_target_pairs={{4,0},{5,1},{6,2},{7,3},{8,4},{9,5},{10,6},{11,7},{12,8},{13,9},{1... | collective-permute-start | bytes 49160 | tf_op jit(solution)/shard_map/ppermute | solution.py:383
  19.0 2.2 %collective-permute-start.4 = (f32[256,256]{1,0:T(8,128)S(1)}, f32[256,256]{1,0:T(8,128)S(1)}, u32[]{:S(2)}, u32[]{:S(2)}) collective-permute-start(f32[256,256]{1,0:T(8,128)S(1)} %get-tuple-element.73.top), channel_id=1, source_target_pairs={{0,16},{1,17},{2,18},{3,19},{4,20},{5,21},{6,22},{7,23},{8,24},{9,... | collective-permute-start | bytes 786440 | tf_op jit(solution)/shard_map/ppermute | solution.py:51
  25.7 4.6 %collective-permute-done.4.refs_0_ = f32[256,256]{1,0:T(8,128)S(1)} collective-permute-done((f32[256,256]{1,0:T(8,128)S(1)}, f32[256,256]{1,0:T(8,128)S(1)}, u32[]{:S(2)}, u32[]{:S(2)}) %collective-permute-start.4) | collective-permute-done | bytes 262176 | tf_op jit(solution)/shard_map/ppermute | solution.py:51
  30.4 20.5 %collective-permute-done.5.refs_1_ = f32[256,256]{1,0:T(8,128)S(1)} collective-permute-done((f32[256,256]{1,0:T(8,128)S(1)}, f32[256,256]{1,0:T(8,128)S(1)}, u32[]{:S(2)}, u32[]{:S(2)}) %collective-permute-start.5) | collective-permute-done | bytes 262176 | tf_op jit(solution)/shard_map/ppermute | solution.py:51
  50.9 4.2 %collective-permute-start.7 = (f32[2,256,256]{2,1,0:T(8,128)S(1)}, f32[2,256,256]{2,1,0:T(8,128)S(1)}, u32[]{:S(2)}, u32[]{:S(2)}) collective-permute-start(f32[2,256,256]{2,1,0:T(8,128)S(1)} %pair.1.refs_0_), channel_id=1, source_target_pairs={{0,6},{1,7},{2,0},{3,1},{4,2},{5,3},{6,4},{7,5},{8,14},{9,15},{10,... | collective-permute-start | bytes 1572872 | tf_op jit(solution)/shard_map/ppermute | solution.py:47
  55.9 2.2 %copy-done = f32[1,16,1,256,256]{4,3,2,1,0:T(8,128)S(1)} copy-done((f32[1,16,1,256,256]{4,3,2,1,0:T(8,128)S(1)}, f32[1,16,1,256,256]{4,3,2,1,0:T(8,128)}, u32[]{:S(2)}) %copy-start) | copy-done | bytes 4194328
  58.1 2.2 %copy-done.5 = f32[1,16,1,256,256]{4,3,2,1,0:T(8,128)S(1)} copy-done((f32[1,16,1,256,256]{4,3,2,1,0:T(8,128)S(1)}, f32[1,16,1,256,256]{4,3,2,1,0:T(8,128)}, u32[]{:S(2)}) %copy-start.5) | copy-done | bytes 4194328
  60.3 7.8 %stencil.2 = (f32[16,256,256]{2,1,0:T(8,128)S(1)}, f32[8,128]{1,0:T(8,128)S(1)}) custom-call(f32[1]{0:T(128)S(6)} %div.3.inverse, s32[4]{0:T(128)S(1)} %add_convert_fusion.inside, f32[16,256,256]{2,1,0:T(8,128)S(1)} %bitcast.30, f32[256,256]{1,0:T(8,128)S(1)} %get-tuple-element.74.bottom, f32[256,256]{1,0:T(8,128)S(1)} %get-tuple-element.73.top, ...), custom_call_target="tpu_custom_call" | custom-call | flops 1024 | bytes 1024 | tf_op jit(solution)/shard_map/stencil/pallas_call | solution.py:365
  69.0 2.7 %collective-permute-start.10 = (f32[256,256]{1,0:T(8,128)S(1)}, f32[256,256]{1,0:T(8,128)S(1)}, u32[]{:S(2)}, u32[]{:S(2)}) collective-permute-start(f32[256,256]{1,0:T(8,128)S(1)} %get-tuple-element.50), channel_id=1, source_target_pairs={{0,6},{1,7},{2,0},{3,1},{4,2},{5,3},{6,4},{7,5},{8,14},{9,15},{10,... | collective-permute-start | bytes 786440 | tf_op jit(solution)/shard_map/ppermute | solution.py:47
  71.8 6.7 %collective-permute-done.9.refs_3_ = f32[256,256]{1,0:T(8,128)S(1)} collective-permute-done((f32[256,256]{1,0:T(8,128)S(1)}, f32[256,256]{1,0:T(8,128)S(1)}, u32[]{:S(2)}, u32[]{:S(2)}) %collective-permute-start.9) | collective-permute-done | bytes 262176 | tf_op jit(solution)/shard_map/ppermute | solution.py:47
  80.5 2.3 %collective-permute-start.17 = (f32[256,256]{1,0:T(8,128)S(1)}, f32[256,256]{1,0:T(8,128)S(1)}, u32[]{:S(2)}, u32[]{:S(2)}) collective-permute-start(f32[256,256]{1,0:T(8,128)S(1)} %slice_bitcast_fusion), channel_id=1, source_target_pairs={{0,16},{1,17},{2,18},{3,19},{4,20},{5,21},{6,22},{7,23},{8,24},{9,... | collective-permute-start | bytes 786440 | tf_op jit(solution)/shard_map/ppermute | solution.py:51
  82.7 2.4 %collective-permute-start.18 = (f32[256,256]{1,0:T(8,128)S(1)}, f32[256,256]{1,0:T(8,128)S(1)}, u32[]{:S(2)}, u32[]{:S(2)}) collective-permute-start(f32[256,256]{1,0:T(8,128)S(1)} %slice_bitcast_fusion), channel_id=1, source_target_pairs={{0,24},{1,25},{2,26},{3,27},{4,28},{5,29},{6,30},{7,31},{8,16},{9,... | collective-permute-start | bytes 786440 | tf_op jit(solution)/shard_map/ppermute | solution.py:51
  86.2 2.2 %collective-permute-start.20 = (f32[256,256]{1,0:T(8,128)S(1)}, f32[256,256]{1,0:T(8,128)S(1)}, u32[]{:S(2)}, u32[]{:S(2)}) collective-permute-start(f32[256,256]{1,0:T(8,128)S(1)} %get-tuple-element.54), channel_id=1, source_target_pairs={{0,6},{1,7},{2,0},{3,1},{4,2},{5,3},{6,4},{7,5},{8,14},{9,15},{10,... | collective-permute-start | bytes 786440 | tf_op jit(solution)/shard_map/ppermute | solution.py:47
  89.2 4.2 %below.1.bottom = f32[256,256]{1,0:T(8,128)S(1)} custom-call(s32[7]{0:T(128)S(1)} %pad_add_fusion.table, f32[4,256,256]{2,1,0:T(8,128)} %bitcast.31, f32[4,256,256]{2,1,0:T(8,128)} %bitcast.35, f32[16,256,256]{2,1,0:T(8,128)} %copy-done.2, f32[16,256,256]{2,1,0:T(8,128)} %bitcast.25, f32[2,256,256]{2,1,0:T(8,128)S(1)} %pair.1.refs_0_, ...), custom_call_target="tpu_custom_call" | custom-call | flops 1024 | bytes 1024 | tf_op jit(solution)/shard_map/below/pallas_call | solution.py:232
  94.8 4.0 %pieces.3 = (f32[8,256,256]{2,1,0:T(8,128)S(1)}, f32[8,256,256]{2,1,0:T(8,128)S(1)}, f32[8,128]{1,0:T(8,128)}) custom-call(s32[7]{0:T(128)S(1)} %pad_add_fusion.table, f32[4,256,256]{2,1,0:T(8,128)S(1)} %bitcast.34, f32[4,256,256]{2,1,0:T(8,128)S(1)} %bitcast.38, f32[256,256]{1,0:T(8,128)S(1)} %below.1.bottom, ...), custom_call_target="tpu_custom_call" | custom-call | flops 1024 | bytes 1024 | tf_op jit(solution)/shard_map/pieces/pallas_call | solution.py:108
  98.8 2.5 %collective-permute-start.24 = (f32[256,256]{1,0:T(8,128)S(1)}, f32[256,256]{1,0:T(8,128)S(1)}, u32[]{:S(2)}, u32[]{:S(2)}) collective-permute-start(f32[256,256]{1,0:T(8,128)S(1)} %get-tuple-element.60), channel_id=1, source_target_pairs={{0,4},{1,5},{2,6},{3,7},{4,0},{5,1},{6,2},{7,3},{8,12},{9,13},{10,... | collective-permute-start | bytes 786440 | tf_op jit(solution)/shard_map/ppermute | solution.py:47
  103.2 2.3 %collective-permute-start.22 = (f32[1,256,256]{2,1,0:T(8,128)S(1)}, f32[1,256,256]{2,1,0:T(8,128)S(1)}, u32[]{:S(2)}, u32[]{:S(2)}) collective-permute-start(f32[1,256,256]{2,1,0:T(8,128)S(1)} %get-tuple-element.58.refs_4_), channel_id=1, source_target_pairs={{0,8},{1,9},{2,10},{3,11},{4,12},{5,13},{6,14},{7,15},{8,0},{9,1},... | collective-permute-start | bytes 786440 | tf_op jit(solution)/shard_map/ppermute | solution.py:418
  105.5 3.6 %collective-permute-done.24.refs_2_ = f32[256,256]{1,0:T(8,128)S(1)} collective-permute-done((f32[256,256]{1,0:T(8,128)S(1)}, f32[256,256]{1,0:T(8,128)S(1)}, u32[]{:S(2)}, u32[]{:S(2)}) %collective-permute-start.24) | collective-permute-done | bytes 262176 | tf_op jit(solution)/shard_map/ppermute | solution.py:47
  109.1 6.2 %collective-permute-start.25 = (f32[256,256]{1,0:T(8,128)S(1)}, f32[256,256]{1,0:T(8,128)S(1)}, u32[]{:S(2)}, u32[]{:S(2)}) collective-permute-start(f32[256,256]{1,0:T(8,128)S(1)} %ghost_sum.2.refs_2_), channel_id=1, source_target_pairs={{0,112},{1,113},{2,114},{3,115},{4,116},{5,117},{6,118},{7,119},{8... | collective-permute-start | bytes 786440 | tf_op jit(solution)/shard_map/ppermute | solution.py:51
  118.8 3.4 %collective-permute-done.25.refs_5_ = f32[256,256]{1,0:T(8,128)S(1)} collective-permute-done((f32[256,256]{1,0:T(8,128)S(1)}, f32[256,256]{1,0:T(8,128)S(1)}, u32[]{:S(2)}, u32[]{:S(2)}) %collective-permute-start.25) | collective-permute-done | bytes 262176 | tf_op jit(solution)/shard_map/ppermute | solution.py:51
  122.2 7.6 %collective-permute-done.30.refs_3_ = f32[256,256]{1,0:T(8,128)S(1)} collective-permute-done((f32[256,256]{1,0:T(8,128)S(1)}, f32[256,256]{1,0:T(8,128)S(1)}, u32[]{:S(2)}, u32[]{:S(2)}) %collective-permute-start.30) | collective-permute-done | bytes 262176 | tf_op jit(solution)/shard_map/ppermute | solution.py:418
  129.9 2.6 %collective-permute-start.31 = (f32[2,256,256]{2,1,0:T(8,128)S(1)}, f32[2,256,256]{2,1,0:T(8,128)S(1)}, u32[]{:S(2)}, u32[]{:S(2)}) collective-permute-start(f32[2,256,256]{2,1,0:T(8,128)S(1)} %new_pair.1.refs_0_), channel_id=1, source_target_pairs={{0,6},{1,7},{2,0},{3,1},{4,2},{5,3},{6,4},{7,5},{8,14},{9,15},{10,... | collective-permute-start | bytes 1572872 | tf_op jit(solution)/shard_map/ppermute | solution.py:47
  135.8 4.0 %collective-permute-start.27 = (f32[16,256]{1,0:T(8,128)S(1)}, f32[16,256]{1,0:T(8,128)S(1)}, u32[]{:S(2)}, u32[]{:S(2)}) collective-permute-start(f32[16,256]{1,0:T(8,128)S(1)} %get-tuple-element.62), channel_id=1, source_target_pairs={{4,0},{5,1},{6,2},{7,3},{8,4},{9,5},{10,6},{11,7},{12,8},{13,9},{1... | collective-permute-start | bytes 49160 | tf_op jit(solution)/shard_map/ppermute | solution.py:383
  139.8 7.8 %collective-permute-done.26.refs_3_.x_low = f32[16,256]{1,0:T(8,128)S(1)} collective-permute-done((f32[16,256]{1,0:T(8,128)S(1)}, f32[16,256]{1,0:T(8,128)S(1)}, u32[]{:S(2)}, u32[]{:S(2)}) %collective-permute-start.26) | collective-permute-done | bytes 16416 | tf_op jit(solution)/shard_map/ppermute | solution.py:382
  152.2 3.2 %collective-permute-start.37 = (f32[256,256]{1,0:T(8,128)S(1)}, f32[256,256]{1,0:T(8,128)S(1)}, u32[]{:S(2)}, u32[]{:S(2)}) collective-permute-start(f32[256,256]{1,0:T(8,128)S(1)} %get-tuple-element.70), channel_id=1, source_target_pairs={{0,6},{1,7},{2,0},{3,1},{4,2},{5,3},{6,4},{7,5},{8,14},{9,15},{10,... | collective-permute-start | bytes 786440 | tf_op jit(solution)/shard_map/ppermute | solution.py:47
  156.4 4.8 %collective-permute-done.33.refs_1_ = f32[256,256]{1,0:T(8,128)S(1)} collective-permute-done((f32[256,256]{1,0:T(8,128)S(1)}, f32[256,256]{1,0:T(8,128)S(1)}, u32[]{:S(2)}, u32[]{:S(2)}) %collective-permute-start.33) | collective-permute-done | bytes 262176 | tf_op jit(solution)/shard_map/ppermute | solution.py:47
  161.2 11.2 %collective-permute-done.36.refs_0_.refs_3_ = f32[256,256]{1,0:T(8,128)S(1)} collective-permute-done((f32[256,256]{1,0:T(8,128)S(1)}, f32[256,256]{1,0:T(8,128)S(1)}, u32[]{:S(2)}, u32[]{:S(2)}) %collective-permute-start.36) | collective-permute-done | bytes 262176 | tf_op jit(solution)/shard_map/ppermute | solution.py:47
  173.0 9.8 %stencil.3 = (f32[16,256,256]{2,1,0:T(8,128)}, f32[8,128]{1,0:T(8,128)S(1)}) custom-call(f32[1]{0:T(128)S(6)} %div.3.inverse, s32[4]{0:T(128)S(1)} %add_convert_fusion.inside, f32[16,256,256]{2,1,0:T(8,128)S(1)} %copy-done.3, f32[256,256]{1,0:T(8,128)S(1)} %below.1.bottom, f32[256,256]{1,0:T(8,128)S(1)} %multiply_add_fusion.top, ...), custom_call_target="tpu_custom_call" | custom-call | flops 1024 | bytes 1024 | tf_op jit(solution)/shard_map/stencil/pallas_call | solution.py:365
  186.3 4.8 %fix_bottom.1.field = f32[16,256,256]{2,1,0:T(8,128)} custom-call(s32[7]{0:T(128)S(1)} %pad_add_fusion.table, f32[4,256,256]{2,1,0:T(8,128)} %bitcast.32, f32[4,256,256]{2,1,0:T(8,128)} %bitcast.36, f32[16,256,256]{2,1,0:T(8,128)} %bitcast.26, f32[2,256,256]{2,1,0:T(8,128)S(1)} %new_pair.1.refs_0_, ...), custom_call_target="tpu_custom_call", output_to_operand_aliasing={{}: (14, {})} | custom-call | flops 1024 | bytes 1024 | tf_op jit(solution)/shard_map/fix_bottom/pallas_call | solution.py:253
  192.7 2.2 %fix_top.1 = f32[16,256,256]{2,1,0:T(8,128)} custom-call(s32[7]{0:T(128)S(1)} %pad_add_fusion.table, f32[256,256]{1,0:T(8,128)S(1)} %collective-permute-done.38.ghost, f32[16,256,256]{2,1,0:T(8,128)} %fix_bottom.1.field), custom_call_target="tpu_custom_call", output_to_operand_aliasing={{}: (2, {})} | custom-call | flops 1024 | bytes 1024 | tf_op jit(solution)/shard_map/fix_top/pallas_call | solution.py:277
  (109 shorter events, 40.5 us)
Async XLA Ops:
  7.7 14.6 %collective-permute-start.6 = (f32[8,256,256]{2,1,0:T(8,128)S(1)}, f32[8,256,256]{2,1,0:T(8,128)S(1)}, u32[]{:S(2)}, u32[]{:S(2)}) collective-permute-start(f32[8,256,256]{2,1,0:T(8,128)S(1)} %get-tuple-element.46), channel_id=1, source_target_pairs={{0,1},{1,0},{2,3},{3,2},{4,5},{5,4},{6,7},{7,6},{8,9},{9,8},{10,11... | collective-permute-start | bytes 6291464 | tf_op jit(solution)/shard_map/ppermute | solution.py:412
  19.0 11.4 %collective-permute-start.4 = (f32[256,256]{1,0:T(8,128)S(1)}, f32[256,256]{1,0:T(8,128)S(1)}, u32[]{:S(2)}, u32[]{:S(2)}) collective-permute-start(f32[256,256]{1,0:T(8,128)S(1)} %get-tuple-element.73.top), channel_id=1, source_target_pairs={{0,16},{1,17},{2,18},{3,19},{4,20},{5,21},{6,22},{7,23},{8,24},{9,... | collective-permute-start | bytes 786440 | tf_op jit(solution)/shard_map/ppermute | solution.py:51
  21.2 29.7 %collective-permute-start.5 = (f32[256,256]{1,0:T(8,128)S(1)}, f32[256,256]{1,0:T(8,128)S(1)}, u32[]{:S(2)}, u32[]{:S(2)}) collective-permute-start(f32[256,256]{1,0:T(8,128)S(1)} %get-tuple-element.73.top), channel_id=1, source_target_pairs={{0,24},{1,25},{2,26},{3,27},{4,28},{5,29},{6,30},{7,31},{8,16},{9,... | collective-permute-start | bytes 786440 | tf_op jit(solution)/shard_map/ppermute | solution.py:51
  23.6 55.4 %collective-permute-start.16 = (f32[4,256,256]{2,1,0:T(8,128)}, f32[4,256,256]{2,1,0:T(8,128)}, u32[]{:S(2)}, u32[]{:S(2)}) collective-permute-start(f32[4,256,256]{2,1,0:T(8,128)} %get-tuple-element.47.refs_2_), channel_id=1, source_target_pairs={{0,8},{1,9},{2,10},{3,11},{4,12},{5,13},{6,14},{7,15},{8,0},{9,1},... | collective-permute-start | bytes 3145736 | tf_op jit(solution)/shard_map/ppermute | solution.py:418
  50.9 17.2 %collective-permute-start.7 = (f32[2,256,256]{2,1,0:T(8,128)S(1)}, f32[2,256,256]{2,1,0:T(8,128)S(1)}, u32[]{:S(2)}, u32[]{:S(2)}) collective-permute-start(f32[2,256,256]{2,1,0:T(8,128)S(1)} %pair.1.refs_0_), channel_id=1, source_target_pairs={{0,6},{1,7},{2,0},{3,1},{4,2},{5,3},{6,4},{7,5},{8,14},{9,15},{10,... | collective-permute-start | bytes 1572872 | tf_op jit(solution)/shard_map/ppermute | solution.py:47
  55.1 13.2 %collective-permute-start.8 = (f32[2,256,256]{2,1,0:T(8,128)S(1)}, f32[2,256,256]{2,1,0:T(8,128)S(1)}, u32[]{:S(2)}, u32[]{:S(2)}) collective-permute-start(f32[2,256,256]{2,1,0:T(8,128)S(1)} %pair.1.refs_0_), channel_id=1, source_target_pairs={{0,2},{1,3},{2,4},{3,5},{4,6},{5,7},{6,0},{7,1},{8,10},{9,11},{10,... | collective-permute-start | bytes 1572872 | tf_op jit(solution)/shard_map/ppermute | solution.py:47
  68.1 12.4 %collective-permute-start.11 = (f32[2,256,256]{2,1,0:T(8,128)S(1)}, f32[2,256,256]{2,1,0:T(8,128)S(1)}, u32[]{:S(2)}, u32[]{:S(2)}) collective-permute-start(f32[2,256,256]{2,1,0:T(8,128)S(1)} %pair.1.refs_0_), channel_id=1, source_target_pairs={{0,1},{1,0},{2,3},{3,2},{4,5},{5,4},{6,7},{7,6},{8,9},{9,8},{10,11... | collective-permute-start | bytes 1572872 | tf_op jit(solution)/shard_map/ppermute | solution.py:394
  68.4 10.1 %collective-permute-start.9 = (f32[256,256]{1,0:T(8,128)S(1)}, f32[256,256]{1,0:T(8,128)S(1)}, u32[]{:S(2)}, u32[]{:S(2)}) collective-permute-start(f32[256,256]{1,0:T(8,128)S(1)} %get-tuple-element.49), channel_id=1, source_target_pairs={{0,2},{1,3},{2,4},{3,5},{4,6},{5,7},{6,0},{7,1},{8,10},{9,11},{10,... | collective-permute-start | bytes 786440 | tf_op jit(solution)/shard_map/ppermute | solution.py:47
  69.0 9.5 %collective-permute-start.10 = (f32[256,256]{1,0:T(8,128)S(1)}, f32[256,256]{1,0:T(8,128)S(1)}, u32[]{:S(2)}, u32[]{:S(2)}) collective-permute-start(f32[256,256]{1,0:T(8,128)S(1)} %get-tuple-element.50), channel_id=1, source_target_pairs={{0,6},{1,7},{2,0},{3,1},{4,2},{5,3},{6,4},{7,5},{8,14},{9,15},{10,... | collective-permute-start | bytes 786440 | tf_op jit(solution)/shard_map/ppermute | solution.py:47
  71.7 14.5 %collective-permute-start.12 = (f32[2,256,256]{2,1,0:T(8,128)S(1)}, f32[2,256,256]{2,1,0:T(8,128)S(1)}, u32[]{:S(2)}, u32[]{:S(2)}) collective-permute-start(f32[2,256,256]{2,1,0:T(8,128)S(1)} %collective-permute-done.7.refs_0_.refs_1_), channel_id=1, source_target_pairs={{0,1},{1,0},{2,3},{3,2},{4,5},{5,4},{6,7},{7,6},{8,9},{9,8},{10,11... | collective-permute-start | bytes 1572872 | tf_op jit(solution)/shard_map/ppermute | solution.py:394
  78.5 9.9 %collective-permute-start.13 = (f32[2,256,256]{2,1,0:T(8,128)S(1)}, f32[2,256,256]{2,1,0:T(8,128)S(1)}, u32[]{:S(2)}, u32[]{:S(2)}) collective-permute-start(f32[2,256,256]{2,1,0:T(8,128)S(1)} %collective-permute-done.8.refs_1_.refs_2_), channel_id=1, source_target_pairs={{0,1},{1,0},{2,3},{3,2},{4,5},{5,4},{6,7},{7,6},{8,9},{9,8},{10,11... | collective-permute-start | bytes 1572872 | tf_op jit(solution)/shard_map/ppermute | solution.py:394
  80.5 13.0 %collective-permute-start.17 = (f32[256,256]{1,0:T(8,128)S(1)}, f32[256,256]{1,0:T(8,128)S(1)}, u32[]{:S(2)}, u32[]{:S(2)}) collective-permute-start(f32[256,256]{1,0:T(8,128)S(1)} %slice_bitcast_fusion), channel_id=1, source_target_pairs={{0,16},{1,17},{2,18},{3,19},{4,20},{5,21},{6,22},{7,23},{8,24},{9,... | collective-permute-start | bytes 786440 | tf_op jit(solution)/shard_map/ppermute | solution.py:51
  82.7 11.0 %collective-permute-start.18 = (f32[256,256]{1,0:T(8,128)S(1)}, f32[256,256]{1,0:T(8,128)S(1)}, u32[]{:S(2)}, u32[]{:S(2)}) collective-permute-start(f32[256,256]{1,0:T(8,128)S(1)} %slice_bitcast_fusion), channel_id=1, source_target_pairs={{0,24},{1,25},{2,26},{3,27},{4,28},{5,29},{6,30},{7,31},{8,16},{9,... | collective-permute-start | bytes 786440 | tf_op jit(solution)/shard_map/ppermute | solution.py:51
  85.2 9.6 %collective-permute-start.19 = (f32[256,256]{1,0:T(8,128)S(1)}, f32[256,256]{1,0:T(8,128)S(1)}, u32[]{:S(2)}, u32[]{:S(2)}) collective-permute-start(f32[256,256]{1,0:T(8,128)S(1)} %get-tuple-element.53), channel_id=1, source_target_pairs={{0,2},{1,3},{2,4},{3,5},{4,6},{5,7},{6,0},{7,1},{8,10},{9,11},{10,... | collective-permute-start | bytes 786440 | tf_op jit(solution)/shard_map/ppermute | solution.py:47
  98.8 10.2 %collective-permute-start.24 = (f32[256,256]{1,0:T(8,128)S(1)}, f32[256,256]{1,0:T(8,128)S(1)}, u32[]{:S(2)}, u32[]{:S(2)}) collective-permute-start(f32[256,256]{1,0:T(8,128)S(1)} %get-tuple-element.60), channel_id=1, source_target_pairs={{0,4},{1,5},{2,6},{3,7},{4,0},{5,1},{6,2},{7,3},{8,12},{9,13},{10,... | collective-permute-start | bytes 786440 | tf_op jit(solution)/shard_map/ppermute | solution.py:47
  103.2 15.6 %collective-permute-start.22 = (f32[1,256,256]{2,1,0:T(8,128)S(1)}, f32[1,256,256]{2,1,0:T(8,128)S(1)}, u32[]{:S(2)}, u32[]{:S(2)}) collective-permute-start(f32[1,256,256]{2,1,0:T(8,128)S(1)} %get-tuple-element.58.refs_4_), channel_id=1, source_target_pairs={{0,8},{1,9},{2,10},{3,11},{4,12},{5,13},{6,14},{7,15},{8,0},{9,1},... | collective-permute-start | bytes 786440 | tf_op jit(solution)/shard_map/ppermute | solution.py:418
  109.1 13.1 %collective-permute-start.25 = (f32[256,256]{1,0:T(8,128)S(1)}, f32[256,256]{1,0:T(8,128)S(1)}, u32[]{:S(2)}, u32[]{:S(2)}) collective-permute-start(f32[256,256]{1,0:T(8,128)S(1)} %ghost_sum.2.refs_2_), channel_id=1, source_target_pairs={{0,112},{1,113},{2,114},{3,115},{4,116},{5,117},{6,118},{7,119},{8... | collective-permute-start | bytes 786440 | tf_op jit(solution)/shard_map/ppermute | solution.py:51
  115.3 14.6 %collective-permute-start.30 = (f32[256,256]{1,0:T(8,128)S(1)}, f32[256,256]{1,0:T(8,128)S(1)}, u32[]{:S(2)}, u32[]{:S(2)}) collective-permute-start(f32[256,256]{1,0:T(8,128)S(1)} %ghost_sum.2.refs_2_), channel_id=1, source_target_pairs={{0,8},{1,9},{2,10},{3,11},{4,12},{5,13},{6,14},{7,15},{8,0},{9,1},... | collective-permute-start | bytes 786440 | tf_op jit(solution)/shard_map/ppermute | solution.py:418
  117.0 33.8 %collective-permute-start.23 = (f32[3,256,256]{2,1,0:T(8,128)S(1)}, f32[3,256,256]{2,1,0:T(8,128)S(1)}, u32[]{:S(2)}, u32[]{:S(2)}) collective-permute-start(f32[3,256,256]{2,1,0:T(8,128)S(1)} %get-tuple-element.59), channel_id=1, source_target_pairs={{0,8},{1,9},{2,10},{3,11},{4,12},{5,13},{6,14},{7,15},{8,0},{9,1},... | collective-permute-start | bytes 2359304 | tf_op jit(solution)/shard_map/ppermute | solution.py:418
  129.9 20.9 %collective-permute-start.31 = (f32[2,256,256]{2,1,0:T(8,128)S(1)}, f32[2,256,256]{2,1,0:T(8,128)S(1)}, u32[]{:S(2)}, u32[]{:S(2)}) collective-permute-start(f32[2,256,256]{2,1,0:T(8,128)S(1)} %new_pair.1.refs_0_), channel_id=1, source_target_pairs={{0,6},{1,7},{2,0},{3,1},{4,2},{5,3},{6,4},{7,5},{8,14},{9,15},{10,... | collective-permute-start | bytes 1572872 | tf_op jit(solution)/shard_map/ppermute | solution.py:47
  132.5 18.3 %collective-permute-start.32 = (f32[2,256,256]{2,1,0:T(8,128)S(1)}, f32[2,256,256]{2,1,0:T(8,128)S(1)}, u32[]{:S(2)}, u32[]{:S(2)}) collective-permute-start(f32[2,256,256]{2,1,0:T(8,128)S(1)} %new_pair.1.refs_0_), channel_id=1, source_target_pairs={{0,2},{1,3},{2,4},{3,5},{4,6},{5,7},{6,0},{7,1},{8,10},{9,11},{10,... | collective-permute-start | bytes 1572872 | tf_op jit(solution)/shard_map/ppermute | solution.py:47
  133.8 13.8 %collective-permute-start.26 = (f32[16,256]{1,0:T(8,128)S(1)}, f32[16,256]{1,0:T(8,128)S(1)}, u32[]{:S(2)}, u32[]{:S(2)}) collective-permute-start(f32[16,256]{1,0:T(8,128)S(1)} %get-tuple-element.61), channel_id=1, source_target_pairs={{0,4},{1,5},{2,6},{3,7},{4,8},{5,9},{6,10},{7,11},{8,12},{9,13},{1... | collective-permute-start | bytes 49160 | tf_op jit(solution)/shard_map/ppermute | solution.py:382
  135.8 11.8 %collective-permute-start.27 = (f32[16,256]{1,0:T(8,128)S(1)}, f32[16,256]{1,0:T(8,128)S(1)}, u32[]{:S(2)}, u32[]{:S(2)}) collective-permute-start(f32[16,256]{1,0:T(8,128)S(1)} %get-tuple-element.62), channel_id=1, source_target_pairs={{4,0},{5,1},{6,2},{7,3},{8,4},{9,5},{10,6},{11,7},{12,8},{13,9},{1... | collective-permute-start | bytes 49160 | tf_op jit(solution)/shard_map/ppermute | solution.py:383
  150.9 10.3 %collective-permute-start.33 = (f32[256,256]{1,0:T(8,128)S(1)}, f32[256,256]{1,0:T(8,128)S(1)}, u32[]{:S(2)}, u32[]{:S(2)}) collective-permute-start(f32[256,256]{1,0:T(8,128)S(1)} %get-tuple-element.66), channel_id=1, source_target_pairs={{0,2},{1,3},{2,4},{3,5},{4,6},{5,7},{6,0},{7,1},{8,10},{9,11},{10,... | collective-permute-start | bytes 786440 | tf_op jit(solution)/shard_map/ppermute | solution.py:47
  152.1 20.4 %collective-permute-start.36 = (f32[256,256]{1,0:T(8,128)S(1)}, f32[256,256]{1,0:T(8,128)S(1)}, u32[]{:S(2)}, u32[]{:S(2)}) collective-permute-start(f32[256,256]{1,0:T(8,128)S(1)} %get-tuple-element.69), channel_id=1, source_target_pairs={{0,2},{1,3},{2,4},{3,5},{4,6},{5,7},{6,0},{7,1},{8,10},{9,11},{10,... | collective-permute-start | bytes 786440 | tf_op jit(solution)/shard_map/ppermute | solution.py:47
  152.2 20.4 %collective-permute-start.37 = (f32[256,256]{1,0:T(8,128)S(1)}, f32[256,256]{1,0:T(8,128)S(1)}, u32[]{:S(2)}, u32[]{:S(2)}) collective-permute-start(f32[256,256]{1,0:T(8,128)S(1)} %get-tuple-element.70), channel_id=1, source_target_pairs={{0,6},{1,7},{2,0},{3,1},{4,2},{5,3},{6,4},{7,5},{8,14},{9,15},{10,... | collective-permute-start | bytes 786440 | tf_op jit(solution)/shard_map/ppermute | solution.py:47
  155.4 28.0 %collective-permute-start.39 = (f32[2,256,256]{2,1,0:T(8,128)S(1)}, f32[2,256,256]{2,1,0:T(8,128)S(1)}, u32[]{:S(2)}, u32[]{:S(2)}) collective-permute-start(f32[2,256,256]{2,1,0:T(8,128)S(1)} %new_pair.1.refs_0_), channel_id=1, source_target_pairs={{0,1},{1,0},{2,3},{3,2},{4,5},{5,4},{6,7},{7,6},{8,9},{9,8},{10,11... | collective-permute-start | bytes 1572872 | tf_op jit(solution)/shard_map/ppermute | solution.py:394
  155.6 27.2 %collective-permute-start.34 = (f32[256,256]{1,0:T(8,128)S(1)}, f32[256,256]{1,0:T(8,128)S(1)}, u32[]{:S(2)}, u32[]{:S(2)}) collective-permute-start(f32[256,256]{1,0:T(8,128)S(1)} %get-tuple-element.67), channel_id=1, source_target_pairs={{0,4},{1,5},{2,6},{3,7},{4,0},{5,1},{6,2},{7,3},{8,12},{9,13},{10,... | collective-permute-start | bytes 786440 | tf_op jit(solution)/shard_map/ppermute | solution.py:47
  161.2 21.8 %collective-permute-start.35 = (f32[256,256]{1,0:T(8,128)S(1)}, f32[256,256]{1,0:T(8,128)S(1)}, u32[]{:S(2)}, u32[]{:S(2)}) collective-permute-start(f32[256,256]{1,0:T(8,128)S(1)} %get-tuple-element.68), channel_id=1, source_target_pairs={{0,6},{1,7},{2,0},{3,1},{4,2},{5,3},{6,4},{7,5},{8,14},{9,15},{10,... | collective-permute-start | bytes 786440 | tf_op jit(solution)/shard_map/ppermute | solution.py:47
  172.4 13.0 %collective-permute-start.40 = (f32[2,256,256]{2,1,0:T(8,128)S(1)}, f32[2,256,256]{2,1,0:T(8,128)S(1)}, u32[]{:S(2)}, u32[]{:S(2)}) collective-permute-start(f32[2,256,256]{2,1,0:T(8,128)S(1)} %collective-permute-done.31.refs_7_.refs_0_.refs_1_), channel_id=1, source_target_pairs={{0,1},{1,0},{2,3},{3,2},{4,5},{5,4},{6,7},{7,6},{8,9},{9,8},{10,11... | collective-permute-start | bytes 1572872 | tf_op jit(solution)/shard_map/ppermute | solution.py:394
  172.6 12.9 %collective-permute-start.41 = (f32[2,256,256]{2,1,0:T(8,128)S(1)}, f32[2,256,256]{2,1,0:T(8,128)S(1)}, u32[]{:S(2)}, u32[]{:S(2)}) collective-permute-start(f32[2,256,256]{2,1,0:T(8,128)S(1)} %collective-permute-done.32.refs_8_.refs_1_.refs_2_), channel_id=1, source_target_pairs={{0,1},{1,0},{2,3},{3,2},{4,5},{5,4},{6,7},{7,6},{8,9},{9,8},{10,11... | collective-permute-start | bytes 1572872 | tf_op jit(solution)/shard_map/ppermute | solution.py:394
  183.4 9.3 %collective-permute-start.38 = (f32[256,256]{1,0:T(8,128)S(1)}, f32[256,256]{1,0:T(8,128)S(1)}, u32[]{:S(2)}, u32[]{:S(2)}) collective-permute-start(f32[256,256]{1,0:T(8,128)S(1)} %ghost_sum.3), channel_id=1, source_target_pairs={{0,112},{1,113},{2,114},{3,115},{4,116},{5,117},{6,118},{7,119},{8... | collective-permute-start | bytes 786440 | tf_op jit(solution)/shard_map/ppermute | solution.py:51
  (26 other events, 218.1 us)

commit v11 on v10

--- a/solution.py
+++ b/solution.py
@@ -445,7 +445,7 @@
     mine, flip = climb(top)
     give, keep, mark = pieces_of(table, px, py, bottom)
     halos = exchange_rims(rims_of(field, bottom, top, mark))
-    give, keep = reduce_cores(give, keep, whole_cores_body, 4, earlier=halos)
+    give, keep = reduce_cores(give, keep, whole_cores_body, 4, earlier=(mine, flip, *halos))
     pair = small_kernel(pair_body, "pair", planes(2), (mine, flip), (give,))
     near = gather_near(pair)
     got = reduce_halves(give)
@@ -466,14 +466,14 @@
     earlier = (got_near, ghost_above)
     pair = small_kernel(new_pair_body, "new_pair", planes(2), (mine, flip, ghost, other_ghost), earlier)
     near = gather_near(pair)
-    far = gather_far(near)
-    tops = [pair, *near, *far]
-    tops = tops + [other_core(value) for value in tops]
     top = high + TIME_STEP * jnp.where(is_top, AMBIENT, ghost_above)
     got_far = reduce_halves(give_far)
     halos = exchange_rims(rims_of(field, bottom, top))
-    field, mark = stencil(inverse, inside, field, bottom, top, speed, inlets, halos, *far)
+    field, mark = stencil(inverse, inside, field, bottom, top, speed, inlets, halos)
     parts = reduce_ring(keep, [got_near, got_far], *halos, *near)
+    far = gather_far(near, mark)
+    tops = [pair, *near, *far]
+    tops = tops + [other_core(value) for value in tops]
     ghost = send_lift(ghost_sum(parts, mark), -1, False)
     field = fix_bottom(table, px, py, speed, tops, field)
     field = fix_top(table, ghost, field)

time: 197 us -> 165 us (0.84)
  waiting for transfers between devices: 76.7 us -> 49.7 us
  starting transfers between devices: 62.8 us -> 57.1 us
    ppermute x6, waiting for transfers between devices: 30.6 us -> 8.17 us  [send_lift(): return lax.ppermute(value, ('lift', 'tile'), to_lift(steps, flip))]
    ppermute x14, waiting for transfers between devices: 27.4 us -> 19.2 us  [send_y(): return lax.ppermute(value, 'tile', along_y(steps))]
    ppermute x6, starting transfers between devices: 16.2 us -> 12.3 us  [send_lift(): return lax.ppermute(value, ('lift', 'tile'), to_lift(steps, flip))]
    ppermute x2, waiting for transfers between devices: 7.81 us -> 10.7 us  [exchange_rims(): x_low = lax.ppermute(row_high, 'tile', up)]
  transfers between devices with their start and end apart: 44 -> 44, of which waited for: 15 -> 16; matrix products, arithmetic and copies ran while one was open for 0% -> 0% of each run, Pallas kernels for 16% -> 19%
where the time goes in v11:
time: 165 us; the launch traced here: 163 us
  starting transfers between devices  57.1 us (35%)
  waiting for transfers between devices  49.7 us (30%)
  Pallas kernels  42.4 us (26%)
  local copies, waits for them, and re-layouts  11.4 us (7%)
    ppermute x14, waiting for transfers between devices, send_y(): return lax.ppermute(value, 'tile', along_y(steps))  19.2 us
    ppermute x14, starting transfers between devices, send_y(): return lax.ppermute(value, 'tile', along_y(steps))  19.1 us
    pallas_call x2, Pallas kernels, stencil(): pl.pallas_call(stencil_kernel, out_shape=(planes(NZ), MARK), in_specs=[SM...  17.6 us
    ppermute x6, starting transfers between devices, send_lift(): return lax.ppermute(value, ('lift', 'tile'), to_lift(steps, flip))  12.3 us
    ppermute x2, waiting for transfers between devices, exchange_rims(): x_low = lax.ppermute(row_high, 'tile', up)  10.7 us
    unnamed x28, local copies, waits for them, and re-layouts  10.3 us
    ppermute x4, starting transfers between devices, reduce_halves(): return lax.ppermute(give, 'tile', OTHER_HALF)  8.4 us
    ppermute x6, waiting for transfers between devices, send_lift(): return lax.ppermute(value, ('lift', 'tile'), to_lift(steps, flip))  8.17 us
  transfers between devices with their start and end apart: 44, of which 16 were waited for; matrix products, arithmetic and copies ran while one was open for 0% of the time, Pallas kernels for 19%

profile of v11, /device:TPU:6, one launch (start us, length us, event | category | flops | bytes accessed | tf_op | source)
XLA Modules:
  0.0 162.5 jit_solution(1255452024401012880)
XLA Ops:
  4.3 3.4 %pieces.2 = (f32[8,256,256]{2,1,0:T(8,128)S(1)}, f32[8,256,256]{2,1,0:T(8,128)S(1)}, f32[8,128]{1,0:T(8,128)S(1)}) custom-call(s32[7]{0:T(128)S(1)} %pad_add_fusion.table, f32[4,256,256]{2,1,0:T(8,128)S(1)} %bitcast.33, f32[4,256,256]{2,1,0:T(8,128)S(1)} %bitcast.37, f32[256,256]{1,0:T(8,128)S(1)} %get-tuple-element.74.bottom), custom_call_target="tpu_custom_call" | custom-call | flops 1024 | bytes 1024 | tf_op jit(solution)/shard_map/pieces/pallas_call | solution.py:108
  7.8 2.2 %collective-permute-start.4 = (f32[256,256]{1,0:T(8,128)S(1)}, f32[256,256]{1,0:T(8,128)S(1)}, u32[]{:S(2)}, u32[]{:S(2)}) collective-permute-start(f32[256,256]{1,0:T(8,128)S(1)} %get-tuple-element.73.top), channel_id=1, source_target_pairs={{0,16},{1,17},{2,18},{3,19},{4,20},{5,21},{6,22},{7,23},{8,24},{9,... | collective-permute-start | bytes 786440 | tf_op jit(solution)/shard_map/ppermute | solution.py:51
  11.2 2.2 %copy-done.4 = f32[1,16,1,256,256]{4,3,2,1,0:T(8,128)S(1)} copy-done((f32[1,16,1,256,256]{4,3,2,1,0:T(8,128)S(1)}, f32[1,16,1,256,256]{4,3,2,1,0:T(8,128)}, u32[]{:S(2)}) %copy-start.4) | copy-done | bytes 4194328
  14.7 3.2 %collective-permute-start = (f32[16,256]{1,0:T(8,128)S(1)}, f32[16,256]{1,0:T(8,128)S(1)}, u32[]{:S(2)}, u32[]{:S(2)}) collective-permute-start(f32[16,256]{1,0:T(8,128)S(1)} %get-tuple-element.40), channel_id=1, source_target_pairs={{0,4},{1,5},{2,6},{3,7},{4,8},{5,9},{6,10},{7,11},{8,12},{9,13},{1... | collective-permute-start | bytes 49160 | tf_op jit(solution)/shard_map/ppermute | solution.py:382
  17.9 2.7 %collective-permute-start.1 = (f32[16,256]{1,0:T(8,128)S(1)}, f32[16,256]{1,0:T(8,128)S(1)}, u32[]{:S(2)}, u32[]{:S(2)}) collective-permute-start(f32[16,256]{1,0:T(8,128)S(1)} %get-tuple-element.41), channel_id=1, source_target_pairs={{4,0},{5,1},{6,2},{7,3},{8,4},{9,5},{10,6},{11,7},{12,8},{13,9},{1... | collective-permute-start | bytes 49160 | tf_op jit(solution)/shard_map/ppermute | solution.py:383
  20.6 2.9 %collective-permute-done.x_low.refs_4_ = f32[16,256]{1,0:T(8,128)S(1)} collective-permute-done((f32[16,256]{1,0:T(8,128)S(1)}, f32[16,256]{1,0:T(8,128)S(1)}, u32[]{:S(2)}, u32[]{:S(2)}) %collective-permute-start) | collective-permute-done | bytes 16416 | tf_op jit(solution)/shard_map/ppermute | solution.py:382
  28.0 3.2 %collective-permute-start.16 = (f32[4,256,256]{2,1,0:T(8,128)}, f32[4,256,256]{2,1,0:T(8,128)}, u32[]{:S(2)}, u32[]{:S(2)}) collective-permute-start(f32[4,256,256]{2,1,0:T(8,128)} %get-tuple-element.47.refs_2_), channel_id=1, source_target_pairs={{0,8},{1,9},{2,10},{3,11},{4,12},{5,13},{6,14},{7,15},{8,0},{9,1},... | collective-permute-start | bytes 3145736 | tf_op jit(solution)/shard_map/ppermute | solution.py:418
  34.1 2.2 %copy-done = f32[1,16,1,256,256]{4,3,2,1,0:T(8,128)S(1)} copy-done((f32[1,16,1,256,256]{4,3,2,1,0:T(8,128)S(1)}, f32[1,16,1,256,256]{4,3,2,1,0:T(8,128)}, u32[]{:S(2)}) %copy-start) | copy-done | bytes 4194328
  36.2 2.2 %copy-done.5 = f32[1,16,1,256,256]{4,3,2,1,0:T(8,128)S(1)} copy-done((f32[1,16,1,256,256]{4,3,2,1,0:T(8,128)S(1)}, f32[1,16,1,256,256]{4,3,2,1,0:T(8,128)}, u32[]{:S(2)}) %copy-start.5) | copy-done | bytes 4194328
  38.4 7.8 %stencil.2 = (f32[16,256,256]{2,1,0:T(8,128)S(1)}, f32[8,128]{1,0:T(8,128)S(1)}) custom-call(f32[1]{0:T(128)S(6)} %div.3.inverse, s32[4]{0:T(128)S(1)} %add_convert_fusion.inside, f32[16,256,256]{2,1,0:T(8,128)S(1)} %bitcast.30, f32[256,256]{1,0:T(8,128)S(1)} %get-tuple-element.74.bottom, f32[256,256]{1,0:T(8,128)S(1)} %get-tuple-element.73.top, ...), custom_call_target="tpu_custom_call" | custom-call | flops 1024 | bytes 1024 | tf_op jit(solution)/shard_map/stencil/pallas_call | solution.py:365
  47.7 2.7 %collective-permute-start.10 = (f32[256,256]{1,0:T(8,128)S(1)}, f32[256,256]{1,0:T(8,128)S(1)}, u32[]{:S(2)}, u32[]{:S(2)}) collective-permute-start(f32[256,256]{1,0:T(8,128)S(1)} %get-tuple-element.50), channel_id=1, source_target_pairs={{0,6},{1,7},{2,0},{3,1},{4,2},{5,3},{6,4},{7,5},{8,14},{9,15},{10,... | collective-permute-start | bytes 786440 | tf_op jit(solution)/shard_map/ppermute | solution.py:47
  50.4 6.0 %collective-permute-done.9.refs_3_ = f32[256,256]{1,0:T(8,128)S(1)} collective-permute-done((f32[256,256]{1,0:T(8,128)S(1)}, f32[256,256]{1,0:T(8,128)S(1)}, u32[]{:S(2)}, u32[]{:S(2)}) %collective-permute-start.9) | collective-permute-done | bytes 262176 | tf_op jit(solution)/shard_map/ppermute | solution.py:47
  59.1 3.1 %collective-permute-start.18 = (f32[256,256]{1,0:T(8,128)S(1)}, f32[256,256]{1,0:T(8,128)S(1)}, u32[]{:S(2)}, u32[]{:S(2)}) collective-permute-start(f32[256,256]{1,0:T(8,128)S(1)} %slice_bitcast_fusion), channel_id=1, source_target_pairs={{0,24},{1,25},{2,26},{3,27},{4,28},{5,29},{6,30},{7,31},{8,16},{9,... | collective-permute-start | bytes 786440 | tf_op jit(solution)/shard_map/ppermute | solution.py:51
  62.9 2.5 %collective-permute-start.20 = (f32[256,256]{1,0:T(8,128)S(1)}, f32[256,256]{1,0:T(8,128)S(1)}, u32[]{:S(2)}, u32[]{:S(2)}) collective-permute-start(f32[256,256]{1,0:T(8,128)S(1)} %get-tuple-element.54), channel_id=1, source_target_pairs={{0,6},{1,7},{2,0},{3,1},{4,2},{5,3},{6,4},{7,5},{8,14},{9,15},{10,... | collective-permute-start | bytes 786440 | tf_op jit(solution)/shard_map/ppermute | solution.py:47
  66.2 4.5 %below.1.bottom = f32[256,256]{1,0:T(8,128)S(1)} custom-call(s32[7]{0:T(128)S(1)} %pad_add_fusion.table, f32[4,256,256]{2,1,0:T(8,128)} %bitcast.31, f32[4,256,256]{2,1,0:T(8,128)} %bitcast.35, f32[16,256,256]{2,1,0:T(8,128)} %copy-done.2, f32[16,256,256]{2,1,0:T(8,128)} %bitcast.25, f32[2,256,256]{2,1,0:T(8,128)S(1)} %pair.1.refs_0_, ...), custom_call_target="tpu_custom_call" | custom-call | flops 1024 | bytes 1024 | tf_op jit(solution)/shard_map/below/pallas_call | solution.py:232
  71.6 4.0 %pieces.3 = (f32[8,256,256]{2,1,0:T(8,128)S(1)}, f32[8,256,256]{2,1,0:T(8,128)S(1)}, f32[8,128]{1,0:T(8,128)}) custom-call(s32[7]{0:T(128)S(1)} %pad_add_fusion.table, f32[4,256,256]{2,1,0:T(8,128)S(1)} %bitcast.34, f32[4,256,256]{2,1,0:T(8,128)S(1)} %bitcast.38, f32[256,256]{1,0:T(8,128)S(1)} %below.1.bottom, ...), custom_call_target="tpu_custom_call" | custom-call | flops 1024 | bytes 1024 | tf_op jit(solution)/shard_map/pieces/pallas_call | solution.py:108
  75.6 2.1 %collective-permute-start.24 = (f32[256,256]{1,0:T(8,128)S(1)}, f32[256,256]{1,0:T(8,128)S(1)}, u32[]{:S(2)}, u32[]{:S(2)}) collective-permute-start(f32[256,256]{1,0:T(8,128)S(1)} %get-tuple-element.60), channel_id=1, source_target_pairs={{0,4},{1,5},{2,6},{3,7},{4,0},{5,1},{6,2},{7,3},{8,12},{9,13},{10,... | collective-permute-start | bytes 786440 | tf_op jit(solution)/shard_map/ppermute | solution.py:47
  77.7 2.1 %collective-permute-done.21.refs_1_ = f32[8,256,256]{2,1,0:T(8,128)S(1)} collective-permute-done((f32[8,256,256]{2,1,0:T(8,128)S(1)}, f32[8,256,256]{2,1,0:T(8,128)S(1)}, u32[]{:S(2)}, u32[]{:S(2)}) %collective-permute-start.21) | collective-permute-done | bytes 2097184 | tf_op jit(solution)/shard_map/ppermute | solution.py:412
  81.7 4.1 %collective-permute-done.24.refs_2_ = f32[256,256]{1,0:T(8,128)S(1)} collective-permute-done((f32[256,256]{1,0:T(8,128)S(1)}, f32[256,256]{1,0:T(8,128)S(1)}, u32[]{:S(2)}, u32[]{:S(2)}) %collective-permute-start.24) | collective-permute-done | bytes 262176 | tf_op jit(solution)/shard_map/ppermute | solution.py:47
  85.9 3.9 %collective-permute-start.25 = (f32[256,256]{1,0:T(8,128)S(1)}, f32[256,256]{1,0:T(8,128)S(1)}, u32[]{:S(2)}, u32[]{:S(2)}) collective-permute-start(f32[256,256]{1,0:T(8,128)S(1)} %ghost_sum.2.refs_2_), channel_id=1, source_target_pairs={{0,112},{1,113},{2,114},{3,115},{4,116},{5,117},{6,118},{7,119},{8... | collective-permute-start | bytes 786440 | tf_op jit(solution)/shard_map/ppermute | solution.py:51
  89.8 2.4 %collective-permute-start.30 = (f32[256,256]{1,0:T(8,128)S(1)}, f32[256,256]{1,0:T(8,128)S(1)}, u32[]{:S(2)}, u32[]{:S(2)}) collective-permute-start(f32[256,256]{1,0:T(8,128)S(1)} %ghost_sum.2.refs_2_), channel_id=1, source_target_pairs={{0,8},{1,9},{2,10},{3,11},{4,12},{5,13},{6,14},{7,15},{8,0},{9,1},... | collective-permute-start | bytes 786440 | tf_op jit(solution)/shard_map/ppermute | solution.py:418
  93.3 5.2 %collective-permute-done.25.refs_5_ = f32[256,256]{1,0:T(8,128)S(1)} collective-permute-done((f32[256,256]{1,0:T(8,128)S(1)}, f32[256,256]{1,0:T(8,128)S(1)}, u32[]{:S(2)}, u32[]{:S(2)}) %collective-permute-start.25) | collective-permute-done | bytes 262176 | tf_op jit(solution)/shard_map/ppermute | solution.py:51
  98.5 6.4 %collective-permute-done.30.refs_3_ = f32[256,256]{1,0:T(8,128)S(1)} collective-permute-done((f32[256,256]{1,0:T(8,128)S(1)}, f32[256,256]{1,0:T(8,128)S(1)}, u32[]{:S(2)}, u32[]{:S(2)}) %collective-permute-start.30) | collective-permute-done | bytes 262176 | tf_op jit(solution)/shard_map/ppermute | solution.py:418
  105.0 2.6 %collective-permute-start.31 = (f32[2,256,256]{2,1,0:T(8,128)S(1)}, f32[2,256,256]{2,1,0:T(8,128)S(1)}, u32[]{:S(2)}, u32[]{:S(2)}) collective-permute-start(f32[2,256,256]{2,1,0:T(8,128)S(1)} %new_pair.1.refs_0_), channel_id=1, source_target_pairs={{0,6},{1,7},{2,0},{3,1},{4,2},{5,3},{6,4},{7,5},{8,14},{9,15},{10,... | collective-permute-start | bytes 1572872 | tf_op jit(solution)/shard_map/ppermute | solution.py:47
  110.9 4.0 %collective-permute-start.27 = (f32[16,256]{1,0:T(8,128)S(1)}, f32[16,256]{1,0:T(8,128)S(1)}, u32[]{:S(2)}, u32[]{:S(2)}) collective-permute-start(f32[16,256]{1,0:T(8,128)S(1)} %get-tuple-element.62), channel_id=1, source_target_pairs={{4,0},{5,1},{6,2},{7,3},{8,4},{9,5},{10,6},{11,7},{12,8},{13,9},{1... | collective-permute-start | bytes 49160 | tf_op jit(solution)/shard_map/ppermute | solution.py:383
  115.0 7.8 %collective-permute-done.26.refs_3_.x_low = f32[16,256]{1,0:T(8,128)S(1)} collective-permute-done((f32[16,256]{1,0:T(8,128)S(1)}, f32[16,256]{1,0:T(8,128)S(1)}, u32[]{:S(2)}, u32[]{:S(2)}) %collective-permute-start.26) | collective-permute-done | bytes 16416 | tf_op jit(solution)/shard_map/ppermute | solution.py:382
  127.1 2.8 %collective-permute-start.35 = (f32[256,256]{1,0:T(8,128)S(1)}, f32[256,256]{1,0:T(8,128)S(1)}, u32[]{:S(2)}, u32[]{:S(2)}) collective-permute-start(f32[256,256]{1,0:T(8,128)S(1)} %get-tuple-element.68), channel_id=1, source_target_pairs={{0,6},{1,7},{2,0},{3,1},{4,2},{5,3},{6,4},{7,5},{8,14},{9,15},{10,... | collective-permute-start | bytes 786440 | tf_op jit(solution)/shard_map/ppermute | solution.py:47
  130.5 9.8 %stencil.3 = (f32[16,256,256]{2,1,0:T(8,128)}, f32[8,128]{1,0:T(8,128)S(1)}) custom-call(f32[1]{0:T(128)S(6)} %div.3.inverse, s32[4]{0:T(128)S(1)} %add_convert_fusion.inside, f32[16,256,256]{2,1,0:T(8,128)S(1)} %copy-done.3, f32[256,256]{1,0:T(8,128)S(1)} %below.1.bottom, f32[256,256]{1,0:T(8,128)S(1)} %multiply_add_fusion.top, ...), custom_call_target="tpu_custom_call" | custom-call | flops 1024 | bytes 1024 | tf_op jit(solution)/shard_map/stencil/pallas_call | solution.py:365
  144.1 5.7 %collective-permute-done.37.refs_3_ = f32[256,256]{1,0:T(8,128)S(1)} collective-permute-done((f32[256,256]{1,0:T(8,128)S(1)}, f32[256,256]{1,0:T(8,128)S(1)}, u32[]{:S(2)}, u32[]{:S(2)}) %collective-permute-start.37) | collective-permute-done | bytes 262176 | tf_op jit(solution)/shard_map/ppermute | solution.py:47
  152.4 4.8 %fix_bottom.1.field = f32[16,256,256]{2,1,0:T(8,128)} custom-call(s32[7]{0:T(128)S(1)} %pad_add_fusion.table, f32[4,256,256]{2,1,0:T(8,128)} %bitcast.32, f32[4,256,256]{2,1,0:T(8,128)} %bitcast.36, f32[16,256,256]{2,1,0:T(8,128)} %bitcast.26, f32[2,256,256]{2,1,0:T(8,128)S(1)} %new_pair.1.refs_0_, ...), custom_call_target="tpu_custom_call", output_to_operand_aliasing={{}: (14, {})} | custom-call | flops 1024 | bytes 1024 | tf_op jit(solution)/shard_map/fix_bottom/pallas_call | solution.py:253
  157.2 3.0 %collective-permute-done.36.ghost = f32[256,256]{1,0:T(8,128)S(1)} collective-permute-done((f32[256,256]{1,0:T(8,128)S(1)}, f32[256,256]{1,0:T(8,128)S(1)}, u32[]{:S(2)}, u32[]{:S(2)}) %collective-permute-start.36) | collective-permute-done | bytes 262176 | tf_op jit(solution)/shard_map/ppermute | solution.py:51
  160.1 2.2 %fix_top.1 = f32[16,256,256]{2,1,0:T(8,128)} custom-call(s32[7]{0:T(128)S(1)} %pad_add_fusion.table, f32[256,256]{1,0:T(8,128)S(1)} %collective-permute-done.36.ghost, f32[16,256,256]{2,1,0:T(8,128)} %fix_bottom.1.field), custom_call_target="tpu_custom_call", output_to_operand_aliasing={{}: (2, {})} | custom-call | flops 1024 | bytes 1024 | tf_op jit(solution)/shard_map/fix_top/pallas_call | solution.py:277
  (109 shorter events, 37.7 us)
Async XLA Ops:
  7.7 19.0 %collective-permute-start.6 = (f32[8,256,256]{2,1,0:T(8,128)S(1)}, f32[8,256,256]{2,1,0:T(8,128)S(1)}, u32[]{:S(2)}, u32[]{:S(2)}) collective-permute-start(f32[8,256,256]{2,1,0:T(8,128)S(1)} %get-tuple-element.46), channel_id=1, source_target_pairs={{0,1},{1,0},{2,3},{3,2},{4,5},{5,4},{6,7},{7,6},{8,9},{9,8},{10,11... | collective-permute-start | bytes 6291464 | tf_op jit(solution)/shard_map/ppermute | solution.py:412
  7.8 18.9 %collective-permute-start.4 = (f32[256,256]{1,0:T(8,128)S(1)}, f32[256,256]{1,0:T(8,128)S(1)}, u32[]{:S(2)}, u32[]{:S(2)}) collective-permute-start(f32[256,256]{1,0:T(8,128)S(1)} %get-tuple-element.73.top), channel_id=1, source_target_pairs={{0,16},{1,17},{2,18},{3,19},{4,20},{5,21},{6,22},{7,23},{8,24},{9,... | collective-permute-start | bytes 786440 | tf_op jit(solution)/shard_map/ppermute | solution.py:51
  10.0 16.7 %collective-permute-start.5 = (f32[256,256]{1,0:T(8,128)S(1)}, f32[256,256]{1,0:T(8,128)S(1)}, u32[]{:S(2)}, u32[]{:S(2)}) collective-permute-start(f32[256,256]{1,0:T(8,128)S(1)} %get-tuple-element.73.top), channel_id=1, source_target_pairs={{0,24},{1,25},{2,26},{3,27},{4,28},{5,29},{6,30},{7,31},{8,16},{9,... | collective-permute-start | bytes 786440 | tf_op jit(solution)/shard_map/ppermute | solution.py:51
  14.7 8.9 %collective-permute-start = (f32[16,256]{1,0:T(8,128)S(1)}, f32[16,256]{1,0:T(8,128)S(1)}, u32[]{:S(2)}, u32[]{:S(2)}) collective-permute-start(f32[16,256]{1,0:T(8,128)S(1)} %get-tuple-element.40), channel_id=1, source_target_pairs={{0,4},{1,5},{2,6},{3,7},{4,8},{5,9},{6,10},{7,11},{8,12},{9,13},{1... | collective-permute-start | bytes 49160 | tf_op jit(solution)/shard_map/ppermute | solution.py:382
  28.0 28.9 %collective-permute-start.16 = (f32[4,256,256]{2,1,0:T(8,128)}, f32[4,256,256]{2,1,0:T(8,128)}, u32[]{:S(2)}, u32[]{:S(2)}) collective-permute-start(f32[4,256,256]{2,1,0:T(8,128)} %get-tuple-element.47.refs_2_), channel_id=1, source_target_pairs={{0,8},{1,9},{2,10},{3,11},{4,12},{5,13},{6,14},{7,15},{8,0},{9,1},... | collective-permute-start | bytes 3145736 | tf_op jit(solution)/shard_map/ppermute | solution.py:418
  31.2 15.2 %collective-permute-start.7 = (f32[2,256,256]{2,1,0:T(8,128)S(1)}, f32[2,256,256]{2,1,0:T(8,128)S(1)}, u32[]{:S(2)}, u32[]{:S(2)}) collective-permute-start(f32[2,256,256]{2,1,0:T(8,128)S(1)} %pair.1.refs_0_), channel_id=1, source_target_pairs={{0,6},{1,7},{2,0},{3,1},{4,2},{5,3},{6,4},{7,5},{8,14},{9,15},{10,... | collective-permute-start | bytes 1572872 | tf_op jit(solution)/shard_map/ppermute | solution.py:47
  32.4 14.6 %collective-permute-start.8 = (f32[2,256,256]{2,1,0:T(8,128)S(1)}, f32[2,256,256]{2,1,0:T(8,128)S(1)}, u32[]{:S(2)}, u32[]{:S(2)}) collective-permute-start(f32[2,256,256]{2,1,0:T(8,128)S(1)} %pair.1.refs_0_), channel_id=1, source_target_pairs={{0,2},{1,3},{2,4},{3,5},{4,6},{5,7},{6,0},{7,1},{8,10},{9,11},{10,... | collective-permute-start | bytes 1572872 | tf_op jit(solution)/shard_map/ppermute | solution.py:47
  46.2 12.1 %collective-permute-start.11 = (f32[2,256,256]{2,1,0:T(8,128)S(1)}, f32[2,256,256]{2,1,0:T(8,128)S(1)}, u32[]{:S(2)}, u32[]{:S(2)}) collective-permute-start(f32[2,256,256]{2,1,0:T(8,128)S(1)} %pair.1.refs_0_), channel_id=1, source_target_pairs={{0,1},{1,0},{2,3},{3,2},{4,5},{5,4},{6,7},{7,6},{8,9},{9,8},{10,11... | collective-permute-start | bytes 1572872 | tf_op jit(solution)/shard_map/ppermute | solution.py:394
  47.1 9.3 %collective-permute-start.9 = (f32[256,256]{1,0:T(8,128)S(1)}, f32[256,256]{1,0:T(8,128)S(1)}, u32[]{:S(2)}, u32[]{:S(2)}) collective-permute-start(f32[256,256]{1,0:T(8,128)S(1)} %get-tuple-element.49), channel_id=1, source_target_pairs={{0,2},{1,3},{2,4},{3,5},{4,6},{5,7},{6,0},{7,1},{8,10},{9,11},{10,... | collective-permute-start | bytes 786440 | tf_op jit(solution)/shard_map/ppermute | solution.py:47
  47.7 8.7 %collective-permute-start.10 = (f32[256,256]{1,0:T(8,128)S(1)}, f32[256,256]{1,0:T(8,128)S(1)}, u32[]{:S(2)}, u32[]{:S(2)}) collective-permute-start(f32[256,256]{1,0:T(8,128)S(1)} %get-tuple-element.50), channel_id=1, source_target_pairs={{0,6},{1,7},{2,0},{3,1},{4,2},{5,3},{6,4},{7,5},{8,14},{9,15},{10,... | collective-permute-start | bytes 786440 | tf_op jit(solution)/shard_map/ppermute | solution.py:47
  50.4 12.5 %collective-permute-start.12 = (f32[2,256,256]{2,1,0:T(8,128)S(1)}, f32[2,256,256]{2,1,0:T(8,128)S(1)}, u32[]{:S(2)}, u32[]{:S(2)}) collective-permute-start(f32[2,256,256]{2,1,0:T(8,128)S(1)} %collective-permute-done.7.refs_0_.refs_1_), channel_id=1, source_target_pairs={{0,1},{1,0},{2,3},{3,2},{4,5},{5,4},{6,7},{7,6},{8,9},{9,8},{10,11... | collective-permute-start | bytes 1572872 | tf_op jit(solution)/shard_map/ppermute | solution.py:394
  56.4 9.1 %collective-permute-start.13 = (f32[2,256,256]{2,1,0:T(8,128)S(1)}, f32[2,256,256]{2,1,0:T(8,128)S(1)}, u32[]{:S(2)}, u32[]{:S(2)}) collective-permute-start(f32[2,256,256]{2,1,0:T(8,128)S(1)} %collective-permute-done.8.refs_1_.refs_2_), channel_id=1, source_target_pairs={{0,1},{1,0},{2,3},{3,2},{4,5},{5,4},{6,7},{7,6},{8,9},{9,8},{10,11... | collective-permute-start | bytes 1572872 | tf_op jit(solution)/shard_map/ppermute | solution.py:394
  58.3 12.4 %collective-permute-start.17 = (f32[256,256]{1,0:T(8,128)S(1)}, f32[256,256]{1,0:T(8,128)S(1)}, u32[]{:S(2)}, u32[]{:S(2)}) collective-permute-start(f32[256,256]{1,0:T(8,128)S(1)} %slice_bitcast_fusion), channel_id=1, source_target_pairs={{0,16},{1,17},{2,18},{3,19},{4,20},{5,21},{6,22},{7,23},{8,24},{9,... | collective-permute-start | bytes 786440 | tf_op jit(solution)/shard_map/ppermute | solution.py:51
  59.1 11.7 %collective-permute-start.18 = (f32[256,256]{1,0:T(8,128)S(1)}, f32[256,256]{1,0:T(8,128)S(1)}, u32[]{:S(2)}, u32[]{:S(2)}) collective-permute-start(f32[256,256]{1,0:T(8,128)S(1)} %slice_bitcast_fusion), channel_id=1, source_target_pairs={{0,24},{1,25},{2,26},{3,27},{4,28},{5,29},{6,30},{7,31},{8,16},{9,... | collective-permute-start | bytes 786440 | tf_op jit(solution)/shard_map/ppermute | solution.py:51
  62.2 9.4 %collective-permute-start.19 = (f32[256,256]{1,0:T(8,128)S(1)}, f32[256,256]{1,0:T(8,128)S(1)}, u32[]{:S(2)}, u32[]{:S(2)}) collective-permute-start(f32[256,256]{1,0:T(8,128)S(1)} %get-tuple-element.53), channel_id=1, source_target_pairs={{0,2},{1,3},{2,4},{3,5},{4,6},{5,7},{6,0},{7,1},{8,10},{9,11},{10,... | collective-permute-start | bytes 786440 | tf_op jit(solution)/shard_map/ppermute | solution.py:47
  62.9 8.6 %collective-permute-start.20 = (f32[256,256]{1,0:T(8,128)S(1)}, f32[256,256]{1,0:T(8,128)S(1)}, u32[]{:S(2)}, u32[]{:S(2)}) collective-permute-start(f32[256,256]{1,0:T(8,128)S(1)} %get-tuple-element.54), channel_id=1, source_target_pairs={{0,6},{1,7},{2,0},{3,1},{4,2},{5,3},{6,4},{7,5},{8,14},{9,15},{10,... | collective-permute-start | bytes 786440 | tf_op jit(solution)/shard_map/ppermute | solution.py:47
  75.6 10.2 %collective-permute-start.24 = (f32[256,256]{1,0:T(8,128)S(1)}, f32[256,256]{1,0:T(8,128)S(1)}, u32[]{:S(2)}, u32[]{:S(2)}) collective-permute-start(f32[256,256]{1,0:T(8,128)S(1)} %get-tuple-element.60), channel_id=1, source_target_pairs={{0,4},{1,5},{2,6},{3,7},{4,0},{5,1},{6,2},{7,3},{8,12},{9,13},{10,... | collective-permute-start | bytes 786440 | tf_op jit(solution)/shard_map/ppermute | solution.py:47
  80.0 13.4 %collective-permute-start.22 = (f32[1,256,256]{2,1,0:T(8,128)S(1)}, f32[1,256,256]{2,1,0:T(8,128)S(1)}, u32[]{:S(2)}, u32[]{:S(2)}) collective-permute-start(f32[1,256,256]{2,1,0:T(8,128)S(1)} %get-tuple-element.58.refs_4_), channel_id=1, source_target_pairs={{0,8},{1,9},{2,10},{3,11},{4,12},{5,13},{6,14},{7,15},{8,0},{9,1},... | collective-permute-start | bytes 786440 | tf_op jit(solution)/shard_map/ppermute | solution.py:418
  85.9 12.6 %collective-permute-start.25 = (f32[256,256]{1,0:T(8,128)S(1)}, f32[256,256]{1,0:T(8,128)S(1)}, u32[]{:S(2)}, u32[]{:S(2)}) collective-permute-start(f32[256,256]{1,0:T(8,128)S(1)} %ghost_sum.2.refs_2_), channel_id=1, source_target_pairs={{0,112},{1,113},{2,114},{3,115},{4,116},{5,117},{6,118},{7,119},{8... | collective-permute-start | bytes 786440 | tf_op jit(solution)/shard_map/ppermute | solution.py:51
  89.8 15.2 %collective-permute-start.30 = (f32[256,256]{1,0:T(8,128)S(1)}, f32[256,256]{1,0:T(8,128)S(1)}, u32[]{:S(2)}, u32[]{:S(2)}) collective-permute-start(f32[256,256]{1,0:T(8,128)S(1)} %ghost_sum.2.refs_2_), channel_id=1, source_target_pairs={{0,8},{1,9},{2,10},{3,11},{4,12},{5,13},{6,14},{7,15},{8,0},{9,1},... | collective-permute-start | bytes 786440 | tf_op jit(solution)/shard_map/ppermute | solution.py:418
  92.2 33.8 %collective-permute-start.23 = (f32[3,256,256]{2,1,0:T(8,128)S(1)}, f32[3,256,256]{2,1,0:T(8,128)S(1)}, u32[]{:S(2)}, u32[]{:S(2)}) collective-permute-start(f32[3,256,256]{2,1,0:T(8,128)S(1)} %get-tuple-element.59), channel_id=1, source_target_pairs={{0,8},{1,9},{2,10},{3,11},{4,12},{5,13},{6,14},{7,15},{8,0},{9,1},... | collective-permute-start | bytes 2359304 | tf_op jit(solution)/shard_map/ppermute | solution.py:418
  105.0 20.9 %collective-permute-start.31 = (f32[2,256,256]{2,1,0:T(8,128)S(1)}, f32[2,256,256]{2,1,0:T(8,128)S(1)}, u32[]{:S(2)}, u32[]{:S(2)}) collective-permute-start(f32[2,256,256]{2,1,0:T(8,128)S(1)} %new_pair.1.refs_0_), channel_id=1, source_target_pairs={{0,6},{1,7},{2,0},{3,1},{4,2},{5,3},{6,4},{7,5},{8,14},{9,15},{10,... | collective-permute-start | bytes 1572872 | tf_op jit(solution)/shard_map/ppermute | solution.py:47
  107.6 18.3 %collective-permute-start.32 = (f32[2,256,256]{2,1,0:T(8,128)S(1)}, f32[2,256,256]{2,1,0:T(8,128)S(1)}, u32[]{:S(2)}, u32[]{:S(2)}) collective-permute-start(f32[2,256,256]{2,1,0:T(8,128)S(1)} %new_pair.1.refs_0_), channel_id=1, source_target_pairs={{0,2},{1,3},{2,4},{3,5},{4,6},{5,7},{6,0},{7,1},{8,10},{9,11},{10,... | collective-permute-start | bytes 1572872 | tf_op jit(solution)/shard_map/ppermute | solution.py:47
  109.0 13.8 %collective-permute-start.26 = (f32[16,256]{1,0:T(8,128)S(1)}, f32[16,256]{1,0:T(8,128)S(1)}, u32[]{:S(2)}, u32[]{:S(2)}) collective-permute-start(f32[16,256]{1,0:T(8,128)S(1)} %get-tuple-element.61), channel_id=1, source_target_pairs={{0,4},{1,5},{2,6},{3,7},{4,8},{5,9},{6,10},{7,11},{8,12},{9,13},{1... | collective-permute-start | bytes 49160 | tf_op jit(solution)/shard_map/ppermute | solution.py:382
  110.9 11.8 %collective-permute-start.27 = (f32[16,256]{1,0:T(8,128)S(1)}, f32[16,256]{1,0:T(8,128)S(1)}, u32[]{:S(2)}, u32[]{:S(2)}) collective-permute-start(f32[16,256]{1,0:T(8,128)S(1)} %get-tuple-element.62), channel_id=1, source_target_pairs={{4,0},{5,1},{6,2},{7,3},{8,4},{9,5},{10,6},{11,7},{12,8},{13,9},{1... | collective-permute-start | bytes 49160 | tf_op jit(solution)/shard_map/ppermute | solution.py:383
  126.1 16.0 %collective-permute-start.33 = (f32[256,256]{1,0:T(8,128)S(1)}, f32[256,256]{1,0:T(8,128)S(1)}, u32[]{:S(2)}, u32[]{:S(2)}) collective-permute-start(f32[256,256]{1,0:T(8,128)S(1)} %get-tuple-element.66), channel_id=1, source_target_pairs={{0,2},{1,3},{2,4},{3,5},{4,6},{5,7},{6,0},{7,1},{8,10},{9,11},{10,... | collective-permute-start | bytes 786440 | tf_op jit(solution)/shard_map/ppermute | solution.py:47
  127.1 16.5 %collective-permute-start.34 = (f32[256,256]{1,0:T(8,128)S(1)}, f32[256,256]{1,0:T(8,128)S(1)}, u32[]{:S(2)}, u32[]{:S(2)}) collective-permute-start(f32[256,256]{1,0:T(8,128)S(1)} %get-tuple-element.67), channel_id=1, source_target_pairs={{0,4},{1,5},{2,6},{3,7},{4,0},{5,1},{6,2},{7,3},{8,12},{9,13},{10,... | collective-permute-start | bytes 786440 | tf_op jit(solution)/shard_map/ppermute | solution.py:47
  127.1 16.5 %collective-permute-start.35 = (f32[256,256]{1,0:T(8,128)S(1)}, f32[256,256]{1,0:T(8,128)S(1)}, u32[]{:S(2)}, u32[]{:S(2)}) collective-permute-start(f32[256,256]{1,0:T(8,128)S(1)} %get-tuple-element.68), channel_id=1, source_target_pairs={{0,6},{1,7},{2,0},{3,1},{4,2},{5,3},{6,4},{7,5},{8,14},{9,15},{10,... | collective-permute-start | bytes 786440 | tf_op jit(solution)/shard_map/ppermute | solution.py:47
  129.9 20.5 %collective-permute-start.39 = (f32[2,256,256]{2,1,0:T(8,128)S(1)}, f32[2,256,256]{2,1,0:T(8,128)S(1)}, u32[]{:S(2)}, u32[]{:S(2)}) collective-permute-start(f32[2,256,256]{2,1,0:T(8,128)S(1)} %new_pair.1.refs_0_), channel_id=1, source_target_pairs={{0,1},{1,0},{2,3},{3,2},{4,5},{5,4},{6,7},{7,6},{8,9},{9,8},{10,11... | collective-permute-start | bytes 1572872 | tf_op jit(solution)/shard_map/ppermute | solution.py:394
  140.3 9.5 %collective-permute-start.37 = (f32[256,256]{1,0:T(8,128)S(1)}, f32[256,256]{1,0:T(8,128)S(1)}, u32[]{:S(2)}, u32[]{:S(2)}) collective-permute-start(f32[256,256]{1,0:T(8,128)S(1)} %get-tuple-element.70), channel_id=1, source_target_pairs={{0,2},{1,3},{2,4},{3,5},{4,6},{5,7},{6,0},{7,1},{8,10},{9,11},{10,... | collective-permute-start | bytes 786440 | tf_op jit(solution)/shard_map/ppermute | solution.py:47
  142.0 8.3 %collective-permute-start.38 = (f32[256,256]{1,0:T(8,128)S(1)}, f32[256,256]{1,0:T(8,128)S(1)}, u32[]{:S(2)}, u32[]{:S(2)}) collective-permute-start(f32[256,256]{1,0:T(8,128)S(1)} %get-tuple-element.71), channel_id=1, source_target_pairs={{0,6},{1,7},{2,0},{3,1},{4,2},{5,3},{6,4},{7,5},{8,14},{9,15},{10,... | collective-permute-start | bytes 786440 | tf_op jit(solution)/shard_map/ppermute | solution.py:47
  150.4 9.7 %collective-permute-start.36 = (f32[256,256]{1,0:T(8,128)S(1)}, f32[256,256]{1,0:T(8,128)S(1)}, u32[]{:S(2)}, u32[]{:S(2)}) collective-permute-start(f32[256,256]{1,0:T(8,128)S(1)} %ghost_sum.3), channel_id=1, source_target_pairs={{0,112},{1,113},{2,114},{3,115},{4,116},{5,117},{6,118},{7,119},{8... | collective-permute-start | bytes 786440 | tf_op jit(solution)/shard_map/ppermute | solution.py:51
  (26 other events, 165.5 us)

commit v12 on v11

--- a/solution.py
+++ b/solution.py
@@ -463,15 +463,15 @@
     got_near = reduce_halves(give_near)
     other_ghost = reduce_halves(ghost)
     ghost_above = send_lift(ghost, -1, False)
-    earlier = (got_near, ghost_above)
+    earlier = (got_near,)
     pair = small_kernel(new_pair_body, "new_pair", planes(2), (mine, flip, ghost, other_ghost), earlier)
     near = gather_near(pair)
     top = high + TIME_STEP * jnp.where(is_top, AMBIENT, ghost_above)
     got_far = reduce_halves(give_far)
     halos = exchange_rims(rims_of(field, bottom, top))
     field, mark = stencil(inverse, inside, field, bottom, top, speed, inlets, halos)
-    parts = reduce_ring(keep, [got_near, got_far], *halos, *near)
-    far = gather_far(near, mark)
+    parts = reduce_ring(keep, [got_near, got_far], *near)
+    far = gather_far(near)
     tops = [pair, *near, *far]
     tops = tops + [other_core(value) for value in tops]
     ghost = send_lift(ghost_sum(parts, mark), -1, False)

time: 165 us -> 169 us (1.024)
  the two profiles are of different devices: /device:TPU:6 before, /device:TPU:1 now
where the time goes in v12:
time: 169 us
  starting transfers between devices  65.2 us (39%)
  waiting for transfers between devices  48.7 us (29%)
  Pallas kernels  41.9 us (25%)
  local copies, waits for them, and re-layouts  10.9 us (6%)
    ppermute x14, starting transfers between devices, send_y(): return lax.ppermute(value, 'tile', along_y(steps))  20.8 us
    pallas_call x2, Pallas kernels, stencil(): pl.pallas_call(stencil_kernel, out_shape=(planes(NZ), MARK), in_specs=[SM...  17.6 us
    ppermute x4, waiting for transfers between devices, reduce_halves(): return lax.ppermute(give, 'tile', OTHER_HALF)  17.3 us
    ppermute x10, starting transfers between devices, other_core(): return lax.ppermute(value, 'tile', OTHER_CORE)  10.1 us
    unnamed x28, local copies, waits for them, and re-layouts  9.84 us
    ppermute x2, starting transfers between devices, exchange_rims(): y_low = lax.ppermute(col_high, 'tile', right)  9.26 us
    pallas_call x2, Pallas kernels, pieces_of(): pl.pallas_call(pieces_kernel, out_shape=(planes(8), planes(8), MARK), in_...  7.47 us
    ppermute x14, waiting for transfers between devices, send_y(): return lax.ppermute(value, 'tile', along_y(steps))  7.04 us
  transfers between devices with their start and end apart: 44, of which 19 were waited for; matrix products, arithmetic and copies ran while one was open for 0% of the time, Pallas kernels for 18%

profile of v12, /device:TPU:1, one launch (start us, length us, event | category | flops | bytes accessed | tf_op | source)
XLA Modules:
  0.0 168.8 jit_solution(13052030820981146632)
XLA Ops:
  4.3 3.4 %pieces.2 = (f32[8,256,256]{2,1,0:T(8,128)S(1)}, f32[8,256,256]{2,1,0:T(8,128)S(1)}, f32[8,128]{1,0:T(8,128)S(1)}) custom-call(s32[7]{0:T(128)S(1)} %pad_add_fusion.table, f32[4,256,256]{2,1,0:T(8,128)S(1)} %bitcast.33, f32[4,256,256]{2,1,0:T(8,128)S(1)} %bitcast.37, f32[256,256]{1,0:T(8,128)S(1)} %get-tuple-element.74.bottom), custom_call_target="tpu_custom_call" | custom-call | flops 1024 | bytes 1024 | tf_op jit(solution)/shard_map/pieces/pallas_call | solution.py:108
  10.5 3.2 %collective-permute-start.5 = (f32[256,256]{1,0:T(8,128)S(1)}, f32[256,256]{1,0:T(8,128)S(1)}, u32[]{:S(2)}, u32[]{:S(2)}) collective-permute-start(f32[256,256]{1,0:T(8,128)S(1)} %get-tuple-element.73.top), channel_id=1, source_target_pairs={{0,24},{1,25},{2,26},{3,27},{4,28},{5,29},{6,30},{7,31},{8,16},{9,... | collective-permute-start | bytes 786440 | tf_op jit(solution)/shard_map/ppermute | solution.py:51
  13.7 2.2 %copy-done.4 = f32[1,16,1,256,256]{4,3,2,1,0:T(8,128)S(1)} copy-done((f32[1,16,1,256,256]{4,3,2,1,0:T(8,128)S(1)}, f32[1,16,1,256,256]{4,3,2,1,0:T(8,128)}, u32[]{:S(2)}) %copy-start.4) | copy-done | bytes 4194328
  17.1 3.0 %collective-permute-start = (f32[16,256]{1,0:T(8,128)S(1)}, f32[16,256]{1,0:T(8,128)S(1)}, u32[]{:S(2)}, u32[]{:S(2)}) collective-permute-start(f32[16,256]{1,0:T(8,128)S(1)} %get-tuple-element.40), channel_id=1, source_target_pairs={{0,4},{1,5},{2,6},{3,7},{4,8},{5,9},{6,10},{7,11},{8,12},{9,13},{1... | collective-permute-start | bytes 49160 | tf_op jit(solution)/shard_map/ppermute | solution.py:382
  20.1 2.5 %collective-permute-start.1 = (f32[16,256]{1,0:T(8,128)S(1)}, f32[16,256]{1,0:T(8,128)S(1)}, u32[]{:S(2)}, u32[]{:S(2)}) collective-permute-start(f32[16,256]{1,0:T(8,128)S(1)} %get-tuple-element.41), channel_id=1, source_target_pairs={{4,0},{5,1},{6,2},{7,3},{8,4},{9,5},{10,6},{11,7},{12,8},{13,9},{1... | collective-permute-start | bytes 49160 | tf_op jit(solution)/shard_map/ppermute | solution.py:383
  23.8 2.9 %collective-permute-start.2 = (f32[16,256]{1,0:T(8,128)S(1)}, f32[16,256]{1,0:T(8,128)S(1)}, u32[]{:S(2)}, u32[]{:S(2)}) collective-permute-start(f32[16,256]{1,0:T(8,128)S(1)} %get-tuple-element.42), channel_id=1, source_target_pairs={{0,1},{1,2},{2,3},{3,0},{4,5},{5,6},{6,7},{7,4},{8,9},{9,10},{10,1... | collective-permute-start | bytes 49160 | tf_op jit(solution)/shard_map/ppermute | solution.py:384
  27.6 2.3 %collective-permute-done.3.y_high.refs_7_ = f32[16,256]{1,0:T(8,128)S(1)} collective-permute-done((f32[16,256]{1,0:T(8,128)S(1)}, f32[16,256]{1,0:T(8,128)S(1)}, u32[]{:S(2)}, u32[]{:S(2)}) %collective-permute-start.3) | collective-permute-done | bytes 16416 | tf_op jit(solution)/shard_map/ppermute | solution.py:385
  31.6 3.2 %collective-permute-start.7 = (f32[2,256,256]{2,1,0:T(8,128)S(1)}, f32[2,256,256]{2,1,0:T(8,128)S(1)}, u32[]{:S(2)}, u32[]{:S(2)}) collective-permute-start(f32[2,256,256]{2,1,0:T(8,128)S(1)} %pair.1.refs_0_), channel_id=1, source_target_pairs={{0,6},{1,7},{2,0},{3,1},{4,2},{5,3},{6,4},{7,5},{8,14},{9,15},{10,... | collective-permute-start | bytes 1572872 | tf_op jit(solution)/shard_map/ppermute | solution.py:47
  35.5 2.2 %copy-done = f32[1,16,1,256,256]{4,3,2,1,0:T(8,128)S(1)} copy-done((f32[1,16,1,256,256]{4,3,2,1,0:T(8,128)S(1)}, f32[1,16,1,256,256]{4,3,2,1,0:T(8,128)}, u32[]{:S(2)}) %copy-start) | copy-done | bytes 4194328
  37.7 2.2 %copy-done.5 = f32[1,16,1,256,256]{4,3,2,1,0:T(8,128)S(1)} copy-done((f32[1,16,1,256,256]{4,3,2,1,0:T(8,128)S(1)}, f32[1,16,1,256,256]{4,3,2,1,0:T(8,128)}, u32[]{:S(2)}) %copy-start.5) | copy-done | bytes 4194328
  39.9 7.8 %stencil.2 = (f32[16,256,256]{2,1,0:T(8,128)S(1)}, f32[8,128]{1,0:T(8,128)S(1)}) custom-call(f32[1]{0:T(128)S(6)} %div.3.inverse, s32[4]{0:T(128)S(1)} %add_convert_fusion.inside, f32[16,256,256]{2,1,0:T(8,128)S(1)} %bitcast.30, f32[256,256]{1,0:T(8,128)S(1)} %get-tuple-element.74.bottom, f32[256,256]{1,0:T(8,128)S(1)} %get-tuple-element.73.top, ...), custom_call_target="tpu_custom_call" | custom-call | flops 1024 | bytes 1024 | tf_op jit(solution)/shard_map/stencil/pallas_call | solution.py:365
  48.9 2.8 %collective-permute-start.10 = (f32[256,256]{1,0:T(8,128)S(1)}, f32[256,256]{1,0:T(8,128)S(1)}, u32[]{:S(2)}, u32[]{:S(2)}) collective-permute-start(f32[256,256]{1,0:T(8,128)S(1)} %get-tuple-element.50), channel_id=1, source_target_pairs={{0,6},{1,7},{2,0},{3,1},{4,2},{5,3},{6,4},{7,5},{8,14},{9,15},{10,... | collective-permute-start | bytes 786440 | tf_op jit(solution)/shard_map/ppermute | solution.py:47
  53.6 3.0 %collective-permute-done.9.refs_3_ = f32[256,256]{1,0:T(8,128)S(1)} collective-permute-done((f32[256,256]{1,0:T(8,128)S(1)}, f32[256,256]{1,0:T(8,128)S(1)}, u32[]{:S(2)}, u32[]{:S(2)}) %collective-permute-start.9) | collective-permute-done | bytes 262176 | tf_op jit(solution)/shard_map/ppermute | solution.py:47
  56.6 2.2 %collective-permute-start.13 = (f32[2,256,256]{2,1,0:T(8,128)S(1)}, f32[2,256,256]{2,1,0:T(8,128)S(1)}, u32[]{:S(2)}, u32[]{:S(2)}) collective-permute-start(f32[2,256,256]{2,1,0:T(8,128)S(1)} %collective-permute-done.8.refs_1_.refs_2_), channel_id=1, source_target_pairs={{0,1},{1,0},{2,3},{3,2},{4,5},{5,4},{6,7},{7,6},{8,9},{9,8},{10,11... | collective-permute-start | bytes 1572872 | tf_op jit(solution)/shard_map/ppermute | solution.py:394
  63.1 2.3 %collective-permute-start.20 = (f32[256,256]{1,0:T(8,128)S(1)}, f32[256,256]{1,0:T(8,128)S(1)}, u32[]{:S(2)}, u32[]{:S(2)}) collective-permute-start(f32[256,256]{1,0:T(8,128)S(1)} %get-tuple-element.54), channel_id=1, source_target_pairs={{0,6},{1,7},{2,0},{3,1},{4,2},{5,3},{6,4},{7,5},{8,14},{9,15},{10,... | collective-permute-start | bytes 786440 | tf_op jit(solution)/shard_map/ppermute | solution.py:47
  66.2 4.2 %below.1.bottom = f32[256,256]{1,0:T(8,128)S(1)} custom-call(s32[7]{0:T(128)S(1)} %pad_add_fusion.table, f32[4,256,256]{2,1,0:T(8,128)} %bitcast.31, f32[4,256,256]{2,1,0:T(8,128)} %bitcast.35, f32[16,256,256]{2,1,0:T(8,128)} %copy-done.2, f32[16,256,256]{2,1,0:T(8,128)} %bitcast.25, f32[2,256,256]{2,1,0:T(8,128)S(1)} %pair.1.refs_0_, ...), custom_call_target="tpu_custom_call" | custom-call | flops 1024 | bytes 1024 | tf_op jit(solution)/shard_map/below/pallas_call | solution.py:232
  70.4 4.7 %collective-permute-done.17.refs_0_.refs_5_ = f32[256,256]{1,0:T(8,128)S(1)} collective-permute-done((f32[256,256]{1,0:T(8,128)S(1)}, f32[256,256]{1,0:T(8,128)S(1)}, u32[]{:S(2)}, u32[]{:S(2)}) %collective-permute-start.17) | collective-permute-done | bytes 262176 | tf_op jit(solution)/shard_map/ppermute | solution.py:51
  75.7 4.0 %pieces.3 = (f32[8,256,256]{2,1,0:T(8,128)S(1)}, f32[8,256,256]{2,1,0:T(8,128)S(1)}, f32[8,128]{1,0:T(8,128)}) custom-call(s32[7]{0:T(128)S(1)} %pad_add_fusion.table, f32[4,256,256]{2,1,0:T(8,128)S(1)} %bitcast.34, f32[4,256,256]{2,1,0:T(8,128)S(1)} %bitcast.38, f32[256,256]{1,0:T(8,128)S(1)} %below.1.bottom, ...), custom_call_target="tpu_custom_call" | custom-call | flops 1024 | bytes 1024 | tf_op jit(solution)/shard_map/pieces/pallas_call | solution.py:108
  81.4 2.1 %collective-permute-start.24 = (f32[256,256]{1,0:T(8,128)S(1)}, f32[256,256]{1,0:T(8,128)S(1)}, u32[]{:S(2)}, u32[]{:S(2)}) collective-permute-start(f32[256,256]{1,0:T(8,128)S(1)} %get-tuple-element.60), channel_id=1, source_target_pairs={{0,4},{1,5},{2,6},{3,7},{4,0},{5,1},{6,2},{7,3},{8,12},{9,13},{10,... | collective-permute-start | bytes 786440 | tf_op jit(solution)/shard_map/ppermute | solution.py:47
  87.0 3.8 %collective-permute-done.24.refs_2_ = f32[256,256]{1,0:T(8,128)S(1)} collective-permute-done((f32[256,256]{1,0:T(8,128)S(1)}, f32[256,256]{1,0:T(8,128)S(1)}, u32[]{:S(2)}, u32[]{:S(2)}) %collective-permute-start.24) | collective-permute-done | bytes 262176 | tf_op jit(solution)/shard_map/ppermute | solution.py:47
  94.5 5.3 %collective-permute-done.25.refs_3_ = f32[256,256]{1,0:T(8,128)S(1)} collective-permute-done((f32[256,256]{1,0:T(8,128)S(1)}, f32[256,256]{1,0:T(8,128)S(1)}, u32[]{:S(2)}, u32[]{:S(2)}) %collective-permute-start.25) | collective-permute-done | bytes 262176 | tf_op jit(solution)/shard_map/ppermute | solution.py:418
  99.8 2.3 %collective-permute-start.26 = (f32[2,256,256]{2,1,0:T(8,128)S(1)}, f32[2,256,256]{2,1,0:T(8,128)S(1)}, u32[]{:S(2)}, u32[]{:S(2)}) collective-permute-start(f32[2,256,256]{2,1,0:T(8,128)S(1)} %new_pair.1.refs_0_), channel_id=1, source_target_pairs={{0,6},{1,7},{2,0},{3,1},{4,2},{5,3},{6,4},{7,5},{8,14},{9,15},{10,... | collective-permute-start | bytes 1572872 | tf_op jit(solution)/shard_map/ppermute | solution.py:47
  102.1 3.0 %collective-permute-start.39 = (f32[2,256,256]{2,1,0:T(8,128)S(1)}, f32[2,256,256]{2,1,0:T(8,128)S(1)}, u32[]{:S(2)}, u32[]{:S(2)}) collective-permute-start(f32[2,256,256]{2,1,0:T(8,128)S(1)} %new_pair.1.refs_0_), channel_id=1, source_target_pairs={{0,1},{1,0},{2,3},{3,2},{4,5},{5,4},{6,7},{7,6},{8,9},{9,8},{10,11... | collective-permute-start | bytes 1572872 | tf_op jit(solution)/shard_map/ppermute | solution.py:394
  105.1 11.5 %collective-permute-done.23.refs_2_ = f32[3,256,256]{2,1,0:T(8,128)S(1)} collective-permute-done((f32[3,256,256]{2,1,0:T(8,128)S(1)}, f32[3,256,256]{2,1,0:T(8,128)S(1)}, u32[]{:S(2)}, u32[]{:S(2)}) %collective-permute-start.23) | collective-permute-done | bytes 786464 | tf_op jit(solution)/shard_map/ppermute | solution.py:418
  117.1 3.1 %collective-permute-start.29 = (f32[256,256]{1,0:T(8,128)S(1)}, f32[256,256]{1,0:T(8,128)S(1)}, u32[]{:S(2)}, u32[]{:S(2)}) collective-permute-start(f32[256,256]{1,0:T(8,128)S(1)} %get-tuple-element.63), channel_id=1, source_target_pairs={{0,4},{1,5},{2,6},{3,7},{4,0},{5,1},{6,2},{7,3},{8,12},{9,13},{10,... | collective-permute-start | bytes 786440 | tf_op jit(solution)/shard_map/ppermute | solution.py:47
  123.2 5.8 %collective-permute-done.32.x_low = f32[16,256]{1,0:T(8,128)S(1)} collective-permute-done((f32[16,256]{1,0:T(8,128)S(1)}, f32[16,256]{1,0:T(8,128)S(1)}, u32[]{:S(2)}, u32[]{:S(2)}) %collective-permute-start.32) | collective-permute-done | bytes 16416 | tf_op jit(solution)/shard_map/ppermute | solution.py:382
  129.0 2.6 %collective-permute-start.33 = (f32[16,256]{1,0:T(8,128)S(1)}, f32[16,256]{1,0:T(8,128)S(1)}, u32[]{:S(2)}, u32[]{:S(2)}) collective-permute-start(f32[16,256]{1,0:T(8,128)S(1)} %get-tuple-element.66), channel_id=1, source_target_pairs={{4,0},{5,1},{6,2},{7,3},{8,4},{9,5},{10,6},{11,7},{12,8},{13,9},{1... | collective-permute-start | bytes 49160 | tf_op jit(solution)/shard_map/ppermute | solution.py:383
  133.2 6.3 %collective-permute-start.34 = (f32[16,256]{1,0:T(8,128)S(1)}, f32[16,256]{1,0:T(8,128)S(1)}, u32[]{:S(2)}, u32[]{:S(2)}) collective-permute-start(f32[16,256]{1,0:T(8,128)S(1)} %get-tuple-element.67), channel_id=1, source_target_pairs={{0,1},{1,2},{2,3},{3,0},{4,5},{5,6},{6,7},{7,4},{8,9},{9,10},{10,1... | collective-permute-start | bytes 49160 | tf_op jit(solution)/shard_map/ppermute | solution.py:384
  144.8 2.6 %collective-permute-start.38 = (f32[256,256]{1,0:T(8,128)S(1)}, f32[256,256]{1,0:T(8,128)S(1)}, u32[]{:S(2)}, u32[]{:S(2)}) collective-permute-start(f32[256,256]{1,0:T(8,128)S(1)} %get-tuple-element.71), channel_id=1, source_target_pairs={{0,6},{1,7},{2,0},{3,1},{4,2},{5,3},{6,4},{7,5},{8,14},{9,15},{10,... | collective-permute-start | bytes 786440 | tf_op jit(solution)/shard_map/ppermute | solution.py:47
  148.3 9.8 %stencil.3 = (f32[16,256,256]{2,1,0:T(8,128)}, f32[8,128]{1,0:T(8,128)S(1)}) custom-call(f32[1]{0:T(128)S(6)} %div.3.inverse, s32[4]{0:T(128)S(1)} %add_convert_fusion.inside, f32[16,256,256]{2,1,0:T(8,128)S(1)} %copy-done.3, f32[256,256]{1,0:T(8,128)S(1)} %below.1.bottom, f32[256,256]{1,0:T(8,128)S(1)} %multiply_add_fusion.top, ...), custom_call_target="tpu_custom_call" | custom-call | flops 1024 | bytes 1024 | tf_op jit(solution)/shard_map/stencil/pallas_call | solution.py:365
  160.2 4.7 %fix_bottom.1.field = f32[16,256,256]{2,1,0:T(8,128)} custom-call(s32[7]{0:T(128)S(1)} %pad_add_fusion.table, f32[4,256,256]{2,1,0:T(8,128)} %bitcast.32, f32[4,256,256]{2,1,0:T(8,128)} %bitcast.36, f32[16,256,256]{2,1,0:T(8,128)} %bitcast.26, f32[2,256,256]{2,1,0:T(8,128)S(1)} %new_pair.1.refs_0_, ...), custom_call_target="tpu_custom_call", output_to_operand_aliasing={{}: (14, {})} | custom-call | flops 1024 | bytes 1024 | tf_op jit(solution)/shard_map/fix_bottom/pallas_call | solution.py:253
  166.4 2.2 %fix_top.1 = f32[16,256,256]{2,1,0:T(8,128)} custom-call(s32[7]{0:T(128)S(1)} %pad_add_fusion.table, f32[256,256]{1,0:T(8,128)S(1)} %collective-permute-done.36.ghost, f32[16,256,256]{2,1,0:T(8,128)} %fix_bottom.1.field), custom_call_target="tpu_custom_call", output_to_operand_aliasing={{}: (2, {})} | custom-call | flops 1024 | bytes 1024 | tf_op jit(solution)/shard_map/fix_top/pallas_call | solution.py:277
  (109 shorter events, 44.6 us)
Async XLA Ops:
  7.7 22.2 %collective-permute-start.6 = (f32[8,256,256]{2,1,0:T(8,128)S(1)}, f32[8,256,256]{2,1,0:T(8,128)S(1)}, u32[]{:S(2)}, u32[]{:S(2)}) collective-permute-start(f32[8,256,256]{2,1,0:T(8,128)S(1)} %get-tuple-element.46), channel_id=1, source_target_pairs={{0,1},{1,0},{2,3},{3,2},{4,5},{5,4},{6,7},{7,6},{8,9},{9,8},{10,11... | collective-permute-start | bytes 6291464 | tf_op jit(solution)/shard_map/ppermute | solution.py:412
  9.2 20.7 %collective-permute-start.4 = (f32[256,256]{1,0:T(8,128)S(1)}, f32[256,256]{1,0:T(8,128)S(1)}, u32[]{:S(2)}, u32[]{:S(2)}) collective-permute-start(f32[256,256]{1,0:T(8,128)S(1)} %get-tuple-element.73.top), channel_id=1, source_target_pairs={{0,16},{1,17},{2,18},{3,19},{4,20},{5,21},{6,22},{7,23},{8,24},{9,... | collective-permute-start | bytes 786440 | tf_op jit(solution)/shard_map/ppermute | solution.py:51
  10.5 19.4 %collective-permute-start.5 = (f32[256,256]{1,0:T(8,128)S(1)}, f32[256,256]{1,0:T(8,128)S(1)}, u32[]{:S(2)}, u32[]{:S(2)}) collective-permute-start(f32[256,256]{1,0:T(8,128)S(1)} %get-tuple-element.73.top), channel_id=1, source_target_pairs={{0,24},{1,25},{2,26},{3,27},{4,28},{5,29},{6,30},{7,31},{8,16},{9,... | collective-permute-start | bytes 786440 | tf_op jit(solution)/shard_map/ppermute | solution.py:51
  31.2 27.7 %collective-permute-start.16 = (f32[4,256,256]{2,1,0:T(8,128)}, f32[4,256,256]{2,1,0:T(8,128)}, u32[]{:S(2)}, u32[]{:S(2)}) collective-permute-start(f32[4,256,256]{2,1,0:T(8,128)} %get-tuple-element.47.refs_2_), channel_id=1, source_target_pairs={{0,8},{1,9},{2,10},{3,11},{4,12},{5,13},{6,14},{7,15},{8,0},{9,1},... | collective-permute-start | bytes 3145736 | tf_op jit(solution)/shard_map/ppermute | solution.py:418
  31.6 17.0 %collective-permute-start.7 = (f32[2,256,256]{2,1,0:T(8,128)S(1)}, f32[2,256,256]{2,1,0:T(8,128)S(1)}, u32[]{:S(2)}, u32[]{:S(2)}) collective-permute-start(f32[2,256,256]{2,1,0:T(8,128)S(1)} %pair.1.refs_0_), channel_id=1, source_target_pairs={{0,6},{1,7},{2,0},{3,1},{4,2},{5,3},{6,4},{7,5},{8,14},{9,15},{10,... | collective-permute-start | bytes 1572872 | tf_op jit(solution)/shard_map/ppermute | solution.py:47
  34.7 14.0 %collective-permute-start.8 = (f32[2,256,256]{2,1,0:T(8,128)S(1)}, f32[2,256,256]{2,1,0:T(8,128)S(1)}, u32[]{:S(2)}, u32[]{:S(2)}) collective-permute-start(f32[2,256,256]{2,1,0:T(8,128)S(1)} %pair.1.refs_0_), channel_id=1, source_target_pairs={{0,2},{1,3},{2,4},{3,5},{4,6},{5,7},{6,0},{7,1},{8,10},{9,11},{10,... | collective-permute-start | bytes 1572872 | tf_op jit(solution)/shard_map/ppermute | solution.py:47
  47.7 13.1 %collective-permute-start.11 = (f32[2,256,256]{2,1,0:T(8,128)S(1)}, f32[2,256,256]{2,1,0:T(8,128)S(1)}, u32[]{:S(2)}, u32[]{:S(2)}) collective-permute-start(f32[2,256,256]{2,1,0:T(8,128)S(1)} %pair.1.refs_0_), channel_id=1, source_target_pairs={{0,1},{1,0},{2,3},{3,2},{4,5},{5,4},{6,7},{7,6},{8,9},{9,8},{10,11... | collective-permute-start | bytes 1572872 | tf_op jit(solution)/shard_map/ppermute | solution.py:394
  48.7 7.9 %collective-permute-start.9 = (f32[256,256]{1,0:T(8,128)S(1)}, f32[256,256]{1,0:T(8,128)S(1)}, u32[]{:S(2)}, u32[]{:S(2)}) collective-permute-start(f32[256,256]{1,0:T(8,128)S(1)} %get-tuple-element.49), channel_id=1, source_target_pairs={{0,2},{1,3},{2,4},{3,5},{4,6},{5,7},{6,0},{7,1},{8,10},{9,11},{10,... | collective-permute-start | bytes 786440 | tf_op jit(solution)/shard_map/ppermute | solution.py:47
  48.9 9.9 %collective-permute-start.10 = (f32[256,256]{1,0:T(8,128)S(1)}, f32[256,256]{1,0:T(8,128)S(1)}, u32[]{:S(2)}, u32[]{:S(2)}) collective-permute-start(f32[256,256]{1,0:T(8,128)S(1)} %get-tuple-element.50), channel_id=1, source_target_pairs={{0,6},{1,7},{2,0},{3,1},{4,2},{5,3},{6,4},{7,5},{8,14},{9,15},{10,... | collective-permute-start | bytes 786440 | tf_op jit(solution)/shard_map/ppermute | solution.py:47
  51.7 11.4 %collective-permute-start.12 = (f32[2,256,256]{2,1,0:T(8,128)S(1)}, f32[2,256,256]{2,1,0:T(8,128)S(1)}, u32[]{:S(2)}, u32[]{:S(2)}) collective-permute-start(f32[2,256,256]{2,1,0:T(8,128)S(1)} %collective-permute-done.7.refs_0_.refs_1_), channel_id=1, source_target_pairs={{0,1},{1,0},{2,3},{3,2},{4,5},{5,4},{6,7},{7,6},{8,9},{9,8},{10,11... | collective-permute-start | bytes 1572872 | tf_op jit(solution)/shard_map/ppermute | solution.py:394
  56.6 8.8 %collective-permute-start.13 = (f32[2,256,256]{2,1,0:T(8,128)S(1)}, f32[2,256,256]{2,1,0:T(8,128)S(1)}, u32[]{:S(2)}, u32[]{:S(2)}) collective-permute-start(f32[2,256,256]{2,1,0:T(8,128)S(1)} %collective-permute-done.8.refs_1_.refs_2_), channel_id=1, source_target_pairs={{0,1},{1,0},{2,3},{3,2},{4,5},{5,4},{6,7},{7,6},{8,9},{9,8},{10,11... | collective-permute-start | bytes 1572872 | tf_op jit(solution)/shard_map/ppermute | solution.py:394
  60.8 14.3 %collective-permute-start.17 = (f32[256,256]{1,0:T(8,128)S(1)}, f32[256,256]{1,0:T(8,128)S(1)}, u32[]{:S(2)}, u32[]{:S(2)}) collective-permute-start(f32[256,256]{1,0:T(8,128)S(1)} %slice_bitcast_fusion), channel_id=1, source_target_pairs={{0,16},{1,17},{2,18},{3,19},{4,20},{5,21},{6,22},{7,23},{8,24},{9,... | collective-permute-start | bytes 786440 | tf_op jit(solution)/shard_map/ppermute | solution.py:51
  61.5 14.1 %collective-permute-start.18 = (f32[256,256]{1,0:T(8,128)S(1)}, f32[256,256]{1,0:T(8,128)S(1)}, u32[]{:S(2)}, u32[]{:S(2)}) collective-permute-start(f32[256,256]{1,0:T(8,128)S(1)} %slice_bitcast_fusion), channel_id=1, source_target_pairs={{0,24},{1,25},{2,26},{3,27},{4,28},{5,29},{6,30},{7,31},{8,16},{9,... | collective-permute-start | bytes 786440 | tf_op jit(solution)/shard_map/ppermute | solution.py:51
  62.7 13.0 %collective-permute-start.19 = (f32[256,256]{1,0:T(8,128)S(1)}, f32[256,256]{1,0:T(8,128)S(1)}, u32[]{:S(2)}, u32[]{:S(2)}) collective-permute-start(f32[256,256]{1,0:T(8,128)S(1)} %get-tuple-element.53), channel_id=1, source_target_pairs={{0,2},{1,3},{2,4},{3,5},{4,6},{5,7},{6,0},{7,1},{8,10},{9,11},{10,... | collective-permute-start | bytes 786440 | tf_op jit(solution)/shard_map/ppermute | solution.py:47
  63.1 12.6 %collective-permute-start.20 = (f32[256,256]{1,0:T(8,128)S(1)}, f32[256,256]{1,0:T(8,128)S(1)}, u32[]{:S(2)}, u32[]{:S(2)}) collective-permute-start(f32[256,256]{1,0:T(8,128)S(1)} %get-tuple-element.54), channel_id=1, source_target_pairs={{0,6},{1,7},{2,0},{3,1},{4,2},{5,3},{6,4},{7,5},{8,14},{9,15},{10,... | collective-permute-start | bytes 786440 | tf_op jit(solution)/shard_map/ppermute | solution.py:47
  81.4 9.4 %collective-permute-start.24 = (f32[256,256]{1,0:T(8,128)S(1)}, f32[256,256]{1,0:T(8,128)S(1)}, u32[]{:S(2)}, u32[]{:S(2)}) collective-permute-start(f32[256,256]{1,0:T(8,128)S(1)} %get-tuple-element.60), channel_id=1, source_target_pairs={{0,4},{1,5},{2,6},{3,7},{4,0},{5,1},{6,2},{7,3},{8,12},{9,13},{10,... | collective-permute-start | bytes 786440 | tf_op jit(solution)/shard_map/ppermute | solution.py:47
  85.4 9.1 %collective-permute-start.22 = (f32[1,256,256]{2,1,0:T(8,128)S(1)}, f32[1,256,256]{2,1,0:T(8,128)S(1)}, u32[]{:S(2)}, u32[]{:S(2)}) collective-permute-start(f32[1,256,256]{2,1,0:T(8,128)S(1)} %get-tuple-element.58.refs_4_), channel_id=1, source_target_pairs={{0,8},{1,9},{2,10},{3,11},{4,12},{5,13},{6,14},{7,15},{8,0},{9,1},... | collective-permute-start | bytes 786440 | tf_op jit(solution)/shard_map/ppermute | solution.py:418
  90.9 8.9 %collective-permute-start.25 = (f32[256,256]{1,0:T(8,128)S(1)}, f32[256,256]{1,0:T(8,128)S(1)}, u32[]{:S(2)}, u32[]{:S(2)}) collective-permute-start(f32[256,256]{1,0:T(8,128)S(1)} %ghost_sum.2.refs_2_), channel_id=1, source_target_pairs={{0,8},{1,9},{2,10},{3,11},{4,12},{5,13},{6,14},{7,15},{8,0},{9,1},... | collective-permute-start | bytes 786440 | tf_op jit(solution)/shard_map/ppermute | solution.py:418
  92.5 24.1 %collective-permute-start.23 = (f32[3,256,256]{2,1,0:T(8,128)S(1)}, f32[3,256,256]{2,1,0:T(8,128)S(1)}, u32[]{:S(2)}, u32[]{:S(2)}) collective-permute-start(f32[3,256,256]{2,1,0:T(8,128)S(1)} %get-tuple-element.59), channel_id=1, source_target_pairs={{0,8},{1,9},{2,10},{3,11},{4,12},{5,13},{6,14},{7,15},{8,0},{9,1},... | collective-permute-start | bytes 2359304 | tf_op jit(solution)/shard_map/ppermute | solution.py:418
  99.8 16.8 %collective-permute-start.26 = (f32[2,256,256]{2,1,0:T(8,128)S(1)}, f32[2,256,256]{2,1,0:T(8,128)S(1)}, u32[]{:S(2)}, u32[]{:S(2)}) collective-permute-start(f32[2,256,256]{2,1,0:T(8,128)S(1)} %new_pair.1.refs_0_), channel_id=1, source_target_pairs={{0,6},{1,7},{2,0},{3,1},{4,2},{5,3},{6,4},{7,5},{8,14},{9,15},{10,... | collective-permute-start | bytes 1572872 | tf_op jit(solution)/shard_map/ppermute | solution.py:47
  102.1 14.5 %collective-permute-start.27 = (f32[2,256,256]{2,1,0:T(8,128)S(1)}, f32[2,256,256]{2,1,0:T(8,128)S(1)}, u32[]{:S(2)}, u32[]{:S(2)}) collective-permute-start(f32[2,256,256]{2,1,0:T(8,128)S(1)} %new_pair.1.refs_0_), channel_id=1, source_target_pairs={{0,2},{1,3},{2,4},{3,5},{4,6},{5,7},{6,0},{7,1},{8,10},{9,11},{10,... | collective-permute-start | bytes 1572872 | tf_op jit(solution)/shard_map/ppermute | solution.py:47
  102.1 18.9 %collective-permute-start.31 = (f32[256,256]{1,0:T(8,128)S(1)}, f32[256,256]{1,0:T(8,128)S(1)}, u32[]{:S(2)}, u32[]{:S(2)}) collective-permute-start(f32[256,256]{1,0:T(8,128)S(1)} %ghost_sum.2.refs_2_), channel_id=1, source_target_pairs={{0,112},{1,113},{2,114},{3,115},{4,116},{5,117},{6,118},{7,119},{8... | collective-permute-start | bytes 786440 | tf_op jit(solution)/shard_map/ppermute | solution.py:51
  102.1 56.7 %collective-permute-start.39 = (f32[2,256,256]{2,1,0:T(8,128)S(1)}, f32[2,256,256]{2,1,0:T(8,128)S(1)}, u32[]{:S(2)}, u32[]{:S(2)}) collective-permute-start(f32[2,256,256]{2,1,0:T(8,128)S(1)} %new_pair.1.refs_0_), channel_id=1, source_target_pairs={{0,1},{1,0},{2,3},{3,2},{4,5},{5,4},{6,7},{7,6},{8,9},{9,8},{10,11... | collective-permute-start | bytes 1572872 | tf_op jit(solution)/shard_map/ppermute | solution.py:394
  116.7 28.0 %collective-permute-start.28 = (f32[256,256]{1,0:T(8,128)S(1)}, f32[256,256]{1,0:T(8,128)S(1)}, u32[]{:S(2)}, u32[]{:S(2)}) collective-permute-start(f32[256,256]{1,0:T(8,128)S(1)} %get-tuple-element.62), channel_id=1, source_target_pairs={{0,2},{1,3},{2,4},{3,5},{4,6},{5,7},{6,0},{7,1},{8,10},{9,11},{10,... | collective-permute-start | bytes 786440 | tf_op jit(solution)/shard_map/ppermute | solution.py:47
  117.1 30.2 %collective-permute-start.29 = (f32[256,256]{1,0:T(8,128)S(1)}, f32[256,256]{1,0:T(8,128)S(1)}, u32[]{:S(2)}, u32[]{:S(2)}) collective-permute-start(f32[256,256]{1,0:T(8,128)S(1)} %get-tuple-element.63), channel_id=1, source_target_pairs={{0,4},{1,5},{2,6},{3,7},{4,0},{5,1},{6,2},{7,3},{8,12},{9,13},{10,... | collective-permute-start | bytes 786440 | tf_op jit(solution)/shard_map/ppermute | solution.py:47
  120.2 28.0 %collective-permute-start.30 = (f32[256,256]{1,0:T(8,128)S(1)}, f32[256,256]{1,0:T(8,128)S(1)}, u32[]{:S(2)}, u32[]{:S(2)}) collective-permute-start(f32[256,256]{1,0:T(8,128)S(1)} %get-tuple-element.64), channel_id=1, source_target_pairs={{0,6},{1,7},{2,0},{3,1},{4,2},{5,3},{6,4},{7,5},{8,14},{9,15},{10,... | collective-permute-start | bytes 786440 | tf_op jit(solution)/shard_map/ppermute | solution.py:47
  133.2 7.2 %collective-permute-start.34 = (f32[16,256]{1,0:T(8,128)S(1)}, f32[16,256]{1,0:T(8,128)S(1)}, u32[]{:S(2)}, u32[]{:S(2)}) collective-permute-start(f32[16,256]{1,0:T(8,128)S(1)} %get-tuple-element.67), channel_id=1, source_target_pairs={{0,1},{1,2},{2,3},{3,0},{4,5},{5,6},{6,7},{7,4},{8,9},{9,10},{10,1... | collective-permute-start | bytes 49160 | tf_op jit(solution)/shard_map/ppermute | solution.py:384
  144.1 14.0 %collective-permute-start.37 = (f32[256,256]{1,0:T(8,128)S(1)}, f32[256,256]{1,0:T(8,128)S(1)}, u32[]{:S(2)}, u32[]{:S(2)}) collective-permute-start(f32[256,256]{1,0:T(8,128)S(1)} %get-tuple-element.70), channel_id=1, source_target_pairs={{0,2},{1,3},{2,4},{3,5},{4,6},{5,7},{6,0},{7,1},{8,10},{9,11},{10,... | collective-permute-start | bytes 786440 | tf_op jit(solution)/shard_map/ppermute | solution.py:47
  144.8 13.9 %collective-permute-start.38 = (f32[256,256]{1,0:T(8,128)S(1)}, f32[256,256]{1,0:T(8,128)S(1)}, u32[]{:S(2)}, u32[]{:S(2)}) collective-permute-start(f32[256,256]{1,0:T(8,128)S(1)} %get-tuple-element.71), channel_id=1, source_target_pairs={{0,6},{1,7},{2,0},{3,1},{4,2},{5,3},{6,4},{7,5},{8,14},{9,15},{10,... | collective-permute-start | bytes 786440 | tf_op jit(solution)/shard_map/ppermute | solution.py:47
  147.3 11.6 %collective-permute-start.40 = (f32[2,256,256]{2,1,0:T(8,128)S(1)}, f32[2,256,256]{2,1,0:T(8,128)S(1)}, u32[]{:S(2)}, u32[]{:S(2)}) collective-permute-start(f32[2,256,256]{2,1,0:T(8,128)S(1)} %collective-permute-done.26.refs_3_.refs_0_.refs_1_), channel_id=1, source_target_pairs={{0,1},{1,0},{2,3},{3,2},{4,5},{5,4},{6,7},{7,6},{8,9},{9,8},{10,11... | collective-permute-start | bytes 1572872 | tf_op jit(solution)/shard_map/ppermute | solution.py:394
  148.2 10.7 %collective-permute-start.41 = (f32[2,256,256]{2,1,0:T(8,128)S(1)}, f32[2,256,256]{2,1,0:T(8,128)S(1)}, u32[]{:S(2)}, u32[]{:S(2)}) collective-permute-start(f32[2,256,256]{2,1,0:T(8,128)S(1)} %collective-permute-done.27.refs_4_.refs_1_.refs_2_), channel_id=1, source_target_pairs={{0,1},{1,0},{2,3},{3,2},{4,5},{5,4},{6,7},{7,6},{8,9},{9,8},{10,11... | collective-permute-start | bytes 1572872 | tf_op jit(solution)/shard_map/ppermute | solution.py:394
  158.8 7.5 %collective-permute-start.36 = (f32[256,256]{1,0:T(8,128)S(1)}, f32[256,256]{1,0:T(8,128)S(1)}, u32[]{:S(2)}, u32[]{:S(2)}) collective-permute-start(f32[256,256]{1,0:T(8,128)S(1)} %ghost_sum.3), channel_id=1, source_target_pairs={{0,112},{1,113},{2,114},{3,115},{4,116},{5,117},{6,118},{7,119},{8... | collective-permute-start | bytes 786440 | tf_op jit(solution)/shard_map/ppermute | solution.py:51
  (26 other events, 185.7 us)

commit v13 on v11

--- a/solution.py
+++ b/solution.py
@@ -445,8 +445,8 @@
     mine, flip = climb(top)
     give, keep, mark = pieces_of(table, px, py, bottom)
     halos = exchange_rims(rims_of(field, bottom, top, mark))
-    give, keep = reduce_cores(give, keep, whole_cores_body, 4, earlier=(mine, flip, *halos))
-    pair = small_kernel(pair_body, "pair", planes(2), (mine, flip), (give,))
+    give, keep = reduce_cores(give, keep, whole_cores_body, 4, earlier=(mine, flip, *halos[:2]))
+    pair = small_kernel(pair_body, "pair", planes(2), (mine, flip), (give, *halos[2:]))
     near = gather_near(pair)
     got = reduce_halves(give)
     field, mark = stencil(inverse, inside, field, bottom, top, speed, inlets, halos)

time: 165 us -> 167 us (1.012)
  starting transfers between devices: 57.1 us -> 62 us
    ppermute x14, starting transfers between devices: 19.1 us -> 23 us  [send_y(): return lax.ppermute(value, 'tile', along_y(steps))]
where the time goes in v13:
time: 167 us; the launch traced here: 166 us
  starting transfers between devices  62 us (37%)
  waiting for transfers between devices  48.9 us (29%)
  Pallas kernels  42 us (25%)
  local copies, waits for them, and re-layouts  10.9 us (7%)
    ppermute x14, starting transfers between devices, send_y(): return lax.ppermute(value, 'tile', along_y(steps))  23 us
    ppermute x14, waiting for transfers between devices, send_y(): return lax.ppermute(value, 'tile', along_y(steps))  17.7 us
    pallas_call x2, Pallas kernels, stencil(): pl.pallas_call(stencil_kernel, out_shape=(planes(NZ), MARK), in_specs=[SM...  17.6 us
    ppermute x6, starting transfers between devices, send_lift(): return lax.ppermute(value, ('lift', 'tile'), to_lift(steps, flip))  12.2 us
    unnamed x28, local copies, waits for them, and re-layouts  9.84 us
    ppermute x4, starting transfers between devices, reduce_halves(): return lax.ppermute(give, 'tile', OTHER_HALF)  9.56 us
    ppermute x2, waiting for transfers between devices, exchange_rims(): x_low = lax.ppermute(row_high, 'tile', up)  9.3 us
    ppermute x6, waiting for transfers between devices, send_lift(): return lax.ppermute(value, ('lift', 'tile'), to_lift(steps, flip))  8.02 us
  transfers between devices with their start and end apart: 44, of which 16 were waited for; matrix products, arithmetic and copies ran while one was open for 0% of the time, Pallas kernels for 19%

profile of v13, /device:TPU:6, one launch (start us, length us, event | category | flops | bytes accessed | tf_op | source)
XLA Modules:
  0.0 165.9 jit_solution(6012589382470620281)
XLA Ops:
  4.3 3.4 %pieces.2 = (f32[8,256,256]{2,1,0:T(8,128)S(1)}, f32[8,256,256]{2,1,0:T(8,128)S(1)}, f32[8,128]{1,0:T(8,128)S(1)}) custom-call(s32[7]{0:T(128)S(1)} %pad_add_fusion.table, f32[4,256,256]{2,1,0:T(8,128)S(1)} %bitcast.33, f32[4,256,256]{2,1,0:T(8,128)S(1)} %bitcast.37, f32[256,256]{1,0:T(8,128)S(1)} %get-tuple-element.74.bottom), custom_call_target="tpu_custom_call" | custom-call | flops 1024 | bytes 1024 | tf_op jit(solution)/shard_map/pieces/pallas_call | solution.py:108
  7.8 2.2 %collective-permute-start.4 = (f32[256,256]{1,0:T(8,128)S(1)}, f32[256,256]{1,0:T(8,128)S(1)}, u32[]{:S(2)}, u32[]{:S(2)}) collective-permute-start(f32[256,256]{1,0:T(8,128)S(1)} %get-tuple-element.73.top), channel_id=1, source_target_pairs={{0,16},{1,17},{2,18},{3,19},{4,20},{5,21},{6,22},{7,23},{8,24},{9,... | collective-permute-start | bytes 786440 | tf_op jit(solution)/shard_map/ppermute | solution.py:51
  14.7 3.2 %collective-permute-start = (f32[16,256]{1,0:T(8,128)S(1)}, f32[16,256]{1,0:T(8,128)S(1)}, u32[]{:S(2)}, u32[]{:S(2)}) collective-permute-start(f32[16,256]{1,0:T(8,128)S(1)} %get-tuple-element.40), channel_id=1, source_target_pairs={{0,4},{1,5},{2,6},{3,7},{4,8},{5,9},{6,10},{7,11},{8,12},{9,13},{1... | collective-permute-start | bytes 49160 | tf_op jit(solution)/shard_map/ppermute | solution.py:382
  17.9 2.7 %collective-permute-start.1 = (f32[16,256]{1,0:T(8,128)S(1)}, f32[16,256]{1,0:T(8,128)S(1)}, u32[]{:S(2)}, u32[]{:S(2)}) collective-permute-start(f32[16,256]{1,0:T(8,128)S(1)} %get-tuple-element.41), channel_id=1, source_target_pairs={{4,0},{5,1},{6,2},{7,3},{8,4},{9,5},{10,6},{11,7},{12,8},{13,9},{1... | collective-permute-start | bytes 49160 | tf_op jit(solution)/shard_map/ppermute | solution.py:383
  20.6 2.9 %collective-permute-done.x_low.refs_4_ = f32[16,256]{1,0:T(8,128)S(1)} collective-permute-done((f32[16,256]{1,0:T(8,128)S(1)}, f32[16,256]{1,0:T(8,128)S(1)}, u32[]{:S(2)}, u32[]{:S(2)}) %collective-permute-start) | collective-permute-done | bytes 16416 | tf_op jit(solution)/shard_map/ppermute | solution.py:382
  24.8 3.2 %collective-permute-start.16 = (f32[4,256,256]{2,1,0:T(8,128)}, f32[4,256,256]{2,1,0:T(8,128)}, u32[]{:S(2)}, u32[]{:S(2)}) collective-permute-start(f32[4,256,256]{2,1,0:T(8,128)} %get-tuple-element.47.refs_2_), channel_id=1, source_target_pairs={{0,8},{1,9},{2,10},{3,11},{4,12},{5,13},{6,14},{7,15},{8,0},{9,1},... | collective-permute-start | bytes 3145736 | tf_op jit(solution)/shard_map/ppermute | solution.py:418
  31.2 3.0 %collective-permute-start.7 = (f32[2,256,256]{2,1,0:T(8,128)S(1)}, f32[2,256,256]{2,1,0:T(8,128)S(1)}, u32[]{:S(2)}, u32[]{:S(2)}) collective-permute-start(f32[2,256,256]{2,1,0:T(8,128)S(1)} %pair.1.refs_0_), channel_id=1, source_target_pairs={{0,6},{1,7},{2,0},{3,1},{4,2},{5,3},{6,4},{7,5},{8,14},{9,15},{10,... | collective-permute-start | bytes 1572872 | tf_op jit(solution)/shard_map/ppermute | solution.py:47
  39.3 7.8 %stencil.2 = (f32[16,256,256]{2,1,0:T(8,128)S(1)}, f32[8,128]{1,0:T(8,128)S(1)}) custom-call(f32[1]{0:T(128)S(6)} %div.3.inverse, s32[4]{0:T(128)S(1)} %add_convert_fusion.inside, f32[16,256,256]{2,1,0:T(8,128)S(1)} %bitcast.30, f32[256,256]{1,0:T(8,128)S(1)} %get-tuple-element.74.bottom, f32[256,256]{1,0:T(8,128)S(1)} %get-tuple-element.73.top, ...), custom_call_target="tpu_custom_call" | custom-call | flops 1024 | bytes 1024 | tf_op jit(solution)/shard_map/stencil/pallas_call | solution.py:365
  49.1 3.2 %collective-permute-start.10 = (f32[256,256]{1,0:T(8,128)S(1)}, f32[256,256]{1,0:T(8,128)S(1)}, u32[]{:S(2)}, u32[]{:S(2)}) collective-permute-start(f32[256,256]{1,0:T(8,128)S(1)} %get-tuple-element.50), channel_id=1, source_target_pairs={{0,6},{1,7},{2,0},{3,1},{4,2},{5,3},{6,4},{7,5},{8,14},{9,15},{10,... | collective-permute-start | bytes 786440 | tf_op jit(solution)/shard_map/ppermute | solution.py:47
  52.4 5.2 %collective-permute-done.9.refs_3_ = f32[256,256]{1,0:T(8,128)S(1)} collective-permute-done((f32[256,256]{1,0:T(8,128)S(1)}, f32[256,256]{1,0:T(8,128)S(1)}, u32[]{:S(2)}, u32[]{:S(2)}) %collective-permute-start.9) | collective-permute-done | bytes 262176 | tf_op jit(solution)/shard_map/ppermute | solution.py:47
  60.8 3.3 %collective-permute-start.18 = (f32[256,256]{1,0:T(8,128)S(1)}, f32[256,256]{1,0:T(8,128)S(1)}, u32[]{:S(2)}, u32[]{:S(2)}) collective-permute-start(f32[256,256]{1,0:T(8,128)S(1)} %slice_bitcast_fusion), channel_id=1, source_target_pairs={{0,24},{1,25},{2,26},{3,27},{4,28},{5,29},{6,30},{7,31},{8,16},{9,... | collective-permute-start | bytes 786440 | tf_op jit(solution)/shard_map/ppermute | solution.py:51
  64.7 2.7 %collective-permute-start.20 = (f32[256,256]{1,0:T(8,128)S(1)}, f32[256,256]{1,0:T(8,128)S(1)}, u32[]{:S(2)}, u32[]{:S(2)}) collective-permute-start(f32[256,256]{1,0:T(8,128)S(1)} %get-tuple-element.54), channel_id=1, source_target_pairs={{0,6},{1,7},{2,0},{3,1},{4,2},{5,3},{6,4},{7,5},{8,14},{9,15},{10,... | collective-permute-start | bytes 786440 | tf_op jit(solution)/shard_map/ppermute | solution.py:47
  68.2 4.2 %below.1.bottom = f32[256,256]{1,0:T(8,128)S(1)} custom-call(s32[7]{0:T(128)S(1)} %pad_add_fusion.table, f32[4,256,256]{2,1,0:T(8,128)} %bitcast.31, f32[4,256,256]{2,1,0:T(8,128)} %bitcast.35, f32[16,256,256]{2,1,0:T(8,128)} %copy-done.2, f32[16,256,256]{2,1,0:T(8,128)} %bitcast.25, f32[2,256,256]{2,1,0:T(8,128)S(1)} %pair.1.refs_0_, ...), custom_call_target="tpu_custom_call" | custom-call | flops 1024 | bytes 1024 | tf_op jit(solution)/shard_map/below/pallas_call | solution.py:232
  73.5 4.0 %pieces.3 = (f32[8,256,256]{2,1,0:T(8,128)S(1)}, f32[8,256,256]{2,1,0:T(8,128)S(1)}, f32[8,128]{1,0:T(8,128)}) custom-call(s32[7]{0:T(128)S(1)} %pad_add_fusion.table, f32[4,256,256]{2,1,0:T(8,128)S(1)} %bitcast.34, f32[4,256,256]{2,1,0:T(8,128)S(1)} %bitcast.38, f32[256,256]{1,0:T(8,128)S(1)} %below.1.bottom, ...), custom_call_target="tpu_custom_call" | custom-call | flops 1024 | bytes 1024 | tf_op jit(solution)/shard_map/pieces/pallas_call | solution.py:108
  77.5 2.4 %collective-permute-start.24 = (f32[256,256]{1,0:T(8,128)S(1)}, f32[256,256]{1,0:T(8,128)S(1)}, u32[]{:S(2)}, u32[]{:S(2)}) collective-permute-start(f32[256,256]{1,0:T(8,128)S(1)} %get-tuple-element.60), channel_id=1, source_target_pairs={{0,4},{1,5},{2,6},{3,7},{4,0},{5,1},{6,2},{7,3},{8,12},{9,13},{10,... | collective-permute-start | bytes 786440 | tf_op jit(solution)/shard_map/ppermute | solution.py:47
  81.9 2.3 %collective-permute-start.22 = (f32[1,256,256]{2,1,0:T(8,128)S(1)}, f32[1,256,256]{2,1,0:T(8,128)S(1)}, u32[]{:S(2)}, u32[]{:S(2)}) collective-permute-start(f32[1,256,256]{2,1,0:T(8,128)S(1)} %get-tuple-element.58.refs_4_), channel_id=1, source_target_pairs={{0,8},{1,9},{2,10},{3,11},{4,12},{5,13},{6,14},{7,15},{8,0},{9,1},... | collective-permute-start | bytes 786440 | tf_op jit(solution)/shard_map/ppermute | solution.py:418
  84.2 3.5 %collective-permute-done.24.refs_2_ = f32[256,256]{1,0:T(8,128)S(1)} collective-permute-done((f32[256,256]{1,0:T(8,128)S(1)}, f32[256,256]{1,0:T(8,128)S(1)}, u32[]{:S(2)}, u32[]{:S(2)}) %collective-permute-start.24) | collective-permute-done | bytes 262176 | tf_op jit(solution)/shard_map/ppermute | solution.py:47
  87.8 4.2 %collective-permute-start.25 = (f32[256,256]{1,0:T(8,128)S(1)}, f32[256,256]{1,0:T(8,128)S(1)}, u32[]{:S(2)}, u32[]{:S(2)}) collective-permute-start(f32[256,256]{1,0:T(8,128)S(1)} %ghost_sum.2.refs_2_), channel_id=1, source_target_pairs={{0,112},{1,113},{2,114},{3,115},{4,116},{5,117},{6,118},{7,119},{8... | collective-permute-start | bytes 786440 | tf_op jit(solution)/shard_map/ppermute | solution.py:51
  92.0 4.1 %collective-permute-start.30 = (f32[256,256]{1,0:T(8,128)S(1)}, f32[256,256]{1,0:T(8,128)S(1)}, u32[]{:S(2)}, u32[]{:S(2)}) collective-permute-start(f32[256,256]{1,0:T(8,128)S(1)} %ghost_sum.2.refs_2_), channel_id=1, source_target_pairs={{0,8},{1,9},{2,10},{3,11},{4,12},{5,13},{6,14},{7,15},{8,0},{9,1},... | collective-permute-start | bytes 786440 | tf_op jit(solution)/shard_map/ppermute | solution.py:418
  96.1 4.8 %collective-permute-done.25.refs_5_ = f32[256,256]{1,0:T(8,128)S(1)} collective-permute-done((f32[256,256]{1,0:T(8,128)S(1)}, f32[256,256]{1,0:T(8,128)S(1)}, u32[]{:S(2)}, u32[]{:S(2)}) %collective-permute-start.25) | collective-permute-done | bytes 262176 | tf_op jit(solution)/shard_map/ppermute | solution.py:51
  100.9 7.9 %collective-permute-done.30.refs_3_ = f32[256,256]{1,0:T(8,128)S(1)} collective-permute-done((f32[256,256]{1,0:T(8,128)S(1)}, f32[256,256]{1,0:T(8,128)S(1)}, u32[]{:S(2)}, u32[]{:S(2)}) %collective-permute-start.30) | collective-permute-done | bytes 262176 | tf_op jit(solution)/shard_map/ppermute | solution.py:418
  108.9 2.5 %collective-permute-start.31 = (f32[2,256,256]{2,1,0:T(8,128)S(1)}, f32[2,256,256]{2,1,0:T(8,128)S(1)}, u32[]{:S(2)}, u32[]{:S(2)}) collective-permute-start(f32[2,256,256]{2,1,0:T(8,128)S(1)} %new_pair.1.refs_0_), channel_id=1, source_target_pairs={{0,6},{1,7},{2,0},{3,1},{4,2},{5,3},{6,4},{7,5},{8,14},{9,15},{10,... | collective-permute-start | bytes 1572872 | tf_op jit(solution)/shard_map/ppermute | solution.py:47
  114.4 4.4 %collective-permute-start.27 = (f32[16,256]{1,0:T(8,128)S(1)}, f32[16,256]{1,0:T(8,128)S(1)}, u32[]{:S(2)}, u32[]{:S(2)}) collective-permute-start(f32[16,256]{1,0:T(8,128)S(1)} %get-tuple-element.62), channel_id=1, source_target_pairs={{4,0},{5,1},{6,2},{7,3},{8,4},{9,5},{10,6},{11,7},{12,8},{13,9},{1... | collective-permute-start | bytes 49160 | tf_op jit(solution)/shard_map/ppermute | solution.py:383
  118.7 6.4 %collective-permute-done.26.refs_3_.x_low = f32[16,256]{1,0:T(8,128)S(1)} collective-permute-done((f32[16,256]{1,0:T(8,128)S(1)}, f32[16,256]{1,0:T(8,128)S(1)}, u32[]{:S(2)}, u32[]{:S(2)}) %collective-permute-start.26) | collective-permute-done | bytes 16416 | tf_op jit(solution)/shard_map/ppermute | solution.py:382
  128.5 2.6 %collective-permute-start.33 = (f32[256,256]{1,0:T(8,128)S(1)}, f32[256,256]{1,0:T(8,128)S(1)}, u32[]{:S(2)}, u32[]{:S(2)}) collective-permute-start(f32[256,256]{1,0:T(8,128)S(1)} %get-tuple-element.66), channel_id=1, source_target_pairs={{0,2},{1,3},{2,4},{3,5},{4,6},{5,7},{6,0},{7,1},{8,10},{9,11},{10,... | collective-permute-start | bytes 786440 | tf_op jit(solution)/shard_map/ppermute | solution.py:47
  131.0 2.8 %collective-permute-start.35 = (f32[256,256]{1,0:T(8,128)S(1)}, f32[256,256]{1,0:T(8,128)S(1)}, u32[]{:S(2)}, u32[]{:S(2)}) collective-permute-start(f32[256,256]{1,0:T(8,128)S(1)} %get-tuple-element.68), channel_id=1, source_target_pairs={{0,6},{1,7},{2,0},{3,1},{4,2},{5,3},{6,4},{7,5},{8,14},{9,15},{10,... | collective-permute-start | bytes 786440 | tf_op jit(solution)/shard_map/ppermute | solution.py:47
  133.8 9.8 %stencil.3 = (f32[16,256,256]{2,1,0:T(8,128)}, f32[8,128]{1,0:T(8,128)S(1)}) custom-call(f32[1]{0:T(128)S(6)} %div.3.inverse, s32[4]{0:T(128)S(1)} %add_convert_fusion.inside, f32[16,256,256]{2,1,0:T(8,128)S(1)} %copy-done.3, f32[256,256]{1,0:T(8,128)S(1)} %below.1.bottom, f32[256,256]{1,0:T(8,128)S(1)} %multiply_add_fusion.top, ...), custom_call_target="tpu_custom_call" | custom-call | flops 1024 | bytes 1024 | tf_op jit(solution)/shard_map/stencil/pallas_call | solution.py:365
  144.5 2.5 %collective-permute-start.38 = (f32[256,256]{1,0:T(8,128)S(1)}, f32[256,256]{1,0:T(8,128)S(1)}, u32[]{:S(2)}, u32[]{:S(2)}) collective-permute-start(f32[256,256]{1,0:T(8,128)S(1)} %get-tuple-element.71), channel_id=1, source_target_pairs={{0,6},{1,7},{2,0},{3,1},{4,2},{5,3},{6,4},{7,5},{8,14},{9,15},{10,... | collective-permute-start | bytes 786440 | tf_op jit(solution)/shard_map/ppermute | solution.py:47
  147.5 6.2 %collective-permute-done.37.refs_3_ = f32[256,256]{1,0:T(8,128)S(1)} collective-permute-done((f32[256,256]{1,0:T(8,128)S(1)}, f32[256,256]{1,0:T(8,128)S(1)}, u32[]{:S(2)}, u32[]{:S(2)}) %collective-permute-start.37) | collective-permute-done | bytes 262176 | tf_op jit(solution)/shard_map/ppermute | solution.py:47
  155.6 4.8 %fix_bottom.1.field = f32[16,256,256]{2,1,0:T(8,128)} custom-call(s32[7]{0:T(128)S(1)} %pad_add_fusion.table, f32[4,256,256]{2,1,0:T(8,128)} %bitcast.32, f32[4,256,256]{2,1,0:T(8,128)} %bitcast.36, f32[16,256,256]{2,1,0:T(8,128)} %bitcast.26, f32[2,256,256]{2,1,0:T(8,128)S(1)} %new_pair.1.refs_0_, ...), custom_call_target="tpu_custom_call", output_to_operand_aliasing={{}: (14, {})} | custom-call | flops 1024 | bytes 1024 | tf_op jit(solution)/shard_map/fix_bottom/pallas_call | solution.py:253
  160.3 3.1 %collective-permute-done.36.ghost = f32[256,256]{1,0:T(8,128)S(1)} collective-permute-done((f32[256,256]{1,0:T(8,128)S(1)}, f32[256,256]{1,0:T(8,128)S(1)}, u32[]{:S(2)}, u32[]{:S(2)}) %collective-permute-start.36) | collective-permute-done | bytes 262176 | tf_op jit(solution)/shard_map/ppermute | solution.py:51
  163.4 2.2 %fix_top.1 = f32[16,256,256]{2,1,0:T(8,128)} custom-call(s32[7]{0:T(128)S(1)} %pad_add_fusion.table, f32[256,256]{1,0:T(8,128)S(1)} %collective-permute-done.36.ghost, f32[16,256,256]{2,1,0:T(8,128)} %fix_bottom.1.field), custom_call_target="tpu_custom_call", output_to_operand_aliasing={{}: (2, {})} | custom-call | flops 1024 | bytes 1024 | tf_op jit(solution)/shard_map/fix_top/pallas_call | solution.py:277
  (109 shorter events, 37.2 us)
Async XLA Ops:
  7.7 15.8 %collective-permute-start.6 = (f32[8,256,256]{2,1,0:T(8,128)S(1)}, f32[8,256,256]{2,1,0:T(8,128)S(1)}, u32[]{:S(2)}, u32[]{:S(2)}) collective-permute-start(f32[8,256,256]{2,1,0:T(8,128)S(1)} %get-tuple-element.46), channel_id=1, source_target_pairs={{0,1},{1,0},{2,3},{3,2},{4,5},{5,4},{6,7},{7,6},{8,9},{9,8},{10,11... | collective-permute-start | bytes 6291464 | tf_op jit(solution)/shard_map/ppermute | solution.py:412
  7.8 15.7 %collective-permute-start.4 = (f32[256,256]{1,0:T(8,128)S(1)}, f32[256,256]{1,0:T(8,128)S(1)}, u32[]{:S(2)}, u32[]{:S(2)}) collective-permute-start(f32[256,256]{1,0:T(8,128)S(1)} %get-tuple-element.73.top), channel_id=1, source_target_pairs={{0,16},{1,17},{2,18},{3,19},{4,20},{5,21},{6,22},{7,23},{8,24},{9,... | collective-permute-start | bytes 786440 | tf_op jit(solution)/shard_map/ppermute | solution.py:51
  10.0 13.5 %collective-permute-start.5 = (f32[256,256]{1,0:T(8,128)S(1)}, f32[256,256]{1,0:T(8,128)S(1)}, u32[]{:S(2)}, u32[]{:S(2)}) collective-permute-start(f32[256,256]{1,0:T(8,128)S(1)} %get-tuple-element.73.top), channel_id=1, source_target_pairs={{0,24},{1,25},{2,26},{3,27},{4,28},{5,29},{6,30},{7,31},{8,16},{9,... | collective-permute-start | bytes 786440 | tf_op jit(solution)/shard_map/ppermute | solution.py:51
  14.7 8.9 %collective-permute-start = (f32[16,256]{1,0:T(8,128)S(1)}, f32[16,256]{1,0:T(8,128)S(1)}, u32[]{:S(2)}, u32[]{:S(2)}) collective-permute-start(f32[16,256]{1,0:T(8,128)S(1)} %get-tuple-element.40), channel_id=1, source_target_pairs={{0,4},{1,5},{2,6},{3,7},{4,8},{5,9},{6,10},{7,11},{8,12},{9,13},{1... | collective-permute-start | bytes 49160 | tf_op jit(solution)/shard_map/ppermute | solution.py:382
  24.8 33.3 %collective-permute-start.16 = (f32[4,256,256]{2,1,0:T(8,128)}, f32[4,256,256]{2,1,0:T(8,128)}, u32[]{:S(2)}, u32[]{:S(2)}) collective-permute-start(f32[4,256,256]{2,1,0:T(8,128)} %get-tuple-element.47.refs_2_), channel_id=1, source_target_pairs={{0,8},{1,9},{2,10},{3,11},{4,12},{5,13},{6,14},{7,15},{8,0},{9,1},... | collective-permute-start | bytes 3145736 | tf_op jit(solution)/shard_map/ppermute | solution.py:418
  31.2 16.0 %collective-permute-start.7 = (f32[2,256,256]{2,1,0:T(8,128)S(1)}, f32[2,256,256]{2,1,0:T(8,128)S(1)}, u32[]{:S(2)}, u32[]{:S(2)}) collective-permute-start(f32[2,256,256]{2,1,0:T(8,128)S(1)} %pair.1.refs_0_), channel_id=1, source_target_pairs={{0,6},{1,7},{2,0},{3,1},{4,2},{5,3},{6,4},{7,5},{8,14},{9,15},{10,... | collective-permute-start | bytes 1572872 | tf_op jit(solution)/shard_map/ppermute | solution.py:47
  34.1 14.9 %collective-permute-start.8 = (f32[2,256,256]{2,1,0:T(8,128)S(1)}, f32[2,256,256]{2,1,0:T(8,128)S(1)}, u32[]{:S(2)}, u32[]{:S(2)}) collective-permute-start(f32[2,256,256]{2,1,0:T(8,128)S(1)} %pair.1.refs_0_), channel_id=1, source_target_pairs={{0,2},{1,3},{2,4},{3,5},{4,6},{5,7},{6,0},{7,1},{8,10},{9,11},{10,... | collective-permute-start | bytes 1572872 | tf_op jit(solution)/shard_map/ppermute | solution.py:47
  47.1 12.5 %collective-permute-start.11 = (f32[2,256,256]{2,1,0:T(8,128)S(1)}, f32[2,256,256]{2,1,0:T(8,128)S(1)}, u32[]{:S(2)}, u32[]{:S(2)}) collective-permute-start(f32[2,256,256]{2,1,0:T(8,128)S(1)} %pair.1.refs_0_), channel_id=1, source_target_pairs={{0,1},{1,0},{2,3},{3,2},{4,5},{5,4},{6,7},{7,6},{8,9},{9,8},{10,11... | collective-permute-start | bytes 1572872 | tf_op jit(solution)/shard_map/ppermute | solution.py:394
  49.0 8.6 %collective-permute-start.9 = (f32[256,256]{1,0:T(8,128)S(1)}, f32[256,256]{1,0:T(8,128)S(1)}, u32[]{:S(2)}, u32[]{:S(2)}) collective-permute-start(f32[256,256]{1,0:T(8,128)S(1)} %get-tuple-element.49), channel_id=1, source_target_pairs={{0,2},{1,3},{2,4},{3,5},{4,6},{5,7},{6,0},{7,1},{8,10},{9,11},{10,... | collective-permute-start | bytes 786440 | tf_op jit(solution)/shard_map/ppermute | solution.py:47
  49.1 8.5 %collective-permute-start.10 = (f32[256,256]{1,0:T(8,128)S(1)}, f32[256,256]{1,0:T(8,128)S(1)}, u32[]{:S(2)}, u32[]{:S(2)}) collective-permute-start(f32[256,256]{1,0:T(8,128)S(1)} %get-tuple-element.50), channel_id=1, source_target_pairs={{0,6},{1,7},{2,0},{3,1},{4,2},{5,3},{6,4},{7,5},{8,14},{9,15},{10,... | collective-permute-start | bytes 786440 | tf_op jit(solution)/shard_map/ppermute | solution.py:47
  52.4 12.3 %collective-permute-start.12 = (f32[2,256,256]{2,1,0:T(8,128)S(1)}, f32[2,256,256]{2,1,0:T(8,128)S(1)}, u32[]{:S(2)}, u32[]{:S(2)}) collective-permute-start(f32[2,256,256]{2,1,0:T(8,128)S(1)} %collective-permute-done.7.refs_0_.refs_1_), channel_id=1, source_target_pairs={{0,1},{1,0},{2,3},{3,2},{4,5},{5,4},{6,7},{7,6},{8,9},{9,8},{10,11... | collective-permute-start | bytes 1572872 | tf_op jit(solution)/shard_map/ppermute | solution.py:394
  57.6 9.7 %collective-permute-start.13 = (f32[2,256,256]{2,1,0:T(8,128)S(1)}, f32[2,256,256]{2,1,0:T(8,128)S(1)}, u32[]{:S(2)}, u32[]{:S(2)}) collective-permute-start(f32[2,256,256]{2,1,0:T(8,128)S(1)} %collective-permute-done.8.refs_1_.refs_2_), channel_id=1, source_target_pairs={{0,1},{1,0},{2,3},{3,2},{4,5},{5,4},{6,7},{7,6},{8,9},{9,8},{10,11... | collective-permute-start | bytes 1572872 | tf_op jit(solution)/shard_map/ppermute | solution.py:394
  59.6 12.8 %collective-permute-start.17 = (f32[256,256]{1,0:T(8,128)S(1)}, f32[256,256]{1,0:T(8,128)S(1)}, u32[]{:S(2)}, u32[]{:S(2)}) collective-permute-start(f32[256,256]{1,0:T(8,128)S(1)} %slice_bitcast_fusion), channel_id=1, source_target_pairs={{0,16},{1,17},{2,18},{3,19},{4,20},{5,21},{6,22},{7,23},{8,24},{9,... | collective-permute-start | bytes 786440 | tf_op jit(solution)/shard_map/ppermute | solution.py:51
  60.8 11.6 %collective-permute-start.18 = (f32[256,256]{1,0:T(8,128)S(1)}, f32[256,256]{1,0:T(8,128)S(1)}, u32[]{:S(2)}, u32[]{:S(2)}) collective-permute-start(f32[256,256]{1,0:T(8,128)S(1)} %slice_bitcast_fusion), channel_id=1, source_target_pairs={{0,24},{1,25},{2,26},{3,27},{4,28},{5,29},{6,30},{7,31},{8,16},{9,... | collective-permute-start | bytes 786440 | tf_op jit(solution)/shard_map/ppermute | solution.py:51
  64.1 9.4 %collective-permute-start.19 = (f32[256,256]{1,0:T(8,128)S(1)}, f32[256,256]{1,0:T(8,128)S(1)}, u32[]{:S(2)}, u32[]{:S(2)}) collective-permute-start(f32[256,256]{1,0:T(8,128)S(1)} %get-tuple-element.53), channel_id=1, source_target_pairs={{0,2},{1,3},{2,4},{3,5},{4,6},{5,7},{6,0},{7,1},{8,10},{9,11},{10,... | collective-permute-start | bytes 786440 | tf_op jit(solution)/shard_map/ppermute | solution.py:47
  64.7 8.8 %collective-permute-start.20 = (f32[256,256]{1,0:T(8,128)S(1)}, f32[256,256]{1,0:T(8,128)S(1)}, u32[]{:S(2)}, u32[]{:S(2)}) collective-permute-start(f32[256,256]{1,0:T(8,128)S(1)} %get-tuple-element.54), channel_id=1, source_target_pairs={{0,6},{1,7},{2,0},{3,1},{4,2},{5,3},{6,4},{7,5},{8,14},{9,15},{10,... | collective-permute-start | bytes 786440 | tf_op jit(solution)/shard_map/ppermute | solution.py:47
  77.5 10.2 %collective-permute-start.24 = (f32[256,256]{1,0:T(8,128)S(1)}, f32[256,256]{1,0:T(8,128)S(1)}, u32[]{:S(2)}, u32[]{:S(2)}) collective-permute-start(f32[256,256]{1,0:T(8,128)S(1)} %get-tuple-element.60), channel_id=1, source_target_pairs={{0,4},{1,5},{2,6},{3,7},{4,0},{5,1},{6,2},{7,3},{8,12},{9,13},{10,... | collective-permute-start | bytes 786440 | tf_op jit(solution)/shard_map/ppermute | solution.py:47
  81.9 14.2 %collective-permute-start.22 = (f32[1,256,256]{2,1,0:T(8,128)S(1)}, f32[1,256,256]{2,1,0:T(8,128)S(1)}, u32[]{:S(2)}, u32[]{:S(2)}) collective-permute-start(f32[1,256,256]{2,1,0:T(8,128)S(1)} %get-tuple-element.58.refs_4_), channel_id=1, source_target_pairs={{0,8},{1,9},{2,10},{3,11},{4,12},{5,13},{6,14},{7,15},{8,0},{9,1},... | collective-permute-start | bytes 786440 | tf_op jit(solution)/shard_map/ppermute | solution.py:418
  87.8 13.1 %collective-permute-start.25 = (f32[256,256]{1,0:T(8,128)S(1)}, f32[256,256]{1,0:T(8,128)S(1)}, u32[]{:S(2)}, u32[]{:S(2)}) collective-permute-start(f32[256,256]{1,0:T(8,128)S(1)} %ghost_sum.2.refs_2_), channel_id=1, source_target_pairs={{0,112},{1,113},{2,114},{3,115},{4,116},{5,117},{6,118},{7,119},{8... | collective-permute-start | bytes 786440 | tf_op jit(solution)/shard_map/ppermute | solution.py:51
  92.0 16.9 %collective-permute-start.30 = (f32[256,256]{1,0:T(8,128)S(1)}, f32[256,256]{1,0:T(8,128)S(1)}, u32[]{:S(2)}, u32[]{:S(2)}) collective-permute-start(f32[256,256]{1,0:T(8,128)S(1)} %ghost_sum.2.refs_2_), channel_id=1, source_target_pairs={{0,8},{1,9},{2,10},{3,11},{4,12},{5,13},{6,14},{7,15},{8,0},{9,1},... | collective-permute-start | bytes 786440 | tf_op jit(solution)/shard_map/ppermute | solution.py:418
  96.0 32.3 %collective-permute-start.23 = (f32[3,256,256]{2,1,0:T(8,128)S(1)}, f32[3,256,256]{2,1,0:T(8,128)S(1)}, u32[]{:S(2)}, u32[]{:S(2)}) collective-permute-start(f32[3,256,256]{2,1,0:T(8,128)S(1)} %get-tuple-element.59), channel_id=1, source_target_pairs={{0,8},{1,9},{2,10},{3,11},{4,12},{5,13},{6,14},{7,15},{8,0},{9,1},... | collective-permute-start | bytes 2359304 | tf_op jit(solution)/shard_map/ppermute | solution.py:418
  108.9 19.4 %collective-permute-start.31 = (f32[2,256,256]{2,1,0:T(8,128)S(1)}, f32[2,256,256]{2,1,0:T(8,128)S(1)}, u32[]{:S(2)}, u32[]{:S(2)}) collective-permute-start(f32[2,256,256]{2,1,0:T(8,128)S(1)} %new_pair.1.refs_0_), channel_id=1, source_target_pairs={{0,6},{1,7},{2,0},{3,1},{4,2},{5,3},{6,4},{7,5},{8,14},{9,15},{10,... | collective-permute-start | bytes 1572872 | tf_op jit(solution)/shard_map/ppermute | solution.py:47
  111.4 16.9 %collective-permute-start.32 = (f32[2,256,256]{2,1,0:T(8,128)S(1)}, f32[2,256,256]{2,1,0:T(8,128)S(1)}, u32[]{:S(2)}, u32[]{:S(2)}) collective-permute-start(f32[2,256,256]{2,1,0:T(8,128)S(1)} %new_pair.1.refs_0_), channel_id=1, source_target_pairs={{0,2},{1,3},{2,4},{3,5},{4,6},{5,7},{6,0},{7,1},{8,10},{9,11},{10,... | collective-permute-start | bytes 1572872 | tf_op jit(solution)/shard_map/ppermute | solution.py:47
  112.8 12.4 %collective-permute-start.26 = (f32[16,256]{1,0:T(8,128)S(1)}, f32[16,256]{1,0:T(8,128)S(1)}, u32[]{:S(2)}, u32[]{:S(2)}) collective-permute-start(f32[16,256]{1,0:T(8,128)S(1)} %get-tuple-element.61), channel_id=1, source_target_pairs={{0,4},{1,5},{2,6},{3,7},{4,8},{5,9},{6,10},{7,11},{8,12},{9,13},{1... | collective-permute-start | bytes 49160 | tf_op jit(solution)/shard_map/ppermute | solution.py:382
  114.4 10.8 %collective-permute-start.27 = (f32[16,256]{1,0:T(8,128)S(1)}, f32[16,256]{1,0:T(8,128)S(1)}, u32[]{:S(2)}, u32[]{:S(2)}) collective-permute-start(f32[16,256]{1,0:T(8,128)S(1)} %get-tuple-element.62), channel_id=1, source_target_pairs={{4,0},{5,1},{6,2},{7,3},{8,4},{9,5},{10,6},{11,7},{12,8},{13,9},{1... | collective-permute-start | bytes 49160 | tf_op jit(solution)/shard_map/ppermute | solution.py:383
  128.5 16.0 %collective-permute-start.33 = (f32[256,256]{1,0:T(8,128)S(1)}, f32[256,256]{1,0:T(8,128)S(1)}, u32[]{:S(2)}, u32[]{:S(2)}) collective-permute-start(f32[256,256]{1,0:T(8,128)S(1)} %get-tuple-element.66), channel_id=1, source_target_pairs={{0,2},{1,3},{2,4},{3,5},{4,6},{5,7},{6,0},{7,1},{8,10},{9,11},{10,... | collective-permute-start | bytes 786440 | tf_op jit(solution)/shard_map/ppermute | solution.py:47
  131.0 15.9 %collective-permute-start.34 = (f32[256,256]{1,0:T(8,128)S(1)}, f32[256,256]{1,0:T(8,128)S(1)}, u32[]{:S(2)}, u32[]{:S(2)}) collective-permute-start(f32[256,256]{1,0:T(8,128)S(1)} %get-tuple-element.67), channel_id=1, source_target_pairs={{0,4},{1,5},{2,6},{3,7},{4,0},{5,1},{6,2},{7,3},{8,12},{9,13},{10,... | collective-permute-start | bytes 786440 | tf_op jit(solution)/shard_map/ppermute | solution.py:47
  131.0 15.9 %collective-permute-start.35 = (f32[256,256]{1,0:T(8,128)S(1)}, f32[256,256]{1,0:T(8,128)S(1)}, u32[]{:S(2)}, u32[]{:S(2)}) collective-permute-start(f32[256,256]{1,0:T(8,128)S(1)} %get-tuple-element.68), channel_id=1, source_target_pairs={{0,6},{1,7},{2,0},{3,1},{4,2},{5,3},{6,4},{7,5},{8,14},{9,15},{10,... | collective-permute-start | bytes 786440 | tf_op jit(solution)/shard_map/ppermute | solution.py:47
  133.8 20.4 %collective-permute-start.39 = (f32[2,256,256]{2,1,0:T(8,128)S(1)}, f32[2,256,256]{2,1,0:T(8,128)S(1)}, u32[]{:S(2)}, u32[]{:S(2)}) collective-permute-start(f32[2,256,256]{2,1,0:T(8,128)S(1)} %new_pair.1.refs_0_), channel_id=1, source_target_pairs={{0,1},{1,0},{2,3},{3,2},{4,5},{5,4},{6,7},{7,6},{8,9},{9,8},{10,11... | collective-permute-start | bytes 1572872 | tf_op jit(solution)/shard_map/ppermute | solution.py:394
  143.7 10.0 %collective-permute-start.37 = (f32[256,256]{1,0:T(8,128)S(1)}, f32[256,256]{1,0:T(8,128)S(1)}, u32[]{:S(2)}, u32[]{:S(2)}) collective-permute-start(f32[256,256]{1,0:T(8,128)S(1)} %get-tuple-element.70), channel_id=1, source_target_pairs={{0,2},{1,3},{2,4},{3,5},{4,6},{5,7},{6,0},{7,1},{8,10},{9,11},{10,... | collective-permute-start | bytes 786440 | tf_op jit(solution)/shard_map/ppermute | solution.py:47
  144.5 9.2 %collective-permute-start.38 = (f32[256,256]{1,0:T(8,128)S(1)}, f32[256,256]{1,0:T(8,128)S(1)}, u32[]{:S(2)}, u32[]{:S(2)}) collective-permute-start(f32[256,256]{1,0:T(8,128)S(1)} %get-tuple-element.71), channel_id=1, source_target_pairs={{0,6},{1,7},{2,0},{3,1},{4,2},{5,3},{6,4},{7,5},{8,14},{9,15},{10,... | collective-permute-start | bytes 786440 | tf_op jit(solution)/shard_map/ppermute | solution.py:47
  154.2 9.2 %collective-permute-start.36 = (f32[256,256]{1,0:T(8,128)S(1)}, f32[256,256]{1,0:T(8,128)S(1)}, u32[]{:S(2)}, u32[]{:S(2)}) collective-permute-start(f32[256,256]{1,0:T(8,128)S(1)} %ghost_sum.3), channel_id=1, source_target_pairs={{0,112},{1,113},{2,114},{3,115},{4,116},{5,117},{6,118},{7,119},{8... | collective-permute-start | bytes 786440 | tf_op jit(solution)/shard_map/ppermute | solution.py:51
  (26 other events, 169.4 us)

commit v14 on v11

--- a/solution.py
+++ b/solution.py
@@ -224,7 +224,7 @@
 BELOW_SCRATCH = [
     pltpu.VMEM((4, W, W), F32),
     pltpu.VMEM((2, W, W), F32),
-    pltpu.SemaphoreType.DMA((7,)),
+    pltpu.SemaphoreType.DMA((8,)),
 ]
 
 
@@ -242,19 +242,22 @@
 
 
 def fix_bottom_kernel(table, px, py, speed, *refs):
-    tops, (field, out, picked, ends, sems) = refs[:10], refs[10:]
+    tops, (field, out, high, picked, ends, sems) = refs[:10], refs[10:]
+    fetch = pltpu.make_async_copy(field.at[NZ - 1], high, sems.at[7])
+    fetch.start()
     ends[0] = below_value(table, px, py, field, speed, tops, picked, ends, sems)
     copy = pltpu.make_async_copy(ends.at[0], out.at[0], sems.at[6])
     copy.start()
+    fetch.wait()
     copy.wait()
 
 
 def fix_bottom(table, px, py, speed, tops, field):
     return pl.pallas_call(
         fix_bottom_kernel,
-        out_shape=planes(NZ),
+        out_shape=(planes(NZ), planes()),
         in_specs=[SMEM_SPEC] + [VMEM_SPEC] * 2 + [ANY_SPEC] * 11 + [pl.BlockSpec(memory_space=pltpu.HBM)],
-        out_specs=pl.BlockSpec(memory_space=pltpu.HBM),
+        out_specs=[pl.BlockSpec(memory_space=pltpu.HBM), VMEM_SPEC],
         scratch_shapes=BELOW_SCRATCH,
         input_output_aliases={14: 0},
         compiler_params=pltpu.CompilerParams(vmem_limit_bytes=50 * MIB),
@@ -263,28 +266,25 @@
     )(table, px, py, speed, *tops, field)
 
 
-def fix_top_kernel(table, ghost, field, out, plane, sems):
-    fetch = pltpu.make_async_copy(field.at[NZ - 1], plane, sems.at[0])
-    fetch.start()
-    fetch.wait()
-    plane[...] = plane[...] + TIME_STEP * jnp.where(table[6] == 1, AMBIENT, ghost[...])
-    store = pltpu.make_async_copy(plane, out.at[NZ - 1], sems.at[1])
+def fix_top_kernel(table, ghost, high, field, out, plane, sems):
+    plane[...] = high[...] + TIME_STEP * jnp.where(table[6] == 1, AMBIENT, ghost[...])
+    store = pltpu.make_async_copy(plane, out.at[NZ - 1], sems.at[0])
     store.start()
     store.wait()
 
 
-def fix_top(table, ghost, field):
+def fix_top(table, ghost, high, field):
     return pl.pallas_call(
         fix_top_kernel,
         out_shape=planes(NZ),
-        in_specs=[SMEM_SPEC, VMEM_SPEC, pl.BlockSpec(memory_space=pltpu.HBM)],
+        in_specs=[SMEM_SPEC, VMEM_SPEC, VMEM_SPEC, pl.BlockSpec(memory_space=pltpu.HBM)],
         out_specs=pl.BlockSpec(memory_space=pltpu.HBM),
-        scratch_shapes=[pltpu.VMEM((W, W), F32), pltpu.SemaphoreType.DMA((2,))],
-        input_output_aliases={2: 0},
+        scratch_shapes=[pltpu.VMEM((W, W), F32), pltpu.SemaphoreType.DMA((1,))],
+        input_output_aliases={3: 0},
         compiler_params=pltpu.CompilerParams(vmem_limit_bytes=8 * MIB),
         cost_estimate=SMALL,
         name="fix_top",
-    )(table, ghost, field)
+    )(table, ghost, high, field)
 
 
 def rims_kernel(field, bottom, top, *refs):
@@ -475,8 +475,8 @@
     tops = [pair, *near, *far]
     tops = tops + [other_core(value) for value in tops]
     ghost = send_lift(ghost_sum(parts, mark), -1, False)
-    field = fix_bottom(table, px, py, speed, tops, field)
-    field = fix_top(table, ghost, field)
+    field, high = fix_bottom(table, px, py, speed, tops, field)
+    field = fix_top(table, ghost, high, field)
     return field.reshape(1, NZ, 1, W, W)
 
 

time: 165 us -> 164 us (level)
  transfers between devices with their start and end apart: 44 -> 44, of which waited for: 16 -> 17; matrix products, arithmetic and copies ran while one was open for 0% -> 0% of each run, Pallas kernels for 19% -> 19%
where the time goes in v14:
time: 164 us; the launch traced here: 162 us
  starting transfers between devices  57.1 us (35%)
  waiting for transfers between devices  50.1 us (31%)
  Pallas kernels  41 us (25%)
  local copies, waits for them, and re-layouts  11.4 us (7%)
    ppermute x14, waiting for transfers between devices, send_y(): return lax.ppermute(value, 'tile', along_y(steps))  19.4 us
    ppermute x14, starting transfers between devices, send_y(): return lax.ppermute(value, 'tile', along_y(steps))  19.1 us
    pallas_call x2, Pallas kernels, stencil(): pl.pallas_call(stencil_kernel, out_shape=(planes(NZ), MARK), in_specs=[SM...  17.6 us
    ppermute x6, starting transfers between devices, send_lift(): return lax.ppermute(value, ('lift', 'tile'), to_lift(steps, flip))  12.3 us
    ppermute x2, waiting for transfers between devices, exchange_rims(): x_low = lax.ppermute(row_high, 'tile', up)  10.7 us
    unnamed x28, local copies, waits for them, and re-layouts  10.3 us
    ppermute x4, starting transfers between devices, reduce_halves(): return lax.ppermute(give, 'tile', OTHER_HALF)  8.42 us
    ppermute x6, waiting for transfers between devices, send_lift(): return lax.ppermute(value, ('lift', 'tile'), to_lift(steps, flip))  8.32 us
  transfers between devices with their start and end apart: 44, of which 17 were waited for; matrix products, arithmetic and copies ran while one was open for 0% of the time, Pallas kernels for 19%

profile of v14, /device:TPU:6, one launch (start us, length us, event | category | flops | bytes accessed | tf_op | source)
XLA Modules:
  0.0 161.6 jit_solution(12058670327309322448)
XLA Ops:
  4.3 3.4 %pieces.2 = (f32[8,256,256]{2,1,0:T(8,128)S(1)}, f32[8,256,256]{2,1,0:T(8,128)S(1)}, f32[8,128]{1,0:T(8,128)S(1)}) custom-call(s32[7]{0:T(128)S(1)} %pad_add_fusion.table, f32[4,256,256]{2,1,0:T(8,128)S(1)} %bitcast.33, f32[4,256,256]{2,1,0:T(8,128)S(1)} %bitcast.37, f32[256,256]{1,0:T(8,128)S(1)} %get-tuple-element.78.bottom), custom_call_target="tpu_custom_call" | custom-call | flops 1024 | bytes 1024 | tf_op jit(solution)/shard_map/pieces/pallas_call | solution.py:108
  7.8 2.3 %collective-permute-start.4 = (f32[256,256]{1,0:T(8,128)S(1)}, f32[256,256]{1,0:T(8,128)S(1)}, u32[]{:S(2)}, u32[]{:S(2)}) collective-permute-start(f32[256,256]{1,0:T(8,128)S(1)} %get-tuple-element.77.top), channel_id=1, source_target_pairs={{0,16},{1,17},{2,18},{3,19},{4,20},{5,21},{6,22},{7,23},{8,24},{9,... | collective-permute-start | bytes 786440 | tf_op jit(solution)/shard_map/ppermute | solution.py:51
  11.2 2.2 %copy-done.4 = f32[1,16,1,256,256]{4,3,2,1,0:T(8,128)S(1)} copy-done((f32[1,16,1,256,256]{4,3,2,1,0:T(8,128)S(1)}, f32[1,16,1,256,256]{4,3,2,1,0:T(8,128)}, u32[]{:S(2)}) %copy-start.4) | copy-done | bytes 4194328
  14.7 3.2 %collective-permute-start = (f32[16,256]{1,0:T(8,128)S(1)}, f32[16,256]{1,0:T(8,128)S(1)}, u32[]{:S(2)}, u32[]{:S(2)}) collective-permute-start(f32[16,256]{1,0:T(8,128)S(1)} %get-tuple-element.42), channel_id=1, source_target_pairs={{0,4},{1,5},{2,6},{3,7},{4,8},{5,9},{6,10},{7,11},{8,12},{9,13},{1... | collective-permute-start | bytes 49160 | tf_op jit(solution)/shard_map/ppermute | solution.py:382
  17.9 2.7 %collective-permute-start.1 = (f32[16,256]{1,0:T(8,128)S(1)}, f32[16,256]{1,0:T(8,128)S(1)}, u32[]{:S(2)}, u32[]{:S(2)}) collective-permute-start(f32[16,256]{1,0:T(8,128)S(1)} %get-tuple-element.43), channel_id=1, source_target_pairs={{4,0},{5,1},{6,2},{7,3},{8,4},{9,5},{10,6},{11,7},{12,8},{13,9},{1... | collective-permute-start | bytes 49160 | tf_op jit(solution)/shard_map/ppermute | solution.py:383
  20.6 2.9 %collective-permute-done.x_low.refs_4_ = f32[16,256]{1,0:T(8,128)S(1)} collective-permute-done((f32[16,256]{1,0:T(8,128)S(1)}, f32[16,256]{1,0:T(8,128)S(1)}, u32[]{:S(2)}, u32[]{:S(2)}) %collective-permute-start) | collective-permute-done | bytes 16416 | tf_op jit(solution)/shard_map/ppermute | solution.py:382
  28.0 3.2 %collective-permute-start.16 = (f32[4,256,256]{2,1,0:T(8,128)}, f32[4,256,256]{2,1,0:T(8,128)}, u32[]{:S(2)}, u32[]{:S(2)}) collective-permute-start(f32[4,256,256]{2,1,0:T(8,128)} %get-tuple-element.49.refs_2_), channel_id=1, source_target_pairs={{0,8},{1,9},{2,10},{3,11},{4,12},{5,13},{6,14},{7,15},{8,0},{9,1},... | collective-permute-start | bytes 3145736 | tf_op jit(solution)/shard_map/ppermute | solution.py:418
  34.0 2.2 %copy-done = f32[1,16,1,256,256]{4,3,2,1,0:T(8,128)S(1)} copy-done((f32[1,16,1,256,256]{4,3,2,1,0:T(8,128)S(1)}, f32[1,16,1,256,256]{4,3,2,1,0:T(8,128)}, u32[]{:S(2)}) %copy-start) | copy-done | bytes 4194328
  36.2 2.2 %copy-done.5 = f32[1,16,1,256,256]{4,3,2,1,0:T(8,128)S(1)} copy-done((f32[1,16,1,256,256]{4,3,2,1,0:T(8,128)S(1)}, f32[1,16,1,256,256]{4,3,2,1,0:T(8,128)}, u32[]{:S(2)}) %copy-start.5) | copy-done | bytes 4194328
  38.4 7.8 %stencil.2 = (f32[16,256,256]{2,1,0:T(8,128)S(1)}, f32[8,128]{1,0:T(8,128)S(1)}) custom-call(f32[1]{0:T(128)S(6)} %div.3.inverse, s32[4]{0:T(128)S(1)} %add_convert_fusion.inside, f32[16,256,256]{2,1,0:T(8,128)S(1)} %bitcast.30, f32[256,256]{1,0:T(8,128)S(1)} %get-tuple-element.78.bottom, f32[256,256]{1,0:T(8,128)S(1)} %get-tuple-element.77.top, ...), custom_call_target="tpu_custom_call" | custom-call | flops 1024 | bytes 1024 | tf_op jit(solution)/shard_map/stencil/pallas_call | solution.py:365
  47.7 2.7 %collective-permute-start.10 = (f32[256,256]{1,0:T(8,128)S(1)}, f32[256,256]{1,0:T(8,128)S(1)}, u32[]{:S(2)}, u32[]{:S(2)}) collective-permute-start(f32[256,256]{1,0:T(8,128)S(1)} %get-tuple-element.52), channel_id=1, source_target_pairs={{0,6},{1,7},{2,0},{3,1},{4,2},{5,3},{6,4},{7,5},{8,14},{9,15},{10,... | collective-permute-start | bytes 786440 | tf_op jit(solution)/shard_map/ppermute | solution.py:47
  50.4 6.0 %collective-permute-done.9.refs_3_ = f32[256,256]{1,0:T(8,128)S(1)} collective-permute-done((f32[256,256]{1,0:T(8,128)S(1)}, f32[256,256]{1,0:T(8,128)S(1)}, u32[]{:S(2)}, u32[]{:S(2)}) %collective-permute-start.9) | collective-permute-done | bytes 262176 | tf_op jit(solution)/shard_map/ppermute | solution.py:47
  59.1 3.1 %collective-permute-start.18 = (f32[256,256]{1,0:T(8,128)S(1)}, f32[256,256]{1,0:T(8,128)S(1)}, u32[]{:S(2)}, u32[]{:S(2)}) collective-permute-start(f32[256,256]{1,0:T(8,128)S(1)} %slice_bitcast_fusion), channel_id=1, source_target_pairs={{0,24},{1,25},{2,26},{3,27},{4,28},{5,29},{6,30},{7,31},{8,16},{9,... | collective-permute-start | bytes 786440 | tf_op jit(solution)/shard_map/ppermute | solution.py:51
  62.9 2.5 %collective-permute-start.20 = (f32[256,256]{1,0:T(8,128)S(1)}, f32[256,256]{1,0:T(8,128)S(1)}, u32[]{:S(2)}, u32[]{:S(2)}) collective-permute-start(f32[256,256]{1,0:T(8,128)S(1)} %get-tuple-element.56), channel_id=1, source_target_pairs={{0,6},{1,7},{2,0},{3,1},{4,2},{5,3},{6,4},{7,5},{8,14},{9,15},{10,... | collective-permute-start | bytes 786440 | tf_op jit(solution)/shard_map/ppermute | solution.py:47
  66.2 4.2 %below.1.bottom = f32[256,256]{1,0:T(8,128)S(1)} custom-call(s32[7]{0:T(128)S(1)} %pad_add_fusion.table, f32[4,256,256]{2,1,0:T(8,128)} %bitcast.31, f32[4,256,256]{2,1,0:T(8,128)} %bitcast.35, f32[16,256,256]{2,1,0:T(8,128)} %copy-done.2, f32[16,256,256]{2,1,0:T(8,128)} %bitcast.25, f32[2,256,256]{2,1,0:T(8,128)S(1)} %pair.1.refs_0_, ...), custom_call_target="tpu_custom_call" | custom-call | flops 1024 | bytes 1024 | tf_op jit(solution)/shard_map/below/pallas_call | solution.py:232
  71.5 4.0 %pieces.3 = (f32[8,256,256]{2,1,0:T(8,128)S(1)}, f32[8,256,256]{2,1,0:T(8,128)S(1)}, f32[8,128]{1,0:T(8,128)}) custom-call(s32[7]{0:T(128)S(1)} %pad_add_fusion.table, f32[4,256,256]{2,1,0:T(8,128)S(1)} %bitcast.34, f32[4,256,256]{2,1,0:T(8,128)S(1)} %bitcast.38, f32[256,256]{1,0:T(8,128)S(1)} %below.1.bottom, ...), custom_call_target="tpu_custom_call" | custom-call | flops 1024 | bytes 1024 | tf_op jit(solution)/shard_map/pieces/pallas_call | solution.py:108
  75.6 2.1 %collective-permute-start.24 = (f32[256,256]{1,0:T(8,128)S(1)}, f32[256,256]{1,0:T(8,128)S(1)}, u32[]{:S(2)}, u32[]{:S(2)}) collective-permute-start(f32[256,256]{1,0:T(8,128)S(1)} %get-tuple-element.62), channel_id=1, source_target_pairs={{0,4},{1,5},{2,6},{3,7},{4,0},{5,1},{6,2},{7,3},{8,12},{9,13},{10,... | collective-permute-start | bytes 786440 | tf_op jit(solution)/shard_map/ppermute | solution.py:47
  77.7 2.1 %collective-permute-done.21.refs_1_ = f32[8,256,256]{2,1,0:T(8,128)S(1)} collective-permute-done((f32[8,256,256]{2,1,0:T(8,128)S(1)}, f32[8,256,256]{2,1,0:T(8,128)S(1)}, u32[]{:S(2)}, u32[]{:S(2)}) %collective-permute-start.21) | collective-permute-done | bytes 2097184 | tf_op jit(solution)/shard_map/ppermute | solution.py:412
  81.7 4.1 %collective-permute-done.24.refs_2_ = f32[256,256]{1,0:T(8,128)S(1)} collective-permute-done((f32[256,256]{1,0:T(8,128)S(1)}, f32[256,256]{1,0:T(8,128)S(1)}, u32[]{:S(2)}, u32[]{:S(2)}) %collective-permute-start.24) | collective-permute-done | bytes 262176 | tf_op jit(solution)/shard_map/ppermute | solution.py:47
  85.9 3.9 %collective-permute-start.25 = (f32[256,256]{1,0:T(8,128)S(1)}, f32[256,256]{1,0:T(8,128)S(1)}, u32[]{:S(2)}, u32[]{:S(2)}) collective-permute-start(f32[256,256]{1,0:T(8,128)S(1)} %ghost_sum.2.refs_2_), channel_id=1, source_target_pairs={{0,112},{1,113},{2,114},{3,115},{4,116},{5,117},{6,118},{7,119},{8... | collective-permute-start | bytes 786440 | tf_op jit(solution)/shard_map/ppermute | solution.py:51
  89.8 2.4 %collective-permute-start.30 = (f32[256,256]{1,0:T(8,128)S(1)}, f32[256,256]{1,0:T(8,128)S(1)}, u32[]{:S(2)}, u32[]{:S(2)}) collective-permute-start(f32[256,256]{1,0:T(8,128)S(1)} %ghost_sum.2.refs_2_), channel_id=1, source_target_pairs={{0,8},{1,9},{2,10},{3,11},{4,12},{5,13},{6,14},{7,15},{8,0},{9,1},... | collective-permute-start | bytes 786440 | tf_op jit(solution)/shard_map/ppermute | solution.py:418
  93.3 5.2 %collective-permute-done.25.refs_5_ = f32[256,256]{1,0:T(8,128)S(1)} collective-permute-done((f32[256,256]{1,0:T(8,128)S(1)}, f32[256,256]{1,0:T(8,128)S(1)}, u32[]{:S(2)}, u32[]{:S(2)}) %collective-permute-start.25) | collective-permute-done | bytes 262176 | tf_op jit(solution)/shard_map/ppermute | solution.py:51
  98.5 6.4 %collective-permute-done.30.refs_3_ = f32[256,256]{1,0:T(8,128)S(1)} collective-permute-done((f32[256,256]{1,0:T(8,128)S(1)}, f32[256,256]{1,0:T(8,128)S(1)}, u32[]{:S(2)}, u32[]{:S(2)}) %collective-permute-start.30) | collective-permute-done | bytes 262176 | tf_op jit(solution)/shard_map/ppermute | solution.py:418
  105.0 2.6 %collective-permute-start.31 = (f32[2,256,256]{2,1,0:T(8,128)S(1)}, f32[2,256,256]{2,1,0:T(8,128)S(1)}, u32[]{:S(2)}, u32[]{:S(2)}) collective-permute-start(f32[2,256,256]{2,1,0:T(8,128)S(1)} %new_pair.1.refs_0_), channel_id=1, source_target_pairs={{0,6},{1,7},{2,0},{3,1},{4,2},{5,3},{6,4},{7,5},{8,14},{9,15},{10,... | collective-permute-start | bytes 1572872 | tf_op jit(solution)/shard_map/ppermute | solution.py:47
  109.0 2.0 %collective-permute-start.26 = (f32[16,256]{1,0:T(8,128)S(1)}, f32[16,256]{1,0:T(8,128)S(1)}, u32[]{:S(2)}, u32[]{:S(2)}) collective-permute-start(f32[16,256]{1,0:T(8,128)S(1)} %get-tuple-element.63), channel_id=1, source_target_pairs={{0,4},{1,5},{2,6},{3,7},{4,8},{5,9},{6,10},{7,11},{8,12},{9,13},{1... | collective-permute-start | bytes 49160 | tf_op jit(solution)/shard_map/ppermute | solution.py:382
  110.9 4.0 %collective-permute-start.27 = (f32[16,256]{1,0:T(8,128)S(1)}, f32[16,256]{1,0:T(8,128)S(1)}, u32[]{:S(2)}, u32[]{:S(2)}) collective-permute-start(f32[16,256]{1,0:T(8,128)S(1)} %get-tuple-element.64), channel_id=1, source_target_pairs={{4,0},{5,1},{6,2},{7,3},{8,4},{9,5},{10,6},{11,7},{12,8},{13,9},{1... | collective-permute-start | bytes 49160 | tf_op jit(solution)/shard_map/ppermute | solution.py:383
  114.9 7.8 %collective-permute-done.26.refs_3_.x_low = f32[16,256]{1,0:T(8,128)S(1)} collective-permute-done((f32[16,256]{1,0:T(8,128)S(1)}, f32[16,256]{1,0:T(8,128)S(1)}, u32[]{:S(2)}, u32[]{:S(2)}) %collective-permute-start.26) | collective-permute-done | bytes 16416 | tf_op jit(solution)/shard_map/ppermute | solution.py:382
  127.1 2.8 %collective-permute-start.35 = (f32[256,256]{1,0:T(8,128)S(1)}, f32[256,256]{1,0:T(8,128)S(1)}, u32[]{:S(2)}, u32[]{:S(2)}) collective-permute-start(f32[256,256]{1,0:T(8,128)S(1)} %get-tuple-element.70), channel_id=1, source_target_pairs={{0,6},{1,7},{2,0},{3,1},{4,2},{5,3},{6,4},{7,5},{8,14},{9,15},{10,... | collective-permute-start | bytes 786440 | tf_op jit(solution)/shard_map/ppermute | solution.py:47
  130.5 9.8 %stencil.3 = (f32[16,256,256]{2,1,0:T(8,128)}, f32[8,128]{1,0:T(8,128)S(1)}) custom-call(f32[1]{0:T(128)S(6)} %div.3.inverse, s32[4]{0:T(128)S(1)} %add_convert_fusion.inside, f32[16,256,256]{2,1,0:T(8,128)S(1)} %copy-done.3, f32[256,256]{1,0:T(8,128)S(1)} %below.1.bottom, f32[256,256]{1,0:T(8,128)S(1)} %multiply_add_fusion.top, ...), custom_call_target="tpu_custom_call" | custom-call | flops 1024 | bytes 1024 | tf_op jit(solution)/shard_map/stencil/pallas_call | solution.py:365
  144.1 5.7 %collective-permute-done.37.refs_3_ = f32[256,256]{1,0:T(8,128)S(1)} collective-permute-done((f32[256,256]{1,0:T(8,128)S(1)}, f32[256,256]{1,0:T(8,128)S(1)}, u32[]{:S(2)}, u32[]{:S(2)}) %collective-permute-start.37) | collective-permute-done | bytes 262176 | tf_op jit(solution)/shard_map/ppermute | solution.py:47
  152.4 4.8 %fix_bottom.1 = (f32[16,256,256]{2,1,0:T(8,128)}, f32[256,256]{1,0:T(8,128)S(1)}) custom-call(s32[7]{0:T(128)S(1)} %pad_add_fusion.table, f32[4,256,256]{2,1,0:T(8,128)} %bitcast.32, f32[4,256,256]{2,1,0:T(8,128)} %bitcast.36, f32[16,256,256]{2,1,0:T(8,128)} %bitcast.26, f32[2,256,256]{2,1,0:T(8,128)S(1)} %new_pair.1.refs_0_, ...), custom_call_target="tpu_custom_call", output_to_operand_aliasing={{0}: (14, {})} | custom-call | flops 1024 | bytes 1024 | tf_op jit(solution)/shard_map/fix_bottom/pallas_call | solution.py:256
  157.2 3.0 %collective-permute-done.36.ghost = f32[256,256]{1,0:T(8,128)S(1)} collective-permute-done((f32[256,256]{1,0:T(8,128)S(1)}, f32[256,256]{1,0:T(8,128)S(1)}, u32[]{:S(2)}, u32[]{:S(2)}) %collective-permute-start.36) | collective-permute-done | bytes 262176 | tf_op jit(solution)/shard_map/ppermute | solution.py:51
  (109 shorter events, 37.5 us)
Async XLA Ops:
  7.7 19.0 %collective-permute-start.6 = (f32[8,256,256]{2,1,0:T(8,128)S(1)}, f32[8,256,256]{2,1,0:T(8,128)S(1)}, u32[]{:S(2)}, u32[]{:S(2)}) collective-permute-start(f32[8,256,256]{2,1,0:T(8,128)S(1)} %get-tuple-element.48), channel_id=1, source_target_pairs={{0,1},{1,0},{2,3},{3,2},{4,5},{5,4},{6,7},{7,6},{8,9},{9,8},{10,11... | collective-permute-start | bytes 6291464 | tf_op jit(solution)/shard_map/ppermute | solution.py:412
  7.8 18.9 %collective-permute-start.4 = (f32[256,256]{1,0:T(8,128)S(1)}, f32[256,256]{1,0:T(8,128)S(1)}, u32[]{:S(2)}, u32[]{:S(2)}) collective-permute-start(f32[256,256]{1,0:T(8,128)S(1)} %get-tuple-element.77.top), channel_id=1, source_target_pairs={{0,16},{1,17},{2,18},{3,19},{4,20},{5,21},{6,22},{7,23},{8,24},{9,... | collective-permute-start | bytes 786440 | tf_op jit(solution)/shard_map/ppermute | solution.py:51
  10.0 16.7 %collective-permute-start.5 = (f32[256,256]{1,0:T(8,128)S(1)}, f32[256,256]{1,0:T(8,128)S(1)}, u32[]{:S(2)}, u32[]{:S(2)}) collective-permute-start(f32[256,256]{1,0:T(8,128)S(1)} %get-tuple-element.77.top), channel_id=1, source_target_pairs={{0,24},{1,25},{2,26},{3,27},{4,28},{5,29},{6,30},{7,31},{8,16},{9,... | collective-permute-start | bytes 786440 | tf_op jit(solution)/shard_map/ppermute | solution.py:51
  14.7 8.9 %collective-permute-start = (f32[16,256]{1,0:T(8,128)S(1)}, f32[16,256]{1,0:T(8,128)S(1)}, u32[]{:S(2)}, u32[]{:S(2)}) collective-permute-start(f32[16,256]{1,0:T(8,128)S(1)} %get-tuple-element.42), channel_id=1, source_target_pairs={{0,4},{1,5},{2,6},{3,7},{4,8},{5,9},{6,10},{7,11},{8,12},{9,13},{1... | collective-permute-start | bytes 49160 | tf_op jit(solution)/shard_map/ppermute | solution.py:382
  28.0 28.9 %collective-permute-start.16 = (f32[4,256,256]{2,1,0:T(8,128)}, f32[4,256,256]{2,1,0:T(8,128)}, u32[]{:S(2)}, u32[]{:S(2)}) collective-permute-start(f32[4,256,256]{2,1,0:T(8,128)} %get-tuple-element.49.refs_2_), channel_id=1, source_target_pairs={{0,8},{1,9},{2,10},{3,11},{4,12},{5,13},{6,14},{7,15},{8,0},{9,1},... | collective-permute-start | bytes 3145736 | tf_op jit(solution)/shard_map/ppermute | solution.py:418
  31.2 15.2 %collective-permute-start.7 = (f32[2,256,256]{2,1,0:T(8,128)S(1)}, f32[2,256,256]{2,1,0:T(8,128)S(1)}, u32[]{:S(2)}, u32[]{:S(2)}) collective-permute-start(f32[2,256,256]{2,1,0:T(8,128)S(1)} %pair.1.refs_0_), channel_id=1, source_target_pairs={{0,6},{1,7},{2,0},{3,1},{4,2},{5,3},{6,4},{7,5},{8,14},{9,15},{10,... | collective-permute-start | bytes 1572872 | tf_op jit(solution)/shard_map/ppermute | solution.py:47
  32.4 14.6 %collective-permute-start.8 = (f32[2,256,256]{2,1,0:T(8,128)S(1)}, f32[2,256,256]{2,1,0:T(8,128)S(1)}, u32[]{:S(2)}, u32[]{:S(2)}) collective-permute-start(f32[2,256,256]{2,1,0:T(8,128)S(1)} %pair.1.refs_0_), channel_id=1, source_target_pairs={{0,2},{1,3},{2,4},{3,5},{4,6},{5,7},{6,0},{7,1},{8,10},{9,11},{10,... | collective-permute-start | bytes 1572872 | tf_op jit(solution)/shard_map/ppermute | solution.py:47
  46.2 12.1 %collective-permute-start.11 = (f32[2,256,256]{2,1,0:T(8,128)S(1)}, f32[2,256,256]{2,1,0:T(8,128)S(1)}, u32[]{:S(2)}, u32[]{:S(2)}) collective-permute-start(f32[2,256,256]{2,1,0:T(8,128)S(1)} %pair.1.refs_0_), channel_id=1, source_target_pairs={{0,1},{1,0},{2,3},{3,2},{4,5},{5,4},{6,7},{7,6},{8,9},{9,8},{10,11... | collective-permute-start | bytes 1572872 | tf_op jit(solution)/shard_map/ppermute | solution.py:394
  47.1 9.3 %collective-permute-start.9 = (f32[256,256]{1,0:T(8,128)S(1)}, f32[256,256]{1,0:T(8,128)S(1)}, u32[]{:S(2)}, u32[]{:S(2)}) collective-permute-start(f32[256,256]{1,0:T(8,128)S(1)} %get-tuple-element.51), channel_id=1, source_target_pairs={{0,2},{1,3},{2,4},{3,5},{4,6},{5,7},{6,0},{7,1},{8,10},{9,11},{10,... | collective-permute-start | bytes 786440 | tf_op jit(solution)/shard_map/ppermute | solution.py:47
  47.7 8.7 %collective-permute-start.10 = (f32[256,256]{1,0:T(8,128)S(1)}, f32[256,256]{1,0:T(8,128)S(1)}, u32[]{:S(2)}, u32[]{:S(2)}) collective-permute-start(f32[256,256]{1,0:T(8,128)S(1)} %get-tuple-element.52), channel_id=1, source_target_pairs={{0,6},{1,7},{2,0},{3,1},{4,2},{5,3},{6,4},{7,5},{8,14},{9,15},{10,... | collective-permute-start | bytes 786440 | tf_op jit(solution)/shard_map/ppermute | solution.py:47
  50.4 12.5 %collective-permute-start.12 = (f32[2,256,256]{2,1,0:T(8,128)S(1)}, f32[2,256,256]{2,1,0:T(8,128)S(1)}, u32[]{:S(2)}, u32[]{:S(2)}) collective-permute-start(f32[2,256,256]{2,1,0:T(8,128)S(1)} %collective-permute-done.7.refs_0_.refs_1_), channel_id=1, source_target_pairs={{0,1},{1,0},{2,3},{3,2},{4,5},{5,4},{6,7},{7,6},{8,9},{9,8},{10,11... | collective-permute-start | bytes 1572872 | tf_op jit(solution)/shard_map/ppermute | solution.py:394
  56.4 9.0 %collective-permute-start.13 = (f32[2,256,256]{2,1,0:T(8,128)S(1)}, f32[2,256,256]{2,1,0:T(8,128)S(1)}, u32[]{:S(2)}, u32[]{:S(2)}) collective-permute-start(f32[2,256,256]{2,1,0:T(8,128)S(1)} %collective-permute-done.8.refs_1_.refs_2_), channel_id=1, source_target_pairs={{0,1},{1,0},{2,3},{3,2},{4,5},{5,4},{6,7},{7,6},{8,9},{9,8},{10,11... | collective-permute-start | bytes 1572872 | tf_op jit(solution)/shard_map/ppermute | solution.py:394
  58.3 12.1 %collective-permute-start.17 = (f32[256,256]{1,0:T(8,128)S(1)}, f32[256,256]{1,0:T(8,128)S(1)}, u32[]{:S(2)}, u32[]{:S(2)}) collective-permute-start(f32[256,256]{1,0:T(8,128)S(1)} %slice_bitcast_fusion), channel_id=1, source_target_pairs={{0,16},{1,17},{2,18},{3,19},{4,20},{5,21},{6,22},{7,23},{8,24},{9,... | collective-permute-start | bytes 786440 | tf_op jit(solution)/shard_map/ppermute | solution.py:51
  59.1 11.5 %collective-permute-start.18 = (f32[256,256]{1,0:T(8,128)S(1)}, f32[256,256]{1,0:T(8,128)S(1)}, u32[]{:S(2)}, u32[]{:S(2)}) collective-permute-start(f32[256,256]{1,0:T(8,128)S(1)} %slice_bitcast_fusion), channel_id=1, source_target_pairs={{0,24},{1,25},{2,26},{3,27},{4,28},{5,29},{6,30},{7,31},{8,16},{9,... | collective-permute-start | bytes 786440 | tf_op jit(solution)/shard_map/ppermute | solution.py:51
  62.2 9.4 %collective-permute-start.19 = (f32[256,256]{1,0:T(8,128)S(1)}, f32[256,256]{1,0:T(8,128)S(1)}, u32[]{:S(2)}, u32[]{:S(2)}) collective-permute-start(f32[256,256]{1,0:T(8,128)S(1)} %get-tuple-element.55), channel_id=1, source_target_pairs={{0,2},{1,3},{2,4},{3,5},{4,6},{5,7},{6,0},{7,1},{8,10},{9,11},{10,... | collective-permute-start | bytes 786440 | tf_op jit(solution)/shard_map/ppermute | solution.py:47
  62.9 8.6 %collective-permute-start.20 = (f32[256,256]{1,0:T(8,128)S(1)}, f32[256,256]{1,0:T(8,128)S(1)}, u32[]{:S(2)}, u32[]{:S(2)}) collective-permute-start(f32[256,256]{1,0:T(8,128)S(1)} %get-tuple-element.56), channel_id=1, source_target_pairs={{0,6},{1,7},{2,0},{3,1},{4,2},{5,3},{6,4},{7,5},{8,14},{9,15},{10,... | collective-permute-start | bytes 786440 | tf_op jit(solution)/shard_map/ppermute | solution.py:47
  75.6 10.2 %collective-permute-start.24 = (f32[256,256]{1,0:T(8,128)S(1)}, f32[256,256]{1,0:T(8,128)S(1)}, u32[]{:S(2)}, u32[]{:S(2)}) collective-permute-start(f32[256,256]{1,0:T(8,128)S(1)} %get-tuple-element.62), channel_id=1, source_target_pairs={{0,4},{1,5},{2,6},{3,7},{4,0},{5,1},{6,2},{7,3},{8,12},{9,13},{10,... | collective-permute-start | bytes 786440 | tf_op jit(solution)/shard_map/ppermute | solution.py:47
  80.0 13.4 %collective-permute-start.22 = (f32[1,256,256]{2,1,0:T(8,128)S(1)}, f32[1,256,256]{2,1,0:T(8,128)S(1)}, u32[]{:S(2)}, u32[]{:S(2)}) collective-permute-start(f32[1,256,256]{2,1,0:T(8,128)S(1)} %get-tuple-element.60.refs_4_), channel_id=1, source_target_pairs={{0,8},{1,9},{2,10},{3,11},{4,12},{5,13},{6,14},{7,15},{8,0},{9,1},... | collective-permute-start | bytes 786440 | tf_op jit(solution)/shard_map/ppermute | solution.py:418
  85.9 12.7 %collective-permute-start.25 = (f32[256,256]{1,0:T(8,128)S(1)}, f32[256,256]{1,0:T(8,128)S(1)}, u32[]{:S(2)}, u32[]{:S(2)}) collective-permute-start(f32[256,256]{1,0:T(8,128)S(1)} %ghost_sum.2.refs_2_), channel_id=1, source_target_pairs={{0,112},{1,113},{2,114},{3,115},{4,116},{5,117},{6,118},{7,119},{8... | collective-permute-start | bytes 786440 | tf_op jit(solution)/shard_map/ppermute | solution.py:51
  89.8 15.2 %collective-permute-start.30 = (f32[256,256]{1,0:T(8,128)S(1)}, f32[256,256]{1,0:T(8,128)S(1)}, u32[]{:S(2)}, u32[]{:S(2)}) collective-permute-start(f32[256,256]{1,0:T(8,128)S(1)} %ghost_sum.2.refs_2_), channel_id=1, source_target_pairs={{0,8},{1,9},{2,10},{3,11},{4,12},{5,13},{6,14},{7,15},{8,0},{9,1},... | collective-permute-start | bytes 786440 | tf_op jit(solution)/shard_map/ppermute | solution.py:418
  92.2 33.8 %collective-permute-start.23 = (f32[3,256,256]{2,1,0:T(8,128)S(1)}, f32[3,256,256]{2,1,0:T(8,128)S(1)}, u32[]{:S(2)}, u32[]{:S(2)}) collective-permute-start(f32[3,256,256]{2,1,0:T(8,128)S(1)} %get-tuple-element.61), channel_id=1, source_target_pairs={{0,8},{1,9},{2,10},{3,11},{4,12},{5,13},{6,14},{7,15},{8,0},{9,1},... | collective-permute-start | bytes 2359304 | tf_op jit(solution)/shard_map/ppermute | solution.py:418
  105.0 20.9 %collective-permute-start.31 = (f32[2,256,256]{2,1,0:T(8,128)S(1)}, f32[2,256,256]{2,1,0:T(8,128)S(1)}, u32[]{:S(2)}, u32[]{:S(2)}) collective-permute-start(f32[2,256,256]{2,1,0:T(8,128)S(1)} %new_pair.1.refs_0_), channel_id=1, source_target_pairs={{0,6},{1,7},{2,0},{3,1},{4,2},{5,3},{6,4},{7,5},{8,14},{9,15},{10,... | collective-permute-start | bytes 1572872 | tf_op jit(solution)/shard_map/ppermute | solution.py:47
  107.6 18.3 %collective-permute-start.32 = (f32[2,256,256]{2,1,0:T(8,128)S(1)}, f32[2,256,256]{2,1,0:T(8,128)S(1)}, u32[]{:S(2)}, u32[]{:S(2)}) collective-permute-start(f32[2,256,256]{2,1,0:T(8,128)S(1)} %new_pair.1.refs_0_), channel_id=1, source_target_pairs={{0,2},{1,3},{2,4},{3,5},{4,6},{5,7},{6,0},{7,1},{8,10},{9,11},{10,... | collective-permute-start | bytes 1572872 | tf_op jit(solution)/shard_map/ppermute | solution.py:47
  109.0 13.8 %collective-permute-start.26 = (f32[16,256]{1,0:T(8,128)S(1)}, f32[16,256]{1,0:T(8,128)S(1)}, u32[]{:S(2)}, u32[]{:S(2)}) collective-permute-start(f32[16,256]{1,0:T(8,128)S(1)} %get-tuple-element.63), channel_id=1, source_target_pairs={{0,4},{1,5},{2,6},{3,7},{4,8},{5,9},{6,10},{7,11},{8,12},{9,13},{1... | collective-permute-start | bytes 49160 | tf_op jit(solution)/shard_map/ppermute | solution.py:382
  110.9 11.8 %collective-permute-start.27 = (f32[16,256]{1,0:T(8,128)S(1)}, f32[16,256]{1,0:T(8,128)S(1)}, u32[]{:S(2)}, u32[]{:S(2)}) collective-permute-start(f32[16,256]{1,0:T(8,128)S(1)} %get-tuple-element.64), channel_id=1, source_target_pairs={{4,0},{5,1},{6,2},{7,3},{8,4},{9,5},{10,6},{11,7},{12,8},{13,9},{1... | collective-permute-start | bytes 49160 | tf_op jit(solution)/shard_map/ppermute | solution.py:383
  126.1 16.0 %collective-permute-start.33 = (f32[256,256]{1,0:T(8,128)S(1)}, f32[256,256]{1,0:T(8,128)S(1)}, u32[]{:S(2)}, u32[]{:S(2)}) collective-permute-start(f32[256,256]{1,0:T(8,128)S(1)} %get-tuple-element.68), channel_id=1, source_target_pairs={{0,2},{1,3},{2,4},{3,5},{4,6},{5,7},{6,0},{7,1},{8,10},{9,11},{10,... | collective-permute-start | bytes 786440 | tf_op jit(solution)/shard_map/ppermute | solution.py:47
  127.1 16.5 %collective-permute-start.34 = (f32[256,256]{1,0:T(8,128)S(1)}, f32[256,256]{1,0:T(8,128)S(1)}, u32[]{:S(2)}, u32[]{:S(2)}) collective-permute-start(f32[256,256]{1,0:T(8,128)S(1)} %get-tuple-element.69), channel_id=1, source_target_pairs={{0,4},{1,5},{2,6},{3,7},{4,0},{5,1},{6,2},{7,3},{8,12},{9,13},{10,... | collective-permute-start | bytes 786440 | tf_op jit(solution)/shard_map/ppermute | solution.py:47
  127.1 16.5 %collective-permute-start.35 = (f32[256,256]{1,0:T(8,128)S(1)}, f32[256,256]{1,0:T(8,128)S(1)}, u32[]{:S(2)}, u32[]{:S(2)}) collective-permute-start(f32[256,256]{1,0:T(8,128)S(1)} %get-tuple-element.70), channel_id=1, source_target_pairs={{0,6},{1,7},{2,0},{3,1},{4,2},{5,3},{6,4},{7,5},{8,14},{9,15},{10,... | collective-permute-start | bytes 786440 | tf_op jit(solution)/shard_map/ppermute | solution.py:47
  129.9 20.6 %collective-permute-start.39 = (f32[2,256,256]{2,1,0:T(8,128)S(1)}, f32[2,256,256]{2,1,0:T(8,128)S(1)}, u32[]{:S(2)}, u32[]{:S(2)}) collective-permute-start(f32[2,256,256]{2,1,0:T(8,128)S(1)} %new_pair.1.refs_0_), channel_id=1, source_target_pairs={{0,1},{1,0},{2,3},{3,2},{4,5},{5,4},{6,7},{7,6},{8,9},{9,8},{10,11... | collective-permute-start | bytes 1572872 | tf_op jit(solution)/shard_map/ppermute | solution.py:394
  140.3 9.5 %collective-permute-start.37 = (f32[256,256]{1,0:T(8,128)S(1)}, f32[256,256]{1,0:T(8,128)S(1)}, u32[]{:S(2)}, u32[]{:S(2)}) collective-permute-start(f32[256,256]{1,0:T(8,128)S(1)} %get-tuple-element.72), channel_id=1, source_target_pairs={{0,2},{1,3},{2,4},{3,5},{4,6},{5,7},{6,0},{7,1},{8,10},{9,11},{10,... | collective-permute-start | bytes 786440 | tf_op jit(solution)/shard_map/ppermute | solution.py:47
  142.0 8.3 %collective-permute-start.38 = (f32[256,256]{1,0:T(8,128)S(1)}, f32[256,256]{1,0:T(8,128)S(1)}, u32[]{:S(2)}, u32[]{:S(2)}) collective-permute-start(f32[256,256]{1,0:T(8,128)S(1)} %get-tuple-element.73), channel_id=1, source_target_pairs={{0,6},{1,7},{2,0},{3,1},{4,2},{5,3},{6,4},{7,5},{8,14},{9,15},{10,... | collective-permute-start | bytes 786440 | tf_op jit(solution)/shard_map/ppermute | solution.py:47
  150.4 9.7 %collective-permute-start.36 = (f32[256,256]{1,0:T(8,128)S(1)}, f32[256,256]{1,0:T(8,128)S(1)}, u32[]{:S(2)}, u32[]{:S(2)}) collective-permute-start(f32[256,256]{1,0:T(8,128)S(1)} %ghost_sum.3), channel_id=1, source_target_pairs={{0,112},{1,113},{2,114},{3,115},{4,116},{5,117},{6,118},{7,119},{8... | collective-permute-start | bytes 786440 | tf_op jit(solution)/shard_map/ppermute | solution.py:51
  (26 other events, 165.5 us)
